TPU v7x, 32 devices: a whole 2x2x4 slice. The times are simulated.
32 devices in a mesh: fsdp: 4 (over y, x), ctx: 4 (over z), tp: 2 (over core).
Axes of the slice: x: 2, y: 2, z: 4, core: 2. Of those that a mesh axis runs over, the one named last changes fastest.
Arguments:
- tokens: bfloat16 [8, 1024, 2048], P('fsdp', 'ctx'), may hold values from -6 to 6
- cotangent: bfloat16 [8, 1024, 2048], P('fsdp', 'ctx'), may hold values from -6 to 6
- prefix_len: int32 [8], P('fsdp'), may hold values from 102 to 512
- group_order: int32 [8], replicated, may hold values from 0 to 7, each once
- ln_gain: bfloat16 [2048], replicated, may hold values from 0.25 to 1.75
- ln_bias: bfloat16 [2048], replicated, may hold values from -4 to 4
- query_weight: bfloat16 [2048, 2048], P('fsdp', 'tp'), may hold values from -0.125 to 0.125
- query_bias: bfloat16 [2048], P('tp'), may hold values from -4 to 4
- key_weight: bfloat16 [2048, 2048], P('fsdp', 'tp'), may hold values from -0.125 to 0.125
- key_bias: bfloat16 [2048], P('tp'), may hold values from -4 to 4
- value_weight: bfloat16 [2048, 2048], P('fsdp', 'tp'), may hold values from -0.125 to 0.125
- value_bias: bfloat16 [2048], P('tp'), may hold values from -4 to 4
- out_weight: bfloat16 [2048, 2048], P('fsdp', 'tp'), may hold values from -1 to 1
- out_bias: bfloat16 [2048], replicated, may hold values from -4 to 4
- up_weight: bfloat16 [2048, 8192], P('fsdp', 'tp'), may hold values from -0.125 to 0.125
- up_bias: bfloat16 [8192], P('tp'), may hold values from -4 to 4
- down_weight: bfloat16 [2048, 8192], P('fsdp', 'tp'), may hold values from -0.0625 to 0.0625
- down_bias: bfloat16 [2048], replicated, may hold values from -4 to 4
Outputs:
- output: bfloat16 [8, 1024, 2048], P('fsdp', 'ctx')
- input_grad: bfloat16 [8, 1024, 2048], P('fsdp', 'ctx')
- ln_gain_grad: float32 [2048], replicated
- ln_bias_grad: float32 [2048], replicated
- query_weight_grad: float32 [2048, 2048], P('fsdp', 'tp')
- query_bias_grad: float32 [2048], P('tp')
- key_weight_grad: float32 [2048, 2048], P('fsdp', 'tp')
- key_bias_grad: float32 [2048], P('tp')
- value_weight_grad: float32 [2048, 2048], P('fsdp', 'tp')
- value_bias_grad: float32 [2048], P('tp')
- out_weight_grad: float32 [2048, 2048], P('fsdp', 'tp')
- up_weight_grad: float32 [2048, 8192], P('fsdp', 'tp')
- up_bias_grad: float32 [8192], P('tp')
- down_weight_grad: float32 [2048, 8192], P('fsdp', 'tp')
- out_biases_grad: float32 [2048], replicated
Inputs may be any that keep to these rules, and one draw needn't show every extreme that they name: Each number of 0 to 7 appears once; storage rows k * 128 to k * 128 + 127 of every sequence hold positions group_order[k] * 128 onwards.
All inputs are finite; a program needn't handle non-finite values.
Results may differ from a plain program's by a relative error of at most 0.012.
Values may be sent and summed in bfloat16 or wider, within the bound.
No kernel may reach another device: no remote copies, remote signals or barrier semaphores. Data moves between devices by JAX's collectives and lax.ppermute only.
A program may use at most 448 MiB of HBM per device.

v0:
```python
import jax
import jax.numpy as jnp
from jax import lax
from jax.sharding import PartitionSpec as P

HD = 64
ROT = 32
SEQ_LEN = 1024


masked_fill = -1e30
norm_eps = 1e-05


def positions(group_order, row_start, row_count, group_len):
    row_index = row_start + jnp.arange(row_count, dtype=jnp.int32)
    slot_index = row_index // group_len
    offset = row_index - slot_index * group_len
    matches = slot_index[:, None] == jnp.arange(group_order.shape[0], dtype=jnp.int32)[None, :]
    anchor = jnp.sum(jnp.where(matches, group_order[None, :], 0), axis=1)
    return anchor * group_len + offset


def rotary_tables(places):
    half_rot = ROT // 2
    frequency = jnp.power(10000.0, -2.0 * jnp.arange(half_rot, dtype=jnp.float32) / ROT)
    angles = places.astype(jnp.float32)[:, None] * frequency[None, :]
    return (jnp.cos(angles), jnp.sin(angles))


def rotate(tensor, cosine, sine_vals):
    half_rot = cosine.shape[-1]
    front_part = tensor[..., :half_rot]
    back_part = tensor[..., half_rot : 2 * half_rot]
    rest_part = tensor[..., 2 * half_rot :]
    cosine_rows = cosine[:, None, :]
    sine_rows = sine_vals[:, None, :]
    return jnp.concatenate(
        [
            front_part * cosine_rows - back_part * sine_rows,
            back_part * cosine_rows + front_part * sine_rows,
            rest_part,
        ],
        axis=-1,
    )


def gelu_tanh(values_in):
    return jax.nn.gelu(values_in, approximate=True)


def local(
    tokens,
    cotangent,
    prefix_len,
    group_order,
    ln_gain,
    ln_bias,
    query_weight,
    query_bias,
    key_weight,
    key_bias,
    value_weight,
    value_bias,
    out_weight,
    out_bias,
    up_weight,
    up_bias,
    down_weight,
    down_bias,
):
    seq_count, local_rows, model_width = tokens.shape
    token_count = seq_count * local_rows
    inner_width = query_weight.shape[1]
    local_heads = inner_width // HD
    hidden_units = up_weight.shape[1]
    group_len = SEQ_LEN // group_order.shape[0]
    score_scale = HD ** (-0.5)
    own_place = positions(group_order, lax.axis_index("ctx") * local_rows, local_rows, group_len)
    key_place = positions(group_order, 0, SEQ_LEN, group_len)
    cosine, sine_vals = rotary_tables(own_place)
    allowed = (key_place[None, None, None, :] <= own_place[None, None, :, None]) | (
        key_place[None, None, None, :] < prefix_len[:, None, None, None]
    )
    gathered = (
        lax.all_gather(query_weight, "fsdp", axis=0, tiled=True),
        lax.all_gather(key_weight, "fsdp", axis=0, tiled=True),
        lax.all_gather(value_weight, "fsdp", axis=0, tiled=True),
        lax.all_gather(out_weight, "fsdp", axis=0, tiled=True),
        lax.all_gather(up_weight, "fsdp", axis=0, tiled=True),
        lax.all_gather(down_weight, "fsdp", axis=0, tiled=True),
    )
    w_query, w_key, w_value, w_out, w_up, w_down = gathered
    inputs = tokens.reshape(token_count, model_width).astype(jnp.float32)
    centre = jnp.mean(inputs, axis=-1, keepdims=True)
    centred = inputs - centre
    inv_std = lax.rsqrt(jnp.mean(centred * centred, axis=-1, keepdims=True) + norm_eps)
    normed = centred * inv_std
    norm_gain = ln_gain.astype(jnp.float32)
    hidden = (normed * norm_gain + ln_bias.astype(jnp.float32)).astype(jnp.bfloat16)

    def project(weight, bias_vec):
        return jnp.dot(hidden, weight, preferred_element_type=jnp.float32) + bias_vec.astype(
            jnp.float32
        )

    query_rot = rotate(
        project(w_query, query_bias).reshape(seq_count, local_rows, local_heads, HD),
        cosine,
        sine_vals,
    ).astype(jnp.bfloat16)
    key_rot = (
        rotate(
            project(w_key, key_bias).reshape(seq_count, local_rows, local_heads, HD),
            cosine,
            sine_vals,
        )
        .astype(jnp.bfloat16)
        .reshape(seq_count, local_rows, inner_width)
    )
    value_rows = (
        project(w_value, value_bias)
        .astype(jnp.bfloat16)
        .reshape(seq_count, local_rows, inner_width)
    )
    keys_all, values_all = (
        lax.all_gather(key_rot, "ctx", axis=1, tiled=True),
        lax.all_gather(value_rows, "ctx", axis=1, tiled=True),
    )

    def scores_for(key_block):
        key_heads = key_block.reshape(seq_count, key_block.shape[1], local_heads, HD)
        raw_scores = (
            jnp.einsum("bqhd,bkhd->bhqk", query_rot, key_heads, preferred_element_type=jnp.float32)
            * score_scale
        )
        return jnp.where(allowed, raw_scores, masked_fill)

    masked = scores_for(keys_all)
    row_max = jnp.max(masked, axis=-1, keepdims=True)
    exponent = jnp.exp(masked - row_max)
    row_total = jnp.sum(exponent, axis=-1, keepdims=True)
    attn_probs = (exponent / row_total).astype(jnp.bfloat16)
    log_total = row_max + jnp.log(row_total)
    value_heads = values_all.reshape(seq_count, values_all.shape[1], local_heads, HD)
    context = jnp.einsum(
        "bhqk,bkhd->bqhd", attn_probs, value_heads, preferred_element_type=jnp.float32
    )
    context = context.reshape(token_count, inner_width).astype(jnp.bfloat16)
    up_proj = project(w_up, up_bias)
    activated = gelu_tanh(up_proj).astype(jnp.bfloat16)
    partial_out = jnp.dot(context, w_out.T, preferred_element_type=jnp.float32) + jnp.dot(
        activated, w_down.T, preferred_element_type=jnp.float32
    )
    branches = lax.psum(partial_out, "tp")
    output = inputs + branches + out_bias.astype(jnp.float32) + down_bias.astype(jnp.float32)
    output = output.astype(jnp.bfloat16).reshape(seq_count, local_rows, model_width)
    back_query, back_key, back_value, back_out, back_up, back_down = (
        lax.all_gather(query_weight, "fsdp", axis=0, tiled=True),
        lax.all_gather(key_weight, "fsdp", axis=0, tiled=True),
        lax.all_gather(value_weight, "fsdp", axis=0, tiled=True),
        lax.all_gather(out_weight, "fsdp", axis=0, tiled=True),
        lax.all_gather(up_weight, "fsdp", axis=0, tiled=True),
        lax.all_gather(down_weight, "fsdp", axis=0, tiled=True),
    )
    keys_back, values_back = (
        lax.all_gather(key_rot, "ctx", axis=1, tiled=True),
        lax.all_gather(value_rows, "ctx", axis=1, tiled=True),
    )
    grad_out = cotangent.reshape(token_count, model_width)
    grad_context = jnp.dot(grad_out, back_out, preferred_element_type=jnp.float32).astype(
        jnp.bfloat16
    )
    grad_heads = grad_context.reshape(seq_count, local_rows, local_heads, HD)
    key_heads_back = keys_back.reshape(seq_count, keys_back.shape[1], local_heads, HD)
    value_heads_back = values_back.reshape(seq_count, values_back.shape[1], local_heads, HD)
    probs_back = jnp.exp(scores_for(keys_back) - log_total)
    grad_probs = jnp.einsum(
        "bqhd,bkhd->bhqk", grad_heads, value_heads_back, preferred_element_type=jnp.float32
    )
    row_delta = jnp.sum(probs_back * grad_probs, axis=-1, keepdims=True)
    grad_scores = (probs_back * (grad_probs - row_delta)).astype(jnp.bfloat16)
    probs_low = probs_back.astype(jnp.bfloat16)
    grad_query_rot = (
        jnp.einsum(
            "bhqk,bkhd->bqhd", grad_scores, key_heads_back, preferred_element_type=jnp.float32
        )
        * score_scale
    )
    row_count = local_rows * lax.axis_size("ctx")
    grad_key_part = (
        jnp.einsum("bhqk,bqhd->kbhd", grad_scores, query_rot, preferred_element_type=jnp.float32)
        * score_scale
    )
    grad_value_part = jnp.einsum(
        "bhqk,bqhd->kbhd", probs_low, grad_heads, preferred_element_type=jnp.float32
    )
    key_grads = lax.psum_scatter(
        jnp.concatenate(
            [
                grad_key_part.reshape(row_count, seq_count, inner_width),
                grad_value_part.reshape(row_count, seq_count, inner_width),
            ],
            axis=2,
        ),
        "ctx",
        scatter_dimension=0,
        tiled=True,
    )
    key_grads = jnp.transpose(key_grads, (1, 0, 2))
    key_grad_rot = key_grads[:, :, :inner_width].reshape(seq_count, local_rows, local_heads, HD)
    grad_value = (
        key_grads[:, :, inner_width:].astype(jnp.bfloat16).reshape(token_count, inner_width)
    )
    grad_query = (
        rotate(grad_query_rot, cosine, -sine_vals)
        .astype(jnp.bfloat16)
        .reshape(token_count, inner_width)
    )
    grad_key = (
        rotate(key_grad_rot, cosine, -sine_vals)
        .astype(jnp.bfloat16)
        .reshape(token_count, inner_width)
    )
    grad_activated = jnp.dot(grad_out, back_down, preferred_element_type=jnp.float32)
    gelu_pull = jax.vjp(gelu_tanh, up_proj)[1]
    grad_up = gelu_pull(grad_activated)[0].astype(jnp.bfloat16)
    partial_hidden = (
        jnp.dot(grad_query, back_query.T, preferred_element_type=jnp.float32)
        + jnp.dot(grad_key, back_key.T, preferred_element_type=jnp.float32)
        + jnp.dot(grad_value, back_value.T, preferred_element_type=jnp.float32)
        + jnp.dot(grad_up, back_up.T, preferred_element_type=jnp.float32)
    )
    grad_hidden = lax.psum(partial_hidden, "tp")
    grad_scaled = grad_hidden * norm_gain
    grad_normed = inv_std * (
        grad_scaled
        - jnp.mean(grad_scaled, axis=-1, keepdims=True)
        - normed * jnp.mean(grad_scaled * normed, axis=-1, keepdims=True)
    )
    grad_float = grad_out.astype(jnp.float32)
    input_grad = (
        (grad_float + grad_normed).astype(jnp.bfloat16).reshape(seq_count, local_rows, model_width)
    )
    small_terms = (
        jnp.sum(grad_hidden * normed, axis=0),
        jnp.sum(grad_hidden, axis=0),
        jnp.sum(grad_query, axis=0, dtype=jnp.float32),
        jnp.sum(grad_key, axis=0, dtype=jnp.float32),
        jnp.sum(grad_value, axis=0, dtype=jnp.float32),
        jnp.sum(grad_up, axis=0, dtype=jnp.float32),
        jnp.sum(grad_float, axis=0),
    )
    gain_grad, shift_grad, qbias_grad, kbias_grad, vbias_grad, ubias_grad, obias_grad = lax.psum(
        (
            small_terms[0],
            small_terms[1],
            small_terms[2],
            small_terms[3],
            small_terms[4],
            small_terms[5],
            small_terms[6],
        ),
        ("fsdp", "ctx"),
    )
    grads_in = jnp.concatenate([grad_query, grad_key, grad_value, grad_up], axis=1)
    acts_out = jnp.concatenate([context, activated], axis=1)
    left_part = jnp.einsum("tc,tn->cn", hidden, grads_in, preferred_element_type=jnp.float32)
    right_part = jnp.einsum("tc,tn->cn", grad_out, acts_out, preferred_element_type=jnp.float32)
    scattered = lax.psum_scatter(
        jnp.concatenate([left_part, right_part], axis=1), "fsdp", scatter_dimension=0, tiled=True
    )
    weight_grads = lax.psum(scattered, "ctx")
    edge_two = 2 * inner_width
    edge_three = 3 * inner_width
    edge_four = edge_three + hidden_units
    edge_five = edge_four + inner_width
    return (
        output,
        input_grad,
        gain_grad,
        shift_grad,
        weight_grads[:, :inner_width],
        qbias_grad,
        weight_grads[:, inner_width:edge_two],
        kbias_grad,
        weight_grads[:, edge_two:edge_three],
        vbias_grad,
        weight_grads[:, edge_four:edge_five],
        weight_grads[:, edge_three:edge_four],
        ubias_grad,
        weight_grads[:, edge_five:],
        obias_grad,
    )


def solution(mesh):
    return jax.shard_map(
        local,
        mesh=mesh,
        in_specs=(
            P("fsdp", "ctx", None),
            P("fsdp", "ctx", None),
            P("fsdp"),
            P(),
            P(),
            P(),
            P("fsdp", "tp"),
            P("tp"),
            P("fsdp", "tp"),
            P("tp"),
            P("fsdp", "tp"),
            P("tp"),
            P("fsdp", "tp"),
            P(),
            P("fsdp", "tp"),
            P("tp"),
            P("fsdp", "tp"),
            P(),
        ),
        out_specs=(
            P("fsdp", "ctx", None),
            P("fsdp", "ctx", None),
            P(),
            P(),
            P("fsdp", "tp"),
            P("tp"),
            P("fsdp", "tp"),
            P("tp"),
            P("fsdp", "tp"),
            P("tp"),
            P("fsdp", "tp"),
            P("fsdp", "tp"),
            P("tp"),
            P("fsdp", "tp"),
            P(),
        ),
        check_vma=False,
    )
```

profile of v0, /device:TPU:19, one launch (start us, length us, event | category | flops | bytes accessed | tf_op | source)
XLA Modules:
  0.0 2833.5 jit_solution(8669938643243681293)
XLA Ops:
  11.8 2.2 fusion.32
  14.0 49.7 %all-gather.9.cloned.1.call-done = bf16[2048,1024]{1,0:T(8,128)(2,1)} async-done(((bf16[512,1024]{1,0:T(8,128)(2,1)}), bf16[2048,1024]{1,0:T(8,128)(2,1)}) %all-gather.9.cloned.1.call-update) | async-done | bytes 4194320 | tf_op jit(solution)/shard_map/all_gather | solution.py:88
  63.7 6.1 add_convert_fusion
  71.0 47.3 %all-gather.15.cloned.1.call-done = bf16[2048,1024]{1,0:T(8,128)(2,1)} async-done(((bf16[512,1024]{1,0:T(8,128)(2,1)}), bf16[2048,1024]{1,0:T(8,128)(2,1)}) %all-gather.15.cloned.1.call-update) | async-done | bytes 4194320 | tf_op jit(solution)/shard_map/all_gather | solution.py:87
  118.3 5.8 convolution_add_fusion.1
  124.1 2.9 copy.73
  127.0 3.6 reshape.388
  130.6 2.5 slice.114
  133.1 39.8 %all-gather.13.cloned.1.call-done = bf16[2048,1024]{1,0:T(8,128)(2,1)} async-done(((bf16[512,1024]{1,0:T(8,128)(2,1)}), bf16[2048,1024]{1,0:T(8,128)(2,1)}) %all-gather.13.cloned.1.call-update) | async-done | bytes 4194320 | tf_op jit(solution)/shard_map/all_gather | solution.py:86
  172.9 5.8 convolution_add_fusion.2
  178.7 4.5 reshape.399
  183.2 8.4 fusion.57
  191.6 3.6 copy.98
  195.3 3.5 copy.97
  200.7 1.5 pad_maximum_fusion.3
  206.4 2.8 slice.85
  209.2 18.1 all-gather.19.cloned.1.call-done
  227.3 5.2 convolution_convert_fusion
  232.5 2.7 reshape.400
  235.2 2.8 copy.81
  238.0 2.4 copy.99
  240.3 68.2 %all-gather.11.cloned.1.call-done = bf16[2,1024,1024]{2,1,0:T(8,128)(2,1)} async-done(((bf16[2,256,1024]{2,1,0:T(8,128)(2,1)}), bf16[2,1024,1024]{2,1,0:T(8,128)(2,1)}) %all-gather.11.cloned.1.call-update) | async-done | bytes 4194320 | tf_op jit(solution)/shard_map/all_gather | solution.py:128
  308.6 6.2 copy.68
  314.8 74.6 %all-gather.17.cloned.1.call-done = bf16[2,1024,1024]{1,2,0:T(8,128)(2,1)} async-done(((bf16[2,256,1024]{1,2,0:T(8,128)(2,1)}), bf16[2,1024,1024]{1,2,0:T(8,128)(2,1)}) %all-gather.17.cloned.1.call-update) | async-done | bytes 4194320 | tf_op jit(solution)/shard_map/all_gather | solution.py:127
  389.4 20.1 fusion.59
  409.5 14.6 fusion
  424.0 22.3 multiply_reduce_fusion
  446.4 29.7 %multiply_convert_fusion = bf16[2,16,256,1024]{3,2,1,0:T(8,128)(2,1)} fusion(f32[2,16,256,1024]{3,2,1,0:T(8,128)} %get-tuple-element.72, f32[2,16,256,1024]{3,2,1,0:T(8,128)} %get-tuple-element.70, f32[2,16,256]{2,1,0:T(8,128)S(1)} %get-tuple-element.71, f32[2,16,256]{2,1,0:T(8,128)S(1)} %log_add_fusion), kind=kLoop, calls=%fused_computation.1 | loop fusion | flops 33554432 | bytes 83951616 | tf_op jit(solution)/shard_map/convert_element_type | solution.py:182
  476.1 12.2 broadcast_multiply_fusion
  488.3 17.0 fusion.2
  505.2 11.9 pad_maximum_fusion.1
  517.8 15.1 fusion.43
  535.2 1.3 copy.88
  536.5 13.7 multiply_bitcast_fusion
  550.2 1.3 slice.91
  551.6 14.7 fusion.61
  566.3 141.7 %all-gather.23.cloned.1.call-done = bf16[2048,4096]{1,0:T(8,128)(2,1)} async-done(((bf16[512,4096]{1,0:T(8,128)(2,1)}), bf16[2048,4096]{1,0:T(8,128)(2,1)}) %all-gather.23.cloned.1.call-update) | async-done | bytes 16777232 | tf_op jit(solution)/shard_map/all_gather | solution.py:91
  708.0 22.4 convert_reduce_fusion
  730.4 22.1 convolution_bitcast_fusion
  752.5 239.0 %reduce-scatter.3.cloned.1.call-done = f32[256,2,2048]{0,2,1:T(8,128)} async-done(((f32[1024,2,2048]{0,2,1:T(8,128)}), f32[256,2,2048]{0,2,1:T(8,128)}) %reduce-scatter.3.cloned.1.call-update) | async-done | bytes 4194320 | tf_op jit(solution)/shard_map/reduce_scatter | solution.py:198
  991.5 4.0 convert_reduce_fusion.3
  996.0 1.9 convert_reduce_fusion.4
  999.2 1.3 copy.87
  1000.5 2.3 copy.82
  1002.8 1.2 copy.103
  1004.0 2.3 copy.86
  1006.3 1.5 copy.85
  1007.8 26.3 fusion.13
  1034.1 65.5 %pad_maximum_fusion = f32[2048,12288]{1,0:T(8,128)} fusion(f32[2048,5120]{1,0:T(8,128)} %convolution_bitcast_fusion, f32[2048,7168]{1,0:T(8,128)} %fusion.13), kind=kLoop, calls=%fused_computation | loop fusion | flops 25165824 | bytes 201326592 | tf_op jit(solution)/shard_map/concatenate | solution.py:271
  1100.8 6.8 fusion.60
  1107.7 16.1 convolution_add_fusion
  1123.8 4.4 fusion.63
  1128.2 4.4 fusion.62
  1132.6 4.4 fusion.64
  1137.0 18.7 add_add_fusion
  1155.8 772.4 %reduce-scatter.5.cloned.1.call-done = f32[512,12288]{1,0:T(8,128)} async-done(((f32[2048,12288]{1,0:T(8,128)}), f32[512,12288]{1,0:T(8,128)}) %reduce-scatter.5.cloned.1.call-update) | async-done | bytes 25165840 | tf_op jit(solution)/shard_map/reduce_scatter | solution.py:270
  1928.8 2.0 convert_reduce_fusion.2
  1931.0 40.1 %all-reduce.7.cloned.1.call-done = (f32[512,2048]{1,0:T(8,128)}, f32[512,2048]{1,0:T(8,128)}) async-done(((f32[512,2048]{1,0:T(8,128)}, f32[512,2048]{1,0:T(8,128)}), (f32[512,2048]{1,0:T(8,128)}, f32[512,2048]{1,0:T(8,128)})) %all-reduce.7.cloned.1.call-update) | async-done | bytes 8388624 | tf_op jit(solution)/shard_map/psum | solution.py:155
  1971.1 3.6 fusion.38
  1974.8 67.2 %all-reduce = (f32[2048]{0:T(1024)}, f32[2048]{0:T(1024)}, f32[1024]{0:T(1024)}, f32[1024]{0:T(1024)}, f32[1024]{0:T(1024)}, /*index=5*/f32[4096]{0:T(1024)}, f32[2048]{0:T(1024)}) all-reduce(f32[2048]{0:T(1024)S(1)} %get-tuple-element.15, f32[2048]{0:T(1024)S(1)} %get-tuple-element.18, ...), channel_id=1, replica_groups=mesh['fsdp'=4,'ctx'=4,'tp'=2] {'fsdp','ctx'}, use_global_device_ids=true, to_apply=%region_13.14 | all-reduce | flops 13312 | bytes 106496 | tf_op jit(solution)/shard_map/psum | solution.py:254
  2042.0 6.8 fusion.37
  2048.8 759.1 %all-reduce.5.cloned.1.call-done = f32[512,12288]{1,0:T(8,128)} async-done(((f32[512,12288]{1,0:T(8,128)}), f32[512,12288]{1,0:T(8,128)}) %all-reduce.5.cloned.1.call-update) | async-done | bytes 25165840 | tf_op jit(solution)/shard_map/psum | solution.py:273
  2807.8 7.5 fusion.56
  2815.3 11.1 fusion.55
  (150 shorter events, 18.5 us)
Async XLA Ops:
  7.2 2.9 copy-start
  7.2 4.0 copy-start.34
  7.2 4.0 copy-start.30
  7.2 4.0 copy-start.31
  7.2 56.5 %all-gather.9.cloned.1.call-start = ((), (), s32[]{:S(2)}) async-start(), calls=%async_computation.2 | async-start | bytes 5242880 | tf_op jit(solution)/shard_map/all_gather | solution.py:88
  8.0 110.3 %all-gather.15.cloned.1.call-start = ((), (), s32[]{:S(2)}) async-start(), calls=%async_computation.5 | async-start | bytes 5242880 | tf_op jit(solution)/shard_map/all_gather | solution.py:87
  8.7 164.2 %all-gather.13.cloned.1.call-start = ((), (), s32[]{:S(2)}) async-start(), calls=%async_computation.4 | async-start | bytes 5242880 | tf_op jit(solution)/shard_map/all_gather | solution.py:86
  9.4 217.9 %all-gather.19.cloned.1.call-start = ((), (), s32[]{:S(2)}) async-start(), calls=%async_computation.7 | async-start | bytes 5242880 | tf_op jit(solution)/shard_map/all_gather | solution.py:89
  10.0 298.6 %all-gather.11.cloned.1.call-start = ((), (), s32[]{:S(2)}) async-start(), calls=%async_computation.3 | async-start | bytes 5242880 | tf_op jit(solution)/shard_map/all_gather | solution.py:128
  10.4 0.8 copy-start.21
  11.2 0.6 copy-start.23
  11.2 0.6 copy-start.18
  14.0 56.1 %copy-start.35 = (bf16[1024]{0:T(1024)(128)(2,1)S(1)}, bf16[1024]{0:T(1024)(128)(2,1)}, u32[]{:S(2)}) copy-start(bf16[1024]{0:T(1024)(128)(2,1)} %param.25) | copy-start | bytes 6148
  14.0 56.1 %copy-start.36 = (bf16[1024]{0:T(1024)(128)(2,1)S(1)}, bf16[1024]{0:T(1024)(128)(2,1)}, u32[]{:S(2)}) copy-start(bf16[1024]{0:T(1024)(128)(2,1)} %param.27) | copy-start | bytes 6148
  14.0 56.2 %copy-start.37 = (s32[8]{0:T(128)S(1)}, s32[8]{0:T(128)}, u32[]{:S(2)}) copy-start(s32[8]{0:T(128)} %param.21) | copy-start | bytes 100
  14.0 104.3 %copy-start.3 = (bf16[512,2048]{1,0:T(8,128)(2,1)S(1)}, bf16[512,2048]{1,0:T(8,128)(2,1)}, u32[]{:S(2)}) copy-start(bf16[512,2048]{1,0:T(8,128)(2,1)} %fusion.32) | copy-start | bytes 6291460
  69.8 319.6 %all-gather.17.cloned.1.call-start = ((), (), s32[]{:S(2)}) async-start(), calls=%async_computation.6 | async-start | bytes 5242880 | tf_op jit(solution)/shard_map/all_gather | solution.py:127
  71.0 128.1 %copy-start.16 = (f32[256,16]{0,1:T(8,128)}, f32[256,16]{0,1:T(8,128)S(1)}, u32[]{:S(2)}) copy-start(f32[256,16]{0,1:T(8,128)S(1)} %get-tuple-element.68) | copy-start | bytes 49156
  191.6 7.1 copy-start.5
  198.7 2.0 copy-start.15
  203.4 1.7 copy-start.38
  203.4 348.2 %all-gather.21.cloned.1.call-start = ((), (), s32[]{:S(2)}) async-start(), calls=%async_computation.8 | async-start | bytes 20971520 | tf_op jit(solution)/shard_map/all_gather | solution.py:90
  204.1 503.8 %all-gather.23.cloned.1.call-start = ((), (), s32[]{:S(2)}) async-start(), calls=%async_computation.9 | async-start | bytes 20971520 | tf_op jit(solution)/shard_map/all_gather | solution.py:91
  204.9 786.6 %reduce-scatter.3.cloned.1.call-start = ((), (), s32[]{:S(2)}) async-start(), calls=%async_computation.10 | async-start | bytes 20971520 | tf_op jit(solution)/shard_map/reduce_scatter | solution.py:198
  240.3 149.1 %copy-start.7 = (bf16[2,256,16,32]{1,3,2,0:T(8,128)(2,1)S(1)}, bf16[2,256,16,32]{1,3,2,0:T(8,128)(2,1)}, u32[]{:S(2)}) copy-start(bf16[2,256,16,32]{1,3,2,0:T(8,128)(2,1)} %copy.99) | copy-start | bytes 1572868
  240.3 149.1 %copy-start.8 = (pred[2,256,1024]{2,1,0:T(8,128)(4,1)S(1)}, pred[2,256,1024]{2,1,0:T(8,128)(4,1)}, u32[]{:S(2)}) copy-start(pred[2,256,1024]{2,1,0:T(8,128)(4,1)} %broadcast_or_fusion) | copy-start | bytes 1572868
  240.3 149.1 %copy-start.14 = (bf16[2,256,16,16]{1,3,2,0:T(8,128)(2,1)S(1)}, bf16[2,256,16,16]{1,3,2,0:T(8,128)(2,1)}, u32[]{:S(2)}) copy-start(bf16[2,256,16,16]{1,3,2,0:T(8,128)(2,1)} %get-tuple-element.57) | copy-start | bytes 786436
  409.5 14.6 copy-start.2
  517.1 0.7 copy-start.29
  517.1 1411.0 %reduce-scatter.5.cloned.1.call-start = ((), (), s32[]{:S(2)}) async-start(), calls=%async_computation.11 | async-start | bytes 125829120 | tf_op jit(solution)/shard_map/reduce_scatter | solution.py:270
  534.3 1.0 copy-start.9
  536.5 15.0 copy-start.4
  752.5 243.1 %copy-start.17 = (f32[256,16]{0,1:T(8,128)S(1)}, f32[256,16]{0,1:T(8,128)}, u32[]{:S(2)}) copy-start(f32[256,16]{0,1:T(8,128)} %copy-done.16) | copy-start | bytes 49156
  752.5 243.1 %copy-start.20 = (f32[256,16]{0,1:T(8,128)S(1)}, f32[256,16]{0,1:T(8,128)}, u32[]{:S(2)}) copy-start(f32[256,16]{0,1:T(8,128)} %get-tuple-element.66) | copy-start | bytes 49156
  991.5 4.1 copy-start.6
  999.2 7.1 copy-start.11
  1099.6 1.2 copy-start.10
  1099.6 871.4 %all-reduce.7.cloned.1.call-start = ((), (), s32[]{:S(2)}) async-start(), calls=%async_computation.13 | async-start | bytes 16777216 | tf_op jit(solution)/shard_map/psum | solution.py:155
  1107.7 16.1 copy-start.12
  1107.7 16.1 copy-start.40
  1123.8 4.4 copy-start.13
  1123.8 4.4 copy-start.41
  1128.2 4.4 copy-start.39
  1155.7 1652.1 %all-reduce.5.cloned.1.call-start = ((), (), s32[]{:S(2)}) async-start(), calls=%async_computation.12 | async-start | bytes 50331648 | tf_op jit(solution)/shard_map/psum | solution.py:273
  1928.1 0.7 copy-start.32
  1928.1 0.7 copy-start.33
  1928.1 2.7 copy-start.26
  1928.1 2.8 copy-start.25
  1928.1 43.0 %copy-start.1 = (bf16[2,256,2048]{2,1,0:T(8,128)(2,1)S(1)}, bf16[2,256,2048]{2,1,0:T(8,128)(2,1)}, u32[]{:S(2)}) copy-start(bf16[2,256,2048]{2,1,0:T(8,128)(2,1)} %param.18) | copy-start | bytes 6291460
  1928.1 43.0 %copy-start.19 = (f32[2048]{0:T(1024)S(1)}, f32[2048]{0:T(1024)}, u32[]{:S(2)}) copy-start(f32[2048]{0:T(1024)} %copy-done.18) | copy-start | bytes 24580
  1928.1 43.0 %copy-start.22 = (f32[1,2,2,128]{3,1,2,0:T(2,128)S(1)}, f32[1,2,2,128]{3,1,2,0:T(2,128)}, u32[]{:S(2)}) copy-start(f32[1,2,2,128]{3,1,2,0:T(2,128)} %copy-done.21) | copy-start | bytes 6148
  1928.2 42.9 %copy-start.24 = (f32[1,2,2,128]{3,1,2,0:T(2,128)S(1)}, f32[1,2,2,128]{3,1,2,0:T(2,128)}, u32[]{:S(2)}) copy-start(f32[1,2,2,128]{3,1,2,0:T(2,128)} %copy-done.23) | copy-start | bytes 6148
  1928.8 45.9 %copy-start.27 = (f32[4096]{0:T(1024)S(1)}, f32[4096]{0:T(1024)}, u32[]{:S(2)}) copy-start(f32[4096]{0:T(1024)} %get-tuple-element.28) | copy-start | bytes 49156
  1928.8 45.9 %copy-start.28 = (f32[1024]{0:T(1024)S(1)}, f32[1024]{0:T(1024)}, u32[]{:S(2)}) copy-start(f32[1024]{0:T(1024)} %get-tuple-element.30) | copy-start | bytes 12292
Sparse Core Ops, SparseCore 0:
  9.9 53.7 all-gather.8
  65.5 52.6 all-gather.14
  120.1 52.6 all-gather.12
  174.6 52.6 all-gather.18
  229.3 79.2 all-gather.10
  310.6 78.7 all-gather.16
  391.2 157.4 all-gather.20
  550.5 157.4 all-gather.22
  710.3 281.1 reduce-scatter.2
  1099.8 828.3 reduce-scatter.4
  1931.3 39.7 all-reduce.6
  1973.4 834.3 all-reduce.4
where the time goes:
time: 2840 us; the launch traced here: 2830 us
  waiting for transfers between devices  2250 us (79%)
  matrix products  264 us (9%)
  other arithmetic  148 us (5%)
  local copies, waits for them, and re-layouts  84.7 us (3%)
  blocking collectives  67.2 us (2%)
    reduce_scatter x1, waiting for transfers between devices, local(): lax.psum_scatter(jnp.concatenate([left_part, right_part], axis=1), 'fsdp'...  772 us
    psum x1, waiting for transfers between devices, local(): weight_grads = lax.psum(scattered, 'ctx')  759 us
    reduce_scatter x1, waiting for transfers between devices, local(): lax.psum_scatter(jnp.concatenate([grad_key_part.reshape(row_count, seq_co...  239 us
    all_gather x1, waiting for transfers between devices, local(): lax.all_gather(down_weight, 'fsdp', axis=0, tiled=True)  142 us
    all_gather x1, waiting for transfers between devices, local(): lax.all_gather(key_rot, 'ctx', axis=1, tiled=True)  74.6 us
    all_gather x1, waiting for transfers between devices, local(): lax.all_gather(value_rows, 'ctx', axis=1, tiled=True)  68.2 us
    psum x1, blocking collectives, local(): lax.psum((small_terms[0], small_terms[1], small_terms[2], small_terms[3],...  67.2 us
    concatenate x1, other arithmetic, local(): jnp.concatenate([left_part, right_part], axis=1)  65.5 us
  transfers between devices with their start and end apart: 12, of which 11 were waited for; matrix products, arithmetic and copies ran while one was open for 13% of the time, Pallas kernels for 0%

commit v1 on v0

v1 whole, which is shorter than its diff:
```python
import functools

import jax
import jax.numpy as jnp
from jax import lax
from jax.experimental import pallas as pl
from jax.experimental.pallas import tpu as pltpu
from jax.sharding import PartitionSpec as P

HD = 64
ROT = 32
HALF = ROT // 2
PAIR = 2 * HD
NEG = -1e30
EPS = 1e-05
LOG2E = 1.4426950408889634
GELU_C = 0.7978845608028654
GELU_A = 0.044715
F32 = jnp.float32
BF16 = jnp.bfloat16


def xor_swap(value, axis, size, step):
    return lax.ppermute(value, axis, [(j, j ^ step) for j in range(size)])


def line_gather(mine, axis, size):
    left, right = [mine], [mine]
    for step in range(1, size):
        left.append(lax.ppermute(left[-1], axis, [(j, j + 1) for j in range(step - 1, size - 1)]))
        right.append(lax.ppermute(right[-1], axis, [(j, j - 1) for j in range(1, size - step + 1)]))
    return left, right


def by_distance(left, right, here):
    size = len(left)
    return [left[0]] + [
        jnp.where(here >= m, left[m], right[size - m]) for m in range(1, size)
    ]


def line_scatter_sum(parts, axis, size):
    add = lambda a, b: (a.astype(F32) + b.astype(F32)).astype(BF16)
    toward_right, toward_left = None, None
    for step in range(1, size):
        out_r = parts[step] if toward_right is None else add(toward_right, parts[step])
        out_l = parts[size - step] if toward_left is None else add(toward_left, parts[size - step])
        toward_right = lax.ppermute(out_r, axis, [(j, j + 1) for j in range(min(step, size - 1))])
        toward_left = lax.ppermute(
            out_l, axis, [(j, j - 1) for j in range(max(size - step, 1), size)]
        )
    return parts[0].astype(F32) + toward_right.astype(F32) + toward_left.astype(F32)


def rotate(x, cos, sa, sb):
    return (
        x * cos + pltpu.roll(x, PAIR - HALF, axis=1) * sa + pltpu.roll(x, HALF, axis=1) * sb
    )


def attention_kernel(
    glen, qblock, most,
    offs_ref, prefix_ref,
    qkv_ref, do_ref, cos_ref, sa_ref, sb_ref,
    ctx_ref, dqkv_ref,
    qm, qtm, k_s, kt_s, v_s, vt_s, dom, dotm, ot, dqt, dk_acc, dv_acc,
):
    length = cos_ref.shape[0]
    blocks = length // glen
    lane = lax.broadcasted_iota(jnp.int32, (glen, PAIR), 1)
    for p in range(blocks):
        rows = pl.ds(pl.multiple_of(offs_ref[p], glen), glen)
        to = slice(p * glen, (p + 1) * glen)
        cos, sa, sb = cos_ref[to, :], sa_ref[to, :], sb_ref[to, :]
        q = rotate(qkv_ref[0, rows, 0:PAIR], cos, sa, sb).astype(BF16).astype(F32) * (HD**-0.5)
        do = do_ref[0, rows, :].astype(F32)
        k_s[to, :] = rotate(qkv_ref[0, rows, PAIR : 2 * PAIR], cos, sa, sb).astype(BF16)
        v_s[to, :] = qkv_ref[0, rows, 2 * PAIR : 3 * PAIR].astype(BF16)
        for h in range(2):
            keep = (lane >= h * HD) & (lane < (h + 1) * HD)
            qm[h, to, :] = jnp.where(keep, q, 0.0).astype(BF16)
            dom[h, to, :] = jnp.where(keep, do, 0.0).astype(BF16)
    for h in range(2):
        qtm[h] = qm[h].T
        dotm[h] = dom[h].T
    kt_s[...] = k_s[...].T.reshape(2, HD, length)
    vt_s[...] = v_s[...].T.reshape(2, HD, length)
    dk_acc[...] = jnp.zeros_like(dk_acc)
    dv_acc[...] = jnp.zeros_like(dv_acc)
    prefix = prefix_ref[pl.program_id(0)]

    dot = functools.partial(jnp.dot, preferred_element_type=F32)
    for b in range(length // qblock):
        first = b * qblock
        reach = max(first + qblock, most)
        cols = slice(first, first + qblock)
        clear = first if first >= most else 0

        def head(h, _):
            s = dot(k_s[0:reach, :], qtm[h, :, cols]) * LOG2E
            kpos = clear + lax.broadcasted_iota(jnp.int32, (reach - clear, qblock), 0)
            qpos = first + lax.broadcasted_iota(jnp.int32, (1, qblock), 1)
            limit = jnp.maximum(qpos + 1, prefix)
            tail = jnp.where(kpos < limit, s[clear:reach], NEG)
            s = jnp.concatenate([s[:clear], tail], axis=0) if clear else tail
            e = jnp.exp2(s - jnp.max(s, axis=0, keepdims=True))
            prob = e * (1.0 / jnp.sum(e, axis=0, keepdims=True))
            low = prob.astype(BF16)
            ot[h, :, cols] = dot(vt_s[h, :, 0:reach], low)
            dv_acc[0:reach, :] += dot(low, dom[h, cols, :])
            dp = dot(v_s[0:reach, :], dotm[h, :, cols])
            delta = jnp.sum(prob * dp, axis=0, keepdims=True)
            ds = (prob * (dp - delta)).astype(BF16)
            dqt[h, :, cols] = dot(kt_s[h, :, 0:reach], ds)
            dk_acc[0:reach, :] += dot(ds, qm[h, cols, :])
            return 0

        lax.fori_loop(0, 2, head, 0)

    for p in range(blocks):
        rows = pl.ds(pl.multiple_of(offs_ref[p], glen), glen)
        to = slice(p * glen, (p + 1) * glen)
        cos, sa, sb = cos_ref[to, :], -sa_ref[to, :], -sb_ref[to, :]
        ctx_ref[0, rows, :] = ot[:, :, to].reshape(PAIR, glen).T.astype(BF16)
        dq = dqt[:, :, to].reshape(PAIR, glen).T * (HD**-0.5)
        dqkv_ref[0, rows, 0:PAIR] = rotate(dq, cos, sa, sb).astype(BF16)
        dqkv_ref[0, rows, PAIR : 2 * PAIR] = rotate(dk_acc[to, :], cos, sa, sb).astype(BF16)
        dqkv_ref[0, rows, 2 * PAIR : 3 * PAIR] = dv_acc[to, :].astype(BF16)


def attention(qkv, grad_context, offs, prefix, tables):
    seqs, length, _ = qkv.shape
    pairs = grad_context.shape[-1] // PAIR
    glen = length // offs.shape[0]
    qblock = min(256, length)
    most = length // 2
    whole = pl.BlockSpec((length, PAIR), lambda s, p, *_: (0, 0))
    wide = pl.BlockSpec((1, length, 3 * PAIR), lambda s, p, *_: (s, 0, p))
    narrow = pl.BlockSpec((1, length, PAIR), lambda s, p, *_: (s, 0, p))
    vm = pltpu.VMEM
    return pl.pallas_call(
        functools.partial(attention_kernel, glen, qblock, most),
        out_shape=(
            jax.ShapeDtypeStruct((seqs, length, pairs * PAIR), BF16),
            jax.ShapeDtypeStruct((seqs, length, pairs * 3 * PAIR), BF16),
        ),
        grid_spec=pltpu.PrefetchScalarGridSpec(
            num_scalar_prefetch=2,
            grid=(seqs, pairs),
            in_specs=[wide, narrow, whole, whole, whole],
            out_specs=(narrow, wide),
            scratch_shapes=[
                vm((2, length, PAIR), BF16),
                vm((2, PAIR, length), BF16),
                vm((length, PAIR), BF16),
                vm((2, HD, length), BF16),
                vm((length, PAIR), BF16),
                vm((2, HD, length), BF16),
                vm((2, length, PAIR), BF16),
                vm((2, PAIR, length), BF16),
                vm((2, HD, length), F32),
                vm((2, HD, length), F32),
                vm((length, PAIR), F32),
                vm((length, PAIR), F32),
            ],
        ),
        compiler_params=pltpu.CompilerParams(vmem_limit_bytes=40 << 20),
        name="attention",
    )(offs, prefix, qkv, grad_context, *tables)


def place_kernel(size, n_out, width, here_ref, *refs):
    blocks = refs[: 2 * size - 1]
    outs = refs[-n_out:]
    here = here_ref[0]
    m = pl.program_id(0)

    def put(value):
        for o in range(n_out):
            pieces = [
                value[:, c : c + width]
                for c in range(o * width, value.shape[1], n_out * width)
            ]
            whole = pieces[0] if len(pieces) == 1 else jnp.concatenate(pieces, axis=1)
            outs[o][...] = whole.astype(F32)

    @pl.when(m == 0)
    def _():
        put(blocks[0][...])

    for k in range(1, size):

        @pl.when((m == k) & (here >= k))
        def _():
            put(blocks[k][...])

        @pl.when((m == k) & (here < k))
        def _():
            put(blocks[2 * size - 1 - k][...])


def place(left, right, here, columns, out=None, n_out=1, width=None, part=0, parts=1):
    size = len(left)
    rows, span = left[0].shape
    width = width or span
    block = span // n_out
    blocks = left + right[1:]
    ops = list(blocks) + ([] if out is None else list(out))
    spec = pl.BlockSpec((rows, span), lambda m, h: (0, 0))
    out_spec = pl.BlockSpec(
        (rows, block), lambda m, h: (0, lax.rem(h[0] - m + size, size) * parts + part)
    )
    return pl.pallas_call(
        functools.partial(place_kernel, size, n_out, width),
        out_shape=tuple(jax.ShapeDtypeStruct((rows, columns), F32) for _ in range(n_out)),
        grid_spec=pltpu.PrefetchScalarGridSpec(
            num_scalar_prefetch=1,
            grid=(size,),
            in_specs=[spec] * len(blocks)
            + ([] if out is None else [pl.BlockSpec(memory_space=pl.ANY)] * n_out),
            out_specs=tuple(out_spec for _ in range(n_out)),
        ),
        input_output_aliases={} if out is None else {1 + len(blocks) + o: o for o in range(n_out)},
        compiler_params=pltpu.CompilerParams(vmem_limit_bytes=40 << 20),
        name="place",
    )(here.reshape(1), *ops)


def gelu_parts(up):
    inner = GELU_C * (up + GELU_A * up * up * up)
    t = jnp.tanh(inner)
    act = 0.5 * up * (1.0 + t)
    slope = 0.5 * (1.0 + t) + 0.5 * up * (1.0 - t * t) * GELU_C * (1.0 + 3.0 * GELU_A * up * up)
    return act, slope


def local(
    tokens, cotangent, prefix_len, group_order, ln_gain, ln_bias,
    query_weight, query_bias, key_weight, key_bias, value_weight, value_bias,
    out_weight, out_bias, up_weight, up_bias, down_weight, down_bias,
):
    nf, nc, nt = lax.axis_size("fsdp"), lax.axis_size("ctx"), lax.axis_size("tp")
    fi, ci, ti = lax.axis_index("fsdp"), lax.axis_index("ctx"), lax.axis_index("tp")
    seqs, rows, width = tokens.shape
    own_seqs = seqs // nt
    length = rows * nc
    own = own_seqs * rows
    db = width // nf
    inner = query_weight.shape[1] // nc
    units = up_weight.shape[1] // nc
    pairs = inner // PAIR

    def relative(x):
        return jnp.concatenate(
            [lax.dynamic_slice_in_dim(x, (fi ^ k) * db, db, axis=-1) for k in range(nf)], axis=-1
        )

    def columns(w):
        return lax.dynamic_slice_in_dim(w, ci * (w.shape[1] // nc), w.shape[1] // nc, axis=1)

    def by_pairs(arrays):
        return jnp.concatenate(
            [a[..., p * PAIR : (p + 1) * PAIR] for p in range(pairs) for a in arrays], axis=-1
        )

    def gather_rows(w):
        return jnp.concatenate(
            [w] + [xor_swap(w, "fsdp", nf, k) for k in range(1, nf)], axis=0
        )

    w_qkv = gather_rows(by_pairs([columns(query_weight), columns(key_weight), columns(value_weight)]))
    w_up = gather_rows(columns(up_weight))
    w_out = gather_rows(columns(out_weight))
    w_down = gather_rows(columns(down_weight))
    bias_cols = lambda b: lax.dynamic_slice_in_dim(b, ci * (b.shape[0] // nc), b.shape[0] // nc)
    b_qkv = by_pairs([bias_cols(query_bias), bias_cols(key_bias), bias_cols(value_bias)]).astype(F32)
    b_up = bias_cols(up_bias).astype(F32)

    x = lax.dynamic_slice_in_dim(tokens, ti * own_seqs, own_seqs, axis=0).reshape(own, width)
    g_own = lax.dynamic_slice_in_dim(cotangent, ti * own_seqs, own_seqs, axis=0).reshape(own, width)
    x = relative(x).astype(F32)
    g_own = relative(g_own)
    gain, shift = relative(ln_gain).astype(F32), relative(ln_bias).astype(F32)
    centred = x - jnp.mean(x, axis=-1, keepdims=True)
    inv_std = lax.rsqrt(jnp.mean(centred * centred, axis=-1, keepdims=True) + EPS)
    normed = centred * inv_std
    h_own = (normed * gain + shift).astype(BF16)

    def gather_tokens(mine):
        chunks = by_distance(*line_gather(mine, "ctx", nc), ci)
        others = []
        for k in range(1, nt):
            others += [xor_swap(c, "tp", nt, k) for c in chunks]
        out = jnp.stack(chunks + others).reshape(nt, nc, own_seqs, rows, width)
        return jnp.transpose(out, (0, 2, 1, 3, 4)).reshape(seqs * length, width)

    hidden = gather_tokens(h_own)
    grad = gather_tokens(g_own)

    def mm(a, b):
        return jnp.dot(a, b, preferred_element_type=F32)

    def mm_nt(a, b):
        return lax.dot_general(a, b, (((1,), (1,)), ((), ())), preferred_element_type=F32)

    def mm_tn(a, b):
        return lax.dot_general(a, b, (((0,), (0,)), ((), ())), preferred_element_type=F32)

    lane = jnp.arange(PAIR, dtype=jnp.int32)[None, :] % HD
    freq = jnp.power(10000.0, -2.0 * (lane % HALF).astype(F32) / ROT)
    angle = jnp.arange(length, dtype=jnp.int32).astype(F32)[:, None] * freq
    cos = jnp.where(lane < ROT, jnp.cos(angle), 1.0)
    sin = jnp.sin(angle)
    sa = jnp.where(lane < HALF, -sin, 0.0)
    sb = jnp.where((lane >= HALF) & (lane < ROT), sin, 0.0)
    groups = group_order.shape[0]
    glen = length // groups
    places = jnp.arange(groups, dtype=jnp.int32)
    slot = jnp.sum(
        jnp.where(group_order[None, :] == places[:, None], places[None, :], 0), axis=1
    ) * glen
    offs = ((ci - slot // rows + nc) % nc) * rows + slot % rows
    seq_ids = jnp.arange(seqs, dtype=jnp.int32)
    seq_of = ((seq_ids // own_seqs) ^ ti) * own_seqs + seq_ids % own_seqs
    prefix = jnp.sum(
        jnp.where(seq_of[:, None] == seq_ids[None, :], prefix_len[None, :], 0), axis=1
    )

    qkv = (mm(hidden, w_qkv) + b_qkv).reshape(seqs, length, 3 * inner)
    grad_context = mm(grad, w_out).astype(BF16).reshape(seqs, length, inner)
    context, dqkv = attention(
        qkv, grad_context, offs.astype(jnp.int32), prefix.astype(jnp.int32), (cos, sa, sb)
    )
    context = context.reshape(seqs * length, inner)
    dqkv = dqkv.reshape(seqs * length, 3 * inner)

    up = mm(hidden, w_up) + b_up
    act, slope = gelu_parts(up)
    act = act.astype(BF16)
    dup = (mm(grad, w_down) * slope).astype(BF16)

    def scatter_tokens(partial):
        part = partial.astype(BF16).reshape(nt, own_seqs, nc, rows, width)
        parts = []
        for m in range(nc):
            total = part[0, :, m].reshape(own, width).astype(F32)
            for k in range(1, nt):
                total = total + xor_swap(part[k, :, m].reshape(own, width), "tp", nt, k).astype(F32)
            parts.append(total.astype(BF16))
        return line_scatter_sum(parts, "ctx", nc)

    branches = scatter_tokens(mm_nt(act, w_down) + mm_nt(context, w_out))
    out_own = x + branches + relative(out_bias).astype(F32) + relative(down_bias).astype(F32)

    grad_hidden = scatter_tokens(mm_nt(dup, w_up) + mm_nt(dqkv, w_qkv))
    gs = grad_hidden * gain
    grad_normed = inv_std * (
        gs - jnp.mean(gs, axis=-1, keepdims=True)
        - normed * jnp.mean(gs * normed, axis=-1, keepdims=True)
    )
    in_own = g_own.astype(F32) + grad_normed

    def whole_tokens(own_rows):
        mine = relative(own_rows.astype(BF16)).reshape(1, own_seqs, rows, width)
        parts = [mine] + [xor_swap(mine, "tp", nt, k) for k in range(1, nt)]
        full = jnp.zeros((nt, own_seqs, rows, width), BF16)
        for k in range(nt):
            full = lax.dynamic_update_slice_in_dim(full, parts[k], ti ^ k, axis=0)
        return full.reshape(seqs, rows, width)

    output = whole_tokens(out_own)
    input_grad = whole_tokens(in_own)

    def weight_grad(left_act, right_act):
        full = mm_tn(left_act, right_act).astype(BF16)
        total = full[0:db].astype(F32)
        for k in range(1, nf):
            total = total + xor_swap(full[k * db : (k + 1) * db], "fsdp", nf, k).astype(F32)
        return line_gather(total.astype(BF16), "ctx", nc)

    chunk = min(512, units)
    parts = units // chunk
    here = ci.astype(jnp.int32)
    dw_down, dw_up = None, None
    for q in range(parts):
        cut = slice(q * chunk, (q + 1) * chunk)
        dw_down = place(*weight_grad(grad, act[:, cut]), here, units * nc, dw_down, part=q, parts=parts)
    for q in range(parts):
        cut = slice(q * chunk, (q + 1) * chunk)
        dw_up = place(*weight_grad(hidden, dup[:, cut]), here, units * nc, dw_up, part=q, parts=parts)
    dw_out = place(*weight_grad(grad, context), here, inner * nc)
    dw_qkv = place(*weight_grad(hidden, dqkv), here, inner * nc, n_out=3, width=PAIR)

    def over_line(v):
        full = jnp.zeros((nc,) + v.shape, v.dtype)
        for k in range(nc):
            got = v if k == 0 else lax.ppermute(v, "ctx", [(j, (j + k) % nc) for j in range(nc)])
            full = lax.dynamic_update_slice_in_dim(full, got[None], (ci - k + nc) % nc, axis=0)
        return full

    def over_fsdp(v):
        return v + sum(xor_swap(v, "fsdp", nf, k) for k in range(1, nf))

    col_sum = lambda a: jnp.sum(a.astype(F32), axis=0)
    bias_sums = over_fsdp(jnp.concatenate([col_sum(dqkv), col_sum(dup)]))
    wide = over_line(bias_sums)
    qkv_sums = wide[:, : 3 * inner].reshape(nc, pairs, 3, PAIR)
    qb, kb, vb = (qkv_sums[:, :, n].reshape(nc * inner) for n in range(3))
    ub = wide[:, 3 * inner :].reshape(nc * units)
    obias = over_fsdp(relative(col_sum(grad)))

    norm_sums = relative(jnp.stack([col_sum(grad_hidden * normed), col_sum(grad_hidden)]))
    for k in range(1, nt):
        norm_sums = norm_sums + xor_swap(norm_sums, "tp", nt, k)
    norm_sums = over_fsdp(norm_sums)
    norm_sums = jnp.sum(over_line(norm_sums), axis=0)

    return (
        output, input_grad, norm_sums[0], norm_sums[1],
        dw_qkv[0], qb, dw_qkv[1], kb, dw_qkv[2], vb,
        dw_out[0], dw_up[0], ub, dw_down[0], obias,
    )


def solution(mesh):
    rows, flat, cols, one = P("fsdp", "ctx", None), P("fsdp", "tp"), P("tp"), P()
    return jax.shard_map(
        local,
        mesh=mesh,
        in_specs=(
            rows, rows, P("fsdp"), one, one, one,
            flat, cols, flat, cols, flat, cols, flat, one, flat, cols, flat, one,
        ),
        out_specs=(
            rows, rows, one, one, flat, cols, flat, cols, flat, cols, flat, flat, cols, flat, one,
        ),
        check_vma=False,
    )
```

time: 2840 us -> 964 us (0.34)
  waiting for transfers between devices: 2250 us -> 355 us
  starting transfers between devices: 0.65 us -> 270 us
  matrix products: 264 us -> 148 us
  other arithmetic: 148 us -> 51.7 us
  blocking collectives: 67.2 us -> 0 us
  Pallas kernels: 0 us -> 62.1 us
  local copies, waits for them, and re-layouts: 84.7 us -> 56.1 us
    reduce_scatter x2 -> x0, waiting for transfers between devices: 1010 us -> none  [the longest x1 772 us: local(): lax.psum_scatter(jnp.concatenate([left_part, right_part], axis=1), 'fsdp'...]
    psum x2 -> x0, waiting for transfers between devices: 799 us -> none  [the longest x1 759 us: local(): weight_grads = lax.psum(scattered, 'ctx')]
    all_gather x8 -> x0, waiting for transfers between devices: 439 us -> none  [the longest x1 142 us: local(): lax.all_gather(down_weight, 'fsdp', axis=0, tiled=True)]
    ppermute x0 -> x124, waiting for transfers between devices: none -> 355 us  [the longest x24 153 us: line_gather(): lax.ppermute(left[-1], axis, [(j, j + 1) for j in range(step - 1, size -...]
    ppermute x0 -> x124, starting transfers between devices: none -> 270 us  [the longest x58 99.6 us: xor_swap(): return lax.ppermute(value, axis, [(j, j ^ step) for j in range(size)])]
    dot_general x20 -> x14, matrix products: 264 us -> 148 us  [the longest x4 53.8 us: mm_nt(): lax.dot_general(a, b, (((1,), (1,)), ((), ())), preferred_element_type=F32)]
    concatenate x3 -> x4, other arithmetic: 78.9 us -> 1.27 us  [the longest x3 1.26 us: relative(): jnp.concatenate([lax.dynamic_slice_in_dim(x, (fi ^ k) * db, db, axis=-1)...]
    psum x1 -> x0, blocking collectives: 67.2 us -> none  [local(): lax.psum((small_terms[0], small_terms[1], small_terms[2], small_terms[3],...]
  transfers between devices with their start and end apart: 12 -> 124, of which waited for: 11 -> 46; matrix products, arithmetic and copies ran while one was open for 13% -> 25% of each run, Pallas kernels for 0% -> 7%
where the time goes in v1:
time: 964 us; the launch traced here: 948 us
  waiting for transfers between devices  355 us (37%)
  starting transfers between devices  270 us (28%)
  matrix products  148 us (15%)
  Pallas kernels  62.1 us (6%)
  local copies, waits for them, and re-layouts  56.1 us (6%)
  other arithmetic  51.7 us (5%)
    ppermute x24, waiting for transfers between devices, line_gather(): lax.ppermute(left[-1], axis, [(j, j + 1) for j in range(step - 1, size -...  153 us
    ppermute x58, waiting for transfers between devices, xor_swap(): return lax.ppermute(value, axis, [(j, j ^ step) for j in range(size)])  108 us
    ppermute x58, starting transfers between devices, xor_swap(): return lax.ppermute(value, axis, [(j, j ^ step) for j in range(size)])  99.6 us
    ppermute x24, waiting for transfers between devices, line_gather(): lax.ppermute(right[-1], axis, [(j, j - 1) for j in range(1, size - step +...  74.9 us
    ppermute x24, starting transfers between devices, line_gather(): lax.ppermute(right[-1], axis, [(j, j - 1) for j in range(1, size - step +...  74 us
    ppermute x24, starting transfers between devices, line_gather(): lax.ppermute(left[-1], axis, [(j, j + 1) for j in range(step - 1, size -...  64 us
    dot_general x4, matrix products, mm_nt(): lax.dot_general(a, b, (((1,), (1,)), ((), ())), preferred_element_type=F32)  53.8 us
    dot_general x4, matrix products, mm(): return jnp.dot(a, b, preferred_element_type=F32)  48.5 us
  transfers between devices with their start and end apart: 124, of which 46 were waited for; matrix products, arithmetic and copies ran while one was open for 25% of the time, Pallas kernels for 7%

profile of v1, /device:TPU:19, one launch (start us, length us, event | category | flops | bytes accessed | tf_op | source)
XLA Modules:
  0.0 947.5 jit_solution(16244097952321137822)
XLA Ops:
  6.1 4.2 collective-permute-start.19
  16.4 4.4 collective-permute-start
  40.9 11.8 %collective-permute-done.1 = bf16[256,2048]{1,0:T(8,128)(2,1)} collective-permute-done((bf16[256,2048]{1,0:T(8,128)(2,1)}, bf16[256,2048]{1,0:T(8,128)(2,1)}, u32[]{:S(2)}, u32[]{:S(2)}) %collective-permute-start.1) | collective-permute-done | bytes 1048608 | tf_op jit(solution)/shard_map/ppermute | solution.py:31
  55.8 17.4 %collective-permute-done.21 = bf16[256,2048]{1,0:T(8,128)(2,1)} collective-permute-done((bf16[256,2048]{1,0:T(8,128)(2,1)}, bf16[256,2048]{1,0:T(8,128)(2,1)}, u32[]{:S(2)}, u32[]{:S(2)}) %collective-permute-start.21) | collective-permute-done | bytes 1048608 | tf_op jit(solution)/shard_map/ppermute | solution.py:31
  83.9 11.7 %collective-permute-done.2 = bf16[256,2048]{1,0:T(8,128)(2,1)} collective-permute-done((bf16[256,2048]{1,0:T(8,128)(2,1)}, bf16[256,2048]{1,0:T(8,128)(2,1)}, u32[]{:S(2)}, u32[]{:S(2)}) %collective-permute-start.2) | collective-permute-done | bytes 1048608 | tf_op jit(solution)/shard_map/ppermute | solution.py:31
  106.2 18.7 %collective-permute-done.4 = bf16[256,2048]{1,0:T(8,128)(2,1)S(1)} collective-permute-done((bf16[256,2048]{1,0:T(8,128)(2,1)}, bf16[256,2048]{1,0:T(8,128)(2,1)S(1)}, u32[]{:S(2)}, u32[]{:S(2)}) %collective-permute-start.4) | collective-permute-done | bytes 1048608 | tf_op jit(solution)/shard_map/ppermute | solution.py:30
  130.1 15.5 %collective-permute-done.24 = bf16[256,2048]{1,0:T(8,128)(2,1)S(1)} collective-permute-done((bf16[256,2048]{1,0:T(8,128)(2,1)}, bf16[256,2048]{1,0:T(8,128)(2,1)S(1)}, u32[]{:S(2)}, u32[]{:S(2)}) %collective-permute-start.24) | collective-permute-done | bytes 1048608 | tf_op jit(solution)/shard_map/ppermute | solution.py:30
  148.5 19.5 %collective-permute-done.5 = bf16[256,2048]{1,0:T(8,128)(2,1)S(1)} collective-permute-done((bf16[256,2048]{1,0:T(8,128)(2,1)S(1)}, bf16[256,2048]{1,0:T(8,128)(2,1)S(1)}, u32[]{:S(2)}, u32[]{:S(2)}) %collective-permute-start.5) | collective-permute-done | bytes 1048608 | tf_op jit(solution)/shard_map/ppermute | solution.py:30
  168.0 4.3 collective-permute-start.26
  185.5 19.5 %collective-permute-done.12 = bf16[512,1024]{1,0:T(8,128)(2,1)S(1)} collective-permute-done((bf16[512,1024]{1,0:T(8,128)(2,1)S(1)}, bf16[512,1024]{1,0:T(8,128)(2,1)S(1)}, u32[]{:S(2)}, u32[]{:S(2)}) %collective-permute-start.12) | collective-permute-done | bytes 1048608 | tf_op jit(solution)/shard_map/ppermute | solution.py:24
  206.3 17.4 %multiply_convert_fusion = (bf16[2048,1024]{1,0:T(8,128)(2,1)}, f32[2048,1024]{1,0:T(8,128)}) fusion(f32[1024]{0:T(1024)S(1)} %dynamic-slice_convert_fusion, bf16[2048,2048]{1,0:T(8,128)(2,1)} %bitcast.231, bf16[512,1024]{1,0:T(8,128)(2,1)S(1)} %collective-permute-done.12, bf16[512,1024]{1,0:T(8,128)(2,1)S(1)} %collective-permute-done.11, ...), kind=kOutput, calls=%fused_computation.13 | convolution fusion | flops 8627683328 | bytes 25169920 | tf_op jit(solution)/shard_map/dot_general | solution.py:301
  223.7 7.5 convolution_convert_fusion.1
  231.2 6.4 convolution_convert_fusion.2
  239.1 10.9 %collective-permute-done.15 = bf16[512,1024]{1,0:T(8,128)(2,1)S(1)} collective-permute-done((bf16[512,1024]{1,0:T(8,128)(2,1)S(1)}, bf16[512,1024]{1,0:T(8,128)(2,1)S(1)}, u32[]{:S(2)}, u32[]{:S(2)}) %collective-permute-start.15) | collective-permute-done | bytes 1048608 | tf_op jit(solution)/shard_map/ppermute | solution.py:24
  251.3 18.9 %convert_reduce_fusion.1 = (f32[1024]{0:T(1024)S(1)}, bf16[2048,1024]{1,0:T(8,128)(2,1)}) fusion(f32[2048,1024]{1,0:T(8,128)} %get-tuple-element.127, f32[1024]{0:T(1024)S(1)} %dynamic-slice_convert_fusion, bf16[2048,2048]{1,0:T(8,128)(2,1)S(1)} %bitcast.212, bf16[512,1024]{1,0:T(8,128)(2,1)S(1)} %collective-permute-done.15, ...), kind=kOutput, calls=%fused_computation.12 | convolution fusion | flops 8652848128 | bytes 25174016 | tf_op jit(solution)/shard_map/dot_general | solution.py:301
  270.1 10.0 %convolution_convert_fusion.3 = bf16[2048,512]{1,0:T(8,128)(2,1)} fusion(bf16[2048,2048]{1,0:T(8,128)(2,1)} %bitcast.232, bf16[2048,1024]{1,0:T(8,128)(2,1)} %get-tuple-element.129), kind=kOutput, calls=%fused_computation.25 | convolution fusion | flops 4296015872 | bytes 12582912 | tf_op jit(solution)/shard_map/dot_general | solution.py:307
  280.1 9.6 %convolution_convert_fusion.4 = bf16[2048,512]{1,0:T(8,128)(2,1)} fusion(bf16[2048,2048]{1,0:T(8,128)(2,1)} %bitcast.233, bf16[2048,1024]{1,0:T(8,128)(2,1)S(1)} %copy-done.134), kind=kOutput, calls=%fused_computation.26 | convolution fusion | flops 4296015872 | bytes 12582912 | tf_op jit(solution)/shard_map/dot_general | solution.py:307
  297.4 11.6 %collective-permute-done.18 = bf16[512,768]{1,0:T(8,128)(2,1)S(1)} collective-permute-done((bf16[512,768]{1,0:T(8,128)(2,1)S(1)}, bf16[512,768]{1,0:T(8,128)(2,1)S(1)}, u32[]{:S(2)}, u32[]{:S(2)}) %collective-permute-start.18) | collective-permute-done | bytes 786464 | tf_op jit(solution)/shard_map/ppermute | solution.py:24
  309.0 9.8 %broadcast_add_fusion = f32[2048,768]{1,0:T(8,128)S(1)} fusion(f32[768]{0:T(1024)S(1)} %convert_element_type.418, bf16[2048,2048]{1,0:T(8,128)(2,1)} %bitcast.234, bf16[512,768]{1,0:T(8,128)(2,1)S(1)} %collective-permute-done.18, bf16[512,768]{1,0:T(8,128)(2,1)} %collective-permute-done.17, bf16[512,768]{1,0:T(8,128)(2,1)} %copy-done.127, ...), kind=kOutput, calls=%fused_computation.19 | convolution fusion | flops 6456606720 | bytes 17828864 | tf_op jit(solution)/shard_map/dot_general | solution.py:301
  318.9 43.5 %attention.1 = (bf16[2,1024,256]{2,1,0:T(8,128)(2,1)S(1)}, bf16[2,1024,768]{2,1,0:T(8,128)(2,1)S(1)}) custom-call(s32[8]{0:T(128)S(1)} %fusion.56.offs_ref, s32[2]{0:T(128)S(1)} %fusion.55.prefix_ref, f32[2,1024,768]{2,1,0:T(8,128)S(1)} %bitcast.180, bf16[2,1024,256]{2,1,0:T(8,128)(2,1)S(1)} %bitcast.185, f32[1024,128]{1,0:T(8,128)S(1)} %get-tuple-element.103.cos_ref, ...), custom_call_target="tpu_custom_call" | custom-call | tf_op jit(solution)/shard_map/attention/pallas_call | solution.py:141
  371.6 8.9 convolution_convert_fusion
  380.6 11.4 %fusion.45 = f32[2048,2048]{1,0:T(8,128)} fusion(bf16[2048,768]{1,0:T(8,128)(2,1)S(1)} %bitcast.182, bf16[512,768]{1,0:T(8,128)(2,1)S(1)} %copy-done.130, bf16[512,768]{1,0:T(8,128)(2,1)} %collective-permute-done.17, bf16[512,768]{1,0:T(8,128)(2,1)S(1)} %copy-done.128, bf16[512,768]{1,0:T(8,128)(2,1)S(1)} %copy-done.117), kind=kOutput, calls=%fused_computation.139 | convolution fusion | flops 6455033856 | bytes 23068672 | tf_op jit(solution)/shard_map/dot_general | solution.py:304
  392.0 8.1 fusion.50
  400.1 17.2 %add_convert_fusion = bf16[2048,2048]{1,0:T(8,128)(2,1)} fusion(f32[2048,2048]{1,0:T(8,128)} %fusion.45, bf16[2048,1024]{1,0:T(8,128)(2,1)} %get-tuple-element.129, bf16[512,1024]{1,0:T(8,128)(2,1)} %copy-done.124, bf16[512,1024]{1,0:T(8,128)(2,1)} %copy-done.123, bf16[512,1024]{1,0:T(8,128)(2,1)} %copy-done.122, bf16[512,1024]{1,0:T(8,128)(2,1)S(1)} %copy-done.92), kind=kOutput, calls=%fused_computation.1 | convolution fusion | flops 8615100416 | bytes 33554432 | tf_op jit(solution)/shard_map/dot_general | solution.py:304
  417.3 17.1 %add_convert_fusion.1 = bf16[2048,2048]{1,0:T(8,128)(2,1)} fusion(f32[2048,2048]{1,0:T(8,128)} %fusion.50, bf16[2048,1024]{1,0:T(8,128)(2,1)} %get-tuple-element.126, bf16[512,1024]{1,0:T(8,128)(2,1)} %copy-done.126, bf16[512,1024]{1,0:T(8,128)(2,1)} %collective-permute-done.14, bf16[512,1024]{1,0:T(8,128)(2,1)} %copy-done.125, ...), kind=kOutput, calls=%fused_computation.2 | convolution fusion | flops 8615100416 | bytes 33554432 | tf_op jit(solution)/shard_map/dot_general | solution.py:304
  447.2 4.8 collective-permute-done.76
  463.9 9.0 collective-permute-done.113
  475.6 4.6 collective-permute-done.103
  481.5 13.8 %collective-permute-done.104 = bf16[512,512]{1,0:T(8,128)(2,1)S(1)} collective-permute-done((bf16[512,512]{1,0:T(8,128)(2,1)S(1)}, bf16[512,512]{1,0:T(8,128)(2,1)S(1)}, u32[]{:S(2)}, u32[]{:S(2)}) %collective-permute-start.104) | collective-permute-done | bytes 524320 | tf_op jit(solution)/shard_map/ppermute | solution.py:24
  504.0 13.7 %collective-permute-done.95 = bf16[512,512]{1,0:T(8,128)(2,1)S(1)} collective-permute-done((bf16[512,512]{1,0:T(8,128)(2,1)S(1)}, bf16[512,512]{1,0:T(8,128)(2,1)S(1)}, u32[]{:S(2)}, u32[]{:S(2)}) %collective-permute-start.95) | collective-permute-done | bytes 524320 | tf_op jit(solution)/shard_map/ppermute | solution.py:24
  517.7 14.4 %collective-permute-start.44 = (bf16[256,2048]{1,0:T(8,128)(2,1)S(1)}, bf16[256,2048]{1,0:T(8,128)(2,1)S(1)}, u32[]{:S(2)}, u32[]{:S(2)}) collective-permute-start(bf16[256,2048]{1,0:T(8,128)(2,1)S(1)} %get-tuple-element.49), channel_id=1, source_target_pairs={{0,1},{1,0},{2,3},{3,2},{4,5},{5,4},{6,7},{7,6},{8,9},{9,8},{10,11... | collective-permute-start | bytes 3145736 | tf_op jit(solution)/shard_map/ppermute | solution.py:24
  534.3 5.9 collective-permute-done.86
  541.7 8.0 collective-permute-start.79
  556.5 4.0 collective-permute-done.82.refs_4_
  560.5 10.1 %collective-permute-start.33 = (bf16[256,2048]{1,0:T(8,128)(2,1)S(1)}, bf16[256,2048]{1,0:T(8,128)(2,1)S(1)}, u32[]{:S(2)}, u32[]{:S(2)}) collective-permute-start(bf16[256,2048]{1,0:T(8,128)(2,1)S(1)} %get-tuple-element.53), channel_id=1, source_target_pairs={{0,1},{1,0},{2,3},{3,2},{4,5},{5,4},{6,7},{7,6},{8,9},{9,8},{10,11... | collective-permute-start | bytes 3145736 | tf_op jit(solution)/shard_map/ppermute | solution.py:24
  572.6 4.1 collective-permute-done.62
  579.4 4.3 collective-permute-start.80
  585.5 4.9 collective-permute-done.80.refs_2_
  612.6 5.7 collective-permute-done.100.refs_4_
  618.3 6.7 collective-permute-start.48
  625.0 4.9 collective-permute-start.35
  629.9 5.6 collective-permute-start.37
  636.2 23.2 %collective-permute-start.91 = (bf16[512,512]{1,0:T(8,128)(2,1)S(1)}, bf16[512,512]{1,0:T(8,128)(2,1)S(1)}, u32[]{:S(2)}, u32[]{:S(2)}) collective-permute-start(bf16[512,512]{1,0:T(8,128)(2,1)S(1)} %add_convert_fusion.11.refs_0_), channel_id=1, source_target_pairs={{2,0},{4,2},{6,4},{3,1},{5,3},{7,5},{10,8},{12,10},{14,12},{11,9},... | collective-permute-start | bytes 1572872 | tf_op jit(solution)/shard_map/ppermute | solution.py:31
  660.0 10.8 %collective-permute-done.91.refs_4_ = bf16[512,512]{1,0:T(8,128)(2,1)S(1)} collective-permute-done((bf16[512,512]{1,0:T(8,128)(2,1)S(1)}, bf16[512,512]{1,0:T(8,128)(2,1)S(1)}, u32[]{:S(2)}, u32[]{:S(2)}) %collective-permute-start.91) | collective-permute-done | bytes 524320 | tf_op jit(solution)/shard_map/ppermute | solution.py:31
  676.1 8.7 collective-permute-start.119
  688.8 4.2 collective-permute-start.110
  693.0 15.9 %collective-permute-done.116.refs_2_ = bf16[512,512]{1,0:T(8,128)(2,1)S(1)} collective-permute-done((bf16[512,512]{1,0:T(8,128)(2,1)S(1)}, bf16[512,512]{1,0:T(8,128)(2,1)S(1)}, u32[]{:S(2)}, u32[]{:S(2)}) %collective-permute-start.116) | collective-permute-done | bytes 524320 | tf_op jit(solution)/shard_map/ppermute | solution.py:30
  715.1 5.0 collective-permute-done.107.refs_2_
  723.7 4.1 collective-permute-start.64
  733.2 31.9 %collective-permute-done.89.refs_2_ = bf16[512,512]{1,0:T(8,128)(2,1)S(1)} collective-permute-done((bf16[512,512]{1,0:T(8,128)(2,1)S(1)}, bf16[512,512]{1,0:T(8,128)(2,1)S(1)}, u32[]{:S(2)}, u32[]{:S(2)}) %collective-permute-start.89) | collective-permute-done | bytes 524320 | tf_op jit(solution)/shard_map/ppermute | solution.py:30
  769.9 5.6 collective-permute-done.92.refs_5_
  776.2 5.8 collective-permute-done.64.refs_1_
  783.4 5.0 collective-permute-start.108
  794.5 4.2 collective-permute-start.51
  803.0 12.0 %collective-permute-done.65.refs_2_ = bf16[512,768]{1,0:T(8,128)(2,1)} collective-permute-done((bf16[512,768]{1,0:T(8,128)(2,1)}, bf16[512,768]{1,0:T(8,128)(2,1)}, u32[]{:S(2)}, u32[]{:S(2)}) %collective-permute-start.65) | collective-permute-done | bytes 786464 | tf_op jit(solution)/shard_map/ppermute | solution.py:30
  814.9 4.1 collective-permute-start.99
  828.7 7.5 collective-permute-done.68.refs_5_
  837.8 4.7 collective-permute-start.40
  845.1 10.8 %collective-permute-done.90.refs_3_ = bf16[512,512]{1,0:T(8,128)(2,1)S(1)} collective-permute-done((bf16[512,512]{1,0:T(8,128)(2,1)S(1)}, bf16[512,512]{1,0:T(8,128)(2,1)S(1)}, u32[]{:S(2)}, u32[]{:S(2)}) %collective-permute-start.90) | collective-permute-done | bytes 524320 | tf_op jit(solution)/shard_map/ppermute | solution.py:30
  861.0 4.1 collective-permute-start.49
  891.0 5.3 place.6
  896.4 4.6 collective-permute-start.38
  911.4 11.9 %collective-permute-done.38 = bf16[256,2048]{1,0:T(8,128)(2,1)S(1)} collective-permute-done((bf16[256,2048]{1,0:T(8,128)(2,1)S(1)}, bf16[256,2048]{1,0:T(8,128)(2,1)S(1)}, u32[]{:S(2)}, u32[]{:S(2)}) %collective-permute-start.38) | collective-permute-done | bytes 1048608 | tf_op jit(solution)/shard_map/ppermute | solution.py:48
  923.3 5.6 collective-permute-done.41
  (630 shorter events, 289.3 us)
Async XLA Ops:
  3.9 31.3 %collective-permute-start.20 = (bf16[256,2048]{1,0:T(8,128)(2,1)}, bf16[256,2048]{1,0:T(8,128)(2,1)}, u32[]{:S(2)}, u32[]{:S(2)}) collective-permute-start(bf16[256,2048]{1,0:T(8,128)(2,1)} %pad_maximum_fusion.4), channel_id=1, source_target_pairs={{2,0},{4,2},{6,4},{3,1},{5,3},{7,5},{10,8},{12,10},{14,12},{11,9},... | collective-permute-start | bytes 3145736 | tf_op jit(solution)/shard_map/ppermute | solution.py:31
  6.1 70.8 %collective-permute-start.19 = (bf16[256,2048]{1,0:T(8,128)(2,1)}, bf16[256,2048]{1,0:T(8,128)(2,1)}, u32[]{:S(2)}, u32[]{:S(2)}) collective-permute-start(bf16[256,2048]{1,0:T(8,128)(2,1)} %pad_maximum_fusion.4), channel_id=1, source_target_pairs={{0,2},{2,4},{4,6},{1,3},{3,5},{5,7},{8,10},{10,12},{12,14},{9,11},... | collective-permute-start | bytes 3145736 | tf_op jit(solution)/shard_map/ppermute | solution.py:30
  10.3 163.7 %collective-permute-start.25 = (bf16[256,2048]{1,0:T(8,128)(2,1)}, bf16[256,2048]{1,0:T(8,128)(2,1)}, u32[]{:S(2)}, u32[]{:S(2)}) collective-permute-start(bf16[256,2048]{1,0:T(8,128)(2,1)} %pad_maximum_fusion.4), channel_id=1, source_target_pairs={{0,1},{1,0},{2,3},{3,2},{4,5},{5,4},{6,7},{7,6},{8,9},{9,8},{10,11... | collective-permute-start | bytes 3145736 | tf_op jit(solution)/shard_map/ppermute | solution.py:24
  14.5 38.2 %collective-permute-start.1 = (bf16[256,2048]{1,0:T(8,128)(2,1)}, bf16[256,2048]{1,0:T(8,128)(2,1)}, u32[]{:S(2)}, u32[]{:S(2)}) collective-permute-start(bf16[256,2048]{1,0:T(8,128)(2,1)} %fusion.14), channel_id=1, source_target_pairs={{2,0},{4,2},{6,4},{3,1},{5,3},{7,5},{10,8},{12,10},{14,12},{11,9},... | collective-permute-start | bytes 3145736 | tf_op jit(solution)/shard_map/ppermute | solution.py:31
  16.4 64.7 %collective-permute-start = (bf16[256,2048]{1,0:T(8,128)(2,1)}, bf16[256,2048]{1,0:T(8,128)(2,1)}, u32[]{:S(2)}, u32[]{:S(2)}) collective-permute-start(bf16[256,2048]{1,0:T(8,128)(2,1)} %fusion.14), channel_id=1, source_target_pairs={{0,2},{2,4},{4,6},{1,3},{3,5},{5,7},{8,10},{10,12},{12,14},{9,11},... | collective-permute-start | bytes 3145736 | tf_op jit(solution)/shard_map/ppermute | solution.py:30
  35.2 38.0 %collective-permute-start.21 = (bf16[256,2048]{1,0:T(8,128)(2,1)}, bf16[256,2048]{1,0:T(8,128)(2,1)}, u32[]{:S(2)}, u32[]{:S(2)}) collective-permute-start(bf16[256,2048]{1,0:T(8,128)(2,1)} %collective-permute-done.20), channel_id=1, source_target_pairs={{2,0},{4,2},{3,1},{5,3},{10,8},{12,10},{11,9},{13,11},{18,16},{20,... | collective-permute-start | bytes 3145736 | tf_op jit(solution)/shard_map/ppermute | solution.py:31
  52.7 42.9 %collective-permute-start.2 = (bf16[256,2048]{1,0:T(8,128)(2,1)}, bf16[256,2048]{1,0:T(8,128)(2,1)}, u32[]{:S(2)}, u32[]{:S(2)}) collective-permute-start(bf16[256,2048]{1,0:T(8,128)(2,1)} %collective-permute-done.1), channel_id=1, source_target_pairs={{2,0},{4,2},{3,1},{5,3},{10,8},{12,10},{11,9},{13,11},{18,16},{20,... | collective-permute-start | bytes 3145736 | tf_op jit(solution)/shard_map/ppermute | solution.py:31
  81.2 94.2 %collective-permute-start.6 = (bf16[256,2048]{1,0:T(8,128)(2,1)}, bf16[256,2048]{1,0:T(8,128)(2,1)S(1)}, u32[]{:S(2)}, u32[]{:S(2)}) collective-permute-start(bf16[256,2048]{1,0:T(8,128)(2,1)} %fusion.14), channel_id=1, source_target_pairs={{0,1},{1,0},{2,3},{3,2},{4,5},{5,4},{6,7},{7,6},{8,9},{9,8},{10,11... | collective-permute-start | bytes 3145736 | tf_op jit(solution)/shard_map/ppermute | solution.py:24
  102.6 81.5 %collective-permute-start.10 = (bf16[512,1024]{1,0:T(8,128)(2,1)S(1)}, bf16[512,1024]{1,0:T(8,128)(2,1)S(1)}, u32[]{:S(2)}, u32[]{:S(2)}) collective-permute-start(bf16[512,1024]{1,0:T(8,128)(2,1)S(1)} %copy-done.91), channel_id=1, source_target_pairs={{0,8},{8,0},{16,24},{24,16},{1,9},{9,1},{17,25},{25,17},{2,10},{10... | collective-permute-start | bytes 3145736 | tf_op jit(solution)/shard_map/ppermute | solution.py:24
  126.3 41.7 %collective-permute-start.5 = (bf16[256,2048]{1,0:T(8,128)(2,1)S(1)}, bf16[256,2048]{1,0:T(8,128)(2,1)S(1)}, u32[]{:S(2)}, u32[]{:S(2)}) collective-permute-start(bf16[256,2048]{1,0:T(8,128)(2,1)S(1)} %collective-permute-done.4), channel_id=1, source_target_pairs={{4,6},{5,7},{12,14},{13,15},{20,22},{21,23},{28,30},{29,31}} | collective-permute-start | bytes 3145736 | tf_op jit(solution)/shard_map/ppermute | solution.py:30
  145.6 39.5 %collective-permute-start.11 = (bf16[512,1024]{1,0:T(8,128)(2,1)S(1)}, bf16[512,1024]{1,0:T(8,128)(2,1)S(1)}, u32[]{:S(2)}, u32[]{:S(2)}) collective-permute-start(bf16[512,1024]{1,0:T(8,128)(2,1)S(1)} %copy-done.91), channel_id=1, source_target_pairs={{0,16},{8,24},{16,0},{24,8},{1,17},{9,25},{17,1},{25,9},{2,18},{10... | collective-permute-start | bytes 3145736 | tf_op jit(solution)/shard_map/ppermute | solution.py:24
  181.2 56.3 %collective-permute-start.13 = (bf16[512,1024]{1,0:T(8,128)(2,1)S(1)}, bf16[512,1024]{1,0:T(8,128)(2,1)S(1)}, u32[]{:S(2)}, u32[]{:S(2)}) collective-permute-start(bf16[512,1024]{1,0:T(8,128)(2,1)S(1)} %copy-done.89), channel_id=1, source_target_pairs={{0,8},{8,0},{16,24},{24,16},{1,9},{9,1},{17,25},{25,17},{2,10},{10... | collective-permute-start | bytes 3145736 | tf_op jit(solution)/shard_map/ppermute | solution.py:24
  182.7 55.8 %collective-permute-start.14 = (bf16[512,1024]{1,0:T(8,128)(2,1)S(1)}, bf16[512,1024]{1,0:T(8,128)(2,1)}, u32[]{:S(2)}, u32[]{:S(2)}) collective-permute-start(bf16[512,1024]{1,0:T(8,128)(2,1)S(1)} %copy-done.89), channel_id=1, source_target_pairs={{0,16},{8,24},{16,0},{24,8},{1,17},{9,25},{17,1},{25,9},{2,18},{10... | collective-permute-start | bytes 3145736 | tf_op jit(solution)/shard_map/ppermute | solution.py:24
  184.1 66.0 %collective-permute-start.15 = (bf16[512,1024]{1,0:T(8,128)(2,1)S(1)}, bf16[512,1024]{1,0:T(8,128)(2,1)S(1)}, u32[]{:S(2)}, u32[]{:S(2)}) collective-permute-start(bf16[512,1024]{1,0:T(8,128)(2,1)S(1)} %copy-done.89), channel_id=1, source_target_pairs={{0,24},{8,16},{16,8},{24,0},{1,25},{9,17},{17,9},{25,1},{2,26},{10... | collective-permute-start | bytes 3145736 | tf_op jit(solution)/shard_map/ppermute | solution.py:24
  185.1 106.2 %collective-permute-start.29 = (bf16[512,256]{1,0:T(8,128)(2,1)S(1)}, bf16[512,256]{1,0:T(8,128)(2,1)S(1)}, u32[]{:S(2)}, u32[]{:S(2)}) collective-permute-start(bf16[512,256]{1,0:T(8,128)(2,1)S(1)} %constant_dynamic-slice_fusion.8), channel_id=1, source_target_pairs={{0,8},{8,0},{16,24},{24,16},{1,9},{9,1},{17,25},{25,17},{2,10},{10... | collective-permute-start | bytes 786440 | tf_op jit(solution)/shard_map/ppermute | solution.py:24
  205.0 87.3 %collective-permute-start.30 = (bf16[512,256]{1,0:T(8,128)(2,1)S(1)}, bf16[512,256]{1,0:T(8,128)(2,1)S(1)}, u32[]{:S(2)}, u32[]{:S(2)}) collective-permute-start(bf16[512,256]{1,0:T(8,128)(2,1)S(1)} %constant_dynamic-slice_fusion.8), channel_id=1, source_target_pairs={{0,16},{8,24},{16,0},{24,8},{1,17},{9,25},{17,1},{25,9},{2,18},{10... | collective-permute-start | bytes 786440 | tf_op jit(solution)/shard_map/ppermute | solution.py:24
  237.5 55.2 %collective-permute-start.31 = (bf16[512,256]{1,0:T(8,128)(2,1)S(1)}, bf16[512,256]{1,0:T(8,128)(2,1)S(1)}, u32[]{:S(2)}, u32[]{:S(2)}) collective-permute-start(bf16[512,256]{1,0:T(8,128)(2,1)S(1)} %constant_dynamic-slice_fusion.8), channel_id=1, source_target_pairs={{0,24},{8,16},{16,8},{24,0},{1,25},{9,17},{17,9},{25,1},{2,26},{10... | collective-permute-start | bytes 786440 | tf_op jit(solution)/shard_map/ppermute | solution.py:24
  238.6 57.9 %collective-permute-start.16 = (bf16[512,768]{1,0:T(8,128)(2,1)S(1)}, bf16[512,768]{1,0:T(8,128)(2,1)S(1)}, u32[]{:S(2)}, u32[]{:S(2)}) collective-permute-start(bf16[512,768]{1,0:T(8,128)(2,1)S(1)} %copy-done.115), channel_id=1, source_target_pairs={{0,8},{8,0},{16,24},{24,16},{1,9},{9,1},{17,25},{25,17},{2,10},{10... | collective-permute-start | bytes 2359304 | tf_op jit(solution)/shard_map/ppermute | solution.py:24
  250.0 46.5 %collective-permute-start.17 = (bf16[512,768]{1,0:T(8,128)(2,1)S(1)}, bf16[512,768]{1,0:T(8,128)(2,1)}, u32[]{:S(2)}, u32[]{:S(2)}) collective-permute-start(bf16[512,768]{1,0:T(8,128)(2,1)S(1)} %copy-done.115), channel_id=1, source_target_pairs={{0,16},{8,24},{16,0},{24,8},{1,17},{9,25},{17,1},{25,9},{2,18},{10... | collective-permute-start | bytes 2359304 | tf_op jit(solution)/shard_map/ppermute | solution.py:24
  292.3 146.7 %collective-permute-start.121 = (f32[2048]{0:T(1024)S(1)}, f32[2048]{0:T(1024)S(1)}, u32[]{:S(2)}, u32[]{:S(2)}) collective-permute-start(f32[2048]{0:T(1024)S(1)} %pad_maximum_fusion.18), channel_id=1, source_target_pairs={{0,8},{8,0},{16,24},{24,16},{1,9},{9,1},{17,25},{25,17},{2,10},{10... | collective-permute-start | bytes 24584 | tf_op jit(solution)/shard_map/ppermute | solution.py:24
  292.8 147.4 %collective-permute-start.122 = (f32[2048]{0:T(1024)S(1)}, f32[2048]{0:T(1024)S(1)}, u32[]{:S(2)}, u32[]{:S(2)}) collective-permute-start(f32[2048]{0:T(1024)S(1)} %pad_maximum_fusion.18), channel_id=1, source_target_pairs={{0,16},{8,24},{16,0},{24,8},{1,17},{9,25},{17,1},{25,9},{2,18},{10... | collective-permute-start | bytes 24584 | tf_op jit(solution)/shard_map/ppermute | solution.py:24
  362.9 73.1 %collective-permute-start.70 = (f32[1792]{0:T(1024)S(1)}, f32[1792]{0:T(1024)S(1)}, u32[]{:S(2)}, u32[]{:S(2)}) collective-permute-start(f32[1792]{0:T(1024)S(1)} %pad_maximum_fusion.17), channel_id=1, source_target_pairs={{0,8},{8,0},{16,24},{24,16},{1,9},{9,1},{17,25},{25,17},{2,10},{10... | collective-permute-start | bytes 21512 | tf_op jit(solution)/shard_map/ppermute | solution.py:24
  363.2 73.9 %collective-permute-start.71 = (f32[1792]{0:T(1024)S(1)}, f32[1792]{0:T(1024)S(1)}, u32[]{:S(2)}, u32[]{:S(2)}) collective-permute-start(f32[1792]{0:T(1024)S(1)} %pad_maximum_fusion.17), channel_id=1, source_target_pairs={{0,16},{8,24},{16,0},{24,8},{1,17},{9,25},{17,1},{25,9},{2,18},{10... | collective-permute-start | bytes 21512 | tf_op jit(solution)/shard_map/ppermute | solution.py:24
  364.2 73.2 %collective-permute-start.72 = (f32[1792]{0:T(1024)S(1)}, f32[1792]{0:T(1024)S(1)}, u32[]{:S(2)}, u32[]{:S(2)}) collective-permute-start(f32[1792]{0:T(1024)S(1)} %pad_maximum_fusion.17), channel_id=1, source_target_pairs={{0,24},{8,16},{16,8},{24,0},{1,25},{9,17},{17,9},{25,1},{2,26},{10... | collective-permute-start | bytes 21512 | tf_op jit(solution)/shard_map/ppermute | solution.py:24
  457.4 37.9 %collective-permute-start.104 = (bf16[512,512]{1,0:T(8,128)(2,1)S(1)}, bf16[512,512]{1,0:T(8,128)(2,1)S(1)}, u32[]{:S(2)}, u32[]{:S(2)}) collective-permute-start(bf16[512,512]{1,0:T(8,128)(2,1)S(1)} %copy-done.100), channel_id=1, source_target_pairs={{0,16},{8,24},{16,0},{24,8},{1,17},{9,25},{17,1},{25,9},{2,18},{10... | collective-permute-start | bytes 1572872 | tf_op jit(solution)/shard_map/ppermute | solution.py:24
  458.5 38.7 %collective-permute-start.105 = (bf16[512,512]{1,0:T(8,128)(2,1)S(1)}, bf16[512,512]{1,0:T(8,128)(2,1)S(1)}, u32[]{:S(2)}, u32[]{:S(2)}) collective-permute-start(bf16[512,512]{1,0:T(8,128)(2,1)S(1)} %copy-done.99), channel_id=1, source_target_pairs={{0,24},{8,16},{16,8},{24,0},{1,25},{9,17},{17,9},{25,1},{2,26},{10... | collective-permute-start | bytes 1572872 | tf_op jit(solution)/shard_map/ppermute | solution.py:24
  474.8 42.9 %collective-permute-start.95 = (bf16[512,512]{1,0:T(8,128)(2,1)S(1)}, bf16[512,512]{1,0:T(8,128)(2,1)S(1)}, u32[]{:S(2)}, u32[]{:S(2)}) collective-permute-start(bf16[512,512]{1,0:T(8,128)(2,1)S(1)} %get-tuple-element.65), channel_id=1, source_target_pairs={{0,16},{8,24},{16,0},{24,8},{1,17},{9,25},{17,1},{25,9},{2,18},{10... | collective-permute-start | bytes 1572872 | tf_op jit(solution)/shard_map/ppermute | solution.py:24
  480.2 52.1 %collective-permute-start.96 = (bf16[512,512]{1,0:T(8,128)(2,1)S(1)}, bf16[512,512]{1,0:T(8,128)(2,1)S(1)}, u32[]{:S(2)}, u32[]{:S(2)}) collective-permute-start(bf16[512,512]{1,0:T(8,128)(2,1)S(1)} %get-tuple-element.64), channel_id=1, source_target_pairs={{0,24},{8,16},{16,8},{24,0},{1,25},{9,17},{17,9},{25,1},{2,26},{10... | collective-permute-start | bytes 1572872 | tf_op jit(solution)/shard_map/ppermute | solution.py:24
  495.3 37.1 %collective-permute-start.85 = (bf16[512,512]{1,0:T(8,128)(2,1)S(1)}, bf16[512,512]{1,0:T(8,128)(2,1)S(1)}, u32[]{:S(2)}, u32[]{:S(2)}) collective-permute-start(bf16[512,512]{1,0:T(8,128)(2,1)S(1)} %get-tuple-element.66), channel_id=1, source_target_pairs={{0,8},{8,0},{16,24},{24,16},{1,9},{9,1},{17,25},{25,17},{2,10},{10... | collective-permute-start | bytes 1572872 | tf_op jit(solution)/shard_map/ppermute | solution.py:24
  497.3 42.9 %collective-permute-start.86 = (bf16[512,512]{1,0:T(8,128)(2,1)S(1)}, bf16[512,512]{1,0:T(8,128)(2,1)S(1)}, u32[]{:S(2)}, u32[]{:S(2)}) collective-permute-start(bf16[512,512]{1,0:T(8,128)(2,1)S(1)} %get-tuple-element.68), channel_id=1, source_target_pairs={{0,16},{8,24},{16,0},{24,8},{1,17},{9,25},{17,1},{25,9},{2,18},{10... | collective-permute-start | bytes 1572872 | tf_op jit(solution)/shard_map/ppermute | solution.py:24
  502.7 39.0 %collective-permute-start.87 = (bf16[512,512]{1,0:T(8,128)(2,1)}, bf16[512,512]{1,0:T(8,128)(2,1)S(1)}, u32[]{:S(2)}, u32[]{:S(2)}) collective-permute-start(bf16[512,512]{1,0:T(8,128)(2,1)} %get-tuple-element.67), channel_id=1, source_target_pairs={{0,24},{8,16},{16,8},{24,0},{1,25},{9,17},{17,9},{25,1},{2,26},{10... | collective-permute-start | bytes 1572872 | tf_op jit(solution)/shard_map/ppermute | solution.py:24
  517.7 66.0 %collective-permute-start.44 = (bf16[256,2048]{1,0:T(8,128)(2,1)S(1)}, bf16[256,2048]{1,0:T(8,128)(2,1)S(1)}, u32[]{:S(2)}, u32[]{:S(2)}) collective-permute-start(bf16[256,2048]{1,0:T(8,128)(2,1)S(1)} %get-tuple-element.49), channel_id=1, source_target_pairs={{0,1},{1,0},{2,3},{3,2},{4,5},{5,4},{6,7},{7,6},{8,9},{9,8},{10,11... | collective-permute-start | bytes 3145736 | tf_op jit(solution)/shard_map/ppermute | solution.py:24
  532.3 38.3 %collective-permute-start.61 = (bf16[512,768]{1,0:T(8,128)(2,1)S(1)}, bf16[512,768]{1,0:T(8,128)(2,1)S(1)}, u32[]{:S(2)}, u32[]{:S(2)}) collective-permute-start(bf16[512,768]{1,0:T(8,128)(2,1)S(1)} %get-tuple-element.54), channel_id=1, source_target_pairs={{0,8},{8,0},{16,24},{24,16},{1,9},{9,1},{17,25},{25,17},{2,10},{10... | collective-permute-start | bytes 2359304 | tf_op jit(solution)/shard_map/ppermute | solution.py:24
  532.4 44.3 %collective-permute-start.62 = (bf16[512,768]{1,0:T(8,128)(2,1)S(1)}, bf16[512,768]{1,0:T(8,128)(2,1)S(1)}, u32[]{:S(2)}, u32[]{:S(2)}) collective-permute-start(bf16[512,768]{1,0:T(8,128)(2,1)S(1)} %get-tuple-element.56), channel_id=1, source_target_pairs={{0,16},{8,24},{16,0},{24,8},{1,17},{9,25},{17,1},{25,9},{2,18},{10... | collective-permute-start | bytes 2359304 | tf_op jit(solution)/shard_map/ppermute | solution.py:24
  540.1 39.3 %collective-permute-start.63 = (bf16[512,768]{1,0:T(8,128)(2,1)S(1)}, bf16[512,768]{1,0:T(8,128)(2,1)S(1)}, u32[]{:S(2)}, u32[]{:S(2)}) collective-permute-start(bf16[512,768]{1,0:T(8,128)(2,1)S(1)} %get-tuple-element.55), channel_id=1, source_target_pairs={{0,24},{8,16},{16,8},{24,0},{1,25},{9,17},{17,9},{25,1},{2,26},{10... | collective-permute-start | bytes 2359304 | tf_op jit(solution)/shard_map/ppermute | solution.py:24
  560.5 49.7 %collective-permute-start.33 = (bf16[256,2048]{1,0:T(8,128)(2,1)S(1)}, bf16[256,2048]{1,0:T(8,128)(2,1)S(1)}, u32[]{:S(2)}, u32[]{:S(2)}) collective-permute-start(bf16[256,2048]{1,0:T(8,128)(2,1)S(1)} %get-tuple-element.53), channel_id=1, source_target_pairs={{0,1},{1,0},{2,3},{3,2},{4,5},{5,4},{6,7},{7,6},{8,9},{9,8},{10,11... | collective-permute-start | bytes 3145736 | tf_op jit(solution)/shard_map/ppermute | solution.py:24
  590.4 45.1 %collective-permute-start.46 = (bf16[256,2048]{1,0:T(8,128)(2,1)S(1)}, bf16[256,2048]{1,0:T(8,128)(2,1)S(1)}, u32[]{:S(2)}, u32[]{:S(2)}) collective-permute-start(bf16[256,2048]{1,0:T(8,128)(2,1)S(1)} %get-tuple-element.48), channel_id=1, source_target_pairs={{0,1},{1,0},{2,3},{3,2},{4,5},{5,4},{6,7},{7,6},{8,9},{9,8},{10,11... | collective-permute-start | bytes 3145736 | tf_op jit(solution)/shard_map/ppermute | solution.py:24
  598.9 37.3 %collective-permute-start.45 = (bf16[256,2048]{1,0:T(8,128)(2,1)S(1)}, bf16[256,2048]{1,0:T(8,128)(2,1)S(1)}, u32[]{:S(2)}, u32[]{:S(2)}) collective-permute-start(bf16[256,2048]{1,0:T(8,128)(2,1)S(1)} %fusion.35), channel_id=1, source_target_pairs={{0,2},{1,3},{8,10},{9,11},{16,18},{17,19},{24,26},{25,27}} | collective-permute-start | bytes 3145736 | tf_op jit(solution)/shard_map/ppermute | solution.py:48
  618.3 53.8 %collective-permute-start.48 = (bf16[256,2048]{1,0:T(8,128)(2,1)S(1)}, bf16[256,2048]{1,0:T(8,128)(2,1)S(1)}, u32[]{:S(2)}, u32[]{:S(2)}) collective-permute-start(bf16[256,2048]{1,0:T(8,128)(2,1)S(1)} %get-tuple-element.47), channel_id=1, source_target_pairs={{0,1},{1,0},{2,3},{3,2},{4,5},{5,4},{6,7},{7,6},{8,9},{9,8},{10,11... | collective-permute-start | bytes 3145736 | tf_op jit(solution)/shard_map/ppermute | solution.py:24
  625.0 48.4 %collective-permute-start.35 = (bf16[256,2048]{1,0:T(8,128)(2,1)S(1)}, bf16[256,2048]{1,0:T(8,128)(2,1)S(1)}, u32[]{:S(2)}, u32[]{:S(2)}) collective-permute-start(bf16[256,2048]{1,0:T(8,128)(2,1)S(1)} %get-tuple-element.52), channel_id=1, source_target_pairs={{0,1},{1,0},{2,3},{3,2},{4,5},{5,4},{6,7},{7,6},{8,9},{9,8},{10,11... | collective-permute-start | bytes 3145736 | tf_op jit(solution)/shard_map/ppermute | solution.py:24
  629.9 44.2 %collective-permute-start.37 = (bf16[256,2048]{1,0:T(8,128)(2,1)S(1)}, bf16[256,2048]{1,0:T(8,128)(2,1)S(1)}, u32[]{:S(2)}, u32[]{:S(2)}) collective-permute-start(bf16[256,2048]{1,0:T(8,128)(2,1)S(1)} %get-tuple-element.51), channel_id=1, source_target_pairs={{0,1},{1,0},{2,3},{3,2},{4,5},{5,4},{6,7},{7,6},{8,9},{9,8},{10,11... | collective-permute-start | bytes 3145736 | tf_op jit(solution)/shard_map/ppermute | solution.py:24
  635.5 40.6 %collective-permute-start.34 = (bf16[256,2048]{1,0:T(8,128)(2,1)S(1)}, bf16[256,2048]{1,0:T(8,128)(2,1)S(1)}, u32[]{:S(2)}, u32[]{:S(2)}) collective-permute-start(bf16[256,2048]{1,0:T(8,128)(2,1)S(1)} %fusion.39), channel_id=1, source_target_pairs={{0,2},{1,3},{8,10},{9,11},{16,18},{17,19},{24,26},{25,27}} | collective-permute-start | bytes 3145736 | tf_op jit(solution)/shard_map/ppermute | solution.py:48
  636.2 34.6 %collective-permute-start.91 = (bf16[512,512]{1,0:T(8,128)(2,1)S(1)}, bf16[512,512]{1,0:T(8,128)(2,1)S(1)}, u32[]{:S(2)}, u32[]{:S(2)}) collective-permute-start(bf16[512,512]{1,0:T(8,128)(2,1)S(1)} %add_convert_fusion.11.refs_0_), channel_id=1, source_target_pairs={{2,0},{4,2},{6,4},{3,1},{5,3},{7,5},{10,8},{12,10},{14,12},{11,9},... | collective-permute-start | bytes 1572872 | tf_op jit(solution)/shard_map/ppermute | solution.py:31
  670.8 41.4 %collective-permute-start.47 = (bf16[256,2048]{1,0:T(8,128)(2,1)S(1)}, bf16[256,2048]{1,0:T(8,128)(2,1)S(1)}, u32[]{:S(2)}, u32[]{:S(2)}) collective-permute-start(bf16[256,2048]{1,0:T(8,128)(2,1)S(1)} %fusion.24), channel_id=1, source_target_pairs={{0,2},{2,4},{1,3},{3,5},{8,10},{10,12},{9,11},{11,13},{16,18},{18,... | collective-permute-start | bytes 3145736 | tf_op jit(solution)/shard_map/ppermute | solution.py:48
  674.1 34.7 %collective-permute-start.116 = (bf16[512,512]{1,0:T(8,128)(2,1)S(1)}, bf16[512,512]{1,0:T(8,128)(2,1)S(1)}, u32[]{:S(2)}, u32[]{:S(2)}) collective-permute-start(bf16[512,512]{1,0:T(8,128)(2,1)S(1)} %collective-permute-done.115.refs_1_), channel_id=1, source_target_pairs={{2,4},{4,6},{3,5},{5,7},{10,12},{12,14},{11,13},{13,15},{18,20},{2... | collective-permute-start | bytes 1572872 | tf_op jit(solution)/shard_map/ppermute | solution.py:30
  676.1 34.1 %collective-permute-start.119 = (bf16[512,512]{1,0:T(8,128)(2,1)S(1)}, bf16[512,512]{1,0:T(8,128)(2,1)S(1)}, u32[]{:S(2)}, u32[]{:S(2)}) collective-permute-start(bf16[512,512]{1,0:T(8,128)(2,1)S(1)} %collective-permute-done.118.refs_4_), channel_id=1, source_target_pairs={{2,0},{4,2},{3,1},{5,3},{10,8},{12,10},{11,9},{13,11},{18,16},{20,... | collective-permute-start | bytes 1572872 | tf_op jit(solution)/shard_map/ppermute | solution.py:31
  686.2 33.9 %collective-permute-start.107 = (bf16[512,512]{1,0:T(8,128)(2,1)S(1)}, bf16[512,512]{1,0:T(8,128)(2,1)S(1)}, u32[]{:S(2)}, u32[]{:S(2)}) collective-permute-start(bf16[512,512]{1,0:T(8,128)(2,1)S(1)} %collective-permute-done.106.refs_1_), channel_id=1, source_target_pairs={{2,4},{4,6},{3,5},{5,7},{10,12},{12,14},{11,13},{13,15},{18,20},{2... | collective-permute-start | bytes 1572872 | tf_op jit(solution)/shard_map/ppermute | solution.py:30
  688.8 33.2 %collective-permute-start.110 = (bf16[512,512]{1,0:T(8,128)(2,1)S(1)}, bf16[512,512]{1,0:T(8,128)(2,1)}, u32[]{:S(2)}, u32[]{:S(2)}) collective-permute-start(bf16[512,512]{1,0:T(8,128)(2,1)S(1)} %collective-permute-done.109.refs_4_), channel_id=1, source_target_pairs={{2,0},{4,2},{3,1},{5,3},{10,8},{12,10},{11,9},{13,11},{18,16},{20,... | collective-permute-start | bytes 1572872 | tf_op jit(solution)/shard_map/ppermute | solution.py:31
  712.1 54.3 %collective-permute-start.36 = (bf16[256,2048]{1,0:T(8,128)(2,1)S(1)}, bf16[256,2048]{1,0:T(8,128)(2,1)S(1)}, u32[]{:S(2)}, u32[]{:S(2)}) collective-permute-start(bf16[256,2048]{1,0:T(8,128)(2,1)S(1)} %fusion.22), channel_id=1, source_target_pairs={{0,2},{2,4},{1,3},{3,5},{8,10},{10,12},{9,11},{11,13},{16,18},{18,... | collective-permute-start | bytes 3145736 | tf_op jit(solution)/shard_map/ppermute | solution.py:48
  720.1 45.0 %collective-permute-start.89 = (bf16[512,512]{1,0:T(8,128)(2,1)S(1)}, bf16[512,512]{1,0:T(8,128)(2,1)S(1)}, u32[]{:S(2)}, u32[]{:S(2)}) collective-permute-start(bf16[512,512]{1,0:T(8,128)(2,1)S(1)} %collective-permute-done.88.refs_1_), channel_id=1, source_target_pairs={{2,4},{4,6},{3,5},{5,7},{10,12},{12,14},{11,13},{13,15},{18,20},{2... | collective-permute-start | bytes 1572872 | tf_op jit(solution)/shard_map/ppermute | solution.py:30
  722.0 68.2 %collective-permute-start.50 = (bf16[256,2048]{1,0:T(8,128)(2,1)S(1)}, bf16[256,2048]{1,0:T(8,128)(2,1)S(1)}, u32[]{:S(2)}, u32[]{:S(2)}) collective-permute-start(bf16[256,2048]{1,0:T(8,128)(2,1)S(1)} %get-tuple-element.31), channel_id=1, source_target_pairs={{6,4},{7,5},{14,12},{15,13},{22,20},{23,21},{30,28},{31,29}} | collective-permute-start | bytes 3145736 | tf_op jit(solution)/shard_map/ppermute | solution.py:49
  723.7 58.3 %collective-permute-start.64 = (bf16[512,768]{1,0:T(8,128)(2,1)S(1)}, bf16[512,768]{1,0:T(8,128)(2,1)}, u32[]{:S(2)}, u32[]{:S(2)}) collective-permute-start(bf16[512,768]{1,0:T(8,128)(2,1)S(1)} %add_convert_fusion.7.refs_0_), channel_id=1, source_target_pairs={{0,2},{2,4},{4,6},{1,3},{3,5},{5,7},{8,10},{10,12},{12,14},{9,11},... | collective-permute-start | bytes 2359304 | tf_op jit(solution)/shard_map/ppermute | solution.py:30
  731.3 52.1 %collective-permute-start.67 = (bf16[512,768]{1,0:T(8,128)(2,1)S(1)}, bf16[512,768]{1,0:T(8,128)(2,1)}, u32[]{:S(2)}, u32[]{:S(2)}) collective-permute-start(bf16[512,768]{1,0:T(8,128)(2,1)S(1)} %add_convert_fusion.7.refs_0_), channel_id=1, source_target_pairs={{2,0},{4,2},{6,4},{3,1},{5,3},{7,5},{10,8},{12,10},{14,12},{11,9},... | collective-permute-start | bytes 2359304 | tf_op jit(solution)/shard_map/ppermute | solution.py:31
  782.0 37.1 %collective-permute-start.39 = (bf16[256,2048]{1,0:T(8,128)(2,1)}, bf16[256,2048]{1,0:T(8,128)(2,1)}, u32[]{:S(2)}, u32[]{:S(2)}) collective-permute-start(bf16[256,2048]{1,0:T(8,128)(2,1)} %get-tuple-element.33), channel_id=1, source_target_pairs={{6,4},{7,5},{14,12},{15,13},{22,20},{23,21},{30,28},{31,29}} | collective-permute-start | bytes 3145736 | tf_op jit(solution)/shard_map/ppermute | solution.py:49
  794.5 43.3 %collective-permute-start.51 = (bf16[256,2048]{1,0:T(8,128)(2,1)}, bf16[256,2048]{1,0:T(8,128)(2,1)}, u32[]{:S(2)}, u32[]{:S(2)}) collective-permute-start(bf16[256,2048]{1,0:T(8,128)(2,1)} %fusion.25), channel_id=1, source_target_pairs={{4,2},{6,4},{5,3},{7,5},{12,10},{14,12},{13,11},{15,13},{20,18},{2... | collective-permute-start | bytes 3145736 | tf_op jit(solution)/shard_map/ppermute | solution.py:49
  799.6 36.6 %collective-permute-start.68 = (bf16[512,768]{1,0:T(8,128)(2,1)}, bf16[512,768]{1,0:T(8,128)(2,1)}, u32[]{:S(2)}, u32[]{:S(2)}) collective-permute-start(bf16[512,768]{1,0:T(8,128)(2,1)} %collective-permute-done.67.refs_4_), channel_id=1, source_target_pairs={{2,0},{4,2},{3,1},{5,3},{10,8},{12,10},{11,9},{13,11},{18,16},{20,... | collective-permute-start | bytes 2359304 | tf_op jit(solution)/shard_map/ppermute | solution.py:31
  819.1 46.1 %collective-permute-start.66 = (bf16[512,768]{1,0:T(8,128)(2,1)}, bf16[512,768]{1,0:T(8,128)(2,1)S(1)}, u32[]{:S(2)}, u32[]{:S(2)}) collective-permute-start(bf16[512,768]{1,0:T(8,128)(2,1)} %collective-permute-done.65.refs_2_), channel_id=1, source_target_pairs={{4,6},{5,7},{12,14},{13,15},{20,22},{21,23},{28,30},{29,31}} | collective-permute-start | bytes 2359304 | tf_op jit(solution)/shard_map/ppermute | solution.py:30
  823.8 32.1 %collective-permute-start.90 = (bf16[512,512]{1,0:T(8,128)(2,1)S(1)}, bf16[512,512]{1,0:T(8,128)(2,1)S(1)}, u32[]{:S(2)}, u32[]{:S(2)}) collective-permute-start(bf16[512,512]{1,0:T(8,128)(2,1)S(1)} %copy-done.31), channel_id=1, source_target_pairs={{4,6},{5,7},{12,14},{13,15},{20,22},{21,23},{28,30},{29,31}} | collective-permute-start | bytes 1572872 | tf_op jit(solution)/shard_map/ppermute | solution.py:30
  828.0 32.3 %collective-permute-start.93 = (bf16[512,512]{1,0:T(8,128)(2,1)S(1)}, bf16[512,512]{1,0:T(8,128)(2,1)S(1)}, u32[]{:S(2)}, u32[]{:S(2)}) collective-permute-start(bf16[512,512]{1,0:T(8,128)(2,1)S(1)} %copy-done.34), channel_id=1, source_target_pairs={{2,0},{3,1},{10,8},{11,9},{18,16},{19,17},{26,24},{27,25}} | collective-permute-start | bytes 1572872 | tf_op jit(solution)/shard_map/ppermute | solution.py:31
  836.1 54.5 %collective-permute-start.69 = (bf16[512,768]{1,0:T(8,128)(2,1)}, bf16[512,768]{1,0:T(8,128)(2,1)}, u32[]{:S(2)}, u32[]{:S(2)}) collective-permute-start(bf16[512,768]{1,0:T(8,128)(2,1)} %collective-permute-done.68.refs_5_), channel_id=1, source_target_pairs={{2,0},{3,1},{10,8},{11,9},{18,16},{19,17},{26,24},{27,25}} | collective-permute-start | bytes 2359304 | tf_op jit(solution)/shard_map/ppermute | solution.py:31
  837.8 58.6 %collective-permute-start.40 = (bf16[256,2048]{1,0:T(8,128)(2,1)}, bf16[256,2048]{1,0:T(8,128)(2,1)}, u32[]{:S(2)}, u32[]{:S(2)}) collective-permute-start(bf16[256,2048]{1,0:T(8,128)(2,1)} %fusion.23), channel_id=1, source_target_pairs={{4,2},{6,4},{5,3},{7,5},{12,10},{14,12},{13,11},{15,13},{20,18},{2... | collective-permute-start | bytes 3145736 | tf_op jit(solution)/shard_map/ppermute | solution.py:49
  856.8 45.9 %collective-permute-start.43 = (bf16[256,2048]{1,0:T(8,128)(2,1)}, bf16[256,2048]{1,0:T(8,128)(2,1)}, u32[]{:S(2)}, u32[]{:S(2)}) collective-permute-start(bf16[256,2048]{1,0:T(8,128)(2,1)} %get-tuple-element.46), channel_id=1, source_target_pairs={{0,1},{1,0},{2,3},{3,2},{4,5},{5,4},{6,7},{7,6},{8,9},{9,8},{10,11... | collective-permute-start | bytes 3145736 | tf_op jit(solution)/shard_map/ppermute | solution.py:24
  861.0 43.6 %collective-permute-start.49 = (bf16[256,2048]{1,0:T(8,128)(2,1)}, bf16[256,2048]{1,0:T(8,128)(2,1)}, u32[]{:S(2)}, u32[]{:S(2)}) collective-permute-start(bf16[256,2048]{1,0:T(8,128)(2,1)} %get-tuple-element.30), channel_id=1, source_target_pairs={{0,2},{2,4},{4,6},{1,3},{3,5},{5,7},{8,10},{10,12},{12,14},{9,11},... | collective-permute-start | bytes 3145736 | tf_op jit(solution)/shard_map/ppermute | solution.py:48
  866.0 38.6 %collective-permute-start.52 = (bf16[256,2048]{1,0:T(8,128)(2,1)}, bf16[256,2048]{1,0:T(8,128)(2,1)}, u32[]{:S(2)}, u32[]{:S(2)}) collective-permute-start(bf16[256,2048]{1,0:T(8,128)(2,1)} %add_convert_fusion.2), channel_id=1, source_target_pairs={{2,0},{4,2},{6,4},{3,1},{5,3},{7,5},{10,8},{12,10},{14,12},{11,9},... | collective-permute-start | bytes 3145736 | tf_op jit(solution)/shard_map/ppermute | solution.py:49
  (201 other events, 4140.9 us)

commit v2 on v1

v2 whole, which is shorter than its diff:
```python
import functools

import jax
import jax.numpy as jnp
from jax import lax
from jax.experimental import pallas as pl
from jax.experimental.pallas import tpu as pltpu
from jax.sharding import PartitionSpec as P

HD = 64
ROT = 32
HALF = ROT // 2
PAIR = 2 * HD
NEG = -1e30
EPS = 1e-05
LOG2E = 1.4426950408889634
GELU_C = 0.7978845608028654
GELU_A = 0.044715
F32 = jnp.float32
BF16 = jnp.bfloat16


def meet(tree):
    return lax.optimization_barrier(tree)


def total(addends):
    out = addends[0].astype(F32)
    for one in addends[1:]:
        out = out + one.astype(F32)
    return out


def xor_swap(value, axis, size, step):
    return lax.ppermute(value, axis, [(j, j ^ step) for j in range(size)])


def to_all(value, axis, size):
    return lax.all_to_all(jnp.broadcast_to(value[None], (size,) + value.shape), axis, 0, 0, tiled=True)


def gather_step(sides, step, size, axis="ctx"):
    left, right = sides
    return (
        lax.ppermute(left, axis, [(j, j + 1) for j in range(step - 1, size - 1)]),
        lax.ppermute(right, axis, [(j, j - 1) for j in range(1, size - step + 1)]),
    )


def sum_step(sides, parts, step, size, axis="ctx"):
    a, b = parts(step), parts(size - step)
    if sides is not None:
        a, b = a + [sides[0]], b + [sides[1]]
    return (
        lax.ppermute(
            total(a).astype(BF16), axis, [(j, j + 1) for j in range(min(step, size - 1))]
        ),
        lax.ppermute(
            total(b).astype(BF16), axis, [(j, j - 1) for j in range(max(size - step, 1), size)]
        ),
    )


def by_distance(blocks, here):
    n = len(blocks)
    return [blocks[0]] + [
        jnp.where(here >= m, blocks[m][0], blocks[n - m][1]) for m in range(1, n)
    ]


FREE = pl.CostEstimate(flops=1, transcendentals=0, bytes_accessed=1)


def rotate(x, cos, sa, sb):
    return (
        x * cos + pltpu.roll(x, PAIR - HALF, axis=1) * sa + pltpu.roll(x, HALF, axis=1) * sb
    )


def masked_scores(k_s, qt, prefix, first, reach, clear):
    s = jnp.dot(k_s[0:reach, :], qt, preferred_element_type=F32) * LOG2E
    count = qt.shape[1]
    kpos = clear + lax.broadcasted_iota(jnp.int32, (reach - clear, count), 0)
    qpos = first + lax.broadcasted_iota(jnp.int32, (1, count), 1)
    tail = jnp.where(kpos < jnp.maximum(qpos + 1, prefix), s[clear:reach], NEG)
    return jnp.concatenate([s[:clear], tail], axis=0) if clear else tail


def spans(length, qblock, most):
    for first in range(0, length, qblock):
        yield first, max(first + qblock, most), first if first >= most else 0


def keep_head(x, h):
    lane = lax.broadcasted_iota(jnp.int32, x.shape, 1)
    return jnp.where((lane >= h * HD) & (lane < (h + 1) * HD), x, 0.0)


def attend_kernel(
    glen, qblock, most,
    offs_ref, prefix_ref,
    qkv_ref, cos_ref, sa_ref, sb_ref,
    ctx_ref, sorted_ref, stat_ref,
    qtm, k_s, vt_s, ot,
):
    length = cos_ref.shape[0]
    for p in range(length // glen):
        rows = pl.ds(pl.multiple_of(offs_ref[p], glen), glen)
        to = slice(p * glen, (p + 1) * glen)
        cos, sa, sb = cos_ref[to, :], sa_ref[to, :], sb_ref[to, :]
        q = rotate(qkv_ref[rows, 0:PAIR], cos, sa, sb).astype(BF16).astype(F32) * (HD**-0.5)
        sorted_ref[to, 0:PAIR] = q.astype(BF16)
        k = rotate(qkv_ref[rows, PAIR : 2 * PAIR], cos, sa, sb).astype(BF16)
        k_s[to, :] = k
        sorted_ref[to, PAIR : 2 * PAIR] = k
        sorted_ref[to, 2 * PAIR : 3 * PAIR] = qkv_ref[rows, 2 * PAIR : 3 * PAIR].astype(BF16)
    q = sorted_ref[:, 0:PAIR].astype(F32)
    for h in range(2):
        qtm[h] = keep_head(q, h).astype(BF16).T
    vt_s[...] = sorted_ref[:, 2 * PAIR : 3 * PAIR].T.reshape(2, HD, length)
    prefix = prefix_ref[0]
    for first, reach, clear in spans(length, qblock, most):
        cols = slice(first, first + qblock)

        def head(h, _):
            s = masked_scores(k_s, qtm[h, :, cols], prefix, first, reach, clear)
            top = jnp.max(s, axis=0, keepdims=True)
            e = jnp.exp2(s - top)
            scale = 1.0 / jnp.sum(e, axis=0, keepdims=True)
            stat_ref[0, h, 0:1, cols] = top
            stat_ref[0, h, 1:2, cols] = scale
            low = (e * scale).astype(BF16)
            ot[h, :, cols] = jnp.dot(vt_s[h, :, 0:reach], low, preferred_element_type=F32)
            return 0

        lax.fori_loop(0, 2, head, 0)
    for p in range(length // glen):
        rows = pl.ds(pl.multiple_of(offs_ref[p], glen), glen)
        to = slice(p * glen, (p + 1) * glen)
        ctx_ref[rows, :] = ot[:, :, to].reshape(PAIR, glen).T.astype(BF16)


def attend_back_kernel(
    glen, qblock, most,
    offs_ref, prefix_ref,
    sorted_ref, stat_ref, do_ref, cos_ref, sa_ref, sb_ref,
    dqkv_ref,
    qm, qtm, k_s, kt_s, v_s, dom, dotm, dqt, dk_acc, dv_acc,
):
    length = cos_ref.shape[0]
    k_s[...] = sorted_ref[:, PAIR : 2 * PAIR]
    v_s[...] = sorted_ref[:, 2 * PAIR : 3 * PAIR]
    q = sorted_ref[:, 0:PAIR].astype(F32)
    for p in range(length // glen):
        rows = pl.ds(pl.multiple_of(offs_ref[p], glen), glen)
        to = slice(p * glen, (p + 1) * glen)
        do = do_ref[rows, :].astype(F32)
        for h in range(2):
            dom[h, to, :] = keep_head(do, h).astype(BF16)
    for h in range(2):
        qm[h] = keep_head(q, h).astype(BF16)
        qtm[h] = qm[h].T
        dotm[h] = dom[h].T
    kt_s[...] = k_s[...].T.reshape(2, HD, length)
    dk_acc[...] = jnp.zeros_like(dk_acc)
    dv_acc[...] = jnp.zeros_like(dv_acc)
    prefix = prefix_ref[0]
    dot = functools.partial(jnp.dot, preferred_element_type=F32)
    for first, reach, clear in spans(length, qblock, most):
        cols = slice(first, first + qblock)

        def head(h, _):
            s = masked_scores(k_s, qtm[h, :, cols], prefix, first, reach, clear)
            prob = jnp.exp2(s - stat_ref[0, h, 0:1, cols]) * stat_ref[0, h, 1:2, cols]
            dv_acc[0:reach, :] += dot(prob.astype(BF16), dom[h, cols, :])
            dp = dot(v_s[0:reach, :], dotm[h, :, cols])
            delta = jnp.sum(prob * dp, axis=0, keepdims=True)
            ds = (prob * (dp - delta)).astype(BF16)
            dqt[h, :, cols] = dot(kt_s[h, :, 0:reach], ds)
            dk_acc[0:reach, :] += dot(ds, qm[h, cols, :])
            return 0

        lax.fori_loop(0, 2, head, 0)
    for p in range(length // glen):
        rows = pl.ds(pl.multiple_of(offs_ref[p], glen), glen)
        to = slice(p * glen, (p + 1) * glen)
        cos, sa, sb = cos_ref[to, :], -sa_ref[to, :], -sb_ref[to, :]
        dq = dqt[:, :, to].reshape(PAIR, glen).T * (HD**-0.5)
        dqkv_ref[rows, 0:PAIR] = rotate(dq, cos, sa, sb).astype(BF16)
        dqkv_ref[rows, PAIR : 2 * PAIR] = rotate(dk_acc[to, :], cos, sa, sb).astype(BF16)
        dqkv_ref[rows, 2 * PAIR : 3 * PAIR] = dv_acc[to, :].astype(BF16)


def attention_specs(length):
    whole = pl.BlockSpec((length, PAIR), lambda p, *_: (0, 0))
    wide = pl.BlockSpec((length, 3 * PAIR), lambda p, *_: (0, p))
    narrow = pl.BlockSpec((length, PAIR), lambda p, *_: (0, p))
    stat = pl.BlockSpec((1, 2, 2, length), lambda p, *_: (p, 0, 0, 0))
    return whole, wide, narrow, stat


def attend(qkv, offs, prefix, tables):
    length, inner = qkv.shape[0], qkv.shape[1] // 3
    whole, wide, narrow, stat = attention_specs(length)
    vm = pltpu.VMEM
    return pl.pallas_call(
        functools.partial(attend_kernel, length // offs.shape[0], min(256, length), length // 2),
        out_shape=(
            jax.ShapeDtypeStruct((length, inner), BF16),
            jax.ShapeDtypeStruct((length, 3 * inner), BF16),
            jax.ShapeDtypeStruct((inner // PAIR, 2, 2, length), F32),
        ),
        grid_spec=pltpu.PrefetchScalarGridSpec(
            num_scalar_prefetch=2,
            grid=(inner // PAIR,),
            in_specs=[wide, whole, whole, whole],
            out_specs=(narrow, wide, stat),
            scratch_shapes=[
                vm((2, PAIR, length), BF16),
                vm((length, PAIR), BF16),
                vm((2, HD, length), BF16),
                vm((2, HD, length), F32),
            ],
        ),
        compiler_params=pltpu.CompilerParams(vmem_limit_bytes=40 << 20),
        cost_estimate=FREE,
        name="attend",
    )(offs, prefix, qkv, *tables)


def attend_back(ordered, stats, grad_context, offs, prefix, tables):
    length, inner = grad_context.shape
    whole, wide, narrow, stat = attention_specs(length)
    vm = pltpu.VMEM
    return pl.pallas_call(
        functools.partial(
            attend_back_kernel, length // offs.shape[0], min(256, length), length // 2
        ),
        out_shape=jax.ShapeDtypeStruct((length, 3 * inner), BF16),
        grid_spec=pltpu.PrefetchScalarGridSpec(
            num_scalar_prefetch=2,
            grid=(inner // PAIR,),
            in_specs=[wide, stat, narrow, whole, whole, whole],
            out_specs=wide,
            scratch_shapes=[
                vm((2, length, PAIR), BF16),
                vm((2, PAIR, length), BF16),
                vm((length, PAIR), BF16),
                vm((2, HD, length), BF16),
                vm((length, PAIR), BF16),
                vm((2, length, PAIR), BF16),
                vm((2, PAIR, length), BF16),
                vm((2, HD, length), F32),
                vm((length, PAIR), F32),
                vm((length, PAIR), F32),
            ],
        ),
        compiler_params=pltpu.CompilerParams(vmem_limit_bytes=40 << 20),
        cost_estimate=FREE,
        name="attend_back",
    )(offs, prefix, ordered, stats, grad_context, *tables)


def pair_kernel(split, a_ref, b_ref, w_ref, o_ref):
    nt = (((1,), (1,)), ((), ()))
    o = lax.dot_general(a_ref[...], w_ref[:, :split], nt, preferred_element_type=F32)
    o += lax.dot_general(b_ref[...], w_ref[:, split:], nt, preferred_element_type=F32)
    o_ref[...] = o.astype(o_ref.dtype)


def pair_product(a, b, w):
    n, depth = w.shape
    m = a.shape[0]
    bn = min(512, n)
    return pl.pallas_call(
        functools.partial(pair_kernel, a.shape[1]),
        out_shape=jax.ShapeDtypeStruct((m, n), BF16),
        grid=(n // bn,),
        in_specs=[
            pl.BlockSpec((m, a.shape[1]), lambda j: (0, 0), pipeline_mode=pl.Buffered(1)),
            pl.BlockSpec((m, b.shape[1]), lambda j: (0, 0), pipeline_mode=pl.Buffered(1)),
            pl.BlockSpec((bn, depth), lambda j: (j, 0)),
        ],
        out_specs=pl.BlockSpec((m, bn), lambda j: (0, j)),
        compiler_params=pltpu.CompilerParams(vmem_limit_bytes=48 << 20),
        cost_estimate=FREE,
        name="pair_product",
    )(a, b, w)


def pack_kernel(pieces, here_ref, *refs):
    o_ref = refs[-1]
    at = 0
    for n, start, size in pieces:
        o_ref[0, :, at : at + size] = refs[n][:, start : start + size]
        at += size


def pack_columns(weights, pieces, here, places, copies):
    rows = weights[0].shape[0]
    span = sum(size for _, _, size in pieces)
    return pl.pallas_call(
        functools.partial(pack_kernel, pieces),
        out_shape=jax.ShapeDtypeStruct((copies, rows, span), weights[0].dtype),
        grid_spec=pltpu.PrefetchScalarGridSpec(
            num_scalar_prefetch=1,
            grid=(copies,),
            in_specs=[
                pl.BlockSpec((rows, w.shape[1] // places), lambda i, h: (0, h[0])) for w in weights
            ],
            out_specs=pl.BlockSpec((1, rows, span), lambda i, h: (i, 0, 0)),
        ),
        compiler_params=pltpu.CompilerParams(vmem_limit_bytes=40 << 20),
        cost_estimate=FREE,
        name="pack_columns",
    )(here.reshape(1), *weights)


def rows_kernel(counts, *refs):
    o_ref = refs[-1]
    tn = (((0,), (0,)), ((), ()))
    at, col = 0, 0
    for count in counts:
        o = 0.0
        for n in range(count):
            o += lax.dot_general(
                refs[at + n][...], refs[at + count + n][...], tn, preferred_element_type=F32
            )
        o_ref[0, :, col : col + o.shape[1]] = o.astype(o_ref.dtype)
        at, col = at + 2 * count, col + o.shape[1]


def rows_product(products, owners):
    args, specs, columns = [], [], 0
    for a, b in products:
        bm = a[0].shape[1] // owners
        args += [*a, *b]
        specs += [pl.BlockSpec((x.shape[0], bm), lambda i: (0, i)) for x in a]
        specs += [
            pl.BlockSpec(x.shape, lambda i: (0, 0), pipeline_mode=pl.Buffered(1)) for x in b
        ]
        columns += b[0].shape[1]
    return pl.pallas_call(
        functools.partial(rows_kernel, [len(a) for a, _ in products]),
        out_shape=jax.ShapeDtypeStruct((owners, bm, columns), BF16),
        grid=(owners,),
        in_specs=specs,
        out_specs=pl.BlockSpec((1, bm, columns), lambda i: (i, 0, 0)),
        compiler_params=pltpu.CompilerParams(vmem_limit_bytes=56 << 20),
        cost_estimate=FREE,
        name="rows_product",
    )(*args)


def order_kernel(size, here_ref, *refs):
    blocks, o_ref = refs[:-1], refs[-1]
    m, here = pl.program_id(0), here_ref[0]

    def put(ref):
        o_ref[0] = ref[...]

    pl.when(m == 0)(lambda: put(blocks[0]))
    for k in range(1, size):
        pl.when((m == k) & (here >= k))(functools.partial(put, blocks[k]))
        pl.when((m == k) & (here < k))(functools.partial(put, blocks[2 * size - 1 - k]))


def in_order(blocks, here):
    size = len(blocks)
    rows, span = blocks[0].shape
    blocks = [blocks[0]] + [x[0] for x in blocks[1:]] + [x[1] for x in blocks[1:]]
    return pl.pallas_call(
        functools.partial(order_kernel, size),
        out_shape=jax.ShapeDtypeStruct((size, rows, span), blocks[0].dtype),
        grid_spec=pltpu.PrefetchScalarGridSpec(
            num_scalar_prefetch=1,
            grid=(size,),
            in_specs=[pl.BlockSpec((rows, span), lambda m, h: (0, 0), pipeline_mode=pl.Buffered(1))]
            * len(blocks),
            out_specs=pl.BlockSpec(
                (1, rows, span), lambda m, h: (lax.rem(h[0] - m + size, size), 0, 0)
            ),
        ),
        compiler_params=pltpu.CompilerParams(vmem_limit_bytes=48 << 20),
        cost_estimate=FREE,
        name="in_order",
    )(here.reshape(1), *blocks)


def place_kernel(size, pairs, here_ref, *refs):
    blocks, outs = refs[: 2 * size - 1], refs[2 * size - 1 :]
    m, here = pl.program_id(0), here_ref[0]
    spans = [[(p * 3 + n) * PAIR for p in range(pairs)] for n in range(3)]
    spans.append([(3 * pairs + p) * PAIR for p in range(pairs)])

    def put(block):
        for out, starts in zip(outs, spans):
            for p, at in enumerate(starts):
                out[:, p * PAIR : (p + 1) * PAIR] = block[:, at : at + PAIR].astype(F32)

    pl.when(m == 0)(lambda: put(blocks[0]))
    for k in range(1, size):
        pl.when((m == k) & (here >= k))(functools.partial(put, blocks[k]))
        pl.when((m == k) & (here < k))(functools.partial(put, blocks[2 * size - 1 - k]))


def place(blocks, here, pairs):
    size = len(blocks)
    rows, span = blocks[0].shape
    blocks = [blocks[0]] + [x[0] for x in blocks[1:]] + [x[1] for x in blocks[1:]]
    width = pairs * PAIR
    return pl.pallas_call(
        functools.partial(place_kernel, size, pairs),
        out_shape=(jax.ShapeDtypeStruct((rows, size * width), F32),) * 4,
        grid_spec=pltpu.PrefetchScalarGridSpec(
            num_scalar_prefetch=1,
            grid=(size,),
            in_specs=[pl.BlockSpec((rows, span), lambda m, h: (0, 0), pipeline_mode=pl.Buffered(1))]
            * len(blocks),
            out_specs=(
                pl.BlockSpec((rows, width), lambda m, h: (0, lax.rem(h[0] - m + size, size))),
            )
            * 4,
        ),
        compiler_params=pltpu.CompilerParams(vmem_limit_bytes=48 << 20),
        cost_estimate=FREE,
        name="place",
    )(here.reshape(1), *blocks)


def widen_kernel(a_ref, o_ref):
    o_ref[...] = a_ref[0].astype(F32)


def widen(blocks):
    n, rows, span = blocks.shape
    return pl.pallas_call(
        widen_kernel,
        out_shape=jax.ShapeDtypeStruct((rows, n * span), F32),
        grid=(n,),
        in_specs=[pl.BlockSpec((1, rows, span), lambda c: (c, 0, 0))],
        out_specs=pl.BlockSpec((rows, span), lambda c: (0, c)),
        compiler_params=pltpu.CompilerParams(vmem_limit_bytes=40 << 20),
        cost_estimate=FREE,
        name="widen",
    )(blocks)


def up_kernel(step, h_ref, w_ref, b_ref, act_ref, slope_ref):
    for c in range(0, act_ref.shape[1], step):
        up = jnp.dot(h_ref[...], w_ref[:, c : c + step], preferred_element_type=F32)
        act, slope = gelu_parts(up + b_ref[:, c : c + step])
        act_ref[:, c : c + step] = act.astype(BF16)
        slope_ref[:, c : c + step] = slope.astype(BF16)


def up_product(hidden, weight, bias):
    m, k = hidden.shape
    n = bias.shape[0]
    bm = min(512, m)
    return pl.pallas_call(
        functools.partial(up_kernel, min(256, n)),
        out_shape=(jax.ShapeDtypeStruct((m, n), BF16),) * 2,
        grid=(m // bm,),
        in_specs=[
            pl.BlockSpec((bm, k), lambda i: (i, 0)),
            pl.BlockSpec((k, n), lambda i: (0, 0), pipeline_mode=pl.Buffered(1)),
            pl.BlockSpec((1, n), lambda i: (0, 0)),
        ],
        out_specs=(pl.BlockSpec((bm, n), lambda i: (i, 0)),) * 2,
        compiler_params=pltpu.CompilerParams(vmem_limit_bytes=56 << 20),
        cost_estimate=FREE,
        name="up_product",
    )(hidden, weight, bias.reshape(1, n))


def down_kernel(units, g_ref, w_ref, s_ref, d_ref, c_ref):
    g = g_ref[...]
    d = jnp.dot(g, w_ref[:, :units], preferred_element_type=F32)
    d_ref[...] = (d * s_ref[...].astype(F32)).astype(BF16)
    c_ref[...] = jnp.dot(g, w_ref[:, units:], preferred_element_type=F32).astype(BF16)


def down_product(grad, weight, slope):
    m, k = grad.shape
    units, n = slope.shape[1], weight.shape[1]
    bm = min(512, m)
    return pl.pallas_call(
        functools.partial(down_kernel, units),
        out_shape=(
            jax.ShapeDtypeStruct((m, units), BF16),
            jax.ShapeDtypeStruct((m, n - units), BF16),
        ),
        grid=(m // bm,),
        in_specs=[
            pl.BlockSpec((bm, k), lambda i: (i, 0)),
            pl.BlockSpec((k, n), lambda i: (0, 0), pipeline_mode=pl.Buffered(1)),
            pl.BlockSpec((bm, units), lambda i: (i, 0)),
        ],
        out_specs=(
            pl.BlockSpec((bm, units), lambda i: (i, 0)),
            pl.BlockSpec((bm, n - units), lambda i: (i, 0)),
        ),
        compiler_params=pltpu.CompilerParams(vmem_limit_bytes=56 << 20),
        cost_estimate=FREE,
        name="down_product",
    )(grad, weight, slope)


def line_kernel(pieces, h_ref, *refs):
    b_ref, o_ref = refs[pieces], refs[-1]
    span = o_ref.shape[1] // pieces
    for n in range(pieces):
        to = slice(n * span, (n + 1) * span)
        o = jnp.dot(h_ref[...], refs[n][...], preferred_element_type=F32)
        o_ref[:, to] = o + b_ref[:, to]


def line_product(hidden, weight, bias, start, pieces):
    m, k = hidden.shape
    n = bias.shape[0]
    span = n // pieces
    bm = min(512, m)
    piece = lambda p: pl.BlockSpec(
        (k, span), lambda i: (0, start // span + p), pipeline_mode=pl.Buffered(1)
    )
    return pl.pallas_call(
        functools.partial(line_kernel, pieces),
        out_shape=jax.ShapeDtypeStruct((m, n), F32),
        grid=(m // bm,),
        in_specs=[pl.BlockSpec((bm, k), lambda i: (i, 0))]
        + [piece(p) for p in range(pieces)]
        + [pl.BlockSpec((1, n), lambda i: (0, 0))],
        out_specs=pl.BlockSpec((bm, n), lambda i: (i, 0)),
        compiler_params=pltpu.CompilerParams(vmem_limit_bytes=56 << 20),
        cost_estimate=FREE,
        name="line_product",
    )(hidden, *[weight] * pieces, bias.reshape(1, n))


def gelu_parts(up):
    square = up * up
    t = jnp.tanh(GELU_C * up * (1.0 + GELU_A * square))
    half = 0.5 * (1.0 + t)
    slope = half + 0.5 * up * (1.0 - t * t) * (GELU_C * (1.0 + 3.0 * GELU_A * square))
    return up * half, slope


def local(
    tokens, cotangent, prefix_len, group_order, ln_gain, ln_bias,
    query_weight, query_bias, key_weight, key_bias, value_weight, value_bias,
    out_weight, out_bias, up_weight, up_bias, down_weight, down_bias,
):
    nf, nc, nt = lax.axis_size("fsdp"), lax.axis_size("ctx"), lax.axis_size("tp")
    ci, ti = lax.axis_index("ctx").astype(jnp.int32), lax.axis_index("tp").astype(jnp.int32)
    seqs, rows, width = tokens.shape
    own_seqs = seqs // nt
    length = rows * nc
    own = own_seqs * rows
    db = width // nf
    inner = query_weight.shape[1] // nc
    units = up_weight.shape[1] // nc
    pairs = inner // PAIR

    def columns(w):
        return lax.dynamic_slice_in_dim(w, ci * (w.shape[-1] // nc), w.shape[-1] // nc, axis=-1)

    def by_pairs(arrays):
        return jnp.concatenate(
            [a[..., p * PAIR : (p + 1) * PAIR] for p in range(pairs) for a in arrays], axis=-1
        )

    x = lax.dynamic_slice_in_dim(tokens, ti * own_seqs, own_seqs, axis=0).reshape(own, width)
    g_own = lax.dynamic_slice_in_dim(cotangent, ti * own_seqs, own_seqs, axis=0).reshape(own, width)
    x = x.astype(F32)
    gain, shift = ln_gain.astype(F32), ln_bias.astype(F32)
    centred = x - jnp.mean(x, axis=-1, keepdims=True)
    inv_std = lax.rsqrt(jnp.mean(centred * centred, axis=-1, keepdims=True) + EPS)
    normed = centred * inv_std
    h_own = (normed * gain + shift).astype(BF16)

    h_in = [h_own]

    def side(blocks):
        return blocks[-1] if len(blocks) > 1 else (blocks[0], blocks[0])

    def gather_on(blocks):
        return blocks + [gather_step(side(blocks), len(blocks), nc)]

    cut = [
        (1 + n, p * PAIR, PAIR) for p in range(pairs) for n in range(3)
    ]
    h_own, early = meet(
        (h_own, (up_weight, query_weight, key_weight, value_weight, down_weight, out_weight))
    )
    first = pack_columns(early[:4], [(0, 0, units)] + cut, ci, nc, nf)
    second = pack_columns(early[4:], [(0, 0, units), (1, 0, inner)], ci, nc, nf)
    b_qkv = by_pairs([columns(query_bias), columns(key_bias), columns(value_bias)]).astype(F32)
    b_up = columns(up_bias).astype(F32)

    lane = jnp.arange(PAIR, dtype=jnp.int32)[None, :] % HD
    freq = jnp.power(10000.0, -2.0 * (lane % HALF).astype(F32) / ROT)
    angle = jnp.arange(length, dtype=jnp.int32).astype(F32)[:, None] * freq
    cos = jnp.where(lane < ROT, jnp.cos(angle), 1.0)
    sin = jnp.sin(angle)
    sa = jnp.where(lane < HALF, -sin, 0.0)
    sb = jnp.where((lane >= HALF) & (lane < ROT), sin, 0.0)
    groups = group_order.shape[0]
    glen = length // groups
    places = jnp.arange(groups, dtype=jnp.int32)
    slot = jnp.sum(
        jnp.where(group_order[None, :] == places[:, None], places[None, :], 0), axis=1
    ) * glen
    offs = slot
    seq_ids = jnp.arange(seqs, dtype=jnp.int32)
    seq_of = ((seq_ids // own_seqs) ^ ti) * own_seqs + seq_ids % own_seqs
    prefix = jnp.sum(
        jnp.where(seq_of[:, None] == seq_ids[None, :], prefix_len[None, :], 0), axis=1
    )
    offs, prefix = offs.astype(jnp.int32), prefix.astype(jnp.int32)

    tables = (cos, sa, sb)
    first_all = lax.all_to_all(first, "fsdp", 0, 0, tiled=True)
    h_in, second, tables = meet((gather_on(h_in), second, tables))
    while len(h_in) < nc:
        h_in = meet(gather_on(h_in))
    g_own, h_in = meet((g_own, h_in))
    g_all = lax.all_gather(g_own.reshape(own_seqs, rows, width), "ctx", axis=1, tiled=True)

    def halves(mine):
        mine = mine.reshape(own_seqs * length, width)
        return [mine] + [xor_swap(mine, "tp", nt, k) for k in range(1, nt)]

    def send_rows(full):
        return lax.all_to_all(full, "fsdp", 0, 0, tiled=True)

    def sum_rows(got):
        return total([got[k] for k in range(nf)]).astype(BF16)

    def gather_cols(mine):
        return lax.all_gather(mine, "ctx", axis=0, tiled=False)

    h_mine = jnp.moveaxis(in_order(h_in, ci).reshape(nc, own_seqs, rows, width), 1, 0)
    hidden = halves(h_mine)
    hidden, first_all = meet((hidden, first_all))
    w_first = first_all.reshape(width, units + 3 * inner)
    second_all = lax.all_to_all(second, "fsdp", 0, 0, tiled=True)
    ups, qkv = [], []
    for n in range(nt):
        ups.append(up_product(hidden[n], w_first, b_up))
        ups, hidden = meet((ups, hidden))
    for n in range(nt):
        qkv.append(line_product(hidden[n], w_first, b_qkv, units, 3))
        qkv, hidden = meet((qkv, hidden))
    act, slope = [u[0] for u in ups], [u[1] for u in ups]
    done = []
    for n in range(seqs):
        at = slice((n % own_seqs) * length, (n % own_seqs + 1) * length)
        done.append(attend(qkv[n // own_seqs][at], offs, prefix[n : n + 1], tables))
        done, qkv = meet((done, qkv))
    context = [
        jnp.concatenate([d[0] for d in done[n * own_seqs : (n + 1) * own_seqs]]) for n in range(nt)
    ]

    def parts_of(mine, got):
        grid = lambda a: a.reshape(own_seqs, nc, rows, width)
        mine, got = grid(mine), [grid(g) for g in got]

        def parts(m):
            at = (ci - m + nc) % nc
            pick = lambda a: lax.dynamic_index_in_dim(a, at, 1, keepdims=False).reshape(own, width)
            return [pick(mine)] + [pick(g) for g in got]

        return parts

    act, context, second_all, g_all = meet((act, context, second_all, g_all))
    w_second = second_all.reshape(width, units + inner)
    grad = halves(g_all)
    theirs, act, context = meet(
        ([pair_product(act[k], context[k], w_second) for k in range(1, nt)], act, context)
    )
    full_down = rows_product([(grad, act)], nf)
    grad, full_down, slope, theirs, act = meet((grad, full_down, slope, theirs, act))
    d_rows = send_rows(full_down)
    o_got = [xor_swap(t, "tp", nt, k) for k, t in zip(range(1, nt), theirs)]
    o_got, o_mine = meet((o_got, pair_product(act[0], context[0], w_second)))
    o_parts = parts_of(o_mine, o_got)
    o_sum = sum_step(None, o_parts, 1, nc)
    downs, step = [], 2
    for n in range(nt):
        downs.append(down_product(grad[n], w_second, slope[n]))
        downs, grad, hidden, o_sum = meet((downs, grad, hidden, o_sum))
        if step < nc:
            o_sum = sum_step(o_sum, o_parts, step, nc)
            step += 1
    dup, grad_context = [d[0] for d in downs], [d[1] for d in downs]
    full_up = rows_product([(hidden, dup)], nf)
    full_up, d_sum, done, grad_context, o_sum = meet(
        (full_up, sum_rows(d_rows), done, grad_context, o_sum)
    )
    for k in range(step, nc):
        o_sum = meet(sum_step(o_sum, o_parts, k, nc))
    d_cols = gather_cols(d_sum)
    u_rows = send_rows(full_up)
    back = []
    for n in range(seqs):
        at = slice((n % own_seqs) * length, (n % own_seqs + 1) * length)
        back.append(
            attend_back(
                done[n][1], done[n][2], grad_context[n // own_seqs][at],
                offs, prefix[n : n + 1], tables,
            )
        )
        back, done, grad_context = meet((back, done, grad_context))
    dqkv = [jnp.concatenate(back[n * own_seqs : (n + 1) * own_seqs]) for n in range(nt)]
    u_sum, dqkv, hidden, grad = meet((sum_rows(u_rows), dqkv, hidden, grad))
    qo_full = rows_product([(hidden, dqkv), (grad, context)], nf)
    qo_full, dqkv, dup, u_sum, d_cols = meet((qo_full, dqkv, dup, u_sum, d_cols))
    u_cols = gather_cols(u_sum)
    qo = send_rows(qo_full)
    theirs, dup, dqkv = meet(
        ([pair_product(dup[k], dqkv[k], w_first) for k in range(1, nt)], dup, dqkv)
    )
    h_got = [xor_swap(t, "tp", nt, k) for k, t in zip(range(1, nt), theirs)]
    h_got, h_mine = meet((h_got, pair_product(dup[0], dqkv[0], w_first)))
    h_parts = parts_of(h_mine, h_got)
    col_sum = lambda a: jnp.sum(a.astype(F32), axis=0)
    bias_sums = jnp.concatenate(
        [total([col_sum(a) for a in array]) for array in (dqkv, dup, grad)]
    )[None]
    bias_sums = jnp.sum(to_all(bias_sums, "fsdp", nf).reshape(nf, -1), axis=0)
    h_sum = meet(sum_step(None, h_parts, 1, nc))
    qo = [sum_rows(qo)]
    for k in range(2, nc + 1):
        if k < nc:
            h_sum = sum_step(h_sum, h_parts, k, nc)
        qo = gather_on(qo)
        qo, h_sum = meet((qo, h_sum))
        if k == nc - 1:
            grad_hidden = total(h_parts(0) + list(h_sum))

    gs = grad_hidden * gain
    grad_normed = inv_std * (
        gs - jnp.mean(gs, axis=-1, keepdims=True)
        - normed * jnp.mean(gs * normed, axis=-1, keepdims=True)
    )
    in_own = g_own.astype(F32) + grad_normed
    norm_sums = jnp.concatenate([col_sum(grad_hidden * normed), col_sum(grad_hidden)])
    out_own = total([x] + o_parts(0) + list(o_sum) + [out_bias, down_bias])

    def whole_tokens(own_rows):
        mine = own_rows.astype(BF16).reshape(1, own_seqs, rows, width)
        pieces = [mine] + [xor_swap(mine, "tp", nt, k) for k in range(1, nt)]
        full = jnp.zeros((nt, own_seqs, rows, width), BF16)
        for k in range(nt):
            full = lax.dynamic_update_slice_in_dim(full, pieces[k], ti ^ k, axis=0)
        return full.reshape(seqs, rows, width)

    output = whole_tokens(out_own)
    input_grad = whole_tokens(in_own)

    dw_down = widen(d_cols)
    dw_up = widen(u_cols)
    dw_qkv = place(qo, ci, pairs)

    small = 3 * inner + units
    obias = bias_sums[small:]
    got = to_all(jnp.concatenate([bias_sums[:small], norm_sums])[None], "ctx", nc).reshape(nc, -1)
    qkv_sums = got[:, : 3 * inner].reshape(nc, pairs, 3, PAIR)
    qb, kb, vb = (qkv_sums[:, :, n].reshape(nc * inner) for n in range(3))
    ub = got[:, 3 * inner : small].reshape(nc * units)
    norm_sums = jnp.sum(got[:, small:], axis=0)[None]
    norm_sums = jnp.sum(to_all(norm_sums, "fsdp", nf).reshape(nf, -1), axis=0)
    norm_sums = total([norm_sums] + [xor_swap(norm_sums, "tp", nt, k) for k in range(1, nt)])
    norm_sums = norm_sums.reshape(2, width)

    return (
        output, input_grad, norm_sums[0], norm_sums[1],
        dw_qkv[0], qb, dw_qkv[1], kb, dw_qkv[2], vb,
        dw_qkv[3], dw_up, ub, dw_down, obias,
    )


def solution(mesh):
    rows, flat, cols, one = P("fsdp", "ctx", None), P("fsdp", "tp"), P("tp"), P()
    return jax.shard_map(
        local,
        mesh=mesh,
        in_specs=(
            rows, rows, P("fsdp"), one, one, one,
            flat, cols, flat, cols, flat, cols, flat, one, flat, cols, flat, one,
        ),
        out_specs=(
            rows, rows, one, one, flat, cols, flat, cols, flat, cols, flat, flat, cols, flat, one,
        ),
        check_vma=False,
    )
```

time: 964 us -> 699 us (0.73)
  Pallas kernels: 62.1 us -> 236 us
  starting transfers between devices: 270 us -> 112 us
  matrix products: 148 us -> 0 us
  waiting for transfers between devices: 355 us -> 216 us
  other arithmetic: 51.7 us -> 68.2 us
  between operations: 3.75 us -> 14.6 us
  local copies, waits for them, and re-layouts: 56.1 us -> 45.4 us
    pallas_call x7 -> x23, Pallas kernels: 62.1 us -> 236 us  [the longest x2 43.3 us: attend_back(): pl.pallas_call(functools.partial(attend_back_kernel, length // offs.shape...]
    dot_general x14 -> x0, matrix products: 148 us -> none  [the longest x4 53.8 us: mm_nt(): lax.dot_general(a, b, (((1,), (1,)), ((), ())), preferred_element_type=F32)]
    ppermute x66 -> x24, starting transfers between devices: 171 us -> 59 us  [the longest x6 17.5 us: sum_step(): lax.ppermute(total(b).astype(BF16), axis, [(j, j - 1) for j in range(max(...]
    ppermute x58 -> x7, waiting for transfers between devices: 108 us -> 0.02 us  [xor_swap(): return lax.ppermute(value, axis, [(j, j ^ step) for j in range(size)])]
    ppermute x58 -> x7, starting transfers between devices: 99.6 us -> 12.7 us  [xor_swap(): return lax.ppermute(value, axis, [(j, j ^ step) for j in range(size)])]
    ppermute x66 -> x24, waiting for transfers between devices: 247 us -> 163 us  [the longest x6 71.3 us: gather_step(): lax.ppermute(left, axis, [(j, j + 1) for j in range(step - 1, size - 1)])]
    all_to_all x0 -> x8, waiting for transfers between devices: none -> 41.7 us  [the longest x3 26.7 us: send_rows(): return lax.all_to_all(full, 'fsdp', 0, 0, tiled=True)]
    all_to_all x0 -> x8, starting transfers between devices: none -> 40.1 us  [the longest x3 15 us: send_rows(): return lax.all_to_all(full, 'fsdp', 0, 0, tiled=True)]
  transfers between devices with their start and end apart: 124 -> 42, of which waited for: 46 -> 22; matrix products, arithmetic and copies ran while one was open for 25% -> 10% of each run, Pallas kernels for 7% -> 31%
where the time goes in v2:
time: 699 us; the launch traced here: 692 us
  Pallas kernels  236 us (34%)
  waiting for transfers between devices  216 us (31%)
  starting transfers between devices  112 us (16%)
  other arithmetic  68.2 us (10%)
  local copies, waits for them, and re-layouts  45.4 us (6%)
  between operations  14.6 us (2%)
    ppermute x6, waiting for transfers between devices, gather_step(): lax.ppermute(left, axis, [(j, j + 1) for j in range(step - 1, size - 1)])  71.3 us
    ppermute x6, waiting for transfers between devices, sum_step(): lax.ppermute(total(b).astype(BF16), axis, [(j, j - 1) for j in range(max(...  44 us
    pallas_call x2, Pallas kernels, attend_back(): pl.pallas_call(functools.partial(attend_back_kernel, length // offs.shape...  43.3 us
    pallas_call x3, Pallas kernels, rows_product(): pl.pallas_call(functools.partial(rows_kernel, [len(a) for a, _ in product...  41.8 us
    pallas_call x4, Pallas kernels, pair_product(): pl.pallas_call(functools.partial(pair_kernel, a.shape[1]), out_shape=jax....  39.2 us
    unnamed x108, local copies, waits for them, and re-layouts  31 us
    pallas_call x2, Pallas kernels, attend(): pl.pallas_call(functools.partial(attend_kernel, length // offs.shape[0],...  30.1 us
    ppermute x6, waiting for transfers between devices, sum_step(): lax.ppermute(total(a).astype(BF16), axis, [(j, j + 1) for j in range(min(...  29.4 us
  transfers between devices with their start and end apart: 42, of which 22 were waited for; matrix products, arithmetic and copies ran while one was open for 10% of the time, Pallas kernels for 31%

profile of v2, /device:TPU:19, one launch (start us, length us, event | category | flops | bytes accessed | tf_op | source)
XLA Modules:
  0.0 691.8 jit_solution(14167119215871294825)
XLA Ops:
  13.2 3.2 collective-permute-start
  23.1 3.6 pack_columns.3
  26.8 5.8 all-to-all-start
  44.9 4.8 collective-permute-start.3
  49.6 17.7 %collective-permute-done.2.refs_2_ = bf16[256,2048]{1,0:T(8,128)(2,1)} collective-permute-done((bf16[256,2048]{1,0:T(8,128)(2,1)}, bf16[256,2048]{1,0:T(8,128)(2,1)}, u32[]{:S(2)}, u32[]{:S(2)}) %collective-permute-start.2) | collective-permute-done | bytes 1048608 | tf_op jit(solution)/shard_map/ppermute | solution.py:45
  74.2 16.2 %collective-permute-done.4.refs_3_ = bf16[256,2048]{1,0:T(8,128)(2,1)} collective-permute-done((bf16[256,2048]{1,0:T(8,128)(2,1)}, bf16[256,2048]{1,0:T(8,128)(2,1)}, u32[]{:S(2)}, u32[]{:S(2)}) %collective-permute-start.4) | collective-permute-done | bytes 1048608 | tf_op jit(solution)/shard_map/ppermute | solution.py:45
  90.5 5.7 in_order.1
  96.2 3.7 collective-permute-start.6
  99.9 12.3 %all-to-all-done = bf16[4,512,1792]{2,1,0:T(8,128)(2,1)} async-done(((bf16[4,512,1792]{2,1,0:T(8,128)(2,1)}), bf16[4,512,1792]{2,1,0:T(8,128)(2,1)}, u32[]{:S(2)}, u32[]{:S(2)}) %all-to-all-start) | async-done | bytes 7340064 | tf_op jit(solution)/shard_map/all_to_all | solution.py:623
  112.2 6.3 all-to-all-start.1
  123.6 11.1 %up_product.2 = (bf16[1024,1024]{1,0:T(8,128)(2,1)}, bf16[1024,1024]{1,0:T(8,128)(2,1)}) custom-call(bf16[1024,2048]{1,0:T(8,128)(2,1)} %bitcast.155, bf16[2048,1792]{1,0:T(8,128)(2,1)} %bitcast.4.w_ref.refs_0_.refs_1_.refs_2_, f32[1,1024]{1,0:T(1,128)} %bitcast.171), custom_call_target="tpu_custom_call" | custom-call | flops 1 | bytes 1 | tf_op jit(solution)/shard_map/up_product/pallas_call | solution.py:461
  134.7 11.1 %up_product.3 = (bf16[1024,1024]{1,0:T(8,128)(2,1)}, bf16[1024,1024]{1,0:T(8,128)(2,1)}) custom-call(bf16[1024,2048]{1,0:T(8,128)(2,1)} %collective-permute-done.6.h_ref.refs_1_, bf16[2048,1792]{1,0:T(8,128)(2,1)} %bitcast.4.w_ref.refs_0_.refs_1_.refs_2_, f32[1,1024]{1,0:T(1,128)} %bitcast.172), custom_call_target="tpu_custom_call" | custom-call | flops 1 | bytes 1 | tf_op jit(solution)/shard_map/up_product/pallas_call | solution.py:461
  145.8 7.3 %line_product.2.qkv_ref = f32[1024,768]{1,0:T(8,128)} custom-call(bf16[1024,2048]{1,0:T(8,128)(2,1)} %bitcast.156, bf16[2048,1792]{1,0:T(8,128)(2,1)} %bitcast.4.w_ref.refs_0_.refs_1_.refs_2_, bf16[2048,1792]{1,0:T(8,128)(2,1)} %bitcast.4.w_ref.refs_0_.refs_1_.refs_2_, bf16[2048,1792]{1,0:T(8,128)(2,1)} %bitcast.4.w_ref.refs_0_.refs_1_.refs_2_, ...), custom_call_target="tpu_custom_call" | custom-call | flops 1 | bytes 1 | tf_op jit(solution)/shard_map/line_product/pallas_call | solution.py:527
  153.2 7.4 %line_product.3.qkv_ref = f32[1024,768]{1,0:T(8,128)} custom-call(bf16[1024,2048]{1,0:T(8,128)(2,1)} %collective-permute-done.6.h_ref.refs_1_, bf16[2048,1792]{1,0:T(8,128)(2,1)} %bitcast.4.w_ref.refs_0_.refs_1_.refs_2_, bf16[2048,1792]{1,0:T(8,128)(2,1)} %bitcast.4.w_ref.refs_0_.refs_1_.refs_2_, bf16[2048,1792]{1,0:T(8,128)(2,1)} %bitcast.4.w_ref.refs_0_.refs_1_.refs_2_, ...), custom_call_target="tpu_custom_call" | custom-call | flops 1 | bytes 1 | tf_op jit(solution)/shard_map/line_product/pallas_call | solution.py:527
  160.6 14.8 %attend.2 = (bf16[1024,256]{1,0:T(8,128)(2,1)S(1)}, bf16[1024,768]{1,0:T(8,128)(2,1)S(1)}, f32[2,2,2,1024]{3,2,1,0:T(2,128)S(1)}) custom-call(s32[8]{0:T(128)S(1)} %broadcast_multiply_fusion.3.offs_ref, s32[1]{0:T(128)} %get-tuple-element.399.prefix_ref, f32[1024,768]{1,0:T(8,128)S(1)} %copy-done.13, f32[1024,128]{1,0:T(8,128)S(1)} %copy-done.11, ...), custom_call_target="tpu_custom_call" | custom-call | flops 1 | bytes 1 | tf_op jit(solution)/shard_map/attend/pallas_call | solution.py:206
  175.5 15.3 %attend.3 = (bf16[1024,256]{1,0:T(8,128)(2,1)S(1)}, bf16[1024,768]{1,0:T(8,128)(2,1)S(1)}, f32[2,2,2,1024]{3,2,1,0:T(2,128)S(1)}) custom-call(s32[8]{0:T(128)S(1)} %broadcast_multiply_fusion.3.offs_ref, s32[1]{0:T(128)} %get-tuple-element.398.prefix_ref, f32[1024,768]{1,0:T(8,128)S(1)} %copy-done.12, f32[1024,128]{1,0:T(8,128)S(1)} %copy-done.11, ...), custom_call_target="tpu_custom_call" | custom-call | flops 1 | bytes 1 | tf_op jit(solution)/shard_map/attend/pallas_call | solution.py:206
  195.3 8.7 %pair_product.4 = bf16[1024,2048]{1,0:T(8,128)(2,1)} custom-call(bf16[1024,1024]{1,0:T(8,128)(2,1)S(1)} %copy-done.15, bf16[1024,256]{1,0:T(8,128)(2,1)S(1)} %get-tuple-element.327.b_ref.refs_7_, bf16[2048,1280]{1,0:T(8,128)(2,1)} %bitcast.14.w_ref), custom_call_target="tpu_custom_call" | custom-call | flops 1 | bytes 1 | tf_op jit(solution)/shard_map/pair_product/pallas_call | solution.py:275
  204.0 13.4 %rows_product.3 = bf16[4,512,1024]{2,1,0:T(8,128)(2,1)} custom-call(bf16[1024,2048]{1,0:T(8,128)(2,1)} %all-gather.7.cloned.1.call-done, bf16[1024,2048]{1,0:T(8,128)(2,1)} %collective-permute-done.7.refs_1_.g_ref.refs_5_, bf16[1024,1024]{1,0:T(8,128)(2,1)} %get-tuple-element.269.refs_2_.a_ref, bf16[1024,1024]{1,0:T(8,128)(2,1)} %get-tuple-element.264.a_ref.refs_3_), custom_call_target="tpu_custom_call" | custom-call | flops 1 | bytes 1 | tf_op jit(solution)/shard_map/rows_product/pallas_call | solution.py:343
  219.2 8.7 %pair_product.5 = bf16[1024,2048]{1,0:T(8,128)(2,1)} custom-call(bf16[1024,1024]{1,0:T(8,128)(2,1)S(1)} %copy-done.14, bf16[1024,256]{1,0:T(8,128)(2,1)S(1)} %get-tuple-element.270.b_ref.refs_6_, bf16[2048,1280]{1,0:T(8,128)(2,1)} %bitcast.14.w_ref), custom_call_target="tpu_custom_call" | custom-call | flops 1 | bytes 1 | tf_op jit(solution)/shard_map/pair_product/pallas_call | solution.py:275
  227.9 4.4 bitcast_convert_fusion.2
  235.3 4.9 all-to-all-start.2
  240.2 10.4 %down_product.2 = (bf16[1024,1024]{1,0:T(8,128)(2,1)}, bf16[1024,256]{1,0:T(8,128)(2,1)}) custom-call(bf16[1024,2048]{1,0:T(8,128)(2,1)} %all-gather.7.cloned.1.call-done, bf16[2048,1280]{1,0:T(8,128)(2,1)} %bitcast.14.w_ref, bf16[1024,1024]{1,0:T(8,128)(2,1)} %get-tuple-element.274.s_ref), custom_call_target="tpu_custom_call" | custom-call | flops 1 | bytes 1 | tf_op jit(solution)/shard_map/down_product/pallas_call | solution.py:488
  250.6 8.9 %collective-permute-done.10 = bf16[256,2048]{1,0:T(8,128)(2,1)S(1)} collective-permute-done((bf16[256,2048]{1,0:T(8,128)(2,1)}, bf16[256,2048]{1,0:T(8,128)(2,1)S(1)}, u32[]{:S(2)}, u32[]{:S(2)}) %collective-permute-start.10) | collective-permute-done | bytes 1048608 | tf_op jit(solution)/shard_map/ppermute | solution.py:58
  259.5 3.7 fusion.29
  264.5 4.0 collective-permute-start.12
  268.6 10.5 %down_product.3 = (bf16[1024,1024]{1,0:T(8,128)(2,1)}, bf16[1024,256]{1,0:T(8,128)(2,1)}) custom-call(bf16[1024,2048]{1,0:T(8,128)(2,1)} %collective-permute-done.7.refs_1_.g_ref.refs_5_, bf16[2048,1280]{1,0:T(8,128)(2,1)} %bitcast.14.w_ref, bf16[1024,1024]{1,0:T(8,128)(2,1)} %get-tuple-element.283.s_ref), custom_call_target="tpu_custom_call" | custom-call | flops 1 | bytes 1 | tf_op jit(solution)/shard_map/down_product/pallas_call | solution.py:488
  279.0 10.3 %collective-permute-done.11 = bf16[256,2048]{1,0:T(8,128)(2,1)S(1)} collective-permute-done((bf16[256,2048]{1,0:T(8,128)(2,1)}, bf16[256,2048]{1,0:T(8,128)(2,1)S(1)}, u32[]{:S(2)}, u32[]{:S(2)}) %collective-permute-start.11) | collective-permute-done | bytes 1048608 | tf_op jit(solution)/shard_map/ppermute | solution.py:55
  290.7 4.5 fusion.31
  297.1 3.6 collective-permute-start.14
  300.7 4.1 fusion.32
  304.8 13.4 %rows_product.4 = bf16[4,512,1024]{2,1,0:T(8,128)(2,1)} custom-call(bf16[1024,2048]{1,0:T(8,128)(2,1)} %bitcast.157, bf16[1024,2048]{1,0:T(8,128)(2,1)} %collective-permute-done.6.h_ref.refs_1_, bf16[1024,1024]{1,0:T(8,128)(2,1)} %get-tuple-element.335.refs_2_.a_ref, bf16[1024,1024]{1,0:T(8,128)(2,1)} %get-tuple-element.350.refs_3_.a_ref), custom_call_target="tpu_custom_call" | custom-call | flops 1 | bytes 1 | tf_op jit(solution)/shard_map/rows_product/pallas_call | solution.py:343
  322.2 4.8 all-to-all-start.3
  329.5 21.7 %attend_back.2.refs_2_.b_ref = bf16[1024,768]{1,0:T(8,128)(2,1)S(1)} custom-call(s32[8]{0:T(128)S(1)} %broadcast_multiply_fusion.3.offs_ref, s32[1]{0:T(128)} %get-tuple-element.399.prefix_ref, bf16[1024,768]{1,0:T(8,128)(2,1)S(1)} %copy-done.25, f32[2,2,2,1024]{3,2,1,0:T(2,128)S(1)} %get-tuple-element.308.stat_ref, bf16[1024,256]{1,0:T(8,128)(2,1)S(1)} %copy-done.32, ...), custom_call_target="tpu_custom_call" | custom-call | flops 1 | bytes 1 | tf_op jit(solution)/shard_map/attend_back/pallas_call | solution.py:235
  352.4 21.6 %attend_back.3.refs_3_.b_ref = bf16[1024,768]{1,0:T(8,128)(2,1)S(1)} custom-call(s32[8]{0:T(128)S(1)} %broadcast_multiply_fusion.3.offs_ref, s32[1]{0:T(128)} %get-tuple-element.398.prefix_ref, bf16[1024,768]{1,0:T(8,128)(2,1)S(1)} %copy-done.23, f32[2,2,2,1024]{3,2,1,0:T(2,128)S(1)} %get-tuple-element.315.stat_ref, bf16[1024,256]{1,0:T(8,128)(2,1)S(1)} %copy-done.33, ...), custom_call_target="tpu_custom_call" | custom-call | flops 1 | bytes 1 | tf_op jit(solution)/shard_map/attend_back/pallas_call | solution.py:235
  375.1 4.1 fusion.33
  379.2 15.0 %rows_product.5 = bf16[4,512,1024]{2,1,0:T(8,128)(2,1)} custom-call(bf16[1024,2048]{1,0:T(8,128)(2,1)} %bitcast.158, bf16[1024,2048]{1,0:T(8,128)(2,1)} %collective-permute-done.6.h_ref.refs_1_, bf16[1024,768]{1,0:T(8,128)(2,1)} %copy-done.2, bf16[1024,768]{1,0:T(8,128)(2,1)} %copy-done.4, bf16[1024,2048]{1,0:T(8,128)(2,1)} %all-gather.7.cloned.1.call-done, ...), custom_call_target="tpu_custom_call" | custom-call | flops 1 | bytes 1 | tf_op jit(solution)/shard_map/rows_product/pallas_call | solution.py:343
  394.3 10.9 %all-gather.9.cloned.1.call-done = bf16[2048,1024]{1,0:T(8,128)(2,1)} async-done(((bf16[512,1024]{1,0:T(8,128)(2,1)}), bf16[2048,1024]{1,0:T(8,128)(2,1)}) %all-gather.9.cloned.1.call-update) | async-done | bytes 4194320 | tf_op jit(solution)/shard_map/all_gather | solution.py:641
  406.8 10.9 %pair_product.6 = bf16[1024,2048]{1,0:T(8,128)(2,1)} custom-call(bf16[1024,1024]{1,0:T(8,128)(2,1)S(1)} %copy-done.9, bf16[1024,768]{1,0:T(8,128)(2,1)S(1)} %copy-done.5, bf16[2048,1792]{1,0:T(8,128)(2,1)} %bitcast.4.w_ref.refs_0_.refs_1_.refs_2_), custom_call_target="tpu_custom_call" | custom-call | flops 1 | bytes 1 | tf_op jit(solution)/shard_map/pair_product/pallas_call | solution.py:275
  418.3 5.3 all-to-all-start.4
  425.9 10.9 %pair_product.7 = bf16[1024,2048]{1,0:T(8,128)(2,1)} custom-call(bf16[1024,1024]{1,0:T(8,128)(2,1)S(1)} %copy-done.7, bf16[1024,768]{1,0:T(8,128)(2,1)S(1)} %copy-done.3, bf16[2048,1792]{1,0:T(8,128)(2,1)} %bitcast.4.w_ref.refs_0_.refs_1_.refs_2_), custom_call_target="tpu_custom_call" | custom-call | flops 1 | bytes 1 | tf_op jit(solution)/shard_map/pair_product/pallas_call | solution.py:275
  436.9 4.4 bitcast_convert_fusion
  444.2 26.7 %all-to-all-done.4 = bf16[4,512,1024]{2,1,0:T(8,128)(2,1)} async-done(((bf16[4,512,1024]{2,1,0:T(8,128)(2,1)}), bf16[4,512,1024]{2,1,0:T(8,128)(2,1)}, u32[]{:S(2)}, u32[]{:S(2)}) %all-to-all-start.4) | async-done | bytes 4194336 | tf_op jit(solution)/shard_map/all_to_all | solution.py:635
  470.9 4.1 fusion.34.refs_0_
  477.0 3.4 collective-permute-start.18
  480.4 12.1 %collective-permute-done.20 = bf16[256,2048]{1,0:T(8,128)(2,1)} collective-permute-done((bf16[256,2048]{1,0:T(8,128)(2,1)}, bf16[256,2048]{1,0:T(8,128)(2,1)}, u32[]{:S(2)}, u32[]{:S(2)}) %collective-permute-start.20) | collective-permute-done | bytes 1048608 | tf_op jit(solution)/shard_map/ppermute | solution.py:58
  492.5 4.4 fusion.26
  498.2 4.0 collective-permute-start.22
  507.0 17.0 %collective-permute-done.17.refs_1_ = bf16[512,1024]{1,0:T(8,128)(2,1)} collective-permute-done((bf16[512,1024]{1,0:T(8,128)(2,1)}, bf16[512,1024]{1,0:T(8,128)(2,1)}, u32[]{:S(2)}, u32[]{:S(2)}) %collective-permute-start.17) | collective-permute-done | bytes 1048608 | tf_op jit(solution)/shard_map/ppermute | solution.py:45
  524.0 13.4 %collective-permute-done.18.refs_4_ = bf16[512,1024]{1,0:T(8,128)(2,1)} collective-permute-done((bf16[512,1024]{1,0:T(8,128)(2,1)}, bf16[512,1024]{1,0:T(8,128)(2,1)}, u32[]{:S(2)}, u32[]{:S(2)}) %collective-permute-start.18) | collective-permute-done | bytes 1048608 | tf_op jit(solution)/shard_map/ppermute | solution.py:46
  537.4 16.2 %collective-permute-done.21 = bf16[256,2048]{1,0:T(8,128)(2,1)} collective-permute-done((bf16[256,2048]{1,0:T(8,128)(2,1)}, bf16[256,2048]{1,0:T(8,128)(2,1)}, u32[]{:S(2)}, u32[]{:S(2)}) %collective-permute-start.21) | collective-permute-done | bytes 1048608 | tf_op jit(solution)/shard_map/ppermute | solution.py:55
  553.6 18.0 %collective-permute-done.22 = bf16[256,2048]{1,0:T(8,128)(2,1)} collective-permute-done((bf16[256,2048]{1,0:T(8,128)(2,1)}, bf16[256,2048]{1,0:T(8,128)(2,1)}, u32[]{:S(2)}, u32[]{:S(2)}) %collective-permute-start.22) | collective-permute-done | bytes 1048608 | tf_op jit(solution)/shard_map/ppermute | solution.py:58
  571.7 4.7 fusion.24
  578.5 3.4 collective-permute-start.26
  584.7 3.8 collective-permute-start.24
  590.0 3.6 all-to-all-start.5
  595.2 4.6 bitcast_dynamic-update-slice_fusion.3
  604.7 20.4 %collective-permute-done.23.refs_2_ = bf16[512,1024]{1,0:T(8,128)(2,1)S(1)} collective-permute-done((bf16[512,1024]{1,0:T(8,128)(2,1)}, bf16[512,1024]{1,0:T(8,128)(2,1)S(1)}, u32[]{:S(2)}, u32[]{:S(2)}) %collective-permute-start.23) | collective-permute-done | bytes 1048608 | tf_op jit(solution)/shard_map/ppermute | solution.py:45
  629.2 5.2 fusion.15
  635.1 5.7 all-to-all-start.6
  642.4 3.6 bitcast_dynamic-update-slice_fusion.1
  652.2 3.6 widen.3
  658.6 3.6 widen.2
  663.0 3.6 all-to-all-start.7
  676.1 6.3 place.1
  (224 shorter events, 116.0 us)
Async XLA Ops:
  7.2 66.0 %copy-start = (bf16[2,256,2048]{2,1,0:T(8,128)(2,1)S(1)}, bf16[2,256,2048]{2,1,0:T(8,128)(2,1)}, u32[]{:S(2)}) copy-start(bf16[2,256,2048]{2,1,0:T(8,128)(2,1)} %param.19) | copy-start | bytes 6291460
  7.2 11.3 %copy-start.26 = (bf16[512,1024]{1,0:T(8,128)(2,1)S(1)}, bf16[512,1024]{1,0:T(8,128)(2,1)}, u32[]{:S(2)}) copy-start(bf16[512,1024]{1,0:T(8,128)(2,1)} %refs_1_.1) | copy-start | bytes 3145732
  13.2 27.5 %collective-permute-start = (bf16[256,2048]{1,0:T(8,128)(2,1)}, bf16[256,2048]{1,0:T(8,128)(2,1)}, u32[]{:S(2)}, u32[]{:S(2)}) collective-permute-start(bf16[256,2048]{1,0:T(8,128)(2,1)} %fusion.9.refs_0_), channel_id=1, source_target_pairs={{0,2},{2,4},{4,6},{1,3},{3,5},{5,7},{8,10},{10,12},{12,14},{9,11},... | collective-permute-start | bytes 3145736 | tf_op jit(solution)/shard_map/ppermute | solution.py:45
  16.4 25.9 %collective-permute-start.1 = (bf16[256,2048]{1,0:T(8,128)(2,1)}, bf16[256,2048]{1,0:T(8,128)(2,1)}, u32[]{:S(2)}, u32[]{:S(2)}) collective-permute-start(bf16[256,2048]{1,0:T(8,128)(2,1)} %fusion.9.refs_0_), channel_id=1, source_target_pairs={{2,0},{4,2},{6,4},{3,1},{5,3},{7,5},{10,8},{12,10},{14,12},{11,9},... | collective-permute-start | bytes 3145736 | tf_op jit(solution)/shard_map/ppermute | solution.py:46
  26.8 85.4 %all-to-all-start = ((bf16[4,512,1792]{2,1,0:T(8,128)(2,1)}), bf16[4,512,1792]{2,1,0:T(8,128)(2,1)}, u32[]{:S(2)}, u32[]{:S(2)}) async-start(bf16[4,512,1792]{2,1,0:T(8,128)(2,1)} %pack_columns.3), calls=%async_computation | async-start | bytes 14680064 | tf_op jit(solution)/shard_map/all_to_all | solution.py:623
  32.6 159.3 %all-gather.7.cloned.1.call-start = ((), (), s32[]{:S(2)}) async-start(), calls=%async_computation.8 | async-start | bytes 5242880 | tf_op jit(solution)/shard_map/all_gather | solution.py:628
  42.3 25.0 %collective-permute-start.2 = (bf16[256,2048]{1,0:T(8,128)(2,1)}, bf16[256,2048]{1,0:T(8,128)(2,1)}, u32[]{:S(2)}, u32[]{:S(2)}) collective-permute-start(bf16[256,2048]{1,0:T(8,128)(2,1)} %collective-permute-done.refs_1_), channel_id=1, source_target_pairs={{2,4},{4,6},{3,5},{5,7},{10,12},{12,14},{11,13},{13,15},{18,20},{2... | collective-permute-start | bytes 3145736 | tf_op jit(solution)/shard_map/ppermute | solution.py:45
  44.9 24.3 %collective-permute-start.3 = (bf16[256,2048]{1,0:T(8,128)(2,1)}, bf16[256,2048]{1,0:T(8,128)(2,1)}, u32[]{:S(2)}, u32[]{:S(2)}) collective-permute-start(bf16[256,2048]{1,0:T(8,128)(2,1)} %collective-permute-done.1.refs_4_), channel_id=1, source_target_pairs={{2,0},{4,2},{3,1},{5,3},{10,8},{12,10},{11,9},{13,11},{18,16},{20,... | collective-permute-start | bytes 3145736 | tf_op jit(solution)/shard_map/ppermute | solution.py:46
  69.2 21.2 %collective-permute-start.4 = (bf16[256,2048]{1,0:T(8,128)(2,1)}, bf16[256,2048]{1,0:T(8,128)(2,1)}, u32[]{:S(2)}, u32[]{:S(2)}) collective-permute-start(bf16[256,2048]{1,0:T(8,128)(2,1)} %collective-permute-done.2.refs_2_), channel_id=1, source_target_pairs={{4,6},{5,7},{12,14},{13,15},{20,22},{21,23},{28,30},{29,31}} | collective-permute-start | bytes 3145736 | tf_op jit(solution)/shard_map/ppermute | solution.py:45
  71.5 19.0 %collective-permute-start.5 = (bf16[256,2048]{1,0:T(8,128)(2,1)}, bf16[256,2048]{1,0:T(8,128)(2,1)}, u32[]{:S(2)}, u32[]{:S(2)}) collective-permute-start(bf16[256,2048]{1,0:T(8,128)(2,1)} %collective-permute-done.3.refs_5_), channel_id=1, source_target_pairs={{2,0},{3,1},{10,8},{11,9},{18,16},{19,17},{26,24},{27,25}} | collective-permute-start | bytes 3145736 | tf_op jit(solution)/shard_map/ppermute | solution.py:46
  96.2 26.5 %copy-start.48 = (s32[2]{0:T(128)S(1)}, s32[2]{0:T(128)}, u32[]{:S(2)}) copy-start(s32[2]{0:T(128)} %param.20) | copy-start | bytes 28
  96.2 27.3 %copy-start.49 = (s32[8]{0:T(128)S(1)}, s32[8]{0:T(128)}, u32[]{:S(2)}) copy-start(s32[8]{0:T(128)} %param.21) | copy-start | bytes 100
  96.2 27.4 %collective-permute-start.6 = (bf16[1024,2048]{1,0:T(8,128)(2,1)}, bf16[1024,2048]{1,0:T(8,128)(2,1)}, u32[]{:S(2)}, u32[]{:S(2)}) collective-permute-start(bf16[1024,2048]{1,0:T(8,128)(2,1)} %bitcast.154), channel_id=1, source_target_pairs={{0,1},{1,0},{2,3},{3,2},{4,5},{5,4},{6,7},{7,6},{8,9},{9,8},{10,11... | collective-permute-start | bytes 12582920 | tf_op jit(solution)/shard_map/ppermute | solution.py:35
  112.2 79.7 %all-to-all-start.1 = ((bf16[4,512,1280]{2,1,0:T(8,128)(2,1)}), bf16[4,512,1280]{2,1,0:T(8,128)(2,1)}, u32[]{:S(2)}, u32[]{:S(2)}) async-start(bf16[4,512,1280]{2,1,0:T(8,128)(2,1)} %copy-done.6), calls=%async_computation.1 | async-start | bytes 10485760 | tf_op jit(solution)/shard_map/all_to_all | solution.py:647
  153.2 7.4 %copy-start.11 = (f32[1024,128]{1,0:T(8,128)S(1)}, f32[1024,128]{1,0:T(8,128)}, u32[]{:S(2)}) copy-start(f32[1024,128]{1,0:T(8,128)} %get-tuple-element.239.cos_ref) | copy-start | bytes 1572868
  153.2 7.4 %copy-start.13 = (f32[1024,768]{1,0:T(8,128)S(1)}, f32[1024,768]{1,0:T(8,128)}, u32[]{:S(2)}) copy-start(f32[1024,768]{1,0:T(8,128)} %line_product.2.qkv_ref) | copy-start | bytes 9437188
  160.6 14.9 %copy-start.12 = (f32[1024,768]{1,0:T(8,128)S(1)}, f32[1024,768]{1,0:T(8,128)}, u32[]{:S(2)}) copy-start(f32[1024,768]{1,0:T(8,128)} %line_product.3.qkv_ref) | copy-start | bytes 9437188
  175.5 15.3 %copy-start.24 = (bf16[1024,768]{1,0:T(8,128)(2,1)}, bf16[1024,768]{1,0:T(8,128)(2,1)S(1)}, u32[]{:S(2)}) copy-start(bf16[1024,768]{1,0:T(8,128)(2,1)S(1)} %get-tuple-element.307.sorted_ref) | copy-start | bytes 4718596
  175.5 42.1 %copy-start.20 = (bf16[1024,256]{1,0:T(8,128)(2,1)}, bf16[1024,256]{1,0:T(8,128)(2,1)S(1)}, u32[]{:S(2)}) copy-start(bf16[1024,256]{1,0:T(8,128)(2,1)S(1)} %get-tuple-element.270.b_ref.refs_6_) | copy-start | bytes 1572868
  191.9 12.0 %copy-start.21 = (bf16[1024,256]{1,0:T(8,128)(2,1)}, bf16[1024,256]{1,0:T(8,128)(2,1)S(1)}, u32[]{:S(2)}) copy-start(bf16[1024,256]{1,0:T(8,128)(2,1)S(1)} %get-tuple-element.327.b_ref.refs_7_) | copy-start | bytes 1572868
  191.9 12.0 %collective-permute-start.7 = (bf16[1024,2048]{1,0:T(8,128)(2,1)}, bf16[1024,2048]{1,0:T(8,128)(2,1)}, u32[]{:S(2)}, u32[]{:S(2)}) collective-permute-start(bf16[1024,2048]{1,0:T(8,128)(2,1)} %all-gather.7.cloned.1.call-done), channel_id=1, source_target_pairs={{0,1},{1,0},{2,3},{3,2},{4,5},{5,4},{6,7},{7,6},{8,9},{9,8},{10,11... | collective-permute-start | bytes 12582920 | tf_op jit(solution)/shard_map/ppermute | solution.py:35
  217.4 10.5 %collective-permute-start.8 = (bf16[1024,2048]{1,0:T(8,128)(2,1)}, bf16[1024,2048]{1,0:T(8,128)(2,1)}, u32[]{:S(2)}, u32[]{:S(2)}) collective-permute-start(bf16[1024,2048]{1,0:T(8,128)(2,1)} %pair_product.4), channel_id=1, source_target_pairs={{0,1},{1,0},{2,3},{3,2},{4,5},{5,4},{6,7},{7,6},{8,9},{9,8},{10,11... | collective-permute-start | bytes 12582920 | tf_op jit(solution)/shard_map/ppermute | solution.py:35
  232.2 27.3 %collective-permute-start.10 = (bf16[256,2048]{1,0:T(8,128)(2,1)}, bf16[256,2048]{1,0:T(8,128)(2,1)S(1)}, u32[]{:S(2)}, u32[]{:S(2)}) collective-permute-start(bf16[256,2048]{1,0:T(8,128)(2,1)} %get-tuple-element.388), channel_id=1, source_target_pairs={{6,4},{7,5},{14,12},{15,13},{22,20},{23,21},{30,28},{31,29}} | collective-permute-start | bytes 3145736 | tf_op jit(solution)/shard_map/ppermute | solution.py:58
  233.5 26.0 %collective-permute-start.9 = (bf16[256,2048]{1,0:T(8,128)(2,1)}, bf16[256,2048]{1,0:T(8,128)(2,1)}, u32[]{:S(2)}, u32[]{:S(2)}) collective-permute-start(bf16[256,2048]{1,0:T(8,128)(2,1)} %get-tuple-element.389), channel_id=1, source_target_pairs={{0,2},{1,3},{8,10},{9,11},{16,18},{17,19},{24,26},{25,27}} | collective-permute-start | bytes 3145736 | tf_op jit(solution)/shard_map/ppermute | solution.py:55
  235.3 65.4 %all-to-all-start.2 = ((bf16[4,512,1024]{2,1,0:T(8,128)(2,1)}), bf16[4,512,1024]{2,1,0:T(8,128)(2,1)}, u32[]{:S(2)}, u32[]{:S(2)}) async-start(bf16[4,512,1024]{2,1,0:T(8,128)(2,1)} %rows_product.3), calls=%async_computation.2 | async-start | bytes 8388608 | tf_op jit(solution)/shard_map/all_to_all | solution.py:635
  240.1 165.1 %all-gather.9.cloned.1.call-start = ((), (), s32[]{:S(2)}) async-start(), calls=%async_computation.9 | async-start | bytes 5242880 | tf_op jit(solution)/shard_map/all_gather | solution.py:641
  240.2 19.3 %copy-start.35 = (bf16[1024,2048]{1,0:T(8,128)(2,1)S(1)}, bf16[1024,2048]{1,0:T(8,128)(2,1)}, u32[]{:S(2)}) copy-start(bf16[1024,2048]{1,0:T(8,128)(2,1)} %pair_product.5) | copy-start | bytes 12582916
  263.2 26.1 %collective-permute-start.11 = (bf16[256,2048]{1,0:T(8,128)(2,1)}, bf16[256,2048]{1,0:T(8,128)(2,1)S(1)}, u32[]{:S(2)}, u32[]{:S(2)}) collective-permute-start(bf16[256,2048]{1,0:T(8,128)(2,1)} %get-tuple-element.387), channel_id=1, source_target_pairs={{0,2},{2,4},{1,3},{3,5},{8,10},{10,12},{9,11},{11,13},{16,18},{18,... | collective-permute-start | bytes 3145736 | tf_op jit(solution)/shard_map/ppermute | solution.py:55
  264.5 26.2 %collective-permute-start.12 = (bf16[256,2048]{1,0:T(8,128)(2,1)}, bf16[256,2048]{1,0:T(8,128)(2,1)}, u32[]{:S(2)}, u32[]{:S(2)}) collective-permute-start(bf16[256,2048]{1,0:T(8,128)(2,1)} %get-tuple-element.386), channel_id=1, source_target_pairs={{4,2},{6,4},{5,3},{7,5},{12,10},{14,12},{13,11},{15,13},{20,18},{2... | collective-permute-start | bytes 3145736 | tf_op jit(solution)/shard_map/ppermute | solution.py:58
  295.2 25.3 %collective-permute-start.13 = (bf16[256,2048]{1,0:T(8,128)(2,1)}, bf16[256,2048]{1,0:T(8,128)(2,1)}, u32[]{:S(2)}, u32[]{:S(2)}) collective-permute-start(bf16[256,2048]{1,0:T(8,128)(2,1)} %get-tuple-element.385), channel_id=1, source_target_pairs={{0,2},{2,4},{4,6},{1,3},{3,5},{5,7},{8,10},{10,12},{12,14},{9,11},... | collective-permute-start | bytes 3145736 | tf_op jit(solution)/shard_map/ppermute | solution.py:55
  297.1 25.1 %collective-permute-start.14 = (bf16[256,2048]{1,0:T(8,128)(2,1)S(1)}, bf16[256,2048]{1,0:T(8,128)(2,1)}, u32[]{:S(2)}, u32[]{:S(2)}) collective-permute-start(bf16[256,2048]{1,0:T(8,128)(2,1)S(1)} %get-tuple-element.384), channel_id=1, source_target_pairs={{2,0},{4,2},{6,4},{3,1},{5,3},{7,5},{10,8},{12,10},{14,12},{11,9},... | collective-permute-start | bytes 3145736 | tf_op jit(solution)/shard_map/ppermute | solution.py:58
  322.2 52.9 %all-to-all-start.3 = ((bf16[4,512,1024]{2,1,0:T(8,128)(2,1)}), bf16[4,512,1024]{2,1,0:T(8,128)(2,1)}, u32[]{:S(2)}, u32[]{:S(2)}) async-start(bf16[4,512,1024]{2,1,0:T(8,128)(2,1)} %rows_product.4), calls=%async_computation.3 | async-start | bytes 8388608 | tf_op jit(solution)/shard_map/all_to_all | solution.py:635
  329.5 22.9 %copy-start.23 = (bf16[1024,768]{1,0:T(8,128)(2,1)S(1)}, bf16[1024,768]{1,0:T(8,128)(2,1)}, u32[]{:S(2)}) copy-start(bf16[1024,768]{1,0:T(8,128)(2,1)} %copy-done.22) | copy-start | bytes 4718596
  329.5 22.9 %copy-start.33 = (bf16[1024,256]{1,0:T(8,128)(2,1)S(1)}, bf16[1024,256]{1,0:T(8,128)(2,1)}, u32[]{:S(2)}) copy-start(bf16[1024,256]{1,0:T(8,128)(2,1)} %get-tuple-element.316.do_ref) | copy-start | bytes 1572868
  379.2 26.0 %copy-start.5 = (bf16[1024,768]{1,0:T(8,128)(2,1)S(1)}, bf16[1024,768]{1,0:T(8,128)(2,1)}, u32[]{:S(2)}) copy-start(bf16[1024,768]{1,0:T(8,128)(2,1)} %copy-done.4) | copy-start | bytes 4718596
  417.7 19.2 %collective-permute-start.16 = (bf16[1024,2048]{1,0:T(8,128)(2,1)}, bf16[1024,2048]{1,0:T(8,128)(2,1)}, u32[]{:S(2)}, u32[]{:S(2)}) collective-permute-start(bf16[1024,2048]{1,0:T(8,128)(2,1)} %pair_product.6), channel_id=1, source_target_pairs={{0,1},{1,0},{2,3},{3,2},{4,5},{5,4},{6,7},{7,6},{8,9},{9,8},{10,11... | collective-permute-start | bytes 12582920 | tf_op jit(solution)/shard_map/ppermute | solution.py:35
  418.3 52.6 %all-to-all-start.4 = ((bf16[4,512,1024]{2,1,0:T(8,128)(2,1)}), bf16[4,512,1024]{2,1,0:T(8,128)(2,1)}, u32[]{:S(2)}, u32[]{:S(2)}) async-start(bf16[4,512,1024]{2,1,0:T(8,128)(2,1)} %rows_product.5), calls=%async_computation.4 | async-start | bytes 8388608 | tf_op jit(solution)/shard_map/all_to_all | solution.py:635
  423.6 232.8 %all-gather.11.cloned.1.call-start = ((), (), s32[]{:S(2)}) async-start(), calls=%async_computation.10 | async-start | bytes 5242880 | tf_op jit(solution)/shard_map/all_gather | solution.py:641
  441.3 39.1 %collective-permute-start.19 = (bf16[256,2048]{1,0:T(8,128)(2,1)}, bf16[256,2048]{1,0:T(8,128)(2,1)}, u32[]{:S(2)}, u32[]{:S(2)}) collective-permute-start(bf16[256,2048]{1,0:T(8,128)(2,1)} %get-tuple-element.383), channel_id=1, source_target_pairs={{0,2},{1,3},{8,10},{9,11},{16,18},{17,19},{24,26},{25,27}} | collective-permute-start | bytes 3145736 | tf_op jit(solution)/shard_map/ppermute | solution.py:55
  442.9 49.6 %collective-permute-start.20 = (bf16[256,2048]{1,0:T(8,128)(2,1)}, bf16[256,2048]{1,0:T(8,128)(2,1)}, u32[]{:S(2)}, u32[]{:S(2)}) collective-permute-start(bf16[256,2048]{1,0:T(8,128)(2,1)} %get-tuple-element.382), channel_id=1, source_target_pairs={{6,4},{7,5},{14,12},{15,13},{22,20},{23,21},{30,28},{31,29}} | collective-permute-start | bytes 3145736 | tf_op jit(solution)/shard_map/ppermute | solution.py:58
  475.0 27.3 %copy-start.46 = (bf16[2048]{0:T(1024)(128)(2,1)S(1)}, bf16[2048]{0:T(1024)(128)(2,1)}, u32[]{:S(2)}) copy-start(bf16[2048]{0:T(1024)(128)(2,1)} %param.31) | copy-start | bytes 12292
  475.0 27.3 %copy-start.47 = (bf16[2048]{0:T(1024)(128)(2,1)S(1)}, bf16[2048]{0:T(1024)(128)(2,1)}, u32[]{:S(2)}) copy-start(bf16[2048]{0:T(1024)(128)(2,1)} %param.35) | copy-start | bytes 12292
  475.0 49.0 %collective-permute-start.17 = (bf16[512,1024]{1,0:T(8,128)(2,1)}, bf16[512,1024]{1,0:T(8,128)(2,1)}, u32[]{:S(2)}, u32[]{:S(2)}) collective-permute-start(bf16[512,1024]{1,0:T(8,128)(2,1)} %fusion.34.refs_0_), channel_id=1, source_target_pairs={{0,2},{2,4},{4,6},{1,3},{3,5},{5,7},{8,10},{10,12},{12,14},{9,11},... | collective-permute-start | bytes 3145736 | tf_op jit(solution)/shard_map/ppermute | solution.py:45
  477.0 60.4 %collective-permute-start.18 = (bf16[512,1024]{1,0:T(8,128)(2,1)}, bf16[512,1024]{1,0:T(8,128)(2,1)}, u32[]{:S(2)}, u32[]{:S(2)}) collective-permute-start(bf16[512,1024]{1,0:T(8,128)(2,1)} %fusion.34.refs_0_), channel_id=1, source_target_pairs={{2,0},{4,2},{6,4},{3,1},{5,3},{7,5},{10,8},{12,10},{14,12},{11,9},... | collective-permute-start | bytes 3145736 | tf_op jit(solution)/shard_map/ppermute | solution.py:46
  496.9 56.7 %collective-permute-start.21 = (bf16[256,2048]{1,0:T(8,128)(2,1)}, bf16[256,2048]{1,0:T(8,128)(2,1)}, u32[]{:S(2)}, u32[]{:S(2)}) collective-permute-start(bf16[256,2048]{1,0:T(8,128)(2,1)} %get-tuple-element.381), channel_id=1, source_target_pairs={{0,2},{2,4},{1,3},{3,5},{8,10},{10,12},{9,11},{11,13},{16,18},{18,... | collective-permute-start | bytes 3145736 | tf_op jit(solution)/shard_map/ppermute | solution.py:55
  498.2 73.5 %collective-permute-start.22 = (bf16[256,2048]{1,0:T(8,128)(2,1)}, bf16[256,2048]{1,0:T(8,128)(2,1)}, u32[]{:S(2)}, u32[]{:S(2)}) collective-permute-start(bf16[256,2048]{1,0:T(8,128)(2,1)} %get-tuple-element.380), channel_id=1, source_target_pairs={{4,2},{6,4},{5,3},{7,5},{12,10},{14,12},{13,11},{15,13},{20,18},{2... | collective-permute-start | bytes 3145736 | tf_op jit(solution)/shard_map/ppermute | solution.py:58
  505.7 65.9 %copy-start.36 = (bf16[1024,2048]{1,0:T(8,128)(2,1)S(1)}, bf16[1024,2048]{1,0:T(8,128)(2,1)}, u32[]{:S(2)}) copy-start(bf16[1024,2048]{1,0:T(8,128)(2,1)} %pair_product.7) | copy-start | bytes 12582916
  507.0 81.6 %copy-start.8 = (bf16[1024,1024]{1,0:T(8,128)(2,1)S(1)}, bf16[1024,1024]{1,0:T(8,128)(2,1)}, u32[]{:S(2)}) copy-start(bf16[1024,1024]{1,0:T(8,128)(2,1)} %get-tuple-element.335.refs_2_.a_ref) | copy-start | bytes 6291460
  576.4 12.5 %copy-start.10 = (bf16[1024,1024]{1,0:T(8,128)(2,1)S(1)}, bf16[1024,1024]{1,0:T(8,128)(2,1)}, u32[]{:S(2)}) copy-start(bf16[1024,1024]{1,0:T(8,128)(2,1)} %get-tuple-element.350.refs_3_.a_ref) | copy-start | bytes 6291460
  576.4 26.4 %collective-permute-start.25 = (bf16[256,2048]{1,0:T(8,128)(2,1)}, bf16[256,2048]{1,0:T(8,128)(2,1)}, u32[]{:S(2)}, u32[]{:S(2)}) collective-permute-start(bf16[256,2048]{1,0:T(8,128)(2,1)} %get-tuple-element.379), channel_id=1, source_target_pairs={{0,2},{2,4},{4,6},{1,3},{3,5},{5,7},{8,10},{10,12},{12,14},{9,11},... | collective-permute-start | bytes 3145736 | tf_op jit(solution)/shard_map/ppermute | solution.py:55
  578.5 26.3 %collective-permute-start.26 = (bf16[256,2048]{1,0:T(8,128)(2,1)}, bf16[256,2048]{1,0:T(8,128)(2,1)}, u32[]{:S(2)}, u32[]{:S(2)}) collective-permute-start(bf16[256,2048]{1,0:T(8,128)(2,1)} %get-tuple-element.378), channel_id=1, source_target_pairs={{2,0},{4,2},{6,4},{3,1},{5,3},{7,5},{10,8},{12,10},{14,12},{11,9},... | collective-permute-start | bytes 3145736 | tf_op jit(solution)/shard_map/ppermute | solution.py:58
  581.8 43.3 %collective-permute-start.23 = (bf16[512,1024]{1,0:T(8,128)(2,1)}, bf16[512,1024]{1,0:T(8,128)(2,1)S(1)}, u32[]{:S(2)}, u32[]{:S(2)}) collective-permute-start(bf16[512,1024]{1,0:T(8,128)(2,1)} %collective-permute-done.17.refs_1_), channel_id=1, source_target_pairs={{2,4},{4,6},{3,5},{5,7},{10,12},{12,14},{11,13},{13,15},{18,20},{2... | collective-permute-start | bytes 3145736 | tf_op jit(solution)/shard_map/ppermute | solution.py:45
  584.7 41.4 %collective-permute-start.24 = (bf16[512,1024]{1,0:T(8,128)(2,1)}, bf16[512,1024]{1,0:T(8,128)(2,1)}, u32[]{:S(2)}, u32[]{:S(2)}) collective-permute-start(bf16[512,1024]{1,0:T(8,128)(2,1)} %collective-permute-done.18.refs_4_), channel_id=1, source_target_pairs={{2,0},{4,2},{3,1},{5,3},{10,8},{12,10},{11,9},{13,11},{18,16},{20,... | collective-permute-start | bytes 3145736 | tf_op jit(solution)/shard_map/ppermute | solution.py:46
  590.0 12.2 %all-to-all-start.5 = ((f32[4,1,3840]{2,1,0:T(1,128)}), f32[4,1,3840]{2,1,0:T(1,128)S(1)}, u32[]{:S(2)}, u32[]{:S(2)}) async-start(f32[4,1,3840]{2,1,0:T(1,128)} %broadcast_in_dim.91), calls=%async_computation.5 | async-start | bytes 122880 | tf_op jit(solution)/shard_map/all_to_all | solution.py:39
  599.8 50.1 %collective-permute-start.15 = (bf16[1,1,256,2048]{3,2,1,0:T(8,128)(2,1)}, bf16[1,1,256,2048]{3,2,1,0:T(8,128)(2,1)}, u32[]{:S(2)}, u32[]{:S(2)}) collective-permute-start(bf16[1,1,256,2048]{3,2,1,0:T(8,128)(2,1)} %bitcast.24), channel_id=1, source_target_pairs={{0,1},{1,0},{2,3},{3,2},{4,5},{5,4},{6,7},{7,6},{8,9},{9,8},{10,11... | collective-permute-start | bytes 3145736 | tf_op jit(solution)/shard_map/ppermute | solution.py:35
  626.1 47.7 %collective-permute-start.29 = (bf16[512,1024]{1,0:T(8,128)(2,1)S(1)}, bf16[512,1024]{1,0:T(8,128)(2,1)S(1)}, u32[]{:S(2)}, u32[]{:S(2)}) collective-permute-start(bf16[512,1024]{1,0:T(8,128)(2,1)S(1)} %collective-permute-done.23.refs_2_), channel_id=1, source_target_pairs={{4,6},{5,7},{12,14},{13,15},{20,22},{21,23},{28,30},{29,31}} | collective-permute-start | bytes 3145736 | tf_op jit(solution)/shard_map/ppermute | solution.py:45
  627.5 47.4 %collective-permute-start.30 = (bf16[512,1024]{1,0:T(8,128)(2,1)}, bf16[512,1024]{1,0:T(8,128)(2,1)}, u32[]{:S(2)}, u32[]{:S(2)}) collective-permute-start(bf16[512,1024]{1,0:T(8,128)(2,1)} %collective-permute-done.24.refs_5_), channel_id=1, source_target_pairs={{2,0},{3,1},{10,8},{11,9},{18,16},{19,17},{26,24},{27,25}} | collective-permute-start | bytes 3145736 | tf_op jit(solution)/shard_map/ppermute | solution.py:46
  629.2 11.9 %copy-start.39 = (bf16[256,2048]{1,0:T(8,128)(2,1)S(1)}, bf16[256,2048]{1,0:T(8,128)(2,1)}, u32[]{:S(2)}) copy-start(bf16[256,2048]{1,0:T(8,128)(2,1)} %dynamic-slice_bitcast_fusion) | copy-start | bytes 3145732
  635.1 27.2 %all-to-all-start.6 = ((f32[4,1,5888]{2,1,0:T(1,128)}), f32[4,1,5888]{2,1,0:T(1,128)S(1)}, u32[]{:S(2)}, u32[]{:S(2)}) async-start(f32[4,1,5888]{2,1,0:T(1,128)} %broadcast_in_dim.92), calls=%async_computation.6 | async-start | bytes 188416 | tf_op jit(solution)/shard_map/all_to_all | solution.py:39
  642.4 9.8 %copy-start.17 = (bf16[2048,1024]{1,0:T(8,128)(2,1)S(1)}, bf16[2048,1024]{1,0:T(8,128)(2,1)}, u32[]{:S(2)}) copy-start(bf16[2048,1024]{1,0:T(8,128)(2,1)} %all-gather.9.cloned.1.call-done) | copy-start | bytes 12582916
  647.4 35.1 %collective-permute-start.27 = (bf16[1,1,256,2048]{3,2,1,0:T(8,128)(2,1)}, bf16[1,1,256,2048]{3,2,1,0:T(8,128)(2,1)}, u32[]{:S(2)}, u32[]{:S(2)}) collective-permute-start(bf16[1,1,256,2048]{3,2,1,0:T(8,128)(2,1)} %bitcast.36), channel_id=1, source_target_pairs={{0,1},{1,0},{2,3},{3,2},{4,5},{5,4},{6,7},{7,6},{8,9},{9,8},{10,11... | collective-permute-start | bytes 3145736 | tf_op jit(solution)/shard_map/ppermute | solution.py:35
  663.0 6.3 all-to-all-start.7
  669.4 3.9 collective-permute-start.28
  676.1 9.0 %copy-start.1 = (bf16[2,256,2048]{2,1,0:T(8,128)(2,1)S(1)}, bf16[2,256,2048]{2,1,0:T(8,128)(2,1)}, u32[]{:S(2)}) copy-start(bf16[2,256,2048]{2,1,0:T(8,128)(2,1)} %param.19) | copy-start | bytes 6291460
  (28 other events, 66.0 us)
Sparse Core Ops, SparseCore 0:
  90.6 86.9 all-gather.6
  322.3 82.8 all-gather.8
  426.0 134.6 all-gather.10

commit v3 on v2

--- a/solution.py
+++ b/solution.py
@@ -261,17 +261,20 @@
     )(offs, prefix, ordered, stats, grad_context, *tables)
 
 
-def pair_kernel(split, a_ref, b_ref, w_ref, o_ref):
+def pair_kernel(split, a_ref, b_ref, w_ref, *refs):
     nt = (((1,), (1,)), ((), ()))
     o = lax.dot_general(a_ref[...], w_ref[:, :split], nt, preferred_element_type=F32)
     o += lax.dot_general(b_ref[...], w_ref[:, split:], nt, preferred_element_type=F32)
-    o_ref[...] = o.astype(o_ref.dtype)
-
-
-def pair_product(a, b, w):
+    for more in refs[:-1]:
+        o += more[...].astype(F32)
+    refs[-1][...] = o.astype(refs[-1].dtype)
+
+
+def pair_product(a, b, w, more=()):
     n, depth = w.shape
     m = a.shape[0]
     bn = min(512, n)
+    out = pl.BlockSpec((m, bn), lambda j: (0, j))
     return pl.pallas_call(
         functools.partial(pair_kernel, a.shape[1]),
         out_shape=jax.ShapeDtypeStruct((m, n), BF16),
@@ -280,12 +283,13 @@
             pl.BlockSpec((m, a.shape[1]), lambda j: (0, 0), pipeline_mode=pl.Buffered(1)),
             pl.BlockSpec((m, b.shape[1]), lambda j: (0, 0), pipeline_mode=pl.Buffered(1)),
             pl.BlockSpec((bn, depth), lambda j: (j, 0)),
-        ],
-        out_specs=pl.BlockSpec((m, bn), lambda j: (0, j)),
+        ]
+        + [out] * len(more),
+        out_specs=out,
         compiler_params=pltpu.CompilerParams(vmem_limit_bytes=48 << 20),
         cost_estimate=FREE,
         name="pair_product",
-    )(a, b, w)
+    )(a, b, w, *more)
 
 
 def pack_kernel(pieces, here_ref, *refs):
@@ -387,45 +391,27 @@
     )(here.reshape(1), *blocks)
 
 
-def place_kernel(size, pairs, here_ref, *refs):
-    blocks, outs = refs[: 2 * size - 1], refs[2 * size - 1 :]
-    m, here = pl.program_id(0), here_ref[0]
-    spans = [[(p * 3 + n) * PAIR for p in range(pairs)] for n in range(3)]
-    spans.append([(3 * pairs + p) * PAIR for p in range(pairs)])
-
-    def put(block):
-        for out, starts in zip(outs, spans):
-            for p, at in enumerate(starts):
-                out[:, p * PAIR : (p + 1) * PAIR] = block[:, at : at + PAIR].astype(F32)
-
-    pl.when(m == 0)(lambda: put(blocks[0]))
-    for k in range(1, size):
-        pl.when((m == k) & (here >= k))(functools.partial(put, blocks[k]))
-        pl.when((m == k) & (here < k))(functools.partial(put, blocks[2 * size - 1 - k]))
-
-
-def place(blocks, here, pairs):
-    size = len(blocks)
-    rows, span = blocks[0].shape
-    blocks = [blocks[0]] + [x[0] for x in blocks[1:]] + [x[1] for x in blocks[1:]]
+def place_kernel(pairs, a_ref, *outs):
+    starts = [[(p * 3 + n) * PAIR for p in range(pairs)] for n in range(3)]
+    starts.append([(3 * pairs + p) * PAIR for p in range(pairs)])
+    for out, at in zip(outs, starts):
+        for p in range(pairs):
+            out[:, p * PAIR : (p + 1) * PAIR] = a_ref[0, :, at[p] : at[p] + PAIR].astype(F32)
+
+
+def place(blocks, pairs):
+    n, rows, span = blocks.shape
     width = pairs * PAIR
     return pl.pallas_call(
-        functools.partial(place_kernel, size, pairs),
-        out_shape=(jax.ShapeDtypeStruct((rows, size * width), F32),) * 4,
-        grid_spec=pltpu.PrefetchScalarGridSpec(
-            num_scalar_prefetch=1,
-            grid=(size,),
-            in_specs=[pl.BlockSpec((rows, span), lambda m, h: (0, 0), pipeline_mode=pl.Buffered(1))]
-            * len(blocks),
-            out_specs=(
-                pl.BlockSpec((rows, width), lambda m, h: (0, lax.rem(h[0] - m + size, size))),
-            )
-            * 4,
-        ),
+        functools.partial(place_kernel, pairs),
+        out_shape=(jax.ShapeDtypeStruct((rows, n * width), F32),) * 4,
+        grid=(n,),
+        in_specs=[pl.BlockSpec((1, rows, span), lambda c: (c, 0, 0))],
+        out_specs=(pl.BlockSpec((rows, width), lambda c: (0, c)),) * 4,
         compiler_params=pltpu.CompilerParams(vmem_limit_bytes=48 << 20),
         cost_estimate=FREE,
         name="place",
-    )(here.reshape(1), *blocks)
+    )(blocks)
 
 
 def widen_kernel(a_ref, o_ref):
@@ -621,7 +607,9 @@
 
     tables = (cos, sa, sb)
     first_all = lax.all_to_all(first, "fsdp", 0, 0, tiled=True)
-    h_in, second, tables = meet((gather_on(h_in), second, tables))
+    h_in, second, tables, b_up, b_qkv, offs, prefix = meet(
+        (gather_on(h_in), second, tables, b_up, b_qkv, offs, prefix)
+    )
     while len(h_in) < nc:
         h_in = meet(gather_on(h_in))
     g_own, h_in = meet((g_own, h_in))
@@ -679,28 +667,22 @@
     theirs, act, context = meet(
         ([pair_product(act[k], context[k], w_second) for k in range(1, nt)], act, context)
     )
+    o_got = [xor_swap(t, "tp", nt, k) for k, t in zip(range(1, nt), theirs)]
     full_down = rows_product([(grad, act)], nf)
-    grad, full_down, slope, theirs, act = meet((grad, full_down, slope, theirs, act))
+    grad, full_down, slope, o_got, act = meet((grad, full_down, slope, o_got, act))
     d_rows = send_rows(full_down)
-    o_got = [xor_swap(t, "tp", nt, k) for k, t in zip(range(1, nt), theirs)]
-    o_got, o_mine = meet((o_got, pair_product(act[0], context[0], w_second)))
-    o_parts = parts_of(o_mine, o_got)
-    o_sum = sum_step(None, o_parts, 1, nc)
-    downs, step = [], 2
+    both = pair_product(act[0], context[0], w_second, o_got)
+    both = jnp.moveaxis(both.reshape(own_seqs, nc, rows, width), 1, 0).reshape(nc, own, width)
+    both, grad, slope = meet((both, grad, slope))
+    o_sum = lax.psum_scatter(both, "ctx", scatter_dimension=0, tiled=True)
+    downs = []
     for n in range(nt):
         downs.append(down_product(grad[n], w_second, slope[n]))
-        downs, grad, hidden, o_sum = meet((downs, grad, hidden, o_sum))
-        if step < nc:
-            o_sum = sum_step(o_sum, o_parts, step, nc)
-            step += 1
+        downs, grad, hidden = meet((downs, grad, hidden))
     dup, grad_context = [d[0] for d in downs], [d[1] for d in downs]
     full_up = rows_product([(hidden, dup)], nf)
-    full_up, d_sum, done, grad_context, o_sum = meet(
-        (full_up, sum_rows(d_rows), done, grad_context, o_sum)
-    )
-    for k in range(step, nc):
-        o_sum = meet(sum_step(o_sum, o_parts, k, nc))
-    d_cols = gather_cols(d_sum)
+    full_up, d_rows = meet((full_up, d_rows))
+    d_sum, done, grad_context = meet((sum_rows(d_rows), done, grad_context))
     u_rows = send_rows(full_up)
     back = []
     for n in range(seqs):
@@ -711,33 +693,37 @@
                 offs, prefix[n : n + 1], tables,
             )
         )
-        back, done, grad_context = meet((back, done, grad_context))
+        back, done, grad_context, o_sum = meet((back, done, grad_context, o_sum))
+        if n == 0:
+            d_cols = gather_cols(d_sum)
     dqkv = [jnp.concatenate(back[n * own_seqs : (n + 1) * own_seqs]) for n in range(nt)]
-    u_sum, dqkv, hidden, grad = meet((sum_rows(u_rows), dqkv, hidden, grad))
+    u_rows, dqkv, hidden, grad, dup = meet((u_rows, dqkv, hidden, grad, dup))
+
+    theirs, dup, dqkv, hidden = meet(
+        ([pair_product(dup[k], dqkv[k], w_first) for k in range(1, nt)], dup, dqkv, hidden)
+    )
+    h_got = [xor_swap(t, "tp", nt, k) for k, t in zip(range(1, nt), theirs)]
+    u_sum = sum_rows(u_rows)
     qo_full = rows_product([(hidden, dqkv), (grad, context)], nf)
-    qo_full, dqkv, dup, u_sum, d_cols = meet((qo_full, dqkv, dup, u_sum, d_cols))
+    qo_full, dqkv, dup, h_got, u_sum = meet((qo_full, dqkv, dup, h_got, u_sum))
+    qo = send_rows(qo_full)
+    h_both, d_cols, u_sum = meet((pair_product(dup[0], dqkv[0], w_first, h_got), d_cols, u_sum))
     u_cols = gather_cols(u_sum)
-    qo = send_rows(qo_full)
-    theirs, dup, dqkv = meet(
-        ([pair_product(dup[k], dqkv[k], w_first) for k in range(1, nt)], dup, dqkv)
-    )
-    h_got = [xor_swap(t, "tp", nt, k) for k, t in zip(range(1, nt), theirs)]
-    h_got, h_mine = meet((h_got, pair_product(dup[0], dqkv[0], w_first)))
-    h_parts = parts_of(h_mine, h_got)
+    h_parts = parts_of(h_both, [])
+    dw_down = widen(d_cols)
+    h_sum, qo, dw_down = meet((sum_step(None, h_parts, 1, nc), qo, dw_down))
+    qo_sum = sum_rows(qo)
+    for k in range(2, nc):
+        h_sum = sum_step(h_sum, h_parts, k, nc)
+        if k == 2:
+            h_sum, qo_sum = meet((h_sum, qo_sum))
+        h_sum = meet(h_sum)
+    grad_hidden = total(h_parts(0) + list(h_sum))
+    u_cols, h_sum = meet((u_cols, h_sum))
+    dw_up = widen(u_cols)
+    qo_cols = gather_cols(qo_sum)
     col_sum = lambda a: jnp.sum(a.astype(F32), axis=0)
-    bias_sums = jnp.concatenate(
-        [total([col_sum(a) for a in array]) for array in (dqkv, dup, grad)]
-    )[None]
-    bias_sums = jnp.sum(to_all(bias_sums, "fsdp", nf).reshape(nf, -1), axis=0)
-    h_sum = meet(sum_step(None, h_parts, 1, nc))
-    qo = [sum_rows(qo)]
-    for k in range(2, nc + 1):
-        if k < nc:
-            h_sum = sum_step(h_sum, h_parts, k, nc)
-        qo = gather_on(qo)
-        qo, h_sum = meet((qo, h_sum))
-        if k == nc - 1:
-            grad_hidden = total(h_parts(0) + list(h_sum))
+    out_own = total([x, o_sum.reshape(own, width), out_bias, down_bias])
 
     gs = grad_hidden * gain
     grad_normed = inv_std * (
@@ -746,7 +732,6 @@
     )
     in_own = g_own.astype(F32) + grad_normed
     norm_sums = jnp.concatenate([col_sum(grad_hidden * normed), col_sum(grad_hidden)])
-    out_own = total([x] + o_parts(0) + list(o_sum) + [out_bias, down_bias])
 
     def whole_tokens(own_rows):
         mine = own_rows.astype(BF16).reshape(1, own_seqs, rows, width)
@@ -759,10 +744,12 @@
     output = whole_tokens(out_own)
     input_grad = whole_tokens(in_own)
 
-    dw_down = widen(d_cols)
-    dw_up = widen(u_cols)
-    dw_qkv = place(qo, ci, pairs)
-
+    dw_qkv = place(qo_cols, pairs)
+
+    bias_sums = jnp.concatenate(
+        [total([col_sum(a) for a in array]) for array in (dqkv, dup, grad)]
+    )[None]
+    bias_sums = jnp.sum(to_all(bias_sums, "fsdp", nf).reshape(nf, -1), axis=0)
     small = 3 * inner + units
     obias = bias_sums[small:]
     got = to_all(jnp.concatenate([bias_sums[:small], norm_sums])[None], "ctx", nc).reshape(nc, -1)

time: 699 us -> 641 us (0.917)
  waiting for transfers between devices: 216 us -> 176 us
  other arithmetic: 68.2 us -> 50.1 us
  local copies, waits for them, and re-layouts: 45.4 us -> 55.4 us
  starting transfers between devices: 112 us -> 103 us
    ppermute x6 -> x3, waiting for transfers between devices: 71.3 us -> 34.6 us  [gather_step(): lax.ppermute(left, axis, [(j, j + 1) for j in range(step - 1, size - 1)])]
    ppermute x6 -> x3, waiting for transfers between devices: 29.4 us -> 52.9 us  [sum_step(): lax.ppermute(total(a).astype(BF16), axis, [(j, j + 1) for j in range(min(...]
    convert_element_type x6 -> x2, other arithmetic: 26.1 us -> 6.81 us  [sum_step(): total(b).astype(BF16)]
    ppermute x7, starting transfers between devices: 12.7 us -> 29.4 us  [xor_swap(): return lax.ppermute(value, axis, [(j, j ^ step) for j in range(size)])]
    ppermute x6 -> x3, waiting for transfers between devices: 17.9 us -> 1.83 us  [gather_step(): lax.ppermute(right, axis, [(j, j - 1) for j in range(1, size - step + 1)])]
    ppermute x6 -> x3, waiting for transfers between devices: 44 us -> 59.4 us  [sum_step(): lax.ppermute(total(b).astype(BF16), axis, [(j, j - 1) for j in range(max(...]
    all_to_all x3, waiting for transfers between devices: 26.7 us -> 12.6 us  [send_rows(): return lax.all_to_all(full, 'fsdp', 0, 0, tiled=True)]
    ppermute x6 -> x3, starting transfers between devices: 17.3 us -> 6.84 us  [gather_step(): lax.ppermute(right, axis, [(j, j - 1) for j in range(1, size - step + 1)])]
  transfers between devices with their start and end apart: 42 -> 32, of which waited for: 22 -> 12; matrix products, arithmetic and copies ran while one was open for 10% -> 10% of each run, Pallas kernels for 31% -> 35%
where the time goes in v3:
time: 641 us; the launch traced here: 632 us
  Pallas kernels  233 us (36%)
  waiting for transfers between devices  176 us (27%)
  starting transfers between devices  103 us (16%)
  local copies, waits for them, and re-layouts  55.4 us (9%)
  other arithmetic  50.1 us (8%)
  between operations  14.5 us (2%)
    ppermute x3, waiting for transfers between devices, sum_step(): lax.ppermute(total(b).astype(BF16), axis, [(j, j - 1) for j in range(max(...  59.4 us
    ppermute x3, waiting for transfers between devices, sum_step(): lax.ppermute(total(a).astype(BF16), axis, [(j, j + 1) for j in range(min(...  52.9 us
    pallas_call x2, Pallas kernels, attend_back(): pl.pallas_call(functools.partial(attend_back_kernel, length // offs.shape...  43.3 us
    pallas_call x3, Pallas kernels, rows_product(): pl.pallas_call(functools.partial(rows_kernel, [len(a) for a, _ in product...  41.8 us
    pallas_call x4, Pallas kernels, pair_product(): pl.pallas_call(functools.partial(pair_kernel, a.shape[1]), out_shape=jax....  40.2 us
    unnamed x102, local copies, waits for them, and re-layouts  36.3 us
    ppermute x3, waiting for transfers between devices, gather_step(): lax.ppermute(left, axis, [(j, j + 1) for j in range(step - 1, size - 1)])  34.6 us
    pallas_call x2, Pallas kernels, attend(): pl.pallas_call(functools.partial(attend_kernel, length // offs.shape[0],...  29.7 us
  transfers between devices with their start and end apart: 32, of which 12 were waited for; matrix products, arithmetic and copies ran while one was open for 10% of the time, Pallas kernels for 35%

profile of v3, /device:TPU:19, one launch (start us, length us, event | category | flops | bytes accessed | tf_op | source)
XLA Modules:
  0.0 632.3 jit_solution(13702479321691836227)
XLA Ops:
  10.5 2.7 fusion.10.refs_0_
  13.2 3.2 collective-permute-start
  23.1 3.6 pack_columns.3
  26.8 5.8 all-to-all-start
  42.8 3.0 fusion.25
  45.8 4.2 collective-permute-start.2
  50.0 3.1 collective-permute-start.3
  53.2 18.1 %collective-permute-done.2.refs_2_ = bf16[256,2048]{1,0:T(8,128)(2,1)} collective-permute-done((bf16[256,2048]{1,0:T(8,128)(2,1)}, bf16[256,2048]{1,0:T(8,128)(2,1)}, u32[]{:S(2)}, u32[]{:S(2)}) %collective-permute-start.2) | collective-permute-done | bytes 1048608 | tf_op jit(solution)/shard_map/ppermute | solution.py:45
  73.1 3.3 collective-permute-start.4
  79.1 16.5 %collective-permute-done.4.refs_3_ = bf16[256,2048]{1,0:T(8,128)(2,1)} collective-permute-done((bf16[256,2048]{1,0:T(8,128)(2,1)}, bf16[256,2048]{1,0:T(8,128)(2,1)}, u32[]{:S(2)}, u32[]{:S(2)}) %collective-permute-start.4) | collective-permute-done | bytes 1048608 | tf_op jit(solution)/shard_map/ppermute | solution.py:45
  95.7 5.7 in_order.1
  101.4 3.4 collective-permute-start.6
  104.8 7.5 %all-to-all-done = bf16[4,512,1792]{2,1,0:T(8,128)(2,1)} async-done(((bf16[4,512,1792]{2,1,0:T(8,128)(2,1)}), bf16[4,512,1792]{2,1,0:T(8,128)(2,1)}, u32[]{:S(2)}, u32[]{:S(2)}) %all-to-all-start) | async-done | bytes 7340064 | tf_op jit(solution)/shard_map/all_to_all | solution.py:609
  112.3 6.1 all-to-all-start.1
  120.0 11.1 %up_product.2 = (bf16[1024,1024]{1,0:T(8,128)(2,1)}, bf16[1024,1024]{1,0:T(8,128)(2,1)}) custom-call(bf16[1024,2048]{1,0:T(8,128)(2,1)} %bitcast.96, bf16[2048,1792]{1,0:T(8,128)(2,1)} %bitcast.4.w_ref.refs_0_.refs_1_.refs_2_, f32[1,1024]{1,0:T(1,128)} %bitcast.108), custom_call_target="tpu_custom_call" | custom-call | flops 1 | bytes 1 | tf_op jit(solution)/shard_map/up_product/pallas_call | solution.py:447
  131.1 11.1 %up_product.3 = (bf16[1024,1024]{1,0:T(8,128)(2,1)}, bf16[1024,1024]{1,0:T(8,128)(2,1)}) custom-call(bf16[1024,2048]{1,0:T(8,128)(2,1)} %collective-permute-done.6.h_ref.refs_1_, bf16[2048,1792]{1,0:T(8,128)(2,1)} %bitcast.4.w_ref.refs_0_.refs_1_.refs_2_, f32[1,1024]{1,0:T(1,128)} %bitcast.109), custom_call_target="tpu_custom_call" | custom-call | flops 1 | bytes 1 | tf_op jit(solution)/shard_map/up_product/pallas_call | solution.py:447
  142.2 7.3 %line_product.2.qkv_ref = f32[1024,768]{1,0:T(8,128)} custom-call(bf16[1024,2048]{1,0:T(8,128)(2,1)} %bitcast.97, bf16[2048,1792]{1,0:T(8,128)(2,1)} %bitcast.4.w_ref.refs_0_.refs_1_.refs_2_, bf16[2048,1792]{1,0:T(8,128)(2,1)} %bitcast.4.w_ref.refs_0_.refs_1_.refs_2_, bf16[2048,1792]{1,0:T(8,128)(2,1)} %bitcast.4.w_ref.refs_0_.refs_1_.refs_2_, ...), custom_call_target="tpu_custom_call" | custom-call | flops 1 | bytes 1 | tf_op jit(solution)/shard_map/line_product/pallas_call | solution.py:513
  149.6 7.4 %line_product.3.qkv_ref = f32[1024,768]{1,0:T(8,128)} custom-call(bf16[1024,2048]{1,0:T(8,128)(2,1)} %collective-permute-done.6.h_ref.refs_1_, bf16[2048,1792]{1,0:T(8,128)(2,1)} %bitcast.4.w_ref.refs_0_.refs_1_.refs_2_, bf16[2048,1792]{1,0:T(8,128)(2,1)} %bitcast.4.w_ref.refs_0_.refs_1_.refs_2_, bf16[2048,1792]{1,0:T(8,128)(2,1)} %bitcast.4.w_ref.refs_0_.refs_1_.refs_2_, ...), custom_call_target="tpu_custom_call" | custom-call | flops 1 | bytes 1 | tf_op jit(solution)/shard_map/line_product/pallas_call | solution.py:513
  158.8 14.8 %attend.2 = (bf16[1024,256]{1,0:T(8,128)(2,1)S(1)}, bf16[1024,768]{1,0:T(8,128)(2,1)S(1)}, f32[2,2,2,1024]{3,2,1,0:T(2,128)S(1)}) custom-call(s32[8]{0:T(128)S(1)} %broadcast_multiply_fusion.3.offs_ref, s32[1]{0:T(128)} %get-tuple-element.389.prefix_ref, f32[1024,768]{1,0:T(8,128)S(1)} %copy-done.14, f32[1024,128]{1,0:T(8,128)S(1)} %copy-done.11, ...), custom_call_target="tpu_custom_call" | custom-call | flops 1 | bytes 1 | tf_op jit(solution)/shard_map/attend/pallas_call | solution.py:206
  174.8 14.8 %attend.3 = (bf16[1024,256]{1,0:T(8,128)(2,1)S(1)}, bf16[1024,768]{1,0:T(8,128)(2,1)S(1)}, f32[2,2,2,1024]{3,2,1,0:T(2,128)S(1)}) custom-call(s32[8]{0:T(128)S(1)} %broadcast_multiply_fusion.3.offs_ref, s32[1]{0:T(128)} %get-tuple-element.388.prefix_ref, f32[1024,768]{1,0:T(8,128)S(1)} %copy-done.13, f32[1024,128]{1,0:T(8,128)S(1)} %copy-done.11, ...), custom_call_target="tpu_custom_call" | custom-call | flops 1 | bytes 1 | tf_op jit(solution)/shard_map/attend/pallas_call | solution.py:206
  196.0 8.7 %pair_product.4 = bf16[1024,2048]{1,0:T(8,128)(2,1)} custom-call(bf16[1024,1024]{1,0:T(8,128)(2,1)S(1)} %copy-done.15, bf16[1024,256]{1,0:T(8,128)(2,1)S(1)} %copy-done.25, bf16[2048,1280]{1,0:T(8,128)(2,1)} %bitcast.8.w_ref), custom_call_target="tpu_custom_call" | custom-call | flops 1 | bytes 1 | tf_op jit(solution)/shard_map/pair_product/pallas_call | solution.py:278
  204.7 13.5 %rows_product.3 = bf16[4,512,1024]{2,1,0:T(8,128)(2,1)} custom-call(bf16[1024,2048]{1,0:T(8,128)(2,1)} %all-gather.9.cloned.1.call-done, bf16[1024,2048]{1,0:T(8,128)(2,1)} %collective-permute-done.7.refs_1_.g_ref.refs_5_, bf16[1024,1024]{1,0:T(8,128)(2,1)} %get-tuple-element.272.refs_2_.a_ref, bf16[1024,1024]{1,0:T(8,128)(2,1)} %get-tuple-element.268.a_ref.refs_3_), custom_call_target="tpu_custom_call" | custom-call | flops 1 | bytes 1 | tf_op jit(solution)/shard_map/rows_product/pallas_call | solution.py:347
  220.3 9.4 %pair_product.5 = bf16[1024,2048]{1,0:T(8,128)(2,1)} custom-call(bf16[1024,1024]{1,0:T(8,128)(2,1)S(1)} %copy-done.16, bf16[1024,256]{1,0:T(8,128)(2,1)S(1)} %copy-done.23, bf16[2048,1280]{1,0:T(8,128)(2,1)} %bitcast.8.w_ref, bf16[1024,2048]{1,0:T(8,128)(2,1)} %copy-done.40), custom_call_target="tpu_custom_call" | custom-call | flops 1 | bytes 1 | tf_op jit(solution)/shard_map/pair_product/pallas_call | solution.py:278
  229.7 4.9 all-to-all-start.2
  234.6 10.3 %down_product.2 = (bf16[1024,1024]{1,0:T(8,128)(2,1)}, bf16[1024,256]{1,0:T(8,128)(2,1)}) custom-call(bf16[1024,2048]{1,0:T(8,128)(2,1)} %all-gather.9.cloned.1.call-done, bf16[2048,1280]{1,0:T(8,128)(2,1)} %bitcast.8.w_ref, bf16[1024,1024]{1,0:T(8,128)(2,1)} %get-tuple-element.280.s_ref), custom_call_target="tpu_custom_call" | custom-call | flops 1 | bytes 1 | tf_op jit(solution)/shard_map/down_product/pallas_call | solution.py:474
  244.9 10.4 %down_product.3 = (bf16[1024,1024]{1,0:T(8,128)(2,1)}, bf16[1024,256]{1,0:T(8,128)(2,1)}) custom-call(bf16[1024,2048]{1,0:T(8,128)(2,1)} %collective-permute-done.7.refs_1_.g_ref.refs_5_, bf16[2048,1280]{1,0:T(8,128)(2,1)} %bitcast.8.w_ref, bf16[1024,1024]{1,0:T(8,128)(2,1)} %get-tuple-element.289.s_ref), custom_call_target="tpu_custom_call" | custom-call | flops 1 | bytes 1 | tf_op jit(solution)/shard_map/down_product/pallas_call | solution.py:474
  255.3 13.4 %rows_product.4 = bf16[4,512,1024]{2,1,0:T(8,128)(2,1)} custom-call(bf16[1024,2048]{1,0:T(8,128)(2,1)} %bitcast.98, bf16[1024,2048]{1,0:T(8,128)(2,1)} %collective-permute-done.6.h_ref.refs_1_, bf16[1024,1024]{1,0:T(8,128)(2,1)} %get-tuple-element.342.refs_2_.a_ref, bf16[1024,1024]{1,0:T(8,128)(2,1)} %get-tuple-element.360.refs_3_.a_ref), custom_call_target="tpu_custom_call" | custom-call | flops 1 | bytes 1 | tf_op jit(solution)/shard_map/rows_product/pallas_call | solution.py:347
  268.6 12.6 %all-to-all-done.2 = bf16[4,512,1024]{2,1,0:T(8,128)(2,1)} async-done(((bf16[4,512,1024]{2,1,0:T(8,128)(2,1)}), bf16[4,512,1024]{2,1,0:T(8,128)(2,1)}, u32[]{:S(2)}, u32[]{:S(2)}) %all-to-all-start.2) | async-done | bytes 4194336 | tf_op jit(solution)/shard_map/all_to_all | solution.py:623
  281.2 5.3 all-to-all-start.3
  286.5 4.2 fusion.21
  291.9 21.8 %attend_back.2.refs_2_.b_ref = bf16[1024,768]{1,0:T(8,128)(2,1)S(1)} custom-call(s32[8]{0:T(128)S(1)} %broadcast_multiply_fusion.3.offs_ref, s32[1]{0:T(128)} %get-tuple-element.389.prefix_ref, bf16[1024,768]{1,0:T(8,128)(2,1)S(1)} %copy-done.29, f32[2,2,2,1024]{3,2,1,0:T(2,128)S(1)} %get-tuple-element.308.stat_ref, bf16[1024,256]{1,0:T(8,128)(2,1)S(1)} %copy-done.35, ...), custom_call_target="tpu_custom_call" | custom-call | flops 1 | bytes 1 | tf_op jit(solution)/shard_map/attend_back/pallas_call | solution.py:235
  317.2 21.6 %attend_back.3.b_ref.refs_3_ = bf16[1024,768]{1,0:T(8,128)(2,1)S(1)} custom-call(s32[8]{0:T(128)S(1)} %broadcast_multiply_fusion.3.offs_ref, s32[1]{0:T(128)} %get-tuple-element.388.prefix_ref, bf16[1024,768]{1,0:T(8,128)(2,1)S(1)} %copy-done.27, f32[2,2,2,1024]{3,2,1,0:T(2,128)S(1)} %get-tuple-element.316.stat_ref, bf16[1024,256]{1,0:T(8,128)(2,1)S(1)} %copy-done.34, ...), custom_call_target="tpu_custom_call" | custom-call | flops 1 | bytes 1 | tf_op jit(solution)/shard_map/attend_back/pallas_call | solution.py:235
  341.0 10.9 %pair_product.6 = bf16[1024,2048]{1,0:T(8,128)(2,1)} custom-call(bf16[1024,1024]{1,0:T(8,128)(2,1)S(1)} %copy-done.9, bf16[1024,768]{1,0:T(8,128)(2,1)S(1)} %attend_back.3.b_ref.refs_3_, bf16[2048,1792]{1,0:T(8,128)(2,1)} %bitcast.4.w_ref.refs_0_.refs_1_.refs_2_), custom_call_target="tpu_custom_call" | custom-call | flops 1 | bytes 1 | tf_op jit(solution)/shard_map/pair_product/pallas_call | solution.py:278
  353.5 14.9 %rows_product.5 = bf16[4,512,1024]{2,1,0:T(8,128)(2,1)} custom-call(bf16[1024,2048]{1,0:T(8,128)(2,1)} %bitcast.99, bf16[1024,2048]{1,0:T(8,128)(2,1)} %collective-permute-done.6.h_ref.refs_1_, bf16[1024,768]{1,0:T(8,128)(2,1)} %copy-done.4, bf16[1024,768]{1,0:T(8,128)(2,1)} %copy-done.2, bf16[1024,2048]{1,0:T(8,128)(2,1)} %all-gather.9.cloned.1.call-done, ...), custom_call_target="tpu_custom_call" | custom-call | flops 1 | bytes 1 | tf_op jit(solution)/shard_map/rows_product/pallas_call | solution.py:347
  368.4 4.2 fusion.23
  374.2 11.2 %pair_product.7 = bf16[1024,2048]{1,0:T(8,128)(2,1)} custom-call(bf16[1024,1024]{1,0:T(8,128)(2,1)S(1)} %copy-done.7, bf16[1024,768]{1,0:T(8,128)(2,1)S(1)} %copy-done.5, bf16[2048,1792]{1,0:T(8,128)(2,1)} %bitcast.4.w_ref.refs_0_.refs_1_.refs_2_, bf16[1024,2048]{1,0:T(8,128)(2,1)} %collective-permute-done.10.refs_0_), custom_call_target="tpu_custom_call" | custom-call | flops 1 | bytes 1 | tf_op jit(solution)/shard_map/pair_product/pallas_call | solution.py:278
  385.4 4.6 all-gather.11.cloned.1.call-done
  390.0 5.1 all-to-all-start.4
  395.1 2.7 dynamic-slice_bitcast_fusion.1
  400.8 2.5 copy-done.19
  403.3 3.6 widen.2
  406.9 41.4 %collective-permute-done.12 = bf16[256,2048]{1,0:T(8,128)(2,1)} collective-permute-done((bf16[256,2048]{1,0:T(8,128)(2,1)S(1)}, bf16[256,2048]{1,0:T(8,128)(2,1)}, u32[]{:S(2)}, u32[]{:S(2)}) %collective-permute-start.12) | collective-permute-done | bytes 1048608 | tf_op jit(solution)/shard_map/ppermute | solution.py:58
  448.4 3.9 fusion.1
  453.6 4.0 collective-permute-start.14
  457.7 3.0 fusion.20
  460.6 2.6 collective-permute-start.9
  463.2 4.0 fusion.24
  467.3 30.5 %collective-permute-done.13 = bf16[256,2048]{1,0:T(8,128)(2,1)} collective-permute-done((bf16[256,2048]{1,0:T(8,128)(2,1)}, bf16[256,2048]{1,0:T(8,128)(2,1)}, u32[]{:S(2)}, u32[]{:S(2)}) %collective-permute-start.13) | collective-permute-done | bytes 1048608 | tf_op jit(solution)/shard_map/ppermute | solution.py:55
  497.8 4.8 collective-permute-done.14
  502.6 3.0 convert_reduce_fusion
  507.0 2.9 add_convert_fusion
  512.1 2.6 add_convert_fusion.1
  514.7 4.5 collective-permute-start.15
  520.9 3.8 all-to-all-start.5
  527.8 13.1 %collective-permute-done.16 = bf16[256,2048]{1,0:T(8,128)(2,1)} collective-permute-done((bf16[256,2048]{1,0:T(8,128)(2,1)}, bf16[256,2048]{1,0:T(8,128)(2,1)}, u32[]{:S(2)}, u32[]{:S(2)}) %collective-permute-start.16) | collective-permute-done | bytes 1048608 | tf_op jit(solution)/shard_map/ppermute | solution.py:58
  540.9 22.3 %collective-permute-done.15 = bf16[256,2048]{1,0:T(8,128)(2,1)} collective-permute-done((bf16[256,2048]{1,0:T(8,128)(2,1)}, bf16[256,2048]{1,0:T(8,128)(2,1)}, u32[]{:S(2)}, u32[]{:S(2)}) %collective-permute-start.15) | collective-permute-done | bytes 1048608 | tf_op jit(solution)/shard_map/ppermute | solution.py:55
  563.2 4.4 fusion.16
  568.3 6.0 all-to-all-start.6
  575.9 3.8 bitcast_dynamic-update-slice_fusion.1
  579.7 18.5 %collective-permute-start.17 = (bf16[1,1,256,2048]{3,2,1,0:T(8,128)(2,1)}, bf16[1,1,256,2048]{3,2,1,0:T(8,128)(2,1)S(1)}, u32[]{:S(2)}, u32[]{:S(2)}) collective-permute-start(bf16[1,1,256,2048]{3,2,1,0:T(8,128)(2,1)} %bitcast.23), channel_id=1, source_target_pairs={{0,1},{1,0},{2,3},{3,2},{4,5},{5,4},{6,7},{7,6},{8,9},{9,8},{10,11... | collective-permute-start | bytes 3145736 | tf_op jit(solution)/shard_map/ppermute | solution.py:35
  601.9 3.6 all-to-all-start.7
  605.6 2.7 all-to-all-done.7
  615.0 3.6 widen.3
  622.0 3.5 place.1
  (204 shorter events, 76.6 us)
Async XLA Ops:
  7.2 70.8 %copy-start = (bf16[2,256,2048]{2,1,0:T(8,128)(2,1)S(1)}, bf16[2,256,2048]{2,1,0:T(8,128)(2,1)}, u32[]{:S(2)}) copy-start(bf16[2,256,2048]{2,1,0:T(8,128)(2,1)} %param.19) | copy-start | bytes 6291460
  7.2 3.3 copy-start.41
  7.2 3.3 copy-start.42
  7.2 11.3 %copy-start.30 = (bf16[512,1024]{1,0:T(8,128)(2,1)S(1)}, bf16[512,1024]{1,0:T(8,128)(2,1)}, u32[]{:S(2)}) copy-start(bf16[512,1024]{1,0:T(8,128)(2,1)} %refs_1_.1) | copy-start | bytes 3145732
  13.2 32.6 %collective-permute-start = (bf16[256,2048]{1,0:T(8,128)(2,1)}, bf16[256,2048]{1,0:T(8,128)(2,1)}, u32[]{:S(2)}, u32[]{:S(2)}) collective-permute-start(bf16[256,2048]{1,0:T(8,128)(2,1)} %fusion.10.refs_0_), channel_id=1, source_target_pairs={{0,2},{2,4},{4,6},{1,3},{3,5},{5,7},{8,10},{10,12},{12,14},{9,11},... | collective-permute-start | bytes 3145736 | tf_op jit(solution)/shard_map/ppermute | solution.py:45
  16.4 29.4 %collective-permute-start.1 = (bf16[256,2048]{1,0:T(8,128)(2,1)}, bf16[256,2048]{1,0:T(8,128)(2,1)}, u32[]{:S(2)}, u32[]{:S(2)}) collective-permute-start(bf16[256,2048]{1,0:T(8,128)(2,1)} %fusion.10.refs_0_), channel_id=1, source_target_pairs={{2,0},{4,2},{6,4},{3,1},{5,3},{7,5},{10,8},{12,10},{14,12},{11,9},... | collective-permute-start | bytes 3145736 | tf_op jit(solution)/shard_map/ppermute | solution.py:46
  18.5 2.2 copy-start.17
  26.8 9.3 %copy-start.33 = (bf16[512,1024]{1,0:T(8,128)(2,1)S(1)}, bf16[512,1024]{1,0:T(8,128)(2,1)}, u32[]{:S(2)}) copy-start(bf16[512,1024]{1,0:T(8,128)(2,1)} %refs_1_) | copy-start | bytes 3145732
  26.8 85.5 %all-to-all-start = ((bf16[4,512,1792]{2,1,0:T(8,128)(2,1)}), bf16[4,512,1792]{2,1,0:T(8,128)(2,1)}, u32[]{:S(2)}, u32[]{:S(2)}) async-start(bf16[4,512,1792]{2,1,0:T(8,128)(2,1)} %pack_columns.3), calls=%async_computation | async-start | bytes 14680064 | tf_op jit(solution)/shard_map/all_to_all | solution.py:609
  32.6 159.0 %all-gather.9.cloned.1.call-start = ((), (), s32[]{:S(2)}) async-start(), calls=%async_computation.10 | async-start | bytes 5242880 | tf_op jit(solution)/shard_map/all_gather | solution.py:616
  36.1 2.2 copy-start.20
  38.3 4.2 copy-start.45
  38.3 4.3 copy-start.46
  38.9 2.4 copy-start.6
  45.8 25.4 %collective-permute-start.2 = (bf16[256,2048]{1,0:T(8,128)(2,1)}, bf16[256,2048]{1,0:T(8,128)(2,1)}, u32[]{:S(2)}, u32[]{:S(2)}) collective-permute-start(bf16[256,2048]{1,0:T(8,128)(2,1)} %collective-permute-done.refs_1_), channel_id=1, source_target_pairs={{2,4},{4,6},{3,5},{5,7},{10,12},{12,14},{11,13},{13,15},{18,20},{2... | collective-permute-start | bytes 3145736 | tf_op jit(solution)/shard_map/ppermute | solution.py:45
  50.0 23.1 %collective-permute-start.3 = (bf16[256,2048]{1,0:T(8,128)(2,1)}, bf16[256,2048]{1,0:T(8,128)(2,1)}, u32[]{:S(2)}, u32[]{:S(2)}) collective-permute-start(bf16[256,2048]{1,0:T(8,128)(2,1)} %collective-permute-done.1.refs_4_), channel_id=1, source_target_pairs={{2,0},{4,2},{3,1},{5,3},{10,8},{12,10},{11,9},{13,11},{18,16},{20,... | collective-permute-start | bytes 3145736 | tf_op jit(solution)/shard_map/ppermute | solution.py:46
  73.1 22.6 %collective-permute-start.4 = (bf16[256,2048]{1,0:T(8,128)(2,1)}, bf16[256,2048]{1,0:T(8,128)(2,1)}, u32[]{:S(2)}, u32[]{:S(2)}) collective-permute-start(bf16[256,2048]{1,0:T(8,128)(2,1)} %collective-permute-done.2.refs_2_), channel_id=1, source_target_pairs={{4,6},{5,7},{12,14},{13,15},{20,22},{21,23},{28,30},{29,31}} | collective-permute-start | bytes 3145736 | tf_op jit(solution)/shard_map/ppermute | solution.py:45
  76.3 19.3 %collective-permute-start.5 = (bf16[256,2048]{1,0:T(8,128)(2,1)}, bf16[256,2048]{1,0:T(8,128)(2,1)}, u32[]{:S(2)}, u32[]{:S(2)}) collective-permute-start(bf16[256,2048]{1,0:T(8,128)(2,1)} %collective-permute-done.3.refs_5_), channel_id=1, source_target_pairs={{2,0},{3,1},{10,8},{11,9},{18,16},{19,17},{26,24},{27,25}} | collective-permute-start | bytes 3145736 | tf_op jit(solution)/shard_map/ppermute | solution.py:46
  101.4 18.6 %collective-permute-start.6 = (bf16[1024,2048]{1,0:T(8,128)(2,1)}, bf16[1024,2048]{1,0:T(8,128)(2,1)}, u32[]{:S(2)}, u32[]{:S(2)}) collective-permute-start(bf16[1024,2048]{1,0:T(8,128)(2,1)} %bitcast.95), channel_id=1, source_target_pairs={{0,1},{1,0},{2,3},{3,2},{4,5},{5,4},{6,7},{7,6},{8,9},{9,8},{10,11... | collective-permute-start | bytes 12582920 | tf_op jit(solution)/shard_map/ppermute | solution.py:35
  112.3 79.4 %all-to-all-start.1 = ((bf16[4,512,1280]{2,1,0:T(8,128)(2,1)}), bf16[4,512,1280]{2,1,0:T(8,128)(2,1)}, u32[]{:S(2)}, u32[]{:S(2)}) async-start(bf16[4,512,1280]{2,1,0:T(8,128)(2,1)} %copy-done.6), calls=%async_computation.1 | async-start | bytes 10485760 | tf_op jit(solution)/shard_map/all_to_all | solution.py:635
  118.3 196.5 %reduce-scatter.2.cloned.1.call-start = ((), (), s32[]{:S(2)}) async-start(), calls=%async_computation.9 | async-start | bytes 5242880 | tf_op jit(solution)/shard_map/reduce_scatter | solution.py:677
  149.5 7.4 %copy-start.11 = (f32[1024,128]{1,0:T(8,128)S(1)}, f32[1024,128]{1,0:T(8,128)}, u32[]{:S(2)}) copy-start(f32[1024,128]{1,0:T(8,128)} %get-tuple-element.243.cos_ref) | copy-start | bytes 1572868
  158.8 16.0 %copy-start.13 = (f32[1024,768]{1,0:T(8,128)S(1)}, f32[1024,768]{1,0:T(8,128)}, u32[]{:S(2)}) copy-start(f32[1024,768]{1,0:T(8,128)} %line_product.3.qkv_ref) | copy-start | bytes 9437188
  174.8 14.9 %copy-start.22 = (bf16[1024,256]{1,0:T(8,128)(2,1)}, bf16[1024,256]{1,0:T(8,128)(2,1)S(1)}, u32[]{:S(2)}) copy-start(bf16[1024,256]{1,0:T(8,128)(2,1)S(1)} %get-tuple-element.273.b_ref.refs_6_) | copy-start | bytes 1572868
  191.6 13.1 %collective-permute-start.7 = (bf16[1024,2048]{1,0:T(8,128)(2,1)}, bf16[1024,2048]{1,0:T(8,128)(2,1)}, u32[]{:S(2)}, u32[]{:S(2)}) collective-permute-start(bf16[1024,2048]{1,0:T(8,128)(2,1)} %all-gather.9.cloned.1.call-done), channel_id=1, source_target_pairs={{0,1},{1,0},{2,3},{3,2},{4,5},{5,4},{6,7},{7,6},{8,9},{9,8},{10,11... | collective-permute-start | bytes 12582920 | tf_op jit(solution)/shard_map/ppermute | solution.py:35
  204.7 15.6 %copy-start.16 = (bf16[1024,1024]{1,0:T(8,128)(2,1)S(1)}, bf16[1024,1024]{1,0:T(8,128)(2,1)}, u32[]{:S(2)}) copy-start(bf16[1024,1024]{1,0:T(8,128)(2,1)} %get-tuple-element.272.refs_2_.a_ref) | copy-start | bytes 6291460
  204.7 15.6 %copy-start.23 = (bf16[1024,256]{1,0:T(8,128)(2,1)S(1)}, bf16[1024,256]{1,0:T(8,128)(2,1)}, u32[]{:S(2)}) copy-start(bf16[1024,256]{1,0:T(8,128)(2,1)} %copy-done.22) | copy-start | bytes 1572868
  204.7 13.5 %collective-permute-start.8 = (bf16[1024,2048]{1,0:T(8,128)(2,1)}, bf16[1024,2048]{1,0:T(8,128)(2,1)S(1)}, u32[]{:S(2)}, u32[]{:S(2)}) collective-permute-start(bf16[1024,2048]{1,0:T(8,128)(2,1)} %pair_product.4), channel_id=1, source_target_pairs={{0,1},{1,0},{2,3},{3,2},{4,5},{5,4},{6,7},{7,6},{8,9},{9,8},{10,11... | collective-permute-start | bytes 12582920 | tf_op jit(solution)/shard_map/ppermute | solution.py:35
  229.7 51.5 %all-to-all-start.2 = ((bf16[4,512,1024]{2,1,0:T(8,128)(2,1)}), bf16[4,512,1024]{2,1,0:T(8,128)(2,1)}, u32[]{:S(2)}, u32[]{:S(2)}) async-start(bf16[4,512,1024]{2,1,0:T(8,128)(2,1)} %rows_product.3), calls=%async_computation.2 | async-start | bytes 8388608 | tf_op jit(solution)/shard_map/all_to_all | solution.py:623
  281.2 57.6 %all-to-all-start.3 = ((bf16[4,512,1024]{2,1,0:T(8,128)(2,1)}), bf16[4,512,1024]{2,1,0:T(8,128)(2,1)}, u32[]{:S(2)}, u32[]{:S(2)}) async-start(bf16[4,512,1024]{2,1,0:T(8,128)(2,1)} %rows_product.4), calls=%async_computation.4 | async-start | bytes 8388608 | tf_op jit(solution)/shard_map/all_to_all | solution.py:623
  286.5 4.3 copy-start.12
  286.5 4.3 copy-start.29
  286.5 103.5 %all-gather.11.cloned.1.call-start = ((), (), s32[]{:S(2)}) async-start(), calls=%async_computation.11 | async-start | bytes 5242880 | tf_op jit(solution)/shard_map/all_gather | solution.py:629
  290.7 322.1 %all-gather.15.cloned.1.call-start = ((), (), s32[]{:S(2)}) async-start(), calls=%async_computation.13 | async-start | bytes 5242880 | tf_op jit(solution)/shard_map/all_gather | solution.py:629
  338.8 13.1 %copy-start.2 = (bf16[1024,768]{1,0:T(8,128)(2,1)}, bf16[1024,768]{1,0:T(8,128)(2,1)S(1)}, u32[]{:S(2)}) copy-start(bf16[1024,768]{1,0:T(8,128)(2,1)S(1)} %attend_back.3.b_ref.refs_3_) | copy-start | bytes 4718596
  351.9 20.7 %collective-permute-start.10 = (bf16[1024,2048]{1,0:T(8,128)(2,1)}, bf16[1024,2048]{1,0:T(8,128)(2,1)}, u32[]{:S(2)}, u32[]{:S(2)}) collective-permute-start(bf16[1024,2048]{1,0:T(8,128)(2,1)} %pair_product.6), channel_id=1, source_target_pairs={{0,1},{1,0},{2,3},{3,2},{4,5},{5,4},{6,7},{7,6},{8,9},{9,8},{10,11... | collective-permute-start | bytes 12582920 | tf_op jit(solution)/shard_map/ppermute | solution.py:35
  368.4 4.2 copy-start.5
  390.0 58.4 %all-to-all-start.4 = ((bf16[4,512,1024]{2,1,0:T(8,128)(2,1)}), bf16[4,512,1024]{2,1,0:T(8,128)(2,1)}, u32[]{:S(2)}, u32[]{:S(2)}) async-start(bf16[4,512,1024]{2,1,0:T(8,128)(2,1)} %rows_product.5), calls=%async_computation.5 | async-start | bytes 8388608 | tf_op jit(solution)/shard_map/all_to_all | solution.py:623
  395.1 224.6 %all-gather.13.cloned.1.call-start = ((), (), s32[]{:S(2)}) async-start(), calls=%async_computation.12 | async-start | bytes 5242880 | tf_op jit(solution)/shard_map/all_gather | solution.py:629
  397.8 9.2 %collective-permute-start.11 = (bf16[256,2048]{1,0:T(8,128)(2,1)}, bf16[256,2048]{1,0:T(8,128)(2,1)}, u32[]{:S(2)}, u32[]{:S(2)}) collective-permute-start(bf16[256,2048]{1,0:T(8,128)(2,1)} %get-tuple-element.379), channel_id=1, source_target_pairs={{0,2},{1,3},{8,10},{9,11},{16,18},{17,19},{24,26},{25,27}} | collective-permute-start | bytes 3145736 | tf_op jit(solution)/shard_map/ppermute | solution.py:55
  399.5 48.9 %collective-permute-start.12 = (bf16[256,2048]{1,0:T(8,128)(2,1)S(1)}, bf16[256,2048]{1,0:T(8,128)(2,1)}, u32[]{:S(2)}, u32[]{:S(2)}) collective-permute-start(bf16[256,2048]{1,0:T(8,128)(2,1)S(1)} %get-tuple-element.378), channel_id=1, source_target_pairs={{6,4},{7,5},{14,12},{15,13},{22,20},{23,21},{30,28},{31,29}} | collective-permute-start | bytes 3145736 | tf_op jit(solution)/shard_map/ppermute | solution.py:58
  400.8 2.5 copy-start.19
  406.9 50.7 %copy-start.43 = (bf16[2048]{0:T(1024)(128)(2,1)S(1)}, bf16[2048]{0:T(1024)(128)(2,1)}, u32[]{:S(2)}) copy-start(bf16[2048]{0:T(1024)(128)(2,1)} %param.31) | copy-start | bytes 12292
  406.9 50.7 %copy-start.44 = (bf16[2048]{0:T(1024)(128)(2,1)S(1)}, bf16[2048]{0:T(1024)(128)(2,1)}, u32[]{:S(2)}) copy-start(bf16[2048]{0:T(1024)(128)(2,1)} %param.35) | copy-start | bytes 12292
  452.3 45.5 %collective-permute-start.13 = (bf16[256,2048]{1,0:T(8,128)(2,1)}, bf16[256,2048]{1,0:T(8,128)(2,1)}, u32[]{:S(2)}, u32[]{:S(2)}) collective-permute-start(bf16[256,2048]{1,0:T(8,128)(2,1)} %get-tuple-element.377), channel_id=1, source_target_pairs={{0,2},{2,4},{1,3},{3,5},{8,10},{10,12},{9,11},{11,13},{16,18},{18,... | collective-permute-start | bytes 3145736 | tf_op jit(solution)/shard_map/ppermute | solution.py:55
  453.6 49.0 %collective-permute-start.14 = (bf16[256,2048]{1,0:T(8,128)(2,1)}, bf16[256,2048]{1,0:T(8,128)(2,1)}, u32[]{:S(2)}, u32[]{:S(2)}) collective-permute-start(bf16[256,2048]{1,0:T(8,128)(2,1)} %get-tuple-element.376), channel_id=1, source_target_pairs={{4,2},{6,4},{5,3},{7,5},{12,10},{14,12},{13,11},{15,13},{20,18},{2... | collective-permute-start | bytes 3145736 | tf_op jit(solution)/shard_map/ppermute | solution.py:58
  460.6 137.6 %collective-permute-start.9 = (bf16[1,1,256,2048]{3,2,1,0:T(8,128)(2,1)}, bf16[1,1,256,2048]{3,2,1,0:T(8,128)(2,1)}, u32[]{:S(2)}, u32[]{:S(2)}) collective-permute-start(bf16[1,1,256,2048]{3,2,1,0:T(8,128)(2,1)} %fusion.20), channel_id=1, source_target_pairs={{0,1},{1,0},{2,3},{3,2},{4,5},{5,4},{6,7},{7,6},{8,9},{9,8},{10,11... | collective-permute-start | bytes 3145736 | tf_op jit(solution)/shard_map/ppermute | solution.py:35
  502.6 3.5 copy-start.36
  509.9 9.3 %copy-start.3 = (bf16[1024,768]{1,0:T(8,128)(2,1)S(1)}, bf16[1024,768]{1,0:T(8,128)(2,1)}, u32[]{:S(2)}) copy-start(bf16[1024,768]{1,0:T(8,128)(2,1)} %copy-done.2) | copy-start | bytes 4718596
  509.9 9.6 %copy-start.8 = (bf16[1024,1024]{1,0:T(8,128)(2,1)S(1)}, bf16[1024,1024]{1,0:T(8,128)(2,1)}, u32[]{:S(2)}) copy-start(bf16[1024,1024]{1,0:T(8,128)(2,1)} %get-tuple-element.342.refs_2_.a_ref) | copy-start | bytes 6291460
  509.9 31.0 %collective-permute-start.16 = (bf16[256,2048]{1,0:T(8,128)(2,1)}, bf16[256,2048]{1,0:T(8,128)(2,1)}, u32[]{:S(2)}, u32[]{:S(2)}) collective-permute-start(bf16[256,2048]{1,0:T(8,128)(2,1)} %add_convert_fusion), channel_id=1, source_target_pairs={{2,0},{4,2},{6,4},{3,1},{5,3},{7,5},{10,8},{12,10},{14,12},{11,9},... | collective-permute-start | bytes 3145736 | tf_op jit(solution)/shard_map/ppermute | solution.py:58
  514.7 5.2 copy-start.10
  514.7 48.6 %collective-permute-start.15 = (bf16[256,2048]{1,0:T(8,128)(2,1)}, bf16[256,2048]{1,0:T(8,128)(2,1)}, u32[]{:S(2)}, u32[]{:S(2)}) collective-permute-start(bf16[256,2048]{1,0:T(8,128)(2,1)} %add_convert_fusion.1), channel_id=1, source_target_pairs={{0,2},{2,4},{4,6},{1,3},{3,5},{5,7},{8,10},{10,12},{12,14},{9,11},... | collective-permute-start | bytes 3145736 | tf_op jit(solution)/shard_map/ppermute | solution.py:55
  519.8 6.5 %copy-start.37 = (bf16[2,256,2048]{2,1,0:T(8,128)(2,1)S(1)}, bf16[2,256,2048]{2,1,0:T(8,128)(2,1)}, u32[]{:S(2)}) copy-start(bf16[2,256,2048]{2,1,0:T(8,128)(2,1)} %param.18) | copy-start | bytes 6291460
  519.9 6.5 %copy-start.39 = (bf16[1,256,2048]{2,1,0:T(8,128)(2,1)S(1)}, bf16[1,256,2048]{2,1,0:T(8,128)(2,1)}, u32[]{:S(2)}) copy-start(bf16[1,256,2048]{2,1,0:T(8,128)(2,1)} %reduce-scatter.2.cloned.1.call-done) | copy-start | bytes 3145732
  520.9 6.8 %all-to-all-start.5 = ((f32[4,1,3840]{2,1,0:T(1,128)}), f32[4,1,3840]{2,1,0:T(1,128)S(1)}, u32[]{:S(2)}, u32[]{:S(2)}) async-start(f32[4,1,3840]{2,1,0:T(1,128)} %broadcast_in_dim.91), calls=%async_computation.6 | async-start | bytes 122880 | tf_op jit(solution)/shard_map/all_to_all | solution.py:39
  567.6 8.3 %copy-start.38 = (bf16[256,2048]{1,0:T(8,128)(2,1)S(1)}, bf16[256,2048]{1,0:T(8,128)(2,1)}, u32[]{:S(2)}) copy-start(bf16[256,2048]{1,0:T(8,128)(2,1)} %dynamic-slice_bitcast_fusion.2) | copy-start | bytes 3145732
  568.3 32.9 %all-to-all-start.6 = ((f32[4,1,5888]{2,1,0:T(1,128)}), f32[4,1,5888]{2,1,0:T(1,128)S(1)}, u32[]{:S(2)}, u32[]{:S(2)}) async-start(f32[4,1,5888]{2,1,0:T(1,128)} %broadcast_in_dim.92), calls=%async_computation.7 | async-start | bytes 188416 | tf_op jit(solution)/shard_map/all_to_all | solution.py:39
  579.7 38.9 %collective-permute-start.17 = (bf16[1,1,256,2048]{3,2,1,0:T(8,128)(2,1)}, bf16[1,1,256,2048]{3,2,1,0:T(8,128)(2,1)S(1)}, u32[]{:S(2)}, u32[]{:S(2)}) collective-permute-start(bf16[1,1,256,2048]{3,2,1,0:T(8,128)(2,1)} %bitcast.23), channel_id=1, source_target_pairs={{0,1},{1,0},{2,3},{3,2},{4,5},{5,4},{6,7},{7,6},{8,9},{9,8},{10,11... | collective-permute-start | bytes 3145736 | tf_op jit(solution)/shard_map/ppermute | solution.py:35
  601.9 6.3 all-to-all-start.7
  608.3 3.9 collective-permute-start.18
  612.8 2.2 copy-start.18
  619.7 5.9 copy-start.1
  619.7 2.3 copy-start.21
  (15 other events, 20.5 us)
Sparse Core Ops, SparseCore 0:
  95.8 85.5 all-gather.8
  229.8 79.1 reduce-scatter.1
  310.7 79.2 all-gather.10
  391.5 123.6 all-gather.14
  516.7 94.4 all-gather.12

commit v4 on v3

--- a/solution.py
+++ b/solution.py
@@ -66,6 +66,10 @@
     return [blocks[0]] + [
         jnp.where(here >= m, blocks[m][0], blocks[n - m][1]) for m in range(1, n)
     ]
+
+
+def in_hbm(arrays):
+    return [pltpu.with_memory_space_constraint(a, pltpu.HBM) for a in arrays]
 
 
 FREE = pl.CostEstimate(flops=1, transcendentals=0, bytes_accessed=1)
@@ -317,7 +321,7 @@
         compiler_params=pltpu.CompilerParams(vmem_limit_bytes=40 << 20),
         cost_estimate=FREE,
         name="pack_columns",
-    )(here.reshape(1), *weights)
+    )(here.reshape(1), *in_hbm(weights))
 
 
 def rows_kernel(counts, *refs):
@@ -356,39 +360,46 @@
     )(*args)
 
 
-def order_kernel(size, here_ref, *refs):
+def order_kernel(size, pieces, here_ref, *refs):
     blocks, o_ref = refs[:-1], refs[-1]
-    m, here = pl.program_id(0), here_ref[0]
+    m, piece, here = pl.program_id(0), pl.program_id(1), here_ref[0]
 
     def put(ref):
         o_ref[0] = ref[...]
 
-    pl.when(m == 0)(lambda: put(blocks[0]))
-    for k in range(1, size):
-        pl.when((m == k) & (here >= k))(functools.partial(put, blocks[k]))
-        pl.when((m == k) & (here < k))(functools.partial(put, blocks[2 * size - 1 - k]))
-
-
-def in_order(blocks, here):
-    size = len(blocks)
-    rows, span = blocks[0].shape
-    blocks = [blocks[0]] + [x[0] for x in blocks[1:]] + [x[1] for x in blocks[1:]]
-    return pl.pallas_call(
-        functools.partial(order_kernel, size),
-        out_shape=jax.ShapeDtypeStruct((size, rows, span), blocks[0].dtype),
+    for p in range(pieces):
+        mine = blocks[p * (2 * size - 1) : (p + 1) * (2 * size - 1)]
+        pl.when((piece == p) & (m == 0))(functools.partial(put, mine[0]))
+        for k in range(1, size):
+            at = (piece == p) & (m == k)
+            pl.when(at & (here >= k))(functools.partial(put, mine[k]))
+            pl.when(at & (here < k))(functools.partial(put, mine[2 * size - 1 - k]))
+
+
+def in_order(pieces, here):
+    size = len(pieces[0])
+    rows, span = pieces[0][0].shape
+    flat = []
+    for one in pieces:
+        flat += [one[0]] + [x[0] for x in one[1:]] + [x[1] for x in one[1:]]
+    return pl.pallas_call(
+        functools.partial(order_kernel, size, len(pieces)),
+        out_shape=jax.ShapeDtypeStruct((size, len(pieces) * rows, span), flat[0].dtype),
         grid_spec=pltpu.PrefetchScalarGridSpec(
             num_scalar_prefetch=1,
-            grid=(size,),
-            in_specs=[pl.BlockSpec((rows, span), lambda m, h: (0, 0), pipeline_mode=pl.Buffered(1))]
-            * len(blocks),
+            grid=(size, len(pieces)),
+            in_specs=[
+                pl.BlockSpec((rows, span), lambda m, p, h: (0, 0), pipeline_mode=pl.Buffered(1))
+            ]
+            * len(flat),
             out_specs=pl.BlockSpec(
-                (1, rows, span), lambda m, h: (lax.rem(h[0] - m + size, size), 0, 0)
+                (1, rows, span), lambda m, p, h: (lax.rem(h[0] - m + size, size), p, 0)
             ),
         ),
         compiler_params=pltpu.CompilerParams(vmem_limit_bytes=48 << 20),
         cost_estimate=FREE,
         name="in_order",
-    )(here.reshape(1), *blocks)
+    )(here.reshape(1), *in_hbm(flat))
 
 
 def place_kernel(pairs, a_ref, *outs):
@@ -411,7 +422,7 @@
         compiler_params=pltpu.CompilerParams(vmem_limit_bytes=48 << 20),
         cost_estimate=FREE,
         name="place",
-    )(blocks)
+    )(*in_hbm([blocks]))
 
 
 def widen_kernel(a_ref, o_ref):
@@ -429,7 +440,7 @@
         compiler_params=pltpu.CompilerParams(vmem_limit_bytes=40 << 20),
         cost_estimate=FREE,
         name="widen",
-    )(blocks)
+    )(*in_hbm([blocks]))
 
 
 def up_kernel(step, h_ref, w_ref, b_ref, act_ref, slope_ref):
@@ -565,8 +576,6 @@
     normed = centred * inv_std
     h_own = (normed * gain + shift).astype(BF16)
 
-    h_in = [h_own]
-
     def side(blocks):
         return blocks[-1] if len(blocks) > 1 else (blocks[0], blocks[0])
 
@@ -576,8 +585,12 @@
     cut = [
         (1 + n, p * PAIR, PAIR) for p in range(pairs) for n in range(3)
     ]
-    h_own, early = meet(
-        (h_own, (up_weight, query_weight, key_weight, value_weight, down_weight, out_weight))
+    col_sum = lambda a: jnp.sum(a.astype(F32), axis=0)
+    h_own, g_cols = meet((h_own, col_sum(g_own)))
+    h_in = [[piece] for piece in jnp.split(h_own, 2)]
+    g_cols = total([g_cols] + [xor_swap(g_cols, "tp", nt, k) for k in range(1, nt)])
+    g_cols, early = meet(
+        (g_cols, (up_weight, query_weight, key_weight, value_weight, down_weight, out_weight))
     )
     first = pack_columns(early[:4], [(0, 0, units)] + cut, ci, nc, nf)
     second = pack_columns(early[4:], [(0, 0, units), (1, 0, inner)], ci, nc, nf)
@@ -607,11 +620,12 @@
 
     tables = (cos, sa, sb)
     first_all = lax.all_to_all(first, "fsdp", 0, 0, tiled=True)
-    h_in, second, tables, b_up, b_qkv, offs, prefix = meet(
-        (gather_on(h_in), second, tables, b_up, b_qkv, offs, prefix)
-    )
-    while len(h_in) < nc:
-        h_in = meet(gather_on(h_in))
+    h_in = [gather_on(h) for h in h_in]
+    h_in[0], second, tables, b_up, b_qkv, offs, prefix = meet(
+        (h_in[0], second, tables, b_up, b_qkv, offs, prefix)
+    )
+    while len(h_in[0]) < nc:
+        h_in = [gather_on(h) for h in h_in]
     g_own, h_in = meet((g_own, h_in))
     g_all = lax.all_gather(g_own.reshape(own_seqs, rows, width), "ctx", axis=1, tiled=True)
 
@@ -641,14 +655,26 @@
         qkv.append(line_product(hidden[n], w_first, b_qkv, units, 3))
         qkv, hidden = meet((qkv, hidden))
     act, slope = [u[0] for u in ups], [u[1] for u in ups]
-    done = []
-    for n in range(seqs):
-        at = slice((n % own_seqs) * length, (n % own_seqs + 1) * length)
-        done.append(attend(qkv[n // own_seqs][at], offs, prefix[n : n + 1], tables))
-        done, qkv = meet((done, qkv))
-    context = [
-        jnp.concatenate([d[0] for d in done[n * own_seqs : (n + 1) * own_seqs]]) for n in range(nt)
-    ]
+
+    def attend_half(n, qkv):
+        out = []
+        for i in range(own_seqs):
+            at = slice(i * length, (i + 1) * length)
+            m = n * own_seqs + i
+            out.append(attend(qkv[at], offs, prefix[m : m + 1], tables))
+        return out
+
+    def back_half(n, kept, grad_context):
+        out = []
+        for i in range(own_seqs):
+            at = slice(i * length, (i + 1) * length)
+            m = n * own_seqs + i
+            out.append(
+                attend_back(
+                    kept[i][1], kept[i][2], grad_context[at], offs, prefix[m : m + 1], tables
+                )
+            )
+        return jnp.concatenate(out)
 
     def parts_of(mine, got):
         grid = lambda a: a.reshape(own_seqs, nc, rows, width)
@@ -661,53 +687,51 @@
 
         return parts
 
-    act, context, second_all, g_all = meet((act, context, second_all, g_all))
+    others = range(1, nt)
+    kept = [None] * nt
+    for n in others:
+        kept[n] = attend_half(n, qkv[n])
+    kept[1:], qkv, act, second_all = meet((kept[1:], qkv, act, second_all))
     w_second = second_all.reshape(width, units + inner)
+    context = [None] + [jnp.concatenate([c[0] for c in kept[n]]) for n in others]
+    theirs, qkv = meet(([pair_product(act[n], context[n], w_second) for n in others], qkv))
+    o_got = [xor_swap(t, "tp", nt, n) for n, t in zip(others, theirs)]
+    kept[0], act, o_got, g_all = meet((attend_half(0, qkv[0]), act, o_got, g_all))
     grad = halves(g_all)
-    theirs, act, context = meet(
-        ([pair_product(act[k], context[k], w_second) for k in range(1, nt)], act, context)
-    )
-    o_got = [xor_swap(t, "tp", nt, k) for k, t in zip(range(1, nt), theirs)]
-    full_down = rows_product([(grad, act)], nf)
-    grad, full_down, slope, o_got, act = meet((grad, full_down, slope, o_got, act))
-    d_rows = send_rows(full_down)
+    context[0] = jnp.concatenate([c[0] for c in kept[0]])
     both = pair_product(act[0], context[0], w_second, o_got)
     both = jnp.moveaxis(both.reshape(own_seqs, nc, rows, width), 1, 0).reshape(nc, own, width)
-    both, grad, slope = meet((both, grad, slope))
+    grad, act, both = meet((grad, act, both))
     o_sum = lax.psum_scatter(both, "ctx", scatter_dimension=0, tiled=True)
+
+    full_down = rows_product([(grad, act)], nf)
+    grad, full_down, slope = meet((grad, full_down, slope))
+    d_rows = send_rows(full_down)
     downs = []
     for n in range(nt):
         downs.append(down_product(grad[n], w_second, slope[n]))
         downs, grad, hidden = meet((downs, grad, hidden))
     dup, grad_context = [d[0] for d in downs], [d[1] for d in downs]
     full_up = rows_product([(hidden, dup)], nf)
-    full_up, d_rows = meet((full_up, d_rows))
-    d_sum, done, grad_context = meet((sum_rows(d_rows), done, grad_context))
+    full_up, kept, grad_context = meet((full_up, kept, grad_context))
+    dqkv = [None] + [back_half(n, kept[n], grad_context[n]) for n in others]
+    dqkv[1:], d_rows, dup = meet((dqkv[1:], d_rows, dup))
+    d_sum, dup = meet((sum_rows(d_rows), dup))
+    d_cols = gather_cols(d_sum)
     u_rows = send_rows(full_up)
-    back = []
-    for n in range(seqs):
-        at = slice((n % own_seqs) * length, (n % own_seqs + 1) * length)
-        back.append(
-            attend_back(
-                done[n][1], done[n][2], grad_context[n // own_seqs][at],
-                offs, prefix[n : n + 1], tables,
-            )
-        )
-        back, done, grad_context, o_sum = meet((back, done, grad_context, o_sum))
-        if n == 0:
-            d_cols = gather_cols(d_sum)
-    dqkv = [jnp.concatenate(back[n * own_seqs : (n + 1) * own_seqs]) for n in range(nt)]
-    u_rows, dqkv, hidden, grad, dup = meet((u_rows, dqkv, hidden, grad, dup))
-
-    theirs, dup, dqkv, hidden = meet(
-        ([pair_product(dup[k], dqkv[k], w_first) for k in range(1, nt)], dup, dqkv, hidden)
-    )
-    h_got = [xor_swap(t, "tp", nt, k) for k, t in zip(range(1, nt), theirs)]
-    u_sum = sum_rows(u_rows)
+
+    theirs, kept, grad_context = meet(
+        ([pair_product(dup[n], dqkv[n], w_first) for n in others], kept, grad_context)
+    )
+    h_got = [xor_swap(t, "tp", nt, n) for n, t in zip(others, theirs)]
+    dqkv[0], o_sum, h_got = meet((back_half(0, kept[0], grad_context[0]), o_sum, h_got))
+    h_both, dqkv, hidden = meet(
+        (pair_product(dup[0], dqkv[0], w_first, h_got), dqkv, hidden)
+    )
     qo_full = rows_product([(hidden, dqkv), (grad, context)], nf)
-    qo_full, dqkv, dup, h_got, u_sum = meet((qo_full, dqkv, dup, h_got, u_sum))
+    qo_full, u_rows = meet((qo_full, u_rows))
+    u_sum, d_cols = meet((sum_rows(u_rows), d_cols))
     qo = send_rows(qo_full)
-    h_both, d_cols, u_sum = meet((pair_product(dup[0], dqkv[0], w_first, h_got), d_cols, u_sum))
     u_cols = gather_cols(u_sum)
     h_parts = parts_of(h_both, [])
     dw_down = widen(d_cols)
@@ -721,6 +745,7 @@
     grad_hidden = total(h_parts(0) + list(h_sum))
     u_cols, h_sum = meet((u_cols, h_sum))
     dw_up = widen(u_cols)
+    grad_hidden, dw_up = meet((grad_hidden, dw_up))
     qo_cols = gather_cols(qo_sum)
     col_sum = lambda a: jnp.sum(a.astype(F32), axis=0)
     out_own = total([x, o_sum.reshape(own, width), out_bias, down_bias])
@@ -747,17 +772,17 @@
     dw_qkv = place(qo_cols, pairs)
 
     bias_sums = jnp.concatenate(
-        [total([col_sum(a) for a in array]) for array in (dqkv, dup, grad)]
+        [total([col_sum(a) for a in array]) for array in (dqkv, dup)]
     )[None]
     bias_sums = jnp.sum(to_all(bias_sums, "fsdp", nf).reshape(nf, -1), axis=0)
     small = 3 * inner + units
-    obias = bias_sums[small:]
-    got = to_all(jnp.concatenate([bias_sums[:small], norm_sums])[None], "ctx", nc).reshape(nc, -1)
+    got = to_all(jnp.concatenate([bias_sums, norm_sums, g_cols])[None], "ctx", nc).reshape(nc, -1)
     qkv_sums = got[:, : 3 * inner].reshape(nc, pairs, 3, PAIR)
     qb, kb, vb = (qkv_sums[:, :, n].reshape(nc * inner) for n in range(3))
     ub = got[:, 3 * inner : small].reshape(nc * units)
-    norm_sums = jnp.sum(got[:, small:], axis=0)[None]
-    norm_sums = jnp.sum(to_all(norm_sums, "fsdp", nf).reshape(nf, -1), axis=0)
+    sums = jnp.sum(got[:, small:], axis=0)[None]
+    sums = jnp.sum(to_all(sums, "fsdp", nf).reshape(nf, -1), axis=0)
+    norm_sums, obias = sums[: 2 * width], sums[2 * width :]
     norm_sums = total([norm_sums] + [xor_swap(norm_sums, "tp", nt, k) for k in range(1, nt)])
     norm_sums = norm_sums.reshape(2, width)
 

time: 641 us -> 611 us (0.953)
  waiting for transfers between devices: 176 us -> 153 us
  local copies, waits for them, and re-layouts: 55.4 us -> 43.7 us
  Pallas kernels: 233 us -> 242 us
    all_gather x3, waiting for transfers between devices: 4.56 us -> 27.6 us  [gather_cols(): return lax.all_gather(mine, 'ctx', axis=0, tiled=False)]
    ppermute x3, waiting for transfers between devices: 52.9 us -> 37.3 us  [sum_step(): lax.ppermute(total(a).astype(BF16), axis, [(j, j + 1) for j in range(min(...]
    all_to_all x3, waiting for transfers between devices: 12.6 us -> 0.01 us  [send_rows(): return lax.all_to_all(full, 'fsdp', 0, 0, tiled=True)]
    unnamed x102 -> x108, local copies, waits for them, and re-layouts: 36.3 us -> 28.1 us
    all_to_all x1, waiting for transfers between devices: 7.51 us -> 0.01 us  [local(): first_all = lax.all_to_all(first, 'fsdp', 0, 0, tiled=True)]
    ppermute x3 -> x6, starting transfers between devices: 10.6 us -> 17.6 us  [gather_step(): lax.ppermute(left, axis, [(j, j + 1) for j in range(step - 1, size - 1)])]
    ppermute x3, waiting for transfers between devices: 59.4 us -> 52.6 us  [sum_step(): lax.ppermute(total(b).astype(BF16), axis, [(j, j - 1) for j in range(max(...]
    ppermute x3 -> x6, waiting for transfers between devices: 34.6 us -> 30.3 us  [gather_step(): lax.ppermute(left, axis, [(j, j + 1) for j in range(step - 1, size - 1)])]
  transfers between devices with their start and end apart: 32 -> 39, of which waited for: 12 -> 13; matrix products, arithmetic and copies ran while one was open for 10% -> 9% of each run, Pallas kernels for 35% -> 39%
where the time goes in v4:
time: 611 us; the launch traced here: 602 us
  Pallas kernels  242 us (40%)
  waiting for transfers between devices  153 us (25%)
  starting transfers between devices  104 us (17%)
  other arithmetic  44.8 us (7%)
  local copies, waits for them, and re-layouts  43.7 us (7%)
  between operations  14.8 us (2%)
    ppermute x3, waiting for transfers between devices, sum_step(): lax.ppermute(total(b).astype(BF16), axis, [(j, j - 1) for j in range(max(...  52.6 us
    pallas_call x2, Pallas kernels, attend_back(): pl.pallas_call(functools.partial(attend_back_kernel, length // offs.shape...  43.3 us
    pallas_call x3, Pallas kernels, rows_product(): pl.pallas_call(functools.partial(rows_kernel, [len(a) for a, _ in product...  41.5 us
    pallas_call x4, Pallas kernels, pair_product(): pl.pallas_call(functools.partial(pair_kernel, a.shape[1]), out_shape=jax....  40.8 us
    ppermute x3, waiting for transfers between devices, sum_step(): lax.ppermute(total(a).astype(BF16), axis, [(j, j + 1) for j in range(min(...  37.3 us
    ppermute x6, waiting for transfers between devices, gather_step(): lax.ppermute(left, axis, [(j, j + 1) for j in range(step - 1, size - 1)])  30.3 us
    pallas_call x2, Pallas kernels, attend(): pl.pallas_call(functools.partial(attend_kernel, length // offs.shape[0],...  29.7 us
    unnamed x108, local copies, waits for them, and re-layouts  28.1 us
  transfers between devices with their start and end apart: 39, of which 13 were waited for; matrix products, arithmetic and copies ran while one was open for 9% of the time, Pallas kernels for 39%

profile of v4, /device:TPU:19, one launch (start us, length us, event | category | flops | bytes accessed | tf_op | source)
XLA Modules:
  0.0 601.9 jit_solution(15978955217083830309)
XLA Ops:
  10.5 2.9 convert_reduce_fusion.5
  15.0 2.3 pack_columns.3
  17.3 3.0 copy-done
  20.4 5.6 all-to-all-start
  27.0 3.2 collective-permute-start
  32.3 3.2 collective-permute-start.7
  46.4 2.3 copy-done.5
  48.8 4.0 collective-permute-start.3
  56.5 3.0 collective-permute-start.10
  59.6 4.7 collective-permute-done.3.refs_2_
  64.2 2.4 collective-permute-start.5
  67.4 8.1 %collective-permute-done.9.refs_9_ = bf16[128,2048]{1,0:T(8,128)(2,1)S(1)} collective-permute-done((bf16[128,2048]{1,0:T(8,128)(2,1)S(1)}, bf16[128,2048]{1,0:T(8,128)(2,1)S(1)}, u32[]{:S(2)}, u32[]{:S(2)}) %collective-permute-start.9) | collective-permute-done | bytes 524320 | tf_op jit(solution)/shard_map/ppermute | solution.py:45
  75.5 2.4 collective-permute-start.11
  78.6 6.3 %collective-permute-done.5.refs_3_ = bf16[128,2048]{1,0:T(8,128)(2,1)S(1)} collective-permute-done((bf16[128,2048]{1,0:T(8,128)(2,1)S(1)}, bf16[128,2048]{1,0:T(8,128)(2,1)S(1)}, u32[]{:S(2)}, u32[]{:S(2)}) %collective-permute-start.5) | collective-permute-done | bytes 524320 | tf_op jit(solution)/shard_map/ppermute | solution.py:45
  84.9 11.2 %collective-permute-done.11.refs_10_ = bf16[128,2048]{1,0:T(8,128)(2,1)S(1)} collective-permute-done((bf16[128,2048]{1,0:T(8,128)(2,1)S(1)}, bf16[128,2048]{1,0:T(8,128)(2,1)S(1)}, u32[]{:S(2)}, u32[]{:S(2)}) %collective-permute-start.11) | collective-permute-done | bytes 524320 | tf_op jit(solution)/shard_map/ppermute | solution.py:45
  97.8 7.0 %in_order.1 = bf16[4,256,2048]{2,1,0:T(8,128)(2,1)} custom-call(s32[1]{0:T(128)} %bitcast.2.here_ref, bf16[128,2048]{1,0:T(8,128)(2,1)} %get-tuple-element.181.refs_0_, bf16[128,2048]{1,0:T(8,128)(2,1)} %copy-done.33, bf16[128,2048]{1,0:T(8,128)(2,1)} %copy-done.36, bf16[128,2048]{1,0:T(8,128)(2,1)} %copy-done.40, bf16[128,2048]{1,0:T(8,128)(2,1)} %copy-done.34, ...), custom_call_target="tpu_custom_call" | custom-call | flops 1 | bytes 1 | tf_op jit(solution)/shard_map/in_order/pallas_call | solution.py:385
  104.7 2.6 collective-permute-start.13
  107.4 5.1 all-to-all-start.1
  114.9 11.1 %up_product.2 = (bf16[1024,1024]{1,0:T(8,128)(2,1)}, bf16[1024,1024]{1,0:T(8,128)(2,1)}) custom-call(bf16[1024,2048]{1,0:T(8,128)(2,1)} %bitcast.3.h_ref.refs_0_, bf16[2048,1792]{1,0:T(8,128)(2,1)} %bitcast.4.w_ref.refs_0_.refs_1_.refs_2_, f32[1,1024]{1,0:T(1,128)} %bitcast.103), custom_call_target="tpu_custom_call" | custom-call | flops 1 | bytes 1 | tf_op jit(solution)/shard_map/up_product/pallas_call | solution.py:458
  125.9 11.4 %up_product.3 = (bf16[1024,1024]{1,0:T(8,128)(2,1)}, bf16[1024,1024]{1,0:T(8,128)(2,1)}) custom-call(bf16[1024,2048]{1,0:T(8,128)(2,1)} %collective-permute-done.13.h_ref.refs_1_, bf16[2048,1792]{1,0:T(8,128)(2,1)} %bitcast.4.w_ref.refs_0_.refs_1_.refs_2_, f32[1,1024]{1,0:T(1,128)} %bitcast.104), custom_call_target="tpu_custom_call" | custom-call | flops 1 | bytes 1 | tf_op jit(solution)/shard_map/up_product/pallas_call | solution.py:458
  137.3 7.3 %line_product.2.qkv_ref = f32[1024,768]{1,0:T(8,128)} custom-call(bf16[1024,2048]{1,0:T(8,128)(2,1)} %bitcast.3.h_ref.refs_0_, bf16[2048,1792]{1,0:T(8,128)(2,1)} %bitcast.4.w_ref.refs_0_.refs_1_.refs_2_, bf16[2048,1792]{1,0:T(8,128)(2,1)} %bitcast.4.w_ref.refs_0_.refs_1_.refs_2_, bf16[2048,1792]{1,0:T(8,128)(2,1)} %bitcast.4.w_ref.refs_0_.refs_1_.refs_2_, ...), custom_call_target="tpu_custom_call" | custom-call | flops 1 | bytes 1 | tf_op jit(solution)/shard_map/line_product/pallas_call | solution.py:524
  144.6 7.3 %line_product.3.qkv_ref = f32[1024,768]{1,0:T(8,128)} custom-call(bf16[1024,2048]{1,0:T(8,128)(2,1)} %collective-permute-done.13.h_ref.refs_1_, bf16[2048,1792]{1,0:T(8,128)(2,1)} %bitcast.4.w_ref.refs_0_.refs_1_.refs_2_, bf16[2048,1792]{1,0:T(8,128)(2,1)} %bitcast.4.w_ref.refs_0_.refs_1_.refs_2_, bf16[2048,1792]{1,0:T(8,128)(2,1)} %bitcast.4.w_ref.refs_0_.refs_1_.refs_2_, ...), custom_call_target="tpu_custom_call" | custom-call | flops 1 | bytes 1 | tf_op jit(solution)/shard_map/line_product/pallas_call | solution.py:524
  153.8 14.7 %attend.2 = (bf16[1024,256]{1,0:T(8,128)(2,1)S(1)}, bf16[1024,768]{1,0:T(8,128)(2,1)S(1)}, f32[2,2,2,1024]{3,2,1,0:T(2,128)S(1)}) custom-call(s32[8]{0:T(128)S(1)} %broadcast_multiply_fusion.3.offs_ref, s32[1]{0:T(128)} %get-tuple-element.351.prefix_ref, f32[1024,768]{1,0:T(8,128)S(1)} %copy-done.10, f32[1024,128]{1,0:T(8,128)S(1)} %get-tuple-element.218.cos_ref, ...), custom_call_target="tpu_custom_call" | custom-call | flops 1 | bytes 1 | tf_op jit(solution)/shard_map/attend/pallas_call | solution.py:210
  171.8 8.8 %pair_product.4 = bf16[1024,2048]{1,0:T(8,128)(2,1)} custom-call(bf16[1024,1024]{1,0:T(8,128)(2,1)S(1)} %copy-done.11, bf16[1024,256]{1,0:T(8,128)(2,1)S(1)} %get-tuple-element.229.b_ref.refs_7_, bf16[2048,1280]{1,0:T(8,128)(2,1)} %bitcast.6.w_ref), custom_call_target="tpu_custom_call" | custom-call | flops 1 | bytes 1 | tf_op jit(solution)/shard_map/pair_product/pallas_call | solution.py:282
  182.2 14.9 %attend.3 = (bf16[1024,256]{1,0:T(8,128)(2,1)S(1)}, bf16[1024,768]{1,0:T(8,128)(2,1)S(1)}, f32[2,2,2,1024]{3,2,1,0:T(2,128)S(1)}) custom-call(s32[8]{0:T(128)S(1)} %broadcast_multiply_fusion.3.offs_ref, s32[1]{0:T(128)} %get-tuple-element.352.prefix_ref, f32[1024,768]{1,0:T(8,128)S(1)} %copy-done.9, f32[1024,128]{1,0:T(8,128)S(1)} %get-tuple-element.218.cos_ref, ...), custom_call_target="tpu_custom_call" | custom-call | flops 1 | bytes 1 | tf_op jit(solution)/shard_map/attend/pallas_call | solution.py:210
  200.1 9.4 %pair_product.5 = bf16[1024,2048]{1,0:T(8,128)(2,1)} custom-call(bf16[1024,1024]{1,0:T(8,128)(2,1)S(1)} %copy-done.12, bf16[1024,256]{1,0:T(8,128)(2,1)S(1)} %get-tuple-element.242.b_ref.refs_6_, bf16[2048,1280]{1,0:T(8,128)(2,1)} %bitcast.6.w_ref, bf16[1024,2048]{1,0:T(8,128)(2,1)} %collective-permute-done.14.refs_0_), custom_call_target="tpu_custom_call" | custom-call | flops 1 | bytes 1 | tf_op jit(solution)/shard_map/pair_product/pallas_call | solution.py:282
  211.5 13.4 %rows_product.3 = bf16[4,512,1024]{2,1,0:T(8,128)(2,1)} custom-call(bf16[1024,2048]{1,0:T(8,128)(2,1)} %all-gather.9.cloned.1.call-done, bf16[1024,2048]{1,0:T(8,128)(2,1)} %copy-done.21, bf16[1024,1024]{1,0:T(8,128)(2,1)} %get-tuple-element.246.a_ref.refs_2_, bf16[1024,1024]{1,0:T(8,128)(2,1)} %get-tuple-element.247.a_ref.refs_3_), custom_call_target="tpu_custom_call" | custom-call | flops 1 | bytes 1 | tf_op jit(solution)/shard_map/rows_product/pallas_call | solution.py:351
  225.0 5.2 all-to-all-start.2
  230.1 10.3 %down_product.2 = (bf16[1024,1024]{1,0:T(8,128)(2,1)}, bf16[1024,256]{1,0:T(8,128)(2,1)}) custom-call(bf16[1024,2048]{1,0:T(8,128)(2,1)} %all-gather.9.cloned.1.call-done, bf16[2048,1280]{1,0:T(8,128)(2,1)} %bitcast.6.w_ref, bf16[1024,1024]{1,0:T(8,128)(2,1)} %get-tuple-element.251.s_ref), custom_call_target="tpu_custom_call" | custom-call | flops 1 | bytes 1 | tf_op jit(solution)/shard_map/down_product/pallas_call | solution.py:485
  240.5 10.3 %down_product.3 = (bf16[1024,1024]{1,0:T(8,128)(2,1)}, bf16[1024,256]{1,0:T(8,128)(2,1)}) custom-call(bf16[1024,2048]{1,0:T(8,128)(2,1)} %copy-done.21, bf16[2048,1280]{1,0:T(8,128)(2,1)} %bitcast.6.w_ref, bf16[1024,1024]{1,0:T(8,128)(2,1)} %get-tuple-element.260.s_ref), custom_call_target="tpu_custom_call" | custom-call | flops 1 | bytes 1 | tf_op jit(solution)/shard_map/down_product/pallas_call | solution.py:485
  250.8 13.6 %rows_product.4 = bf16[4,512,1024]{2,1,0:T(8,128)(2,1)} custom-call(bf16[1024,2048]{1,0:T(8,128)(2,1)} %bitcast.3.h_ref.refs_0_, bf16[1024,2048]{1,0:T(8,128)(2,1)} %collective-permute-done.13.h_ref.refs_1_, bf16[1024,1024]{1,0:T(8,128)(2,1)} %get-tuple-element.294.refs_2_.a_ref, bf16[1024,1024]{1,0:T(8,128)(2,1)} %get-tuple-element.283.refs_3_.a_ref), custom_call_target="tpu_custom_call" | custom-call | flops 1 | bytes 1 | tf_op jit(solution)/shard_map/rows_product/pallas_call | solution.py:351
  264.3 21.6 %attend_back.2.b_ref.refs_3_ = bf16[1024,768]{1,0:T(8,128)(2,1)S(1)} custom-call(s32[8]{0:T(128)S(1)} %broadcast_multiply_fusion.3.offs_ref, s32[1]{0:T(128)} %get-tuple-element.351.prefix_ref, bf16[1024,768]{1,0:T(8,128)(2,1)S(1)} %copy-done.18, f32[2,2,2,1024]{3,2,1,0:T(2,128)S(1)} %get-tuple-element.277.stat_ref, bf16[1024,256]{1,0:T(8,128)(2,1)S(1)} %copy-done.20, ...), custom_call_target="tpu_custom_call" | custom-call | flops 1 | bytes 1 | tf_op jit(solution)/shard_map/attend_back/pallas_call | solution.py:239
  286.0 4.6 fusion.21
  292.3 11.3 %pair_product.6 = bf16[1024,2048]{1,0:T(8,128)(2,1)} custom-call(bf16[1024,1024]{1,0:T(8,128)(2,1)S(1)} %copy-done.8, bf16[1024,768]{1,0:T(8,128)(2,1)S(1)} %attend_back.2.b_ref.refs_3_, bf16[2048,1792]{1,0:T(8,128)(2,1)} %bitcast.4.w_ref.refs_0_.refs_1_.refs_2_), custom_call_target="tpu_custom_call" | custom-call | flops 1 | bytes 1 | tf_op jit(solution)/shard_map/pair_product/pallas_call | solution.py:282
  304.1 4.8 all-to-all-start.3
  311.4 21.6 %attend_back.3.b_ref.refs_2_ = bf16[1024,768]{1,0:T(8,128)(2,1)S(1)} custom-call(s32[8]{0:T(128)S(1)} %broadcast_multiply_fusion.3.offs_ref, s32[1]{0:T(128)} %get-tuple-element.352.prefix_ref, bf16[1024,768]{1,0:T(8,128)(2,1)S(1)} %copy-done.16, f32[2,2,2,1024]{3,2,1,0:T(2,128)S(1)} %get-tuple-element.289.stat_ref, bf16[1024,256]{1,0:T(8,128)(2,1)S(1)} %copy-done.19, ...), custom_call_target="tpu_custom_call" | custom-call | flops 1 | bytes 1 | tf_op jit(solution)/shard_map/attend_back/pallas_call | solution.py:239
  335.3 11.3 %pair_product.7 = bf16[1024,2048]{1,0:T(8,128)(2,1)} custom-call(bf16[1024,1024]{1,0:T(8,128)(2,1)S(1)} %copy-done.6, bf16[1024,768]{1,0:T(8,128)(2,1)S(1)} %attend_back.3.b_ref.refs_2_, bf16[2048,1792]{1,0:T(8,128)(2,1)} %bitcast.4.w_ref.refs_0_.refs_1_.refs_2_, bf16[1024,2048]{1,0:T(8,128)(2,1)} %collective-permute-done.16.refs_0_), custom_call_target="tpu_custom_call" | custom-call | flops 1 | bytes 1 | tf_op jit(solution)/shard_map/pair_product/pallas_call | solution.py:282
  346.5 14.5 %rows_product.5 = bf16[4,512,1024]{2,1,0:T(8,128)(2,1)} custom-call(bf16[1024,2048]{1,0:T(8,128)(2,1)} %bitcast.3.h_ref.refs_0_, bf16[1024,2048]{1,0:T(8,128)(2,1)} %collective-permute-done.13.h_ref.refs_1_, bf16[1024,768]{1,0:T(8,128)(2,1)} %copy-done.3, bf16[1024,768]{1,0:T(8,128)(2,1)} %copy-done.1, bf16[1024,2048]{1,0:T(8,128)(2,1)} %all-gather.9.cloned.1.call-done, ...), custom_call_target="tpu_custom_call" | custom-call | flops 1 | bytes 1 | tf_op jit(solution)/shard_map/rows_product/pallas_call | solution.py:351
  361.0 4.1 fusion.23
  365.1 7.1 %all-gather.11.cloned.1.call-done = bf16[2048,1024]{1,0:T(8,128)(2,1)} async-done(((bf16[512,1024]{1,0:T(8,128)(2,1)}), bf16[2048,1024]{1,0:T(8,128)(2,1)}) %all-gather.11.cloned.1.call-update) | async-done | bytes 4194320 | tf_op jit(solution)/shard_map/all_gather | solution.py:643
  372.2 5.1 all-to-all-start.4
  381.0 6.1 %widen.2 = f32[512,4096]{1,0:T(8,128)} custom-call(bf16[4,512,1024]{2,1,0:T(8,128)(2,1)} %bitcast.97), custom_call_target="tpu_custom_call" | custom-call | flops 1 | bytes 1 | tf_op jit(solution)/shard_map/widen/pallas_call | solution.py:434
  387.2 40.3 %collective-permute-done.19 = bf16[256,2048]{1,0:T(8,128)(2,1)} collective-permute-done((bf16[256,2048]{1,0:T(8,128)(2,1)S(1)}, bf16[256,2048]{1,0:T(8,128)(2,1)}, u32[]{:S(2)}, u32[]{:S(2)}) %collective-permute-start.19) | collective-permute-done | bytes 1048608 | tf_op jit(solution)/shard_map/ppermute | solution.py:58
  427.4 3.5 fusion.1
  432.6 4.0 collective-permute-start.21
  439.4 4.2 fusion.24
  443.6 37.3 %collective-permute-done.20 = bf16[256,2048]{1,0:T(8,128)(2,1)} collective-permute-done((bf16[256,2048]{1,0:T(8,128)(2,1)}, bf16[256,2048]{1,0:T(8,128)(2,1)}, u32[]{:S(2)}, u32[]{:S(2)}) %collective-permute-start.20) | collective-permute-done | bytes 1048608 | tf_op jit(solution)/shard_map/ppermute | solution.py:55
  482.7 2.6 add_convert_fusion
  485.3 2.9 collective-permute-start.23
  488.2 2.6 add_convert_fusion.1
  490.8 3.5 collective-permute-start.22
  494.9 3.6 all-to-all-start.5
  498.5 2.7 fusion.20
  501.2 4.4 collective-permute-start.17
  508.6 11.7 %collective-permute-done.23 = bf16[256,2048]{1,0:T(8,128)(2,1)} collective-permute-done((bf16[256,2048]{1,0:T(8,128)(2,1)}, bf16[256,2048]{1,0:T(8,128)(2,1)}, u32[]{:S(2)}, u32[]{:S(2)}) %collective-permute-start.23) | collective-permute-done | bytes 1048608 | tf_op jit(solution)/shard_map/ppermute | solution.py:58
  520.4 3.4 fusion.18
  523.8 6.1 %widen.3 = f32[512,4096]{1,0:T(8,128)} custom-call(bf16[4,512,1024]{2,1,0:T(8,128)(2,1)} %bitcast.96), custom_call_target="tpu_custom_call" | custom-call | flops 1 | bytes 1 | tf_op jit(solution)/shard_map/widen/pallas_call | solution.py:434
  531.6 3.6 all-to-all-start.6
  540.1 13.7 %collective-permute-start.24 = (bf16[1,1,256,2048]{3,2,1,0:T(8,128)(2,1)}, bf16[1,1,256,2048]{3,2,1,0:T(8,128)(2,1)S(1)}, u32[]{:S(2)}, u32[]{:S(2)}) collective-permute-start(bf16[1,1,256,2048]{3,2,1,0:T(8,128)(2,1)} %bitcast.24), channel_id=1, source_target_pairs={{0,1},{1,0},{2,3},{3,2},{4,5},{5,4},{6,7},{7,6},{8,9},{9,8},{10,11... | collective-permute-start | bytes 3145736 | tf_op jit(solution)/shard_map/ppermute | solution.py:35
  553.8 2.3 bitcast_dynamic-update-slice_fusion.2
  556.9 3.6 all-to-all-start.7
  560.4 2.9 all-to-all-done.7
  568.8 20.5 %all-gather.15.cloned.1.call-done = bf16[2048,1024]{1,0:T(8,128)(2,1)} async-done(((bf16[512,1024]{1,0:T(8,128)(2,1)}), bf16[2048,1024]{1,0:T(8,128)(2,1)}) %all-gather.15.cloned.1.call-update) | async-done | bytes 4194320 | tf_op jit(solution)/shard_map/all_gather | solution.py:643
  589.3 5.9 place.1
  (223 shorter events, 72.5 us)
Async XLA Ops:
  13.5 1.5 collective-permute-start.2
  20.4 87.0 %all-to-all-start = ((bf16[4,512,1792]{2,1,0:T(8,128)(2,1)}), bf16[4,512,1792]{2,1,0:T(8,128)(2,1)}, u32[]{:S(2)}, u32[]{:S(2)}) async-start(bf16[4,512,1792]{2,1,0:T(8,128)(2,1)} %copy-done), calls=%async_computation | async-start | bytes 14680064 | tf_op jit(solution)/shard_map/all_to_all | solution.py:622
  26.0 15.2 %copy-start.48 = (s32[8]{0:T(128)S(1)}, s32[8]{0:T(128)}, u32[]{:S(2)}) copy-start(s32[8]{0:T(128)} %param.21) | copy-start | bytes 100
  26.0 15.3 %copy-start.49 = (s32[2]{0:T(128)S(1)}, s32[2]{0:T(128)}, u32[]{:S(2)}) copy-start(s32[2]{0:T(128)} %param.20) | copy-start | bytes 28
  27.0 21.8 %collective-permute-start = (bf16[128,2048]{1,0:T(8,128)(2,1)}, bf16[128,2048]{1,0:T(8,128)(2,1)S(1)}, u32[]{:S(2)}, u32[]{:S(2)}) collective-permute-start(bf16[128,2048]{1,0:T(8,128)(2,1)} %get-tuple-element.181.refs_0_), channel_id=1, source_target_pairs={{0,2},{2,4},{4,6},{1,3},{3,5},{5,7},{8,10},{10,12},{12,14},{9,11},... | collective-permute-start | bytes 1572872 | tf_op jit(solution)/shard_map/ppermute | solution.py:45
  30.2 18.6 %collective-permute-start.1 = (bf16[128,2048]{1,0:T(8,128)(2,1)}, bf16[128,2048]{1,0:T(8,128)(2,1)S(1)}, u32[]{:S(2)}, u32[]{:S(2)}) collective-permute-start(bf16[128,2048]{1,0:T(8,128)(2,1)} %get-tuple-element.181.refs_0_), channel_id=1, source_target_pairs={{2,0},{4,2},{6,4},{3,1},{5,3},{7,5},{10,8},{12,10},{14,12},{11,9},... | collective-permute-start | bytes 1572872 | tf_op jit(solution)/shard_map/ppermute | solution.py:46
  32.3 21.9 %collective-permute-start.7 = (bf16[128,2048]{1,0:T(8,128)(2,1)}, bf16[128,2048]{1,0:T(8,128)(2,1)S(1)}, u32[]{:S(2)}, u32[]{:S(2)}) collective-permute-start(bf16[128,2048]{1,0:T(8,128)(2,1)} %get-tuple-element.188.refs_7_), channel_id=1, source_target_pairs={{0,2},{2,4},{4,6},{1,3},{3,5},{5,7},{8,10},{10,12},{12,14},{9,11},... | collective-permute-start | bytes 1572872 | tf_op jit(solution)/shard_map/ppermute | solution.py:45
  35.5 21.0 %collective-permute-start.8 = (bf16[128,2048]{1,0:T(8,128)(2,1)}, bf16[128,2048]{1,0:T(8,128)(2,1)}, u32[]{:S(2)}, u32[]{:S(2)}) collective-permute-start(bf16[128,2048]{1,0:T(8,128)(2,1)} %get-tuple-element.188.refs_7_), channel_id=1, source_target_pairs={{2,0},{4,2},{6,4},{3,1},{5,3},{7,5},{10,8},{12,10},{14,12},{11,9},... | collective-permute-start | bytes 1572872 | tf_op jit(solution)/shard_map/ppermute | solution.py:46
  48.8 48.9 %copy-start.33 = (bf16[128,2048]{1,0:T(8,128)(2,1)}, bf16[128,2048]{1,0:T(8,128)(2,1)S(1)}, u32[]{:S(2)}) copy-start(bf16[128,2048]{1,0:T(8,128)(2,1)S(1)} %collective-permute-done.refs_1_) | copy-start | bytes 1572868
  48.8 48.9 %copy-start.34 = (bf16[128,2048]{1,0:T(8,128)(2,1)}, bf16[128,2048]{1,0:T(8,128)(2,1)S(1)}, u32[]{:S(2)}) copy-start(bf16[128,2048]{1,0:T(8,128)(2,1)S(1)} %collective-permute-done.1.refs_4_) | copy-start | bytes 1572868
  48.8 15.4 %collective-permute-start.3 = (bf16[128,2048]{1,0:T(8,128)(2,1)S(1)}, bf16[128,2048]{1,0:T(8,128)(2,1)S(1)}, u32[]{:S(2)}, u32[]{:S(2)}) collective-permute-start(bf16[128,2048]{1,0:T(8,128)(2,1)S(1)} %collective-permute-done.refs_1_), channel_id=1, source_target_pairs={{2,4},{4,6},{3,5},{5,7},{10,12},{12,14},{11,13},{13,15},{18,20},{2... | collective-permute-start | bytes 1572872 | tf_op jit(solution)/shard_map/ppermute | solution.py:45
  52.8 13.8 %collective-permute-start.4 = (bf16[128,2048]{1,0:T(8,128)(2,1)S(1)}, bf16[128,2048]{1,0:T(8,128)(2,1)S(1)}, u32[]{:S(2)}, u32[]{:S(2)}) collective-permute-start(bf16[128,2048]{1,0:T(8,128)(2,1)S(1)} %collective-permute-done.1.refs_4_), channel_id=1, source_target_pairs={{2,0},{4,2},{3,1},{5,3},{10,8},{12,10},{11,9},{13,11},{18,16},{20,... | collective-permute-start | bytes 1572872 | tf_op jit(solution)/shard_map/ppermute | solution.py:46
  54.2 43.6 %copy-start.35 = (bf16[128,2048]{1,0:T(8,128)(2,1)}, bf16[128,2048]{1,0:T(8,128)(2,1)S(1)}, u32[]{:S(2)}) copy-start(bf16[128,2048]{1,0:T(8,128)(2,1)S(1)} %collective-permute-done.7.refs_8_) | copy-start | bytes 1572868
  54.2 21.3 %collective-permute-start.9 = (bf16[128,2048]{1,0:T(8,128)(2,1)S(1)}, bf16[128,2048]{1,0:T(8,128)(2,1)S(1)}, u32[]{:S(2)}, u32[]{:S(2)}) collective-permute-start(bf16[128,2048]{1,0:T(8,128)(2,1)S(1)} %collective-permute-done.7.refs_8_), channel_id=1, source_target_pairs={{2,4},{4,6},{3,5},{5,7},{10,12},{12,14},{11,13},{13,15},{18,20},{2... | collective-permute-start | bytes 1572872 | tf_op jit(solution)/shard_map/ppermute | solution.py:45
  56.5 21.4 %collective-permute-start.10 = (bf16[128,2048]{1,0:T(8,128)(2,1)}, bf16[128,2048]{1,0:T(8,128)(2,1)S(1)}, u32[]{:S(2)}, u32[]{:S(2)}) collective-permute-start(bf16[128,2048]{1,0:T(8,128)(2,1)} %collective-permute-done.8.refs_11_), channel_id=1, source_target_pairs={{2,0},{4,2},{3,1},{5,3},{10,8},{12,10},{11,9},{13,11},{18,16},{20,... | collective-permute-start | bytes 1572872 | tf_op jit(solution)/shard_map/ppermute | solution.py:46
  64.2 11.2 %copy-start.36 = (bf16[128,2048]{1,0:T(8,128)(2,1)}, bf16[128,2048]{1,0:T(8,128)(2,1)S(1)}, u32[]{:S(2)}) copy-start(bf16[128,2048]{1,0:T(8,128)(2,1)S(1)} %collective-permute-done.3.refs_2_) | copy-start | bytes 1572868
  64.2 20.6 %collective-permute-start.5 = (bf16[128,2048]{1,0:T(8,128)(2,1)S(1)}, bf16[128,2048]{1,0:T(8,128)(2,1)S(1)}, u32[]{:S(2)}, u32[]{:S(2)}) collective-permute-start(bf16[128,2048]{1,0:T(8,128)(2,1)S(1)} %collective-permute-done.3.refs_2_), channel_id=1, source_target_pairs={{4,6},{5,7},{12,14},{13,15},{20,22},{21,23},{28,30},{29,31}} | collective-permute-start | bytes 1572872 | tf_op jit(solution)/shard_map/ppermute | solution.py:45
  66.7 18.2 %copy-start.37 = (bf16[128,2048]{1,0:T(8,128)(2,1)}, bf16[128,2048]{1,0:T(8,128)(2,1)S(1)}, u32[]{:S(2)}) copy-start(bf16[128,2048]{1,0:T(8,128)(2,1)S(1)} %collective-permute-done.4.refs_5_) | copy-start | bytes 1572868
  66.7 18.2 %collective-permute-start.6 = (bf16[128,2048]{1,0:T(8,128)(2,1)S(1)}, bf16[128,2048]{1,0:T(8,128)(2,1)S(1)}, u32[]{:S(2)}, u32[]{:S(2)}) collective-permute-start(bf16[128,2048]{1,0:T(8,128)(2,1)S(1)} %collective-permute-done.4.refs_5_), channel_id=1, source_target_pairs={{2,0},{3,1},{10,8},{11,9},{18,16},{19,17},{26,24},{27,25}} | collective-permute-start | bytes 1572872 | tf_op jit(solution)/shard_map/ppermute | solution.py:46
  75.5 9.4 %copy-start.38 = (bf16[128,2048]{1,0:T(8,128)(2,1)}, bf16[128,2048]{1,0:T(8,128)(2,1)S(1)}, u32[]{:S(2)}) copy-start(bf16[128,2048]{1,0:T(8,128)(2,1)S(1)} %collective-permute-done.9.refs_9_) | copy-start | bytes 1572868
  75.5 20.6 %collective-permute-start.11 = (bf16[128,2048]{1,0:T(8,128)(2,1)S(1)}, bf16[128,2048]{1,0:T(8,128)(2,1)S(1)}, u32[]{:S(2)}, u32[]{:S(2)}) collective-permute-start(bf16[128,2048]{1,0:T(8,128)(2,1)S(1)} %collective-permute-done.9.refs_9_), channel_id=1, source_target_pairs={{4,6},{5,7},{12,14},{13,15},{20,22},{21,23},{28,30},{29,31}} | collective-permute-start | bytes 1572872 | tf_op jit(solution)/shard_map/ppermute | solution.py:45
  77.9 18.2 %copy-start.39 = (bf16[128,2048]{1,0:T(8,128)(2,1)}, bf16[128,2048]{1,0:T(8,128)(2,1)S(1)}, u32[]{:S(2)}) copy-start(bf16[128,2048]{1,0:T(8,128)(2,1)S(1)} %collective-permute-done.10.refs_12_) | copy-start | bytes 1572868
  77.9 18.2 %collective-permute-start.12 = (bf16[128,2048]{1,0:T(8,128)(2,1)S(1)}, bf16[128,2048]{1,0:T(8,128)(2,1)S(1)}, u32[]{:S(2)}, u32[]{:S(2)}) collective-permute-start(bf16[128,2048]{1,0:T(8,128)(2,1)S(1)} %collective-permute-done.10.refs_12_), channel_id=1, source_target_pairs={{2,0},{3,1},{10,8},{11,9},{18,16},{19,17},{26,24},{27,25}} | collective-permute-start | bytes 1572872 | tf_op jit(solution)/shard_map/ppermute | solution.py:46
  84.9 11.2 %copy-start.40 = (bf16[128,2048]{1,0:T(8,128)(2,1)}, bf16[128,2048]{1,0:T(8,128)(2,1)S(1)}, u32[]{:S(2)}) copy-start(bf16[128,2048]{1,0:T(8,128)(2,1)S(1)} %collective-permute-done.5.refs_3_) | copy-start | bytes 1572868
  84.9 11.2 %copy-start.41 = (bf16[128,2048]{1,0:T(8,128)(2,1)}, bf16[128,2048]{1,0:T(8,128)(2,1)S(1)}, u32[]{:S(2)}) copy-start(bf16[128,2048]{1,0:T(8,128)(2,1)S(1)} %collective-permute-done.6.refs_6_) | copy-start | bytes 1572868
  104.7 10.1 %collective-permute-start.13 = (bf16[1024,2048]{1,0:T(8,128)(2,1)}, bf16[1024,2048]{1,0:T(8,128)(2,1)}, u32[]{:S(2)}, u32[]{:S(2)}) collective-permute-start(bf16[1024,2048]{1,0:T(8,128)(2,1)} %bitcast.3.h_ref.refs_0_), channel_id=1, source_target_pairs={{0,1},{1,0},{2,3},{3,2},{4,5},{5,4},{6,7},{7,6},{8,9},{9,8},{10,11... | collective-permute-start | bytes 12582920 | tf_op jit(solution)/shard_map/ppermute | solution.py:35
  107.4 62.9 %all-to-all-start.1 = ((bf16[4,512,1280]{2,1,0:T(8,128)(2,1)}), bf16[4,512,1280]{2,1,0:T(8,128)(2,1)}, u32[]{:S(2)}, u32[]{:S(2)}) async-start(bf16[4,512,1280]{2,1,0:T(8,128)(2,1)} %copy-done.5), calls=%async_computation.1 | async-start | bytes 10485760 | tf_op jit(solution)/shard_map/all_to_all | solution.py:649
  112.5 85.8 %all-gather.9.cloned.1.call-start = ((), (), s32[]{:S(2)}) async-start(), calls=%async_computation.10 | async-start | bytes 5242880 | tf_op jit(solution)/shard_map/all_gather | solution.py:630
  113.2 219.9 %reduce-scatter.2.cloned.1.call-start = ((), (), s32[]{:S(2)}) async-start(), calls=%async_computation.9 | async-start | bytes 5242880 | tf_op jit(solution)/shard_map/reduce_scatter | solution.py:705
  169.7 11.0 %copy-start.13 = (bf16[1024,256]{1,0:T(8,128)(2,1)}, bf16[1024,256]{1,0:T(8,128)(2,1)S(1)}, u32[]{:S(2)}) copy-start(bf16[1024,256]{1,0:T(8,128)(2,1)S(1)} %get-tuple-element.229.b_ref.refs_7_) | copy-start | bytes 1572868
  171.8 10.4 %copy-start.9 = (f32[1024,768]{1,0:T(8,128)S(1)}, f32[1024,768]{1,0:T(8,128)}, u32[]{:S(2)}) copy-start(f32[1024,768]{1,0:T(8,128)} %line_product.2.qkv_ref) | copy-start | bytes 9437188
  180.7 17.6 %collective-permute-start.14 = (bf16[1024,2048]{1,0:T(8,128)(2,1)}, bf16[1024,2048]{1,0:T(8,128)(2,1)}, u32[]{:S(2)}, u32[]{:S(2)}) collective-permute-start(bf16[1024,2048]{1,0:T(8,128)(2,1)} %pair_product.4), channel_id=1, source_target_pairs={{0,1},{1,0},{2,3},{3,2},{4,5},{5,4},{6,7},{7,6},{8,9},{9,8},{10,11... | collective-permute-start | bytes 12582920 | tf_op jit(solution)/shard_map/ppermute | solution.py:35
  198.3 11.2 %copy-start.14 = (bf16[1024,256]{1,0:T(8,128)(2,1)}, bf16[1024,256]{1,0:T(8,128)(2,1)S(1)}, u32[]{:S(2)}) copy-start(bf16[1024,256]{1,0:T(8,128)(2,1)S(1)} %get-tuple-element.242.b_ref.refs_6_) | copy-start | bytes 1572868
  198.3 11.2 %collective-permute-start.15 = (bf16[1024,2048]{1,0:T(8,128)(2,1)}, bf16[1024,2048]{1,0:T(8,128)(2,1)S(1)}, u32[]{:S(2)}, u32[]{:S(2)}) collective-permute-start(bf16[1024,2048]{1,0:T(8,128)(2,1)} %all-gather.9.cloned.1.call-done), channel_id=1, source_target_pairs={{0,1},{1,0},{2,3},{3,2},{4,5},{5,4},{6,7},{7,6},{8,9},{9,8},{10,11... | collective-permute-start | bytes 12582920 | tf_op jit(solution)/shard_map/ppermute | solution.py:35
  225.0 61.1 %all-to-all-start.2 = ((bf16[4,512,1024]{2,1,0:T(8,128)(2,1)}), bf16[4,512,1024]{2,1,0:T(8,128)(2,1)}, u32[]{:S(2)}, u32[]{:S(2)}) async-start(bf16[4,512,1024]{2,1,0:T(8,128)(2,1)} %rows_product.3), calls=%async_computation.2 | async-start | bytes 8388608 | tf_op jit(solution)/shard_map/all_to_all | solution.py:637
  230.1 142.0 %all-gather.11.cloned.1.call-start = ((), (), s32[]{:S(2)}) async-start(), calls=%async_computation.11 | async-start | bytes 5242880 | tf_op jit(solution)/shard_map/all_gather | solution.py:643
  250.8 13.6 %copy-start.18 = (bf16[1024,768]{1,0:T(8,128)(2,1)S(1)}, bf16[1024,768]{1,0:T(8,128)(2,1)}, u32[]{:S(2)}) copy-start(bf16[1024,768]{1,0:T(8,128)(2,1)} %copy-done.17) | copy-start | bytes 4718596
  250.8 13.6 %copy-start.20 = (bf16[1024,256]{1,0:T(8,128)(2,1)S(1)}, bf16[1024,256]{1,0:T(8,128)(2,1)}, u32[]{:S(2)}) copy-start(bf16[1024,256]{1,0:T(8,128)(2,1)} %get-tuple-element.278.do_ref) | copy-start | bytes 1572868
  303.6 29.5 %collective-permute-start.16 = (bf16[1024,2048]{1,0:T(8,128)(2,1)}, bf16[1024,2048]{1,0:T(8,128)(2,1)}, u32[]{:S(2)}, u32[]{:S(2)}) collective-permute-start(bf16[1024,2048]{1,0:T(8,128)(2,1)} %pair_product.6), channel_id=1, source_target_pairs={{0,1},{1,0},{2,3},{3,2},{4,5},{5,4},{6,7},{7,6},{8,9},{9,8},{10,11... | collective-permute-start | bytes 12582920 | tf_op jit(solution)/shard_map/ppermute | solution.py:35
  304.1 56.9 %all-to-all-start.3 = ((bf16[4,512,1024]{2,1,0:T(8,128)(2,1)}), bf16[4,512,1024]{2,1,0:T(8,128)(2,1)}, u32[]{:S(2)}, u32[]{:S(2)}) async-start(bf16[4,512,1024]{2,1,0:T(8,128)(2,1)} %rows_product.4), calls=%async_computation.4 | async-start | bytes 8388608 | tf_op jit(solution)/shard_map/all_to_all | solution.py:637
  308.9 214.9 %all-gather.13.cloned.1.call-start = ((), (), s32[]{:S(2)}) async-start(), calls=%async_computation.12 | async-start | bytes 5242880 | tf_op jit(solution)/shard_map/all_gather | solution.py:643
  333.1 13.5 %copy-start.3 = (bf16[1024,768]{1,0:T(8,128)(2,1)}, bf16[1024,768]{1,0:T(8,128)(2,1)S(1)}, u32[]{:S(2)}) copy-start(bf16[1024,768]{1,0:T(8,128)(2,1)S(1)} %attend_back.3.b_ref.refs_2_) | copy-start | bytes 4718596
  372.2 55.3 %all-to-all-start.4 = ((bf16[4,512,1024]{2,1,0:T(8,128)(2,1)}), bf16[4,512,1024]{2,1,0:T(8,128)(2,1)}, u32[]{:S(2)}, u32[]{:S(2)}) async-start(bf16[4,512,1024]{2,1,0:T(8,128)(2,1)} %rows_product.5), calls=%async_computation.5 | async-start | bytes 8388608 | tf_op jit(solution)/shard_map/all_to_all | solution.py:637
  377.3 212.0 %all-gather.15.cloned.1.call-start = ((), (), s32[]{:S(2)}) async-start(), calls=%async_computation.13 | async-start | bytes 5242880 | tf_op jit(solution)/shard_map/all_gather | solution.py:643
  378.9 8.2 %copy-start.27 = (bf16[256,2048]{1,0:T(8,128)(2,1)}, bf16[256,2048]{1,0:T(8,128)(2,1)S(1)}, u32[]{:S(2)}) copy-start(bf16[256,2048]{1,0:T(8,128)(2,1)S(1)} %get-tuple-element.340) | copy-start | bytes 3145732
  378.9 8.2 %collective-permute-start.18 = (bf16[256,2048]{1,0:T(8,128)(2,1)S(1)}, bf16[256,2048]{1,0:T(8,128)(2,1)S(1)}, u32[]{:S(2)}, u32[]{:S(2)}) collective-permute-start(bf16[256,2048]{1,0:T(8,128)(2,1)S(1)} %get-tuple-element.340), channel_id=1, source_target_pairs={{0,2},{1,3},{8,10},{9,11},{16,18},{17,19},{24,26},{25,27}} | collective-permute-start | bytes 3145736 | tf_op jit(solution)/shard_map/ppermute | solution.py:55
  379.7 47.8 %collective-permute-start.19 = (bf16[256,2048]{1,0:T(8,128)(2,1)S(1)}, bf16[256,2048]{1,0:T(8,128)(2,1)}, u32[]{:S(2)}, u32[]{:S(2)}) collective-permute-start(bf16[256,2048]{1,0:T(8,128)(2,1)S(1)} %get-tuple-element.339), channel_id=1, source_target_pairs={{6,4},{7,5},{14,12},{15,13},{22,20},{23,21},{30,28},{31,29}} | collective-permute-start | bytes 3145736 | tf_op jit(solution)/shard_map/ppermute | solution.py:58
  387.2 49.4 %copy-start.46 = (bf16[2048]{0:T(1024)(128)(2,1)S(1)}, bf16[2048]{0:T(1024)(128)(2,1)}, u32[]{:S(2)}) copy-start(bf16[2048]{0:T(1024)(128)(2,1)} %param.31) | copy-start | bytes 12292
  387.2 49.5 %copy-start.47 = (bf16[2048]{0:T(1024)(128)(2,1)S(1)}, bf16[2048]{0:T(1024)(128)(2,1)}, u32[]{:S(2)}) copy-start(bf16[2048]{0:T(1024)(128)(2,1)} %param.35) | copy-start | bytes 12292
  431.0 49.9 %collective-permute-start.20 = (bf16[256,2048]{1,0:T(8,128)(2,1)}, bf16[256,2048]{1,0:T(8,128)(2,1)}, u32[]{:S(2)}, u32[]{:S(2)}) collective-permute-start(bf16[256,2048]{1,0:T(8,128)(2,1)} %get-tuple-element.338), channel_id=1, source_target_pairs={{0,2},{2,4},{1,3},{3,5},{8,10},{10,12},{9,11},{11,13},{16,18},{18,... | collective-permute-start | bytes 3145736 | tf_op jit(solution)/shard_map/ppermute | solution.py:55
  432.6 48.9 %collective-permute-start.21 = (bf16[256,2048]{1,0:T(8,128)(2,1)}, bf16[256,2048]{1,0:T(8,128)(2,1)}, u32[]{:S(2)}, u32[]{:S(2)}) collective-permute-start(bf16[256,2048]{1,0:T(8,128)(2,1)} %get-tuple-element.337), channel_id=1, source_target_pairs={{4,2},{6,4},{5,3},{7,5},{12,10},{14,12},{13,11},{15,13},{20,18},{2... | collective-permute-start | bytes 3145736 | tf_op jit(solution)/shard_map/ppermute | solution.py:58
  439.4 42.0 %copy-start.4 = (bf16[1024,768]{1,0:T(8,128)(2,1)S(1)}, bf16[1024,768]{1,0:T(8,128)(2,1)}, u32[]{:S(2)}) copy-start(bf16[1024,768]{1,0:T(8,128)(2,1)} %copy-done.3) | copy-start | bytes 4718596
  485.3 13.3 %copy-start.23 = (bf16[2,256,2048]{2,1,0:T(8,128)(2,1)S(1)}, bf16[2,256,2048]{2,1,0:T(8,128)(2,1)}, u32[]{:S(2)}) copy-start(bf16[2,256,2048]{2,1,0:T(8,128)(2,1)} %param.18) | copy-start | bytes 6291460
  485.3 35.1 %collective-permute-start.23 = (bf16[256,2048]{1,0:T(8,128)(2,1)}, bf16[256,2048]{1,0:T(8,128)(2,1)}, u32[]{:S(2)}, u32[]{:S(2)}) collective-permute-start(bf16[256,2048]{1,0:T(8,128)(2,1)} %add_convert_fusion), channel_id=1, source_target_pairs={{2,0},{4,2},{6,4},{3,1},{5,3},{7,5},{10,8},{12,10},{14,12},{11,9},... | collective-permute-start | bytes 3145736 | tf_op jit(solution)/shard_map/ppermute | solution.py:58
  490.8 29.6 %collective-permute-start.22 = (bf16[256,2048]{1,0:T(8,128)(2,1)}, bf16[256,2048]{1,0:T(8,128)(2,1)S(1)}, u32[]{:S(2)}, u32[]{:S(2)}) collective-permute-start(bf16[256,2048]{1,0:T(8,128)(2,1)} %add_convert_fusion.1), channel_id=1, source_target_pairs={{0,2},{2,4},{4,6},{1,3},{3,5},{5,7},{8,10},{10,12},{12,14},{9,11},... | collective-permute-start | bytes 3145736 | tf_op jit(solution)/shard_map/ppermute | solution.py:55
  494.9 13.7 %all-to-all-start.5 = ((f32[4,1,1792]{2,1,0:T(1,128)}), f32[4,1,1792]{2,1,0:T(1,128)S(1)}, u32[]{:S(2)}, u32[]{:S(2)}) async-start(f32[4,1,1792]{2,1,0:T(1,128)} %broadcast_in_dim.91), calls=%async_computation.6 | async-start | bytes 57344 | tf_op jit(solution)/shard_map/all_to_all | solution.py:39
  498.5 8.7 %copy-start.29 = (bf16[1,256,2048]{2,1,0:T(8,128)(2,1)S(1)}, bf16[1,256,2048]{2,1,0:T(8,128)(2,1)}, u32[]{:S(2)}) copy-start(bf16[1,256,2048]{2,1,0:T(8,128)(2,1)} %reduce-scatter.2.cloned.1.call-done) | copy-start | bytes 3145732
  501.2 52.5 %collective-permute-start.17 = (bf16[1,1,256,2048]{3,2,1,0:T(8,128)(2,1)}, bf16[1,1,256,2048]{3,2,1,0:T(8,128)(2,1)}, u32[]{:S(2)}, u32[]{:S(2)}) collective-permute-start(bf16[1,1,256,2048]{3,2,1,0:T(8,128)(2,1)} %fusion.20), channel_id=1, source_target_pairs={{0,1},{1,0},{2,3},{3,2},{4,5},{5,4},{6,7},{7,6},{8,9},{9,8},{10,11... | collective-permute-start | bytes 3145736 | tf_op jit(solution)/shard_map/ppermute | solution.py:35
  531.6 24.5 %all-to-all-start.6 = ((f32[4,1,7936]{2,1,0:T(1,128)}), f32[4,1,7936]{2,1,0:T(1,128)S(1)}, u32[]{:S(2)}, u32[]{:S(2)}) async-start(f32[4,1,7936]{2,1,0:T(1,128)} %broadcast_in_dim.92), calls=%async_computation.7 | async-start | bytes 253952 | tf_op jit(solution)/shard_map/all_to_all | solution.py:39
  540.1 28.6 %copy-start.31 = (bf16[2,256,2048]{2,1,0:T(8,128)(2,1)S(1)}, bf16[2,256,2048]{2,1,0:T(8,128)(2,1)}, u32[]{:S(2)}) copy-start(bf16[2,256,2048]{2,1,0:T(8,128)(2,1)} %copy-done.30) | copy-start | bytes 6291460
  540.1 28.6 %collective-permute-start.24 = (bf16[1,1,256,2048]{3,2,1,0:T(8,128)(2,1)}, bf16[1,1,256,2048]{3,2,1,0:T(8,128)(2,1)S(1)}, u32[]{:S(2)}, u32[]{:S(2)}) collective-permute-start(bf16[1,1,256,2048]{3,2,1,0:T(8,128)(2,1)} %bitcast.24), channel_id=1, source_target_pairs={{0,1},{1,0},{2,3},{3,2},{4,5},{5,4},{6,7},{7,6},{8,9},{9,8},{10,11... | collective-permute-start | bytes 3145736 | tf_op jit(solution)/shard_map/ppermute | solution.py:35
  556.9 6.4 %all-to-all-start.7 = ((f32[4,1,6144]{2,1,0:T(1,128)}), f32[4,1,6144]{2,1,0:T(1,128)S(1)}, u32[]{:S(2)}, u32[]{:S(2)}) async-start(f32[4,1,6144]{2,1,0:T(1,128)} %broadcast_in_dim.93), calls=%async_computation.8 | async-start | bytes 196608 | tf_op jit(solution)/shard_map/all_to_all | solution.py:39
  563.4 4.7 collective-permute-start.25
  568.8 26.4 %copy-start.32 = (bf16[2,256,2048]{2,1,0:T(8,128)(2,1)}, bf16[2,256,2048]{2,1,0:T(8,128)(2,1)S(1)}, u32[]{:S(2)}) copy-start(bf16[2,256,2048]{2,1,0:T(8,128)(2,1)S(1)} %bitcast_dynamic-update-slice_fusion) | copy-start | bytes 6291460
  (25 other events, 63.5 us)
Sparse Core Ops, SparseCore 0:
  114.9 80.8 all-gather.8
  211.6 78.0 reduce-scatter.1
  292.0 80.1 all-gather.10
  373.6 128.3 all-gather.12
  504.1 85.1 all-gather.14

commit v5 on v4

--- a/solution.py
+++ b/solution.py
@@ -137,7 +137,7 @@
             ot[h, :, cols] = jnp.dot(vt_s[h, :, 0:reach], low, preferred_element_type=F32)
             return 0
 
-        lax.fori_loop(0, 2, head, 0)
+        lax.fori_loop(0, 2, head, 0, unroll=True)
     for p in range(length // glen):
         rows = pl.ds(pl.multiple_of(offs_ref[p], glen), glen)
         to = slice(p * glen, (p + 1) * glen)
@@ -184,7 +184,7 @@
             dk_acc[0:reach, :] += dot(ds, qm[h, cols, :])
             return 0
 
-        lax.fori_loop(0, 2, head, 0)
+        lax.fori_loop(0, 2, head, 0, unroll=True)
     for p in range(length // glen):
         rows = pl.ds(pl.multiple_of(offs_ref[p], glen), glen)
         to = slice(p * glen, (p + 1) * glen)

time: 611 us -> 608 us (level)
  Pallas kernels: 242 us -> 220 us
  waiting for transfers between devices: 153 us -> 173 us
    pallas_call x2, Pallas kernels: 43.3 us -> 24.6 us  [attend_back(): pl.pallas_call(functools.partial(attend_back_kernel, length // offs.shape...]
    all_gather x3, waiting for transfers between devices: 27.6 us -> 40.6 us  [gather_cols(): return lax.all_gather(mine, 'ctx', axis=0, tiled=False)]
  transfers between devices with their start and end apart: 39 -> 39, of which waited for: 13 -> 15; matrix products, arithmetic and copies ran while one was open for 9% -> 9% of each run, Pallas kernels for 39% -> 35%
where the time goes in v5:
time: 608 us; the launch traced here: 599 us
  Pallas kernels  220 us (36%)
  waiting for transfers between devices  173 us (28%)
  starting transfers between devices  104 us (17%)
  other arithmetic  44.5 us (7%)
  local copies, waits for them, and re-layouts  43.7 us (7%)
  between operations  15 us (2%)
    ppermute x3, waiting for transfers between devices, sum_step(): lax.ppermute(total(b).astype(BF16), axis, [(j, j - 1) for j in range(max(...  52.2 us
    pallas_call x3, Pallas kernels, rows_product(): pl.pallas_call(functools.partial(rows_kernel, [len(a) for a, _ in product...  41.5 us
    pallas_call x4, Pallas kernels, pair_product(): pl.pallas_call(functools.partial(pair_kernel, a.shape[1]), out_shape=jax....  40.6 us
    all_gather x3, waiting for transfers between devices, gather_cols(): return lax.all_gather(mine, 'ctx', axis=0, tiled=False)  40.6 us
    ppermute x3, waiting for transfers between devices, sum_step(): lax.ppermute(total(a).astype(BF16), axis, [(j, j + 1) for j in range(min(...  37.4 us
    ppermute x6, waiting for transfers between devices, gather_step(): lax.ppermute(left, axis, [(j, j + 1) for j in range(step - 1, size - 1)])  30.3 us
    unnamed x108, local copies, waits for them, and re-layouts  28 us
    pallas_call x2, Pallas kernels, attend(): pl.pallas_call(functools.partial(attend_kernel, length // offs.shape[0],...  25.5 us
  transfers between devices with their start and end apart: 39, of which 15 were waited for; matrix products, arithmetic and copies ran while one was open for 9% of the time, Pallas kernels for 35%

profile of v5, /device:TPU:19, one launch (start us, length us, event | category | flops | bytes accessed | tf_op | source)
XLA Modules:
  0.0 598.9 jit_solution(9340739466319649661)
XLA Ops:
  10.5 2.9 convert_reduce_fusion.5
  17.3 3.0 copy-done
  20.4 5.6 all-to-all-start
  27.0 3.2 collective-permute-start
  32.3 3.2 collective-permute-start.7
  46.4 2.3 copy-done.5
  48.8 4.0 collective-permute-start.3
  56.5 3.0 collective-permute-start.10
  59.6 4.7 collective-permute-done.3.refs_2_
  64.2 2.4 collective-permute-start.5
  67.4 8.1 %collective-permute-done.9.refs_9_ = bf16[128,2048]{1,0:T(8,128)(2,1)S(1)} collective-permute-done((bf16[128,2048]{1,0:T(8,128)(2,1)S(1)}, bf16[128,2048]{1,0:T(8,128)(2,1)S(1)}, u32[]{:S(2)}, u32[]{:S(2)}) %collective-permute-start.9) | collective-permute-done | bytes 524320 | tf_op jit(solution)/shard_map/ppermute | solution.py:45
  75.5 2.4 collective-permute-start.11
  78.6 6.3 %collective-permute-done.5.refs_3_ = bf16[128,2048]{1,0:T(8,128)(2,1)S(1)} collective-permute-done((bf16[128,2048]{1,0:T(8,128)(2,1)S(1)}, bf16[128,2048]{1,0:T(8,128)(2,1)S(1)}, u32[]{:S(2)}, u32[]{:S(2)}) %collective-permute-start.5) | collective-permute-done | bytes 524320 | tf_op jit(solution)/shard_map/ppermute | solution.py:45
  84.9 11.2 %collective-permute-done.11.refs_10_ = bf16[128,2048]{1,0:T(8,128)(2,1)S(1)} collective-permute-done((bf16[128,2048]{1,0:T(8,128)(2,1)S(1)}, bf16[128,2048]{1,0:T(8,128)(2,1)S(1)}, u32[]{:S(2)}, u32[]{:S(2)}) %collective-permute-start.11) | collective-permute-done | bytes 524320 | tf_op jit(solution)/shard_map/ppermute | solution.py:45
  97.8 7.0 %in_order.1 = bf16[4,256,2048]{2,1,0:T(8,128)(2,1)} custom-call(s32[1]{0:T(128)} %bitcast.2.here_ref, bf16[128,2048]{1,0:T(8,128)(2,1)} %get-tuple-element.181.refs_0_, bf16[128,2048]{1,0:T(8,128)(2,1)} %copy-done.33, bf16[128,2048]{1,0:T(8,128)(2,1)} %copy-done.36, bf16[128,2048]{1,0:T(8,128)(2,1)} %copy-done.40, bf16[128,2048]{1,0:T(8,128)(2,1)} %copy-done.34, ...), custom_call_target="tpu_custom_call" | custom-call | flops 1 | bytes 1 | tf_op jit(solution)/shard_map/in_order/pallas_call | solution.py:385
  104.7 2.6 collective-permute-start.13
  107.4 5.1 all-to-all-start.1
  114.6 11.1 %up_product.2 = (bf16[1024,1024]{1,0:T(8,128)(2,1)}, bf16[1024,1024]{1,0:T(8,128)(2,1)}) custom-call(bf16[1024,2048]{1,0:T(8,128)(2,1)} %bitcast.3.h_ref.refs_0_, bf16[2048,1792]{1,0:T(8,128)(2,1)} %bitcast.4.w_ref.refs_0_.refs_1_.refs_2_, f32[1,1024]{1,0:T(1,128)} %bitcast.103), custom_call_target="tpu_custom_call" | custom-call | flops 1 | bytes 1 | tf_op jit(solution)/shard_map/up_product/pallas_call | solution.py:458
  125.7 11.4 %up_product.3 = (bf16[1024,1024]{1,0:T(8,128)(2,1)}, bf16[1024,1024]{1,0:T(8,128)(2,1)}) custom-call(bf16[1024,2048]{1,0:T(8,128)(2,1)} %collective-permute-done.13.h_ref.refs_1_, bf16[2048,1792]{1,0:T(8,128)(2,1)} %bitcast.4.w_ref.refs_0_.refs_1_.refs_2_, f32[1,1024]{1,0:T(1,128)} %bitcast.104), custom_call_target="tpu_custom_call" | custom-call | flops 1 | bytes 1 | tf_op jit(solution)/shard_map/up_product/pallas_call | solution.py:458
  137.1 7.3 %line_product.2.qkv_ref = f32[1024,768]{1,0:T(8,128)} custom-call(bf16[1024,2048]{1,0:T(8,128)(2,1)} %bitcast.3.h_ref.refs_0_, bf16[2048,1792]{1,0:T(8,128)(2,1)} %bitcast.4.w_ref.refs_0_.refs_1_.refs_2_, bf16[2048,1792]{1,0:T(8,128)(2,1)} %bitcast.4.w_ref.refs_0_.refs_1_.refs_2_, bf16[2048,1792]{1,0:T(8,128)(2,1)} %bitcast.4.w_ref.refs_0_.refs_1_.refs_2_, ...), custom_call_target="tpu_custom_call" | custom-call | flops 1 | bytes 1 | tf_op jit(solution)/shard_map/line_product/pallas_call | solution.py:524
  144.3 7.3 %line_product.3.qkv_ref = f32[1024,768]{1,0:T(8,128)} custom-call(bf16[1024,2048]{1,0:T(8,128)(2,1)} %collective-permute-done.13.h_ref.refs_1_, bf16[2048,1792]{1,0:T(8,128)(2,1)} %bitcast.4.w_ref.refs_0_.refs_1_.refs_2_, bf16[2048,1792]{1,0:T(8,128)(2,1)} %bitcast.4.w_ref.refs_0_.refs_1_.refs_2_, bf16[2048,1792]{1,0:T(8,128)(2,1)} %bitcast.4.w_ref.refs_0_.refs_1_.refs_2_, ...), custom_call_target="tpu_custom_call" | custom-call | flops 1 | bytes 1 | tf_op jit(solution)/shard_map/line_product/pallas_call | solution.py:524
  153.6 13.0 %attend.2 = (bf16[1024,256]{1,0:T(8,128)(2,1)S(1)}, bf16[1024,768]{1,0:T(8,128)(2,1)S(1)}, f32[2,2,2,1024]{3,2,1,0:T(2,128)S(1)}) custom-call(s32[8]{0:T(128)S(1)} %broadcast_multiply_fusion.3.offs_ref, s32[1]{0:T(128)} %get-tuple-element.351.prefix_ref, f32[1024,768]{1,0:T(8,128)S(1)} %copy-done.10, f32[1024,128]{1,0:T(8,128)S(1)} %get-tuple-element.218.cos_ref, ...), custom_call_target="tpu_custom_call" | custom-call | flops 1 | bytes 1 | tf_op jit(solution)/shard_map/attend/pallas_call | solution.py:210
  167.7 2.6 all-to-all-done.1
  171.8 8.8 %pair_product.4 = bf16[1024,2048]{1,0:T(8,128)(2,1)} custom-call(bf16[1024,1024]{1,0:T(8,128)(2,1)S(1)} %copy-done.11, bf16[1024,256]{1,0:T(8,128)(2,1)S(1)} %get-tuple-element.229.b_ref.refs_7_, bf16[2048,1280]{1,0:T(8,128)(2,1)} %bitcast.6.w_ref), custom_call_target="tpu_custom_call" | custom-call | flops 1 | bytes 1 | tf_op jit(solution)/shard_map/pair_product/pallas_call | solution.py:282
  182.2 12.6 %attend.3 = (bf16[1024,256]{1,0:T(8,128)(2,1)S(1)}, bf16[1024,768]{1,0:T(8,128)(2,1)S(1)}, f32[2,2,2,1024]{3,2,1,0:T(2,128)S(1)}) custom-call(s32[8]{0:T(128)S(1)} %broadcast_multiply_fusion.3.offs_ref, s32[1]{0:T(128)} %get-tuple-element.352.prefix_ref, f32[1024,768]{1,0:T(8,128)S(1)} %copy-done.9, f32[1024,128]{1,0:T(8,128)S(1)} %get-tuple-element.218.cos_ref, ...), custom_call_target="tpu_custom_call" | custom-call | flops 1 | bytes 1 | tf_op jit(solution)/shard_map/attend/pallas_call | solution.py:210
  198.0 9.4 %pair_product.5 = bf16[1024,2048]{1,0:T(8,128)(2,1)} custom-call(bf16[1024,1024]{1,0:T(8,128)(2,1)S(1)} %copy-done.12, bf16[1024,256]{1,0:T(8,128)(2,1)S(1)} %get-tuple-element.242.b_ref.refs_6_, bf16[2048,1280]{1,0:T(8,128)(2,1)} %bitcast.6.w_ref, bf16[1024,2048]{1,0:T(8,128)(2,1)} %collective-permute-done.14.refs_0_), custom_call_target="tpu_custom_call" | custom-call | flops 1 | bytes 1 | tf_op jit(solution)/shard_map/pair_product/pallas_call | solution.py:282
  209.5 13.4 %rows_product.3 = bf16[4,512,1024]{2,1,0:T(8,128)(2,1)} custom-call(bf16[1024,2048]{1,0:T(8,128)(2,1)} %all-gather.9.cloned.1.call-done, bf16[1024,2048]{1,0:T(8,128)(2,1)} %copy-done.21, bf16[1024,1024]{1,0:T(8,128)(2,1)} %get-tuple-element.246.a_ref.refs_2_, bf16[1024,1024]{1,0:T(8,128)(2,1)} %get-tuple-element.247.a_ref.refs_3_), custom_call_target="tpu_custom_call" | custom-call | flops 1 | bytes 1 | tf_op jit(solution)/shard_map/rows_product/pallas_call | solution.py:351
  222.9 5.1 all-to-all-start.2
  228.0 10.5 %down_product.2 = (bf16[1024,1024]{1,0:T(8,128)(2,1)}, bf16[1024,256]{1,0:T(8,128)(2,1)}) custom-call(bf16[1024,2048]{1,0:T(8,128)(2,1)} %all-gather.9.cloned.1.call-done, bf16[2048,1280]{1,0:T(8,128)(2,1)} %bitcast.6.w_ref, bf16[1024,1024]{1,0:T(8,128)(2,1)} %get-tuple-element.251.s_ref), custom_call_target="tpu_custom_call" | custom-call | flops 1 | bytes 1 | tf_op jit(solution)/shard_map/down_product/pallas_call | solution.py:485
  238.5 10.3 %down_product.3 = (bf16[1024,1024]{1,0:T(8,128)(2,1)}, bf16[1024,256]{1,0:T(8,128)(2,1)}) custom-call(bf16[1024,2048]{1,0:T(8,128)(2,1)} %copy-done.21, bf16[2048,1280]{1,0:T(8,128)(2,1)} %bitcast.6.w_ref, bf16[1024,1024]{1,0:T(8,128)(2,1)} %get-tuple-element.260.s_ref), custom_call_target="tpu_custom_call" | custom-call | flops 1 | bytes 1 | tf_op jit(solution)/shard_map/down_product/pallas_call | solution.py:485
  248.9 13.6 %rows_product.4 = bf16[4,512,1024]{2,1,0:T(8,128)(2,1)} custom-call(bf16[1024,2048]{1,0:T(8,128)(2,1)} %bitcast.3.h_ref.refs_0_, bf16[1024,2048]{1,0:T(8,128)(2,1)} %collective-permute-done.13.h_ref.refs_1_, bf16[1024,1024]{1,0:T(8,128)(2,1)} %get-tuple-element.294.refs_2_.a_ref, bf16[1024,1024]{1,0:T(8,128)(2,1)} %get-tuple-element.283.refs_3_.a_ref), custom_call_target="tpu_custom_call" | custom-call | flops 1 | bytes 1 | tf_op jit(solution)/shard_map/rows_product/pallas_call | solution.py:351
  262.5 12.3 %attend_back.2.b_ref.refs_3_ = bf16[1024,768]{1,0:T(8,128)(2,1)S(1)} custom-call(s32[8]{0:T(128)S(1)} %broadcast_multiply_fusion.3.offs_ref, s32[1]{0:T(128)} %get-tuple-element.351.prefix_ref, bf16[1024,768]{1,0:T(8,128)(2,1)S(1)} %copy-done.18, f32[2,2,2,1024]{3,2,1,0:T(2,128)S(1)} %get-tuple-element.277.stat_ref, bf16[1024,256]{1,0:T(8,128)(2,1)S(1)} %copy-done.20, ...), custom_call_target="tpu_custom_call" | custom-call | flops 1 | bytes 1 | tf_op jit(solution)/shard_map/attend_back/pallas_call | solution.py:239
  275.3 4.2 fusion.21
  281.1 11.1 %pair_product.6 = bf16[1024,2048]{1,0:T(8,128)(2,1)} custom-call(bf16[1024,1024]{1,0:T(8,128)(2,1)S(1)} %copy-done.8, bf16[1024,768]{1,0:T(8,128)(2,1)S(1)} %attend_back.2.b_ref.refs_3_, bf16[2048,1792]{1,0:T(8,128)(2,1)} %bitcast.4.w_ref.refs_0_.refs_1_.refs_2_), custom_call_target="tpu_custom_call" | custom-call | flops 1 | bytes 1 | tf_op jit(solution)/shard_map/pair_product/pallas_call | solution.py:282
  293.0 5.2 all-to-all-start.3
  300.8 12.3 %attend_back.3.b_ref.refs_2_ = bf16[1024,768]{1,0:T(8,128)(2,1)S(1)} custom-call(s32[8]{0:T(128)S(1)} %broadcast_multiply_fusion.3.offs_ref, s32[1]{0:T(128)} %get-tuple-element.352.prefix_ref, bf16[1024,768]{1,0:T(8,128)(2,1)S(1)} %copy-done.16, f32[2,2,2,1024]{3,2,1,0:T(2,128)S(1)} %get-tuple-element.289.stat_ref, bf16[1024,256]{1,0:T(8,128)(2,1)S(1)} %copy-done.19, ...), custom_call_target="tpu_custom_call" | custom-call | flops 1 | bytes 1 | tf_op jit(solution)/shard_map/attend_back/pallas_call | solution.py:239
  315.3 11.3 %pair_product.7 = bf16[1024,2048]{1,0:T(8,128)(2,1)} custom-call(bf16[1024,1024]{1,0:T(8,128)(2,1)S(1)} %copy-done.6, bf16[1024,768]{1,0:T(8,128)(2,1)S(1)} %attend_back.3.b_ref.refs_2_, bf16[2048,1792]{1,0:T(8,128)(2,1)} %bitcast.4.w_ref.refs_0_.refs_1_.refs_2_, bf16[1024,2048]{1,0:T(8,128)(2,1)} %collective-permute-done.16.refs_0_), custom_call_target="tpu_custom_call" | custom-call | flops 1 | bytes 1 | tf_op jit(solution)/shard_map/pair_product/pallas_call | solution.py:282
  326.6 14.5 %rows_product.5 = bf16[4,512,1024]{2,1,0:T(8,128)(2,1)} custom-call(bf16[1024,2048]{1,0:T(8,128)(2,1)} %bitcast.3.h_ref.refs_0_, bf16[1024,2048]{1,0:T(8,128)(2,1)} %collective-permute-done.13.h_ref.refs_1_, bf16[1024,768]{1,0:T(8,128)(2,1)} %copy-done.3, bf16[1024,768]{1,0:T(8,128)(2,1)} %copy-done.1, bf16[1024,2048]{1,0:T(8,128)(2,1)} %all-gather.9.cloned.1.call-done, ...), custom_call_target="tpu_custom_call" | custom-call | flops 1 | bytes 1 | tf_op jit(solution)/shard_map/rows_product/pallas_call | solution.py:351
  341.0 4.4 all-to-all-done.3
  345.4 4.1 fusion.23
  349.5 19.4 %all-gather.11.cloned.1.call-done = bf16[2048,1024]{1,0:T(8,128)(2,1)} async-done(((bf16[512,1024]{1,0:T(8,128)(2,1)}), bf16[2048,1024]{1,0:T(8,128)(2,1)}) %all-gather.11.cloned.1.call-update) | async-done | bytes 4194320 | tf_op jit(solution)/shard_map/all_gather | solution.py:643
  368.9 5.1 all-to-all-start.4
  377.7 6.4 %widen.2 = f32[512,4096]{1,0:T(8,128)} custom-call(bf16[4,512,1024]{2,1,0:T(8,128)(2,1)} %bitcast.97), custom_call_target="tpu_custom_call" | custom-call | flops 1 | bytes 1 | tf_op jit(solution)/shard_map/widen/pallas_call | solution.py:434
  384.2 40.0 %collective-permute-done.19 = bf16[256,2048]{1,0:T(8,128)(2,1)} collective-permute-done((bf16[256,2048]{1,0:T(8,128)(2,1)S(1)}, bf16[256,2048]{1,0:T(8,128)(2,1)}, u32[]{:S(2)}, u32[]{:S(2)}) %collective-permute-start.19) | collective-permute-done | bytes 1048608 | tf_op jit(solution)/shard_map/ppermute | solution.py:58
  424.2 3.5 fusion.1
  429.1 4.0 collective-permute-start.21
  436.0 4.2 fusion.24
  440.1 37.4 %collective-permute-done.20 = bf16[256,2048]{1,0:T(8,128)(2,1)} collective-permute-done((bf16[256,2048]{1,0:T(8,128)(2,1)}, bf16[256,2048]{1,0:T(8,128)(2,1)}, u32[]{:S(2)}, u32[]{:S(2)}) %collective-permute-start.20) | collective-permute-done | bytes 1048608 | tf_op jit(solution)/shard_map/ppermute | solution.py:55
  479.3 2.6 add_convert_fusion
  481.8 2.9 collective-permute-start.23
  484.7 2.6 add_convert_fusion.1
  487.3 3.5 collective-permute-start.22
  491.5 3.6 all-to-all-start.5
  495.1 2.7 fusion.20
  497.8 4.5 collective-permute-start.17
  505.2 11.7 %collective-permute-done.23 = bf16[256,2048]{1,0:T(8,128)(2,1)} collective-permute-done((bf16[256,2048]{1,0:T(8,128)(2,1)}, bf16[256,2048]{1,0:T(8,128)(2,1)}, u32[]{:S(2)}, u32[]{:S(2)}) %collective-permute-start.23) | collective-permute-done | bytes 1048608 | tf_op jit(solution)/shard_map/ppermute | solution.py:58
  516.9 3.4 fusion.18
  520.3 6.1 %widen.3 = f32[512,4096]{1,0:T(8,128)} custom-call(bf16[4,512,1024]{2,1,0:T(8,128)(2,1)} %bitcast.96), custom_call_target="tpu_custom_call" | custom-call | flops 1 | bytes 1 | tf_op jit(solution)/shard_map/widen/pallas_call | solution.py:434
  528.2 3.6 all-to-all-start.6
  536.6 13.1 %collective-permute-start.24 = (bf16[1,1,256,2048]{3,2,1,0:T(8,128)(2,1)}, bf16[1,1,256,2048]{3,2,1,0:T(8,128)(2,1)S(1)}, u32[]{:S(2)}, u32[]{:S(2)}) collective-permute-start(bf16[1,1,256,2048]{3,2,1,0:T(8,128)(2,1)} %bitcast.24), channel_id=1, source_target_pairs={{0,1},{1,0},{2,3},{3,2},{4,5},{5,4},{6,7},{7,6},{8,9},{9,8},{10,11... | collective-permute-start | bytes 3145736 | tf_op jit(solution)/shard_map/ppermute | solution.py:35
  552.8 3.6 all-to-all-start.7
  556.4 3.0 all-to-all-done.7
  564.8 21.2 %all-gather.15.cloned.1.call-done = bf16[2048,1024]{1,0:T(8,128)(2,1)} async-done(((bf16[512,1024]{1,0:T(8,128)(2,1)}), bf16[2048,1024]{1,0:T(8,128)(2,1)}) %all-gather.15.cloned.1.call-update) | async-done | bytes 4194320 | tf_op jit(solution)/shard_map/all_gather | solution.py:643
  586.0 5.9 place.1
  (223 shorter events, 77.0 us)
Async XLA Ops:
  13.5 1.5 collective-permute-start.2
  20.4 87.0 %all-to-all-start = ((bf16[4,512,1792]{2,1,0:T(8,128)(2,1)}), bf16[4,512,1792]{2,1,0:T(8,128)(2,1)}, u32[]{:S(2)}, u32[]{:S(2)}) async-start(bf16[4,512,1792]{2,1,0:T(8,128)(2,1)} %copy-done), calls=%async_computation | async-start | bytes 14680064 | tf_op jit(solution)/shard_map/all_to_all | solution.py:622
  26.0 15.2 %copy-start.48 = (s32[8]{0:T(128)S(1)}, s32[8]{0:T(128)}, u32[]{:S(2)}) copy-start(s32[8]{0:T(128)} %param.21) | copy-start | bytes 100
  26.0 15.3 %copy-start.49 = (s32[2]{0:T(128)S(1)}, s32[2]{0:T(128)}, u32[]{:S(2)}) copy-start(s32[2]{0:T(128)} %param.20) | copy-start | bytes 28
  27.0 21.8 %collective-permute-start = (bf16[128,2048]{1,0:T(8,128)(2,1)}, bf16[128,2048]{1,0:T(8,128)(2,1)S(1)}, u32[]{:S(2)}, u32[]{:S(2)}) collective-permute-start(bf16[128,2048]{1,0:T(8,128)(2,1)} %get-tuple-element.181.refs_0_), channel_id=1, source_target_pairs={{0,2},{2,4},{4,6},{1,3},{3,5},{5,7},{8,10},{10,12},{12,14},{9,11},... | collective-permute-start | bytes 1572872 | tf_op jit(solution)/shard_map/ppermute | solution.py:45
  30.2 18.6 %collective-permute-start.1 = (bf16[128,2048]{1,0:T(8,128)(2,1)}, bf16[128,2048]{1,0:T(8,128)(2,1)S(1)}, u32[]{:S(2)}, u32[]{:S(2)}) collective-permute-start(bf16[128,2048]{1,0:T(8,128)(2,1)} %get-tuple-element.181.refs_0_), channel_id=1, source_target_pairs={{2,0},{4,2},{6,4},{3,1},{5,3},{7,5},{10,8},{12,10},{14,12},{11,9},... | collective-permute-start | bytes 1572872 | tf_op jit(solution)/shard_map/ppermute | solution.py:46
  32.3 21.9 %collective-permute-start.7 = (bf16[128,2048]{1,0:T(8,128)(2,1)}, bf16[128,2048]{1,0:T(8,128)(2,1)S(1)}, u32[]{:S(2)}, u32[]{:S(2)}) collective-permute-start(bf16[128,2048]{1,0:T(8,128)(2,1)} %get-tuple-element.188.refs_7_), channel_id=1, source_target_pairs={{0,2},{2,4},{4,6},{1,3},{3,5},{5,7},{8,10},{10,12},{12,14},{9,11},... | collective-permute-start | bytes 1572872 | tf_op jit(solution)/shard_map/ppermute | solution.py:45
  35.5 21.0 %collective-permute-start.8 = (bf16[128,2048]{1,0:T(8,128)(2,1)}, bf16[128,2048]{1,0:T(8,128)(2,1)}, u32[]{:S(2)}, u32[]{:S(2)}) collective-permute-start(bf16[128,2048]{1,0:T(8,128)(2,1)} %get-tuple-element.188.refs_7_), channel_id=1, source_target_pairs={{2,0},{4,2},{6,4},{3,1},{5,3},{7,5},{10,8},{12,10},{14,12},{11,9},... | collective-permute-start | bytes 1572872 | tf_op jit(solution)/shard_map/ppermute | solution.py:46
  48.8 48.9 %copy-start.33 = (bf16[128,2048]{1,0:T(8,128)(2,1)}, bf16[128,2048]{1,0:T(8,128)(2,1)S(1)}, u32[]{:S(2)}) copy-start(bf16[128,2048]{1,0:T(8,128)(2,1)S(1)} %collective-permute-done.refs_1_) | copy-start | bytes 1572868
  48.8 48.9 %copy-start.34 = (bf16[128,2048]{1,0:T(8,128)(2,1)}, bf16[128,2048]{1,0:T(8,128)(2,1)S(1)}, u32[]{:S(2)}) copy-start(bf16[128,2048]{1,0:T(8,128)(2,1)S(1)} %collective-permute-done.1.refs_4_) | copy-start | bytes 1572868
  48.8 15.4 %collective-permute-start.3 = (bf16[128,2048]{1,0:T(8,128)(2,1)S(1)}, bf16[128,2048]{1,0:T(8,128)(2,1)S(1)}, u32[]{:S(2)}, u32[]{:S(2)}) collective-permute-start(bf16[128,2048]{1,0:T(8,128)(2,1)S(1)} %collective-permute-done.refs_1_), channel_id=1, source_target_pairs={{2,4},{4,6},{3,5},{5,7},{10,12},{12,14},{11,13},{13,15},{18,20},{2... | collective-permute-start | bytes 1572872 | tf_op jit(solution)/shard_map/ppermute | solution.py:45
  52.8 13.8 %collective-permute-start.4 = (bf16[128,2048]{1,0:T(8,128)(2,1)S(1)}, bf16[128,2048]{1,0:T(8,128)(2,1)S(1)}, u32[]{:S(2)}, u32[]{:S(2)}) collective-permute-start(bf16[128,2048]{1,0:T(8,128)(2,1)S(1)} %collective-permute-done.1.refs_4_), channel_id=1, source_target_pairs={{2,0},{4,2},{3,1},{5,3},{10,8},{12,10},{11,9},{13,11},{18,16},{20,... | collective-permute-start | bytes 1572872 | tf_op jit(solution)/shard_map/ppermute | solution.py:46
  54.2 43.6 %copy-start.35 = (bf16[128,2048]{1,0:T(8,128)(2,1)}, bf16[128,2048]{1,0:T(8,128)(2,1)S(1)}, u32[]{:S(2)}) copy-start(bf16[128,2048]{1,0:T(8,128)(2,1)S(1)} %collective-permute-done.7.refs_8_) | copy-start | bytes 1572868
  54.2 21.3 %collective-permute-start.9 = (bf16[128,2048]{1,0:T(8,128)(2,1)S(1)}, bf16[128,2048]{1,0:T(8,128)(2,1)S(1)}, u32[]{:S(2)}, u32[]{:S(2)}) collective-permute-start(bf16[128,2048]{1,0:T(8,128)(2,1)S(1)} %collective-permute-done.7.refs_8_), channel_id=1, source_target_pairs={{2,4},{4,6},{3,5},{5,7},{10,12},{12,14},{11,13},{13,15},{18,20},{2... | collective-permute-start | bytes 1572872 | tf_op jit(solution)/shard_map/ppermute | solution.py:45
  56.5 21.4 %collective-permute-start.10 = (bf16[128,2048]{1,0:T(8,128)(2,1)}, bf16[128,2048]{1,0:T(8,128)(2,1)S(1)}, u32[]{:S(2)}, u32[]{:S(2)}) collective-permute-start(bf16[128,2048]{1,0:T(8,128)(2,1)} %collective-permute-done.8.refs_11_), channel_id=1, source_target_pairs={{2,0},{4,2},{3,1},{5,3},{10,8},{12,10},{11,9},{13,11},{18,16},{20,... | collective-permute-start | bytes 1572872 | tf_op jit(solution)/shard_map/ppermute | solution.py:46
  64.2 11.2 %copy-start.36 = (bf16[128,2048]{1,0:T(8,128)(2,1)}, bf16[128,2048]{1,0:T(8,128)(2,1)S(1)}, u32[]{:S(2)}) copy-start(bf16[128,2048]{1,0:T(8,128)(2,1)S(1)} %collective-permute-done.3.refs_2_) | copy-start | bytes 1572868
  64.2 20.6 %collective-permute-start.5 = (bf16[128,2048]{1,0:T(8,128)(2,1)S(1)}, bf16[128,2048]{1,0:T(8,128)(2,1)S(1)}, u32[]{:S(2)}, u32[]{:S(2)}) collective-permute-start(bf16[128,2048]{1,0:T(8,128)(2,1)S(1)} %collective-permute-done.3.refs_2_), channel_id=1, source_target_pairs={{4,6},{5,7},{12,14},{13,15},{20,22},{21,23},{28,30},{29,31}} | collective-permute-start | bytes 1572872 | tf_op jit(solution)/shard_map/ppermute | solution.py:45
  66.7 18.2 %copy-start.37 = (bf16[128,2048]{1,0:T(8,128)(2,1)}, bf16[128,2048]{1,0:T(8,128)(2,1)S(1)}, u32[]{:S(2)}) copy-start(bf16[128,2048]{1,0:T(8,128)(2,1)S(1)} %collective-permute-done.4.refs_5_) | copy-start | bytes 1572868
  66.7 18.2 %collective-permute-start.6 = (bf16[128,2048]{1,0:T(8,128)(2,1)S(1)}, bf16[128,2048]{1,0:T(8,128)(2,1)S(1)}, u32[]{:S(2)}, u32[]{:S(2)}) collective-permute-start(bf16[128,2048]{1,0:T(8,128)(2,1)S(1)} %collective-permute-done.4.refs_5_), channel_id=1, source_target_pairs={{2,0},{3,1},{10,8},{11,9},{18,16},{19,17},{26,24},{27,25}} | collective-permute-start | bytes 1572872 | tf_op jit(solution)/shard_map/ppermute | solution.py:46
  75.5 9.4 %copy-start.38 = (bf16[128,2048]{1,0:T(8,128)(2,1)}, bf16[128,2048]{1,0:T(8,128)(2,1)S(1)}, u32[]{:S(2)}) copy-start(bf16[128,2048]{1,0:T(8,128)(2,1)S(1)} %collective-permute-done.9.refs_9_) | copy-start | bytes 1572868
  75.5 20.6 %collective-permute-start.11 = (bf16[128,2048]{1,0:T(8,128)(2,1)S(1)}, bf16[128,2048]{1,0:T(8,128)(2,1)S(1)}, u32[]{:S(2)}, u32[]{:S(2)}) collective-permute-start(bf16[128,2048]{1,0:T(8,128)(2,1)S(1)} %collective-permute-done.9.refs_9_), channel_id=1, source_target_pairs={{4,6},{5,7},{12,14},{13,15},{20,22},{21,23},{28,30},{29,31}} | collective-permute-start | bytes 1572872 | tf_op jit(solution)/shard_map/ppermute | solution.py:45
  77.9 18.2 %copy-start.39 = (bf16[128,2048]{1,0:T(8,128)(2,1)}, bf16[128,2048]{1,0:T(8,128)(2,1)S(1)}, u32[]{:S(2)}) copy-start(bf16[128,2048]{1,0:T(8,128)(2,1)S(1)} %collective-permute-done.10.refs_12_) | copy-start | bytes 1572868
  77.9 18.2 %collective-permute-start.12 = (bf16[128,2048]{1,0:T(8,128)(2,1)S(1)}, bf16[128,2048]{1,0:T(8,128)(2,1)S(1)}, u32[]{:S(2)}, u32[]{:S(2)}) collective-permute-start(bf16[128,2048]{1,0:T(8,128)(2,1)S(1)} %collective-permute-done.10.refs_12_), channel_id=1, source_target_pairs={{2,0},{3,1},{10,8},{11,9},{18,16},{19,17},{26,24},{27,25}} | collective-permute-start | bytes 1572872 | tf_op jit(solution)/shard_map/ppermute | solution.py:46
  84.9 11.2 %copy-start.40 = (bf16[128,2048]{1,0:T(8,128)(2,1)}, bf16[128,2048]{1,0:T(8,128)(2,1)S(1)}, u32[]{:S(2)}) copy-start(bf16[128,2048]{1,0:T(8,128)(2,1)S(1)} %collective-permute-done.5.refs_3_) | copy-start | bytes 1572868
  84.9 11.2 %copy-start.41 = (bf16[128,2048]{1,0:T(8,128)(2,1)}, bf16[128,2048]{1,0:T(8,128)(2,1)S(1)}, u32[]{:S(2)}) copy-start(bf16[128,2048]{1,0:T(8,128)(2,1)S(1)} %collective-permute-done.6.refs_6_) | copy-start | bytes 1572868
  104.7 9.9 %collective-permute-start.13 = (bf16[1024,2048]{1,0:T(8,128)(2,1)}, bf16[1024,2048]{1,0:T(8,128)(2,1)}, u32[]{:S(2)}, u32[]{:S(2)}) collective-permute-start(bf16[1024,2048]{1,0:T(8,128)(2,1)} %bitcast.3.h_ref.refs_0_), channel_id=1, source_target_pairs={{0,1},{1,0},{2,3},{3,2},{4,5},{5,4},{6,7},{7,6},{8,9},{9,8},{10,11... | collective-permute-start | bytes 12582920 | tf_op jit(solution)/shard_map/ppermute | solution.py:35
  107.4 62.9 %all-to-all-start.1 = ((bf16[4,512,1280]{2,1,0:T(8,128)(2,1)}), bf16[4,512,1280]{2,1,0:T(8,128)(2,1)}, u32[]{:S(2)}, u32[]{:S(2)}) async-start(bf16[4,512,1280]{2,1,0:T(8,128)(2,1)} %copy-done.5), calls=%async_computation.1 | async-start | bytes 10485760 | tf_op jit(solution)/shard_map/all_to_all | solution.py:649
  112.5 83.5 %all-gather.9.cloned.1.call-start = ((), (), s32[]{:S(2)}) async-start(), calls=%async_computation.10 | async-start | bytes 5242880 | tf_op jit(solution)/shard_map/all_gather | solution.py:630
  113.2 199.9 %reduce-scatter.2.cloned.1.call-start = ((), (), s32[]{:S(2)}) async-start(), calls=%async_computation.9 | async-start | bytes 5242880 | tf_op jit(solution)/shard_map/reduce_scatter | solution.py:705
  167.7 13.0 %copy-start.13 = (bf16[1024,256]{1,0:T(8,128)(2,1)}, bf16[1024,256]{1,0:T(8,128)(2,1)S(1)}, u32[]{:S(2)}) copy-start(bf16[1024,256]{1,0:T(8,128)(2,1)S(1)} %get-tuple-element.229.b_ref.refs_7_) | copy-start | bytes 1572868
  171.8 10.4 %copy-start.9 = (f32[1024,768]{1,0:T(8,128)S(1)}, f32[1024,768]{1,0:T(8,128)}, u32[]{:S(2)}) copy-start(f32[1024,768]{1,0:T(8,128)} %line_product.2.qkv_ref) | copy-start | bytes 9437188
  180.7 15.3 %collective-permute-start.14 = (bf16[1024,2048]{1,0:T(8,128)(2,1)}, bf16[1024,2048]{1,0:T(8,128)(2,1)}, u32[]{:S(2)}, u32[]{:S(2)}) collective-permute-start(bf16[1024,2048]{1,0:T(8,128)(2,1)} %pair_product.4), channel_id=1, source_target_pairs={{0,1},{1,0},{2,3},{3,2},{4,5},{5,4},{6,7},{7,6},{8,9},{9,8},{10,11... | collective-permute-start | bytes 12582920 | tf_op jit(solution)/shard_map/ppermute | solution.py:35
  195.9 11.5 %copy-start.14 = (bf16[1024,256]{1,0:T(8,128)(2,1)}, bf16[1024,256]{1,0:T(8,128)(2,1)S(1)}, u32[]{:S(2)}) copy-start(bf16[1024,256]{1,0:T(8,128)(2,1)S(1)} %get-tuple-element.242.b_ref.refs_6_) | copy-start | bytes 1572868
  195.9 11.5 %collective-permute-start.15 = (bf16[1024,2048]{1,0:T(8,128)(2,1)}, bf16[1024,2048]{1,0:T(8,128)(2,1)S(1)}, u32[]{:S(2)}, u32[]{:S(2)}) collective-permute-start(bf16[1024,2048]{1,0:T(8,128)(2,1)} %all-gather.9.cloned.1.call-done), channel_id=1, source_target_pairs={{0,1},{1,0},{2,3},{3,2},{4,5},{5,4},{6,7},{7,6},{8,9},{9,8},{10,11... | collective-permute-start | bytes 12582920 | tf_op jit(solution)/shard_map/ppermute | solution.py:35
  222.9 52.4 %all-to-all-start.2 = ((bf16[4,512,1024]{2,1,0:T(8,128)(2,1)}), bf16[4,512,1024]{2,1,0:T(8,128)(2,1)}, u32[]{:S(2)}, u32[]{:S(2)}) async-start(bf16[4,512,1024]{2,1,0:T(8,128)(2,1)} %rows_product.3), calls=%async_computation.2 | async-start | bytes 8388608 | tf_op jit(solution)/shard_map/all_to_all | solution.py:637
  228.0 140.9 %all-gather.11.cloned.1.call-start = ((), (), s32[]{:S(2)}) async-start(), calls=%async_computation.11 | async-start | bytes 5242880 | tf_op jit(solution)/shard_map/all_gather | solution.py:643
  248.8 13.6 %copy-start.18 = (bf16[1024,768]{1,0:T(8,128)(2,1)S(1)}, bf16[1024,768]{1,0:T(8,128)(2,1)}, u32[]{:S(2)}) copy-start(bf16[1024,768]{1,0:T(8,128)(2,1)} %copy-done.17) | copy-start | bytes 4718596
  248.8 13.6 %copy-start.20 = (bf16[1024,256]{1,0:T(8,128)(2,1)S(1)}, bf16[1024,256]{1,0:T(8,128)(2,1)}, u32[]{:S(2)}) copy-start(bf16[1024,256]{1,0:T(8,128)(2,1)} %get-tuple-element.278.do_ref) | copy-start | bytes 1572868
  292.2 20.9 %collective-permute-start.16 = (bf16[1024,2048]{1,0:T(8,128)(2,1)}, bf16[1024,2048]{1,0:T(8,128)(2,1)}, u32[]{:S(2)}, u32[]{:S(2)}) collective-permute-start(bf16[1024,2048]{1,0:T(8,128)(2,1)} %pair_product.6), channel_id=1, source_target_pairs={{0,1},{1,0},{2,3},{3,2},{4,5},{5,4},{6,7},{7,6},{8,9},{9,8},{10,11... | collective-permute-start | bytes 12582920 | tf_op jit(solution)/shard_map/ppermute | solution.py:35
  293.0 52.5 %all-to-all-start.3 = ((bf16[4,512,1024]{2,1,0:T(8,128)(2,1)}), bf16[4,512,1024]{2,1,0:T(8,128)(2,1)}, u32[]{:S(2)}, u32[]{:S(2)}) async-start(bf16[4,512,1024]{2,1,0:T(8,128)(2,1)} %rows_product.4), calls=%async_computation.4 | async-start | bytes 8388608 | tf_op jit(solution)/shard_map/all_to_all | solution.py:637
  298.2 222.2 %all-gather.13.cloned.1.call-start = ((), (), s32[]{:S(2)}) async-start(), calls=%async_computation.12 | async-start | bytes 5242880 | tf_op jit(solution)/shard_map/all_gather | solution.py:643
  313.1 13.5 %copy-start.3 = (bf16[1024,768]{1,0:T(8,128)(2,1)}, bf16[1024,768]{1,0:T(8,128)(2,1)S(1)}, u32[]{:S(2)}) copy-start(bf16[1024,768]{1,0:T(8,128)(2,1)S(1)} %attend_back.3.b_ref.refs_2_) | copy-start | bytes 4718596
  368.9 55.3 %all-to-all-start.4 = ((bf16[4,512,1024]{2,1,0:T(8,128)(2,1)}), bf16[4,512,1024]{2,1,0:T(8,128)(2,1)}, u32[]{:S(2)}, u32[]{:S(2)}) async-start(bf16[4,512,1024]{2,1,0:T(8,128)(2,1)} %rows_product.5), calls=%async_computation.5 | async-start | bytes 8388608 | tf_op jit(solution)/shard_map/all_to_all | solution.py:637
  374.0 212.0 %all-gather.15.cloned.1.call-start = ((), (), s32[]{:S(2)}) async-start(), calls=%async_computation.13 | async-start | bytes 5242880 | tf_op jit(solution)/shard_map/all_gather | solution.py:643
  375.7 8.5 %copy-start.27 = (bf16[256,2048]{1,0:T(8,128)(2,1)}, bf16[256,2048]{1,0:T(8,128)(2,1)S(1)}, u32[]{:S(2)}) copy-start(bf16[256,2048]{1,0:T(8,128)(2,1)S(1)} %get-tuple-element.340) | copy-start | bytes 3145732
  375.7 8.5 %collective-permute-start.18 = (bf16[256,2048]{1,0:T(8,128)(2,1)S(1)}, bf16[256,2048]{1,0:T(8,128)(2,1)S(1)}, u32[]{:S(2)}, u32[]{:S(2)}) collective-permute-start(bf16[256,2048]{1,0:T(8,128)(2,1)S(1)} %get-tuple-element.340), channel_id=1, source_target_pairs={{0,2},{1,3},{8,10},{9,11},{16,18},{17,19},{24,26},{25,27}} | collective-permute-start | bytes 3145736 | tf_op jit(solution)/shard_map/ppermute | solution.py:55
  376.4 47.8 %collective-permute-start.19 = (bf16[256,2048]{1,0:T(8,128)(2,1)S(1)}, bf16[256,2048]{1,0:T(8,128)(2,1)}, u32[]{:S(2)}, u32[]{:S(2)}) collective-permute-start(bf16[256,2048]{1,0:T(8,128)(2,1)S(1)} %get-tuple-element.339), channel_id=1, source_target_pairs={{6,4},{7,5},{14,12},{15,13},{22,20},{23,21},{30,28},{31,29}} | collective-permute-start | bytes 3145736 | tf_op jit(solution)/shard_map/ppermute | solution.py:58
  384.1 49.0 %copy-start.46 = (bf16[2048]{0:T(1024)(128)(2,1)S(1)}, bf16[2048]{0:T(1024)(128)(2,1)}, u32[]{:S(2)}) copy-start(bf16[2048]{0:T(1024)(128)(2,1)} %param.31) | copy-start | bytes 12292
  384.1 49.0 %copy-start.47 = (bf16[2048]{0:T(1024)(128)(2,1)S(1)}, bf16[2048]{0:T(1024)(128)(2,1)}, u32[]{:S(2)}) copy-start(bf16[2048]{0:T(1024)(128)(2,1)} %param.35) | copy-start | bytes 12292
  427.7 49.9 %collective-permute-start.20 = (bf16[256,2048]{1,0:T(8,128)(2,1)}, bf16[256,2048]{1,0:T(8,128)(2,1)}, u32[]{:S(2)}, u32[]{:S(2)}) collective-permute-start(bf16[256,2048]{1,0:T(8,128)(2,1)} %get-tuple-element.338), channel_id=1, source_target_pairs={{0,2},{2,4},{1,3},{3,5},{8,10},{10,12},{9,11},{11,13},{16,18},{18,... | collective-permute-start | bytes 3145736 | tf_op jit(solution)/shard_map/ppermute | solution.py:55
  429.1 48.9 %collective-permute-start.21 = (bf16[256,2048]{1,0:T(8,128)(2,1)}, bf16[256,2048]{1,0:T(8,128)(2,1)}, u32[]{:S(2)}, u32[]{:S(2)}) collective-permute-start(bf16[256,2048]{1,0:T(8,128)(2,1)} %get-tuple-element.337), channel_id=1, source_target_pairs={{4,2},{6,4},{5,3},{7,5},{12,10},{14,12},{13,11},{15,13},{20,18},{2... | collective-permute-start | bytes 3145736 | tf_op jit(solution)/shard_map/ppermute | solution.py:58
  436.0 42.0 %copy-start.4 = (bf16[1024,768]{1,0:T(8,128)(2,1)S(1)}, bf16[1024,768]{1,0:T(8,128)(2,1)}, u32[]{:S(2)}) copy-start(bf16[1024,768]{1,0:T(8,128)(2,1)} %copy-done.3) | copy-start | bytes 4718596
  481.8 13.3 %copy-start.23 = (bf16[2,256,2048]{2,1,0:T(8,128)(2,1)S(1)}, bf16[2,256,2048]{2,1,0:T(8,128)(2,1)}, u32[]{:S(2)}) copy-start(bf16[2,256,2048]{2,1,0:T(8,128)(2,1)} %param.18) | copy-start | bytes 6291460
  481.8 35.1 %collective-permute-start.23 = (bf16[256,2048]{1,0:T(8,128)(2,1)}, bf16[256,2048]{1,0:T(8,128)(2,1)}, u32[]{:S(2)}, u32[]{:S(2)}) collective-permute-start(bf16[256,2048]{1,0:T(8,128)(2,1)} %add_convert_fusion), channel_id=1, source_target_pairs={{2,0},{4,2},{6,4},{3,1},{5,3},{7,5},{10,8},{12,10},{14,12},{11,9},... | collective-permute-start | bytes 3145736 | tf_op jit(solution)/shard_map/ppermute | solution.py:58
  487.3 29.6 %collective-permute-start.22 = (bf16[256,2048]{1,0:T(8,128)(2,1)}, bf16[256,2048]{1,0:T(8,128)(2,1)S(1)}, u32[]{:S(2)}, u32[]{:S(2)}) collective-permute-start(bf16[256,2048]{1,0:T(8,128)(2,1)} %add_convert_fusion.1), channel_id=1, source_target_pairs={{0,2},{2,4},{4,6},{1,3},{3,5},{5,7},{8,10},{10,12},{12,14},{9,11},... | collective-permute-start | bytes 3145736 | tf_op jit(solution)/shard_map/ppermute | solution.py:55
  491.5 13.7 %all-to-all-start.5 = ((f32[4,1,1792]{2,1,0:T(1,128)}), f32[4,1,1792]{2,1,0:T(1,128)S(1)}, u32[]{:S(2)}, u32[]{:S(2)}) async-start(f32[4,1,1792]{2,1,0:T(1,128)} %broadcast_in_dim.91), calls=%async_computation.6 | async-start | bytes 57344 | tf_op jit(solution)/shard_map/all_to_all | solution.py:39
  495.1 8.7 %copy-start.29 = (bf16[1,256,2048]{2,1,0:T(8,128)(2,1)S(1)}, bf16[1,256,2048]{2,1,0:T(8,128)(2,1)}, u32[]{:S(2)}) copy-start(bf16[1,256,2048]{2,1,0:T(8,128)(2,1)} %reduce-scatter.2.cloned.1.call-done) | copy-start | bytes 3145732
  497.8 51.9 %collective-permute-start.17 = (bf16[1,1,256,2048]{3,2,1,0:T(8,128)(2,1)}, bf16[1,1,256,2048]{3,2,1,0:T(8,128)(2,1)}, u32[]{:S(2)}, u32[]{:S(2)}) collective-permute-start(bf16[1,1,256,2048]{3,2,1,0:T(8,128)(2,1)} %fusion.20), channel_id=1, source_target_pairs={{0,1},{1,0},{2,3},{3,2},{4,5},{5,4},{6,7},{7,6},{8,9},{9,8},{10,11... | collective-permute-start | bytes 3145736 | tf_op jit(solution)/shard_map/ppermute | solution.py:35
  528.2 23.9 %all-to-all-start.6 = ((f32[4,1,7936]{2,1,0:T(1,128)}), f32[4,1,7936]{2,1,0:T(1,128)S(1)}, u32[]{:S(2)}, u32[]{:S(2)}) async-start(f32[4,1,7936]{2,1,0:T(1,128)} %broadcast_in_dim.92), calls=%async_computation.7 | async-start | bytes 253952 | tf_op jit(solution)/shard_map/all_to_all | solution.py:39
  536.6 28.0 %copy-start.31 = (bf16[2,256,2048]{2,1,0:T(8,128)(2,1)S(1)}, bf16[2,256,2048]{2,1,0:T(8,128)(2,1)}, u32[]{:S(2)}) copy-start(bf16[2,256,2048]{2,1,0:T(8,128)(2,1)} %copy-done.30) | copy-start | bytes 6291460
  536.6 28.0 %collective-permute-start.24 = (bf16[1,1,256,2048]{3,2,1,0:T(8,128)(2,1)}, bf16[1,1,256,2048]{3,2,1,0:T(8,128)(2,1)S(1)}, u32[]{:S(2)}, u32[]{:S(2)}) collective-permute-start(bf16[1,1,256,2048]{3,2,1,0:T(8,128)(2,1)} %bitcast.24), channel_id=1, source_target_pairs={{0,1},{1,0},{2,3},{3,2},{4,5},{5,4},{6,7},{7,6},{8,9},{9,8},{10,11... | collective-permute-start | bytes 3145736 | tf_op jit(solution)/shard_map/ppermute | solution.py:35
  552.8 6.6 %all-to-all-start.7 = ((f32[4,1,6144]{2,1,0:T(1,128)}), f32[4,1,6144]{2,1,0:T(1,128)S(1)}, u32[]{:S(2)}, u32[]{:S(2)}) async-start(f32[4,1,6144]{2,1,0:T(1,128)} %broadcast_in_dim.93), calls=%async_computation.8 | async-start | bytes 196608 | tf_op jit(solution)/shard_map/all_to_all | solution.py:39
  559.5 4.6 collective-permute-start.25
  564.8 27.2 %copy-start.32 = (bf16[2,256,2048]{2,1,0:T(8,128)(2,1)}, bf16[2,256,2048]{2,1,0:T(8,128)(2,1)S(1)}, u32[]{:S(2)}) copy-start(bf16[2,256,2048]{2,1,0:T(8,128)(2,1)S(1)} %bitcast_dynamic-update-slice_fusion) | copy-start | bytes 6291460
  (25 other events, 63.3 us)
Sparse Core Ops, SparseCore 0:
  114.9 80.8 all-gather.8
  209.6 77.7 reduce-scatter.1
  289.6 79.2 all-gather.10
  370.4 128.5 all-gather.12
  501.0 84.9 all-gather.14

commit v6 on v5

--- a/solution.py
+++ b/solution.py
@@ -208,7 +208,7 @@
     whole, wide, narrow, stat = attention_specs(length)
     vm = pltpu.VMEM
     return pl.pallas_call(
-        functools.partial(attend_kernel, length // offs.shape[0], min(256, length), length // 2),
+        functools.partial(attend_kernel, length // offs.shape[0], min(512, length), length // 2),
         out_shape=(
             jax.ShapeDtypeStruct((length, inner), BF16),
             jax.ShapeDtypeStruct((length, 3 * inner), BF16),

time: 608 us -> 607 us (level)
  Pallas kernels: 220 us -> 213 us
    pallas_call x2, Pallas kernels: 25.5 us -> 18.7 us  [attend(): pl.pallas_call(functools.partial(attend_kernel, length // offs.shape[0],...]
  transfers between devices with their start and end apart: 39 -> 39, of which waited for: 15 -> 16; matrix products, arithmetic and copies ran while one was open for 9% -> 9% of each run, Pallas kernels for 35% -> 34%
where the time goes in v6:
time: 607 us; the launch traced here: 598 us
  Pallas kernels  213 us (35%)
  waiting for transfers between devices  178 us (29%)
  starting transfers between devices  104 us (17%)
  other arithmetic  44.5 us (7%)
  local copies, waits for them, and re-layouts  43.7 us (7%)
  between operations  15 us (2%)
    ppermute x3, waiting for transfers between devices, sum_step(): lax.ppermute(total(b).astype(BF16), axis, [(j, j - 1) for j in range(max(...  52.1 us
    pallas_call x3, Pallas kernels, rows_product(): pl.pallas_call(functools.partial(rows_kernel, [len(a) for a, _ in product...  41.5 us
    pallas_call x4, Pallas kernels, pair_product(): pl.pallas_call(functools.partial(pair_kernel, a.shape[1]), out_shape=jax....  41 us
    all_gather x3, waiting for transfers between devices, gather_cols(): return lax.all_gather(mine, 'ctx', axis=0, tiled=False)  39.6 us
    ppermute x3, waiting for transfers between devices, sum_step(): lax.ppermute(total(a).astype(BF16), axis, [(j, j + 1) for j in range(min(...  37.5 us
    ppermute x6, waiting for transfers between devices, gather_step(): lax.ppermute(left, axis, [(j, j + 1) for j in range(step - 1, size - 1)])  30.3 us
    unnamed x108, local copies, waits for them, and re-layouts  28.1 us
    ppermute x8, starting transfers between devices, xor_swap(): return lax.ppermute(value, axis, [(j, j ^ step) for j in range(size)])  25.2 us
  transfers between devices with their start and end apart: 39, of which 16 were waited for; matrix products, arithmetic and copies ran while one was open for 9% of the time, Pallas kernels for 34%

profile of v6, /device:TPU:19, one launch (start us, length us, event | category | flops | bytes accessed | tf_op | source)
XLA Modules:
  0.0 598.0 jit_solution(3084030862427928598)
XLA Ops:
  10.5 2.9 convert_reduce_fusion.5
  17.3 3.0 copy-done
  20.4 5.6 all-to-all-start
  27.0 3.2 collective-permute-start
  32.3 3.2 collective-permute-start.7
  48.8 4.0 collective-permute-start.3
  56.5 3.0 collective-permute-start.10
  59.6 4.7 collective-permute-done.3.refs_2_
  64.2 2.4 collective-permute-start.5
  67.4 8.1 %collective-permute-done.9.refs_9_ = bf16[128,2048]{1,0:T(8,128)(2,1)S(1)} collective-permute-done((bf16[128,2048]{1,0:T(8,128)(2,1)S(1)}, bf16[128,2048]{1,0:T(8,128)(2,1)S(1)}, u32[]{:S(2)}, u32[]{:S(2)}) %collective-permute-start.9) | collective-permute-done | bytes 524320 | tf_op jit(solution)/shard_map/ppermute | solution.py:45
  75.5 2.4 collective-permute-start.11
  78.6 6.3 %collective-permute-done.5.refs_3_ = bf16[128,2048]{1,0:T(8,128)(2,1)S(1)} collective-permute-done((bf16[128,2048]{1,0:T(8,128)(2,1)S(1)}, bf16[128,2048]{1,0:T(8,128)(2,1)S(1)}, u32[]{:S(2)}, u32[]{:S(2)}) %collective-permute-start.5) | collective-permute-done | bytes 524320 | tf_op jit(solution)/shard_map/ppermute | solution.py:45
  84.9 11.2 %collective-permute-done.11.refs_10_ = bf16[128,2048]{1,0:T(8,128)(2,1)S(1)} collective-permute-done((bf16[128,2048]{1,0:T(8,128)(2,1)S(1)}, bf16[128,2048]{1,0:T(8,128)(2,1)S(1)}, u32[]{:S(2)}, u32[]{:S(2)}) %collective-permute-start.11) | collective-permute-done | bytes 524320 | tf_op jit(solution)/shard_map/ppermute | solution.py:45
  97.8 7.0 %in_order.1 = bf16[4,256,2048]{2,1,0:T(8,128)(2,1)} custom-call(s32[1]{0:T(128)} %bitcast.2.here_ref, bf16[128,2048]{1,0:T(8,128)(2,1)} %get-tuple-element.181.refs_0_, bf16[128,2048]{1,0:T(8,128)(2,1)} %copy-done.33, bf16[128,2048]{1,0:T(8,128)(2,1)} %copy-done.36, bf16[128,2048]{1,0:T(8,128)(2,1)} %copy-done.40, bf16[128,2048]{1,0:T(8,128)(2,1)} %copy-done.34, ...), custom_call_target="tpu_custom_call" | custom-call | flops 1 | bytes 1 | tf_op jit(solution)/shard_map/in_order/pallas_call | solution.py:385
  104.7 2.6 collective-permute-start.13
  107.4 5.1 all-to-all-start.1
  114.6 11.1 %up_product.2 = (bf16[1024,1024]{1,0:T(8,128)(2,1)}, bf16[1024,1024]{1,0:T(8,128)(2,1)}) custom-call(bf16[1024,2048]{1,0:T(8,128)(2,1)} %bitcast.3.h_ref.refs_0_, bf16[2048,1792]{1,0:T(8,128)(2,1)} %bitcast.4.w_ref.refs_0_.refs_1_.refs_2_, f32[1,1024]{1,0:T(1,128)} %bitcast.103), custom_call_target="tpu_custom_call" | custom-call | flops 1 | bytes 1 | tf_op jit(solution)/shard_map/up_product/pallas_call | solution.py:458
  125.7 11.4 %up_product.3 = (bf16[1024,1024]{1,0:T(8,128)(2,1)}, bf16[1024,1024]{1,0:T(8,128)(2,1)}) custom-call(bf16[1024,2048]{1,0:T(8,128)(2,1)} %collective-permute-done.13.h_ref.refs_1_, bf16[2048,1792]{1,0:T(8,128)(2,1)} %bitcast.4.w_ref.refs_0_.refs_1_.refs_2_, f32[1,1024]{1,0:T(1,128)} %bitcast.104), custom_call_target="tpu_custom_call" | custom-call | flops 1 | bytes 1 | tf_op jit(solution)/shard_map/up_product/pallas_call | solution.py:458
  137.1 7.3 %line_product.2.qkv_ref = f32[1024,768]{1,0:T(8,128)} custom-call(bf16[1024,2048]{1,0:T(8,128)(2,1)} %bitcast.3.h_ref.refs_0_, bf16[2048,1792]{1,0:T(8,128)(2,1)} %bitcast.4.w_ref.refs_0_.refs_1_.refs_2_, bf16[2048,1792]{1,0:T(8,128)(2,1)} %bitcast.4.w_ref.refs_0_.refs_1_.refs_2_, bf16[2048,1792]{1,0:T(8,128)(2,1)} %bitcast.4.w_ref.refs_0_.refs_1_.refs_2_, ...), custom_call_target="tpu_custom_call" | custom-call | flops 1 | bytes 1 | tf_op jit(solution)/shard_map/line_product/pallas_call | solution.py:524
  144.3 7.3 %line_product.3.qkv_ref = f32[1024,768]{1,0:T(8,128)} custom-call(bf16[1024,2048]{1,0:T(8,128)(2,1)} %collective-permute-done.13.h_ref.refs_1_, bf16[2048,1792]{1,0:T(8,128)(2,1)} %bitcast.4.w_ref.refs_0_.refs_1_.refs_2_, bf16[2048,1792]{1,0:T(8,128)(2,1)} %bitcast.4.w_ref.refs_0_.refs_1_.refs_2_, bf16[2048,1792]{1,0:T(8,128)(2,1)} %bitcast.4.w_ref.refs_0_.refs_1_.refs_2_, ...), custom_call_target="tpu_custom_call" | custom-call | flops 1 | bytes 1 | tf_op jit(solution)/shard_map/line_product/pallas_call | solution.py:524
  153.6 9.3 %attend.2 = (bf16[1024,256]{1,0:T(8,128)(2,1)S(1)}, bf16[1024,768]{1,0:T(8,128)(2,1)S(1)}, f32[2,2,2,1024]{3,2,1,0:T(2,128)S(1)}) custom-call(s32[8]{0:T(128)S(1)} %broadcast_multiply_fusion.3.offs_ref, s32[1]{0:T(128)} %get-tuple-element.351.prefix_ref, f32[1024,768]{1,0:T(8,128)S(1)} %copy-done.10, f32[1024,128]{1,0:T(8,128)S(1)} %get-tuple-element.218.cos_ref, ...), custom_call_target="tpu_custom_call" | custom-call | flops 1 | bytes 1 | tf_op jit(solution)/shard_map/attend/pallas_call | solution.py:210
  164.1 6.2 %all-to-all-done.1 = bf16[4,512,1280]{2,1,0:T(8,128)(2,1)} async-done(((bf16[4,512,1280]{2,1,0:T(8,128)(2,1)}), bf16[4,512,1280]{2,1,0:T(8,128)(2,1)}, u32[]{:S(2)}, u32[]{:S(2)}) %all-to-all-start.1) | async-done | bytes 5242912 | tf_op jit(solution)/shard_map/all_to_all | solution.py:649
  171.8 9.3 %pair_product.4 = bf16[1024,2048]{1,0:T(8,128)(2,1)} custom-call(bf16[1024,1024]{1,0:T(8,128)(2,1)S(1)} %copy-done.11, bf16[1024,256]{1,0:T(8,128)(2,1)S(1)} %get-tuple-element.229.b_ref.refs_7_, bf16[2048,1280]{1,0:T(8,128)(2,1)} %bitcast.6.w_ref), custom_call_target="tpu_custom_call" | custom-call | flops 1 | bytes 1 | tf_op jit(solution)/shard_map/pair_product/pallas_call | solution.py:282
  182.7 9.3 %attend.3 = (bf16[1024,256]{1,0:T(8,128)(2,1)S(1)}, bf16[1024,768]{1,0:T(8,128)(2,1)S(1)}, f32[2,2,2,1024]{3,2,1,0:T(2,128)S(1)}) custom-call(s32[8]{0:T(128)S(1)} %broadcast_multiply_fusion.3.offs_ref, s32[1]{0:T(128)} %get-tuple-element.352.prefix_ref, f32[1024,768]{1,0:T(8,128)S(1)} %copy-done.9, f32[1024,128]{1,0:T(8,128)S(1)} %get-tuple-element.218.cos_ref, ...), custom_call_target="tpu_custom_call" | custom-call | flops 1 | bytes 1 | tf_op jit(solution)/shard_map/attend/pallas_call | solution.py:210
  193.2 2.6 all-gather.9.cloned.1.call-done
  198.0 9.4 %pair_product.5 = bf16[1024,2048]{1,0:T(8,128)(2,1)} custom-call(bf16[1024,1024]{1,0:T(8,128)(2,1)S(1)} %copy-done.12, bf16[1024,256]{1,0:T(8,128)(2,1)S(1)} %get-tuple-element.242.b_ref.refs_6_, bf16[2048,1280]{1,0:T(8,128)(2,1)} %bitcast.6.w_ref, bf16[1024,2048]{1,0:T(8,128)(2,1)} %collective-permute-done.14.refs_0_), custom_call_target="tpu_custom_call" | custom-call | flops 1 | bytes 1 | tf_op jit(solution)/shard_map/pair_product/pallas_call | solution.py:282
  209.5 13.4 %rows_product.3 = bf16[4,512,1024]{2,1,0:T(8,128)(2,1)} custom-call(bf16[1024,2048]{1,0:T(8,128)(2,1)} %all-gather.9.cloned.1.call-done, bf16[1024,2048]{1,0:T(8,128)(2,1)} %copy-done.21, bf16[1024,1024]{1,0:T(8,128)(2,1)} %get-tuple-element.246.a_ref.refs_2_, bf16[1024,1024]{1,0:T(8,128)(2,1)} %get-tuple-element.247.a_ref.refs_3_), custom_call_target="tpu_custom_call" | custom-call | flops 1 | bytes 1 | tf_op jit(solution)/shard_map/rows_product/pallas_call | solution.py:351
  222.9 5.1 all-to-all-start.2
  228.0 10.6 %down_product.2 = (bf16[1024,1024]{1,0:T(8,128)(2,1)}, bf16[1024,256]{1,0:T(8,128)(2,1)}) custom-call(bf16[1024,2048]{1,0:T(8,128)(2,1)} %all-gather.9.cloned.1.call-done, bf16[2048,1280]{1,0:T(8,128)(2,1)} %bitcast.6.w_ref, bf16[1024,1024]{1,0:T(8,128)(2,1)} %get-tuple-element.251.s_ref), custom_call_target="tpu_custom_call" | custom-call | flops 1 | bytes 1 | tf_op jit(solution)/shard_map/down_product/pallas_call | solution.py:485
  238.5 10.3 %down_product.3 = (bf16[1024,1024]{1,0:T(8,128)(2,1)}, bf16[1024,256]{1,0:T(8,128)(2,1)}) custom-call(bf16[1024,2048]{1,0:T(8,128)(2,1)} %copy-done.21, bf16[2048,1280]{1,0:T(8,128)(2,1)} %bitcast.6.w_ref, bf16[1024,1024]{1,0:T(8,128)(2,1)} %get-tuple-element.260.s_ref), custom_call_target="tpu_custom_call" | custom-call | flops 1 | bytes 1 | tf_op jit(solution)/shard_map/down_product/pallas_call | solution.py:485
  248.8 13.6 %rows_product.4 = bf16[4,512,1024]{2,1,0:T(8,128)(2,1)} custom-call(bf16[1024,2048]{1,0:T(8,128)(2,1)} %bitcast.3.h_ref.refs_0_, bf16[1024,2048]{1,0:T(8,128)(2,1)} %collective-permute-done.13.h_ref.refs_1_, bf16[1024,1024]{1,0:T(8,128)(2,1)} %get-tuple-element.294.refs_2_.a_ref, bf16[1024,1024]{1,0:T(8,128)(2,1)} %get-tuple-element.283.refs_3_.a_ref), custom_call_target="tpu_custom_call" | custom-call | flops 1 | bytes 1 | tf_op jit(solution)/shard_map/rows_product/pallas_call | solution.py:351
  262.4 12.3 %attend_back.2.b_ref.refs_3_ = bf16[1024,768]{1,0:T(8,128)(2,1)S(1)} custom-call(s32[8]{0:T(128)S(1)} %broadcast_multiply_fusion.3.offs_ref, s32[1]{0:T(128)} %get-tuple-element.351.prefix_ref, bf16[1024,768]{1,0:T(8,128)(2,1)S(1)} %copy-done.18, f32[2,2,2,1024]{3,2,1,0:T(2,128)S(1)} %get-tuple-element.277.stat_ref, bf16[1024,256]{1,0:T(8,128)(2,1)S(1)} %copy-done.20, ...), custom_call_target="tpu_custom_call" | custom-call | flops 1 | bytes 1 | tf_op jit(solution)/shard_map/attend_back/pallas_call | solution.py:239
  275.2 4.2 fusion.21
  281.0 11.1 %pair_product.6 = bf16[1024,2048]{1,0:T(8,128)(2,1)} custom-call(bf16[1024,1024]{1,0:T(8,128)(2,1)S(1)} %copy-done.8, bf16[1024,768]{1,0:T(8,128)(2,1)S(1)} %attend_back.2.b_ref.refs_3_, bf16[2048,1792]{1,0:T(8,128)(2,1)} %bitcast.4.w_ref.refs_0_.refs_1_.refs_2_), custom_call_target="tpu_custom_call" | custom-call | flops 1 | bytes 1 | tf_op jit(solution)/shard_map/pair_product/pallas_call | solution.py:282
  292.9 5.3 all-to-all-start.3
  300.8 12.3 %attend_back.3.b_ref.refs_2_ = bf16[1024,768]{1,0:T(8,128)(2,1)S(1)} custom-call(s32[8]{0:T(128)S(1)} %broadcast_multiply_fusion.3.offs_ref, s32[1]{0:T(128)} %get-tuple-element.352.prefix_ref, bf16[1024,768]{1,0:T(8,128)(2,1)S(1)} %copy-done.16, f32[2,2,2,1024]{3,2,1,0:T(2,128)S(1)} %get-tuple-element.289.stat_ref, bf16[1024,256]{1,0:T(8,128)(2,1)S(1)} %copy-done.19, ...), custom_call_target="tpu_custom_call" | custom-call | flops 1 | bytes 1 | tf_op jit(solution)/shard_map/attend_back/pallas_call | solution.py:239
  315.3 11.3 %pair_product.7 = bf16[1024,2048]{1,0:T(8,128)(2,1)} custom-call(bf16[1024,1024]{1,0:T(8,128)(2,1)S(1)} %copy-done.6, bf16[1024,768]{1,0:T(8,128)(2,1)S(1)} %attend_back.3.b_ref.refs_2_, bf16[2048,1792]{1,0:T(8,128)(2,1)} %bitcast.4.w_ref.refs_0_.refs_1_.refs_2_, bf16[1024,2048]{1,0:T(8,128)(2,1)} %collective-permute-done.16.refs_0_), custom_call_target="tpu_custom_call" | custom-call | flops 1 | bytes 1 | tf_op jit(solution)/shard_map/pair_product/pallas_call | solution.py:282
  326.6 14.5 %rows_product.5 = bf16[4,512,1024]{2,1,0:T(8,128)(2,1)} custom-call(bf16[1024,2048]{1,0:T(8,128)(2,1)} %bitcast.3.h_ref.refs_0_, bf16[1024,2048]{1,0:T(8,128)(2,1)} %collective-permute-done.13.h_ref.refs_1_, bf16[1024,768]{1,0:T(8,128)(2,1)} %copy-done.3, bf16[1024,768]{1,0:T(8,128)(2,1)} %copy-done.1, bf16[1024,2048]{1,0:T(8,128)(2,1)} %all-gather.9.cloned.1.call-done, ...), custom_call_target="tpu_custom_call" | custom-call | flops 1 | bytes 1 | tf_op jit(solution)/shard_map/rows_product/pallas_call | solution.py:351
  341.1 4.4 all-to-all-done.3
  345.5 4.1 fusion.23
  349.6 18.3 %all-gather.11.cloned.1.call-done = bf16[2048,1024]{1,0:T(8,128)(2,1)} async-done(((bf16[512,1024]{1,0:T(8,128)(2,1)}), bf16[2048,1024]{1,0:T(8,128)(2,1)}) %all-gather.11.cloned.1.call-update) | async-done | bytes 4194320 | tf_op jit(solution)/shard_map/all_gather | solution.py:643
  368.0 5.1 all-to-all-start.4
  376.8 6.4 %widen.2 = f32[512,4096]{1,0:T(8,128)} custom-call(bf16[4,512,1024]{2,1,0:T(8,128)(2,1)} %bitcast.97), custom_call_target="tpu_custom_call" | custom-call | flops 1 | bytes 1 | tf_op jit(solution)/shard_map/widen/pallas_call | solution.py:434
  383.2 40.0 %collective-permute-done.19 = bf16[256,2048]{1,0:T(8,128)(2,1)} collective-permute-done((bf16[256,2048]{1,0:T(8,128)(2,1)S(1)}, bf16[256,2048]{1,0:T(8,128)(2,1)}, u32[]{:S(2)}, u32[]{:S(2)}) %collective-permute-start.19) | collective-permute-done | bytes 1048608 | tf_op jit(solution)/shard_map/ppermute | solution.py:58
  423.2 3.5 fusion.1
  428.2 4.0 collective-permute-start.21
  435.0 4.2 fusion.24
  439.2 37.5 %collective-permute-done.20 = bf16[256,2048]{1,0:T(8,128)(2,1)} collective-permute-done((bf16[256,2048]{1,0:T(8,128)(2,1)}, bf16[256,2048]{1,0:T(8,128)(2,1)}, u32[]{:S(2)}, u32[]{:S(2)}) %collective-permute-start.20) | collective-permute-done | bytes 1048608 | tf_op jit(solution)/shard_map/ppermute | solution.py:55
  478.3 2.6 add_convert_fusion
  480.9 2.9 collective-permute-start.23
  483.7 2.6 add_convert_fusion.1
  486.3 3.5 collective-permute-start.22
  490.5 3.6 all-to-all-start.5
  494.1 2.7 fusion.20
  496.8 4.5 collective-permute-start.17
  504.2 11.7 %collective-permute-done.23 = bf16[256,2048]{1,0:T(8,128)(2,1)} collective-permute-done((bf16[256,2048]{1,0:T(8,128)(2,1)}, bf16[256,2048]{1,0:T(8,128)(2,1)}, u32[]{:S(2)}, u32[]{:S(2)}) %collective-permute-start.23) | collective-permute-done | bytes 1048608 | tf_op jit(solution)/shard_map/ppermute | solution.py:58
  516.0 3.4 fusion.18
  519.4 6.1 %widen.3 = f32[512,4096]{1,0:T(8,128)} custom-call(bf16[4,512,1024]{2,1,0:T(8,128)(2,1)} %bitcast.96), custom_call_target="tpu_custom_call" | custom-call | flops 1 | bytes 1 | tf_op jit(solution)/shard_map/widen/pallas_call | solution.py:434
  527.2 3.6 all-to-all-start.6
  535.6 13.1 %collective-permute-start.24 = (bf16[1,1,256,2048]{3,2,1,0:T(8,128)(2,1)}, bf16[1,1,256,2048]{3,2,1,0:T(8,128)(2,1)S(1)}, u32[]{:S(2)}, u32[]{:S(2)}) collective-permute-start(bf16[1,1,256,2048]{3,2,1,0:T(8,128)(2,1)} %bitcast.24), channel_id=1, source_target_pairs={{0,1},{1,0},{2,3},{3,2},{4,5},{5,4},{6,7},{7,6},{8,9},{9,8},{10,11... | collective-permute-start | bytes 3145736 | tf_op jit(solution)/shard_map/ppermute | solution.py:35
  551.8 3.6 all-to-all-start.7
  555.4 3.0 all-to-all-done.7
  563.8 21.3 %all-gather.15.cloned.1.call-done = bf16[2048,1024]{1,0:T(8,128)(2,1)} async-done(((bf16[512,1024]{1,0:T(8,128)(2,1)}), bf16[2048,1024]{1,0:T(8,128)(2,1)}) %all-gather.15.cloned.1.call-update) | async-done | bytes 4194320 | tf_op jit(solution)/shard_map/all_gather | solution.py:643
  585.1 5.9 place.1
  (223 shorter events, 79.4 us)
Async XLA Ops:
  13.5 1.5 collective-permute-start.2
  20.4 87.0 %all-to-all-start = ((bf16[4,512,1792]{2,1,0:T(8,128)(2,1)}), bf16[4,512,1792]{2,1,0:T(8,128)(2,1)}, u32[]{:S(2)}, u32[]{:S(2)}) async-start(bf16[4,512,1792]{2,1,0:T(8,128)(2,1)} %copy-done), calls=%async_computation | async-start | bytes 14680064 | tf_op jit(solution)/shard_map/all_to_all | solution.py:622
  26.0 15.2 %copy-start.48 = (s32[8]{0:T(128)S(1)}, s32[8]{0:T(128)}, u32[]{:S(2)}) copy-start(s32[8]{0:T(128)} %param.21) | copy-start | bytes 100
  26.0 15.3 %copy-start.49 = (s32[2]{0:T(128)S(1)}, s32[2]{0:T(128)}, u32[]{:S(2)}) copy-start(s32[2]{0:T(128)} %param.20) | copy-start | bytes 28
  27.0 21.8 %collective-permute-start = (bf16[128,2048]{1,0:T(8,128)(2,1)}, bf16[128,2048]{1,0:T(8,128)(2,1)S(1)}, u32[]{:S(2)}, u32[]{:S(2)}) collective-permute-start(bf16[128,2048]{1,0:T(8,128)(2,1)} %get-tuple-element.181.refs_0_), channel_id=1, source_target_pairs={{0,2},{2,4},{4,6},{1,3},{3,5},{5,7},{8,10},{10,12},{12,14},{9,11},... | collective-permute-start | bytes 1572872 | tf_op jit(solution)/shard_map/ppermute | solution.py:45
  30.2 18.6 %collective-permute-start.1 = (bf16[128,2048]{1,0:T(8,128)(2,1)}, bf16[128,2048]{1,0:T(8,128)(2,1)S(1)}, u32[]{:S(2)}, u32[]{:S(2)}) collective-permute-start(bf16[128,2048]{1,0:T(8,128)(2,1)} %get-tuple-element.181.refs_0_), channel_id=1, source_target_pairs={{2,0},{4,2},{6,4},{3,1},{5,3},{7,5},{10,8},{12,10},{14,12},{11,9},... | collective-permute-start | bytes 1572872 | tf_op jit(solution)/shard_map/ppermute | solution.py:46
  32.3 21.9 %collective-permute-start.7 = (bf16[128,2048]{1,0:T(8,128)(2,1)}, bf16[128,2048]{1,0:T(8,128)(2,1)S(1)}, u32[]{:S(2)}, u32[]{:S(2)}) collective-permute-start(bf16[128,2048]{1,0:T(8,128)(2,1)} %get-tuple-element.188.refs_7_), channel_id=1, source_target_pairs={{0,2},{2,4},{4,6},{1,3},{3,5},{5,7},{8,10},{10,12},{12,14},{9,11},... | collective-permute-start | bytes 1572872 | tf_op jit(solution)/shard_map/ppermute | solution.py:45
  35.5 21.0 %collective-permute-start.8 = (bf16[128,2048]{1,0:T(8,128)(2,1)}, bf16[128,2048]{1,0:T(8,128)(2,1)}, u32[]{:S(2)}, u32[]{:S(2)}) collective-permute-start(bf16[128,2048]{1,0:T(8,128)(2,1)} %get-tuple-element.188.refs_7_), channel_id=1, source_target_pairs={{2,0},{4,2},{6,4},{3,1},{5,3},{7,5},{10,8},{12,10},{14,12},{11,9},... | collective-permute-start | bytes 1572872 | tf_op jit(solution)/shard_map/ppermute | solution.py:46
  48.8 48.9 %copy-start.33 = (bf16[128,2048]{1,0:T(8,128)(2,1)}, bf16[128,2048]{1,0:T(8,128)(2,1)S(1)}, u32[]{:S(2)}) copy-start(bf16[128,2048]{1,0:T(8,128)(2,1)S(1)} %collective-permute-done.refs_1_) | copy-start | bytes 1572868
  48.8 48.9 %copy-start.34 = (bf16[128,2048]{1,0:T(8,128)(2,1)}, bf16[128,2048]{1,0:T(8,128)(2,1)S(1)}, u32[]{:S(2)}) copy-start(bf16[128,2048]{1,0:T(8,128)(2,1)S(1)} %collective-permute-done.1.refs_4_) | copy-start | bytes 1572868
  48.8 15.4 %collective-permute-start.3 = (bf16[128,2048]{1,0:T(8,128)(2,1)S(1)}, bf16[128,2048]{1,0:T(8,128)(2,1)S(1)}, u32[]{:S(2)}, u32[]{:S(2)}) collective-permute-start(bf16[128,2048]{1,0:T(8,128)(2,1)S(1)} %collective-permute-done.refs_1_), channel_id=1, source_target_pairs={{2,4},{4,6},{3,5},{5,7},{10,12},{12,14},{11,13},{13,15},{18,20},{2... | collective-permute-start | bytes 1572872 | tf_op jit(solution)/shard_map/ppermute | solution.py:45
  52.8 13.8 %collective-permute-start.4 = (bf16[128,2048]{1,0:T(8,128)(2,1)S(1)}, bf16[128,2048]{1,0:T(8,128)(2,1)S(1)}, u32[]{:S(2)}, u32[]{:S(2)}) collective-permute-start(bf16[128,2048]{1,0:T(8,128)(2,1)S(1)} %collective-permute-done.1.refs_4_), channel_id=1, source_target_pairs={{2,0},{4,2},{3,1},{5,3},{10,8},{12,10},{11,9},{13,11},{18,16},{20,... | collective-permute-start | bytes 1572872 | tf_op jit(solution)/shard_map/ppermute | solution.py:46
  54.2 43.6 %copy-start.35 = (bf16[128,2048]{1,0:T(8,128)(2,1)}, bf16[128,2048]{1,0:T(8,128)(2,1)S(1)}, u32[]{:S(2)}) copy-start(bf16[128,2048]{1,0:T(8,128)(2,1)S(1)} %collective-permute-done.7.refs_8_) | copy-start | bytes 1572868
  54.2 21.3 %collective-permute-start.9 = (bf16[128,2048]{1,0:T(8,128)(2,1)S(1)}, bf16[128,2048]{1,0:T(8,128)(2,1)S(1)}, u32[]{:S(2)}, u32[]{:S(2)}) collective-permute-start(bf16[128,2048]{1,0:T(8,128)(2,1)S(1)} %collective-permute-done.7.refs_8_), channel_id=1, source_target_pairs={{2,4},{4,6},{3,5},{5,7},{10,12},{12,14},{11,13},{13,15},{18,20},{2... | collective-permute-start | bytes 1572872 | tf_op jit(solution)/shard_map/ppermute | solution.py:45
  56.5 21.4 %collective-permute-start.10 = (bf16[128,2048]{1,0:T(8,128)(2,1)}, bf16[128,2048]{1,0:T(8,128)(2,1)S(1)}, u32[]{:S(2)}, u32[]{:S(2)}) collective-permute-start(bf16[128,2048]{1,0:T(8,128)(2,1)} %collective-permute-done.8.refs_11_), channel_id=1, source_target_pairs={{2,0},{4,2},{3,1},{5,3},{10,8},{12,10},{11,9},{13,11},{18,16},{20,... | collective-permute-start | bytes 1572872 | tf_op jit(solution)/shard_map/ppermute | solution.py:46
  64.2 11.2 %copy-start.36 = (bf16[128,2048]{1,0:T(8,128)(2,1)}, bf16[128,2048]{1,0:T(8,128)(2,1)S(1)}, u32[]{:S(2)}) copy-start(bf16[128,2048]{1,0:T(8,128)(2,1)S(1)} %collective-permute-done.3.refs_2_) | copy-start | bytes 1572868
  64.2 20.6 %collective-permute-start.5 = (bf16[128,2048]{1,0:T(8,128)(2,1)S(1)}, bf16[128,2048]{1,0:T(8,128)(2,1)S(1)}, u32[]{:S(2)}, u32[]{:S(2)}) collective-permute-start(bf16[128,2048]{1,0:T(8,128)(2,1)S(1)} %collective-permute-done.3.refs_2_), channel_id=1, source_target_pairs={{4,6},{5,7},{12,14},{13,15},{20,22},{21,23},{28,30},{29,31}} | collective-permute-start | bytes 1572872 | tf_op jit(solution)/shard_map/ppermute | solution.py:45
  66.7 18.2 %copy-start.37 = (bf16[128,2048]{1,0:T(8,128)(2,1)}, bf16[128,2048]{1,0:T(8,128)(2,1)S(1)}, u32[]{:S(2)}) copy-start(bf16[128,2048]{1,0:T(8,128)(2,1)S(1)} %collective-permute-done.4.refs_5_) | copy-start | bytes 1572868
  66.7 18.2 %collective-permute-start.6 = (bf16[128,2048]{1,0:T(8,128)(2,1)S(1)}, bf16[128,2048]{1,0:T(8,128)(2,1)S(1)}, u32[]{:S(2)}, u32[]{:S(2)}) collective-permute-start(bf16[128,2048]{1,0:T(8,128)(2,1)S(1)} %collective-permute-done.4.refs_5_), channel_id=1, source_target_pairs={{2,0},{3,1},{10,8},{11,9},{18,16},{19,17},{26,24},{27,25}} | collective-permute-start | bytes 1572872 | tf_op jit(solution)/shard_map/ppermute | solution.py:46
  75.5 9.4 %copy-start.38 = (bf16[128,2048]{1,0:T(8,128)(2,1)}, bf16[128,2048]{1,0:T(8,128)(2,1)S(1)}, u32[]{:S(2)}) copy-start(bf16[128,2048]{1,0:T(8,128)(2,1)S(1)} %collective-permute-done.9.refs_9_) | copy-start | bytes 1572868
  75.5 20.6 %collective-permute-start.11 = (bf16[128,2048]{1,0:T(8,128)(2,1)S(1)}, bf16[128,2048]{1,0:T(8,128)(2,1)S(1)}, u32[]{:S(2)}, u32[]{:S(2)}) collective-permute-start(bf16[128,2048]{1,0:T(8,128)(2,1)S(1)} %collective-permute-done.9.refs_9_), channel_id=1, source_target_pairs={{4,6},{5,7},{12,14},{13,15},{20,22},{21,23},{28,30},{29,31}} | collective-permute-start | bytes 1572872 | tf_op jit(solution)/shard_map/ppermute | solution.py:45
  77.9 18.2 %copy-start.39 = (bf16[128,2048]{1,0:T(8,128)(2,1)}, bf16[128,2048]{1,0:T(8,128)(2,1)S(1)}, u32[]{:S(2)}) copy-start(bf16[128,2048]{1,0:T(8,128)(2,1)S(1)} %collective-permute-done.10.refs_12_) | copy-start | bytes 1572868
  77.9 18.2 %collective-permute-start.12 = (bf16[128,2048]{1,0:T(8,128)(2,1)S(1)}, bf16[128,2048]{1,0:T(8,128)(2,1)S(1)}, u32[]{:S(2)}, u32[]{:S(2)}) collective-permute-start(bf16[128,2048]{1,0:T(8,128)(2,1)S(1)} %collective-permute-done.10.refs_12_), channel_id=1, source_target_pairs={{2,0},{3,1},{10,8},{11,9},{18,16},{19,17},{26,24},{27,25}} | collective-permute-start | bytes 1572872 | tf_op jit(solution)/shard_map/ppermute | solution.py:46
  84.9 11.2 %copy-start.40 = (bf16[128,2048]{1,0:T(8,128)(2,1)}, bf16[128,2048]{1,0:T(8,128)(2,1)S(1)}, u32[]{:S(2)}) copy-start(bf16[128,2048]{1,0:T(8,128)(2,1)S(1)} %collective-permute-done.5.refs_3_) | copy-start | bytes 1572868
  84.9 11.2 %copy-start.41 = (bf16[128,2048]{1,0:T(8,128)(2,1)}, bf16[128,2048]{1,0:T(8,128)(2,1)S(1)}, u32[]{:S(2)}) copy-start(bf16[128,2048]{1,0:T(8,128)(2,1)S(1)} %collective-permute-done.6.refs_6_) | copy-start | bytes 1572868
  104.7 9.9 %collective-permute-start.13 = (bf16[1024,2048]{1,0:T(8,128)(2,1)}, bf16[1024,2048]{1,0:T(8,128)(2,1)}, u32[]{:S(2)}, u32[]{:S(2)}) collective-permute-start(bf16[1024,2048]{1,0:T(8,128)(2,1)} %bitcast.3.h_ref.refs_0_), channel_id=1, source_target_pairs={{0,1},{1,0},{2,3},{3,2},{4,5},{5,4},{6,7},{7,6},{8,9},{9,8},{10,11... | collective-permute-start | bytes 12582920 | tf_op jit(solution)/shard_map/ppermute | solution.py:35
  107.4 62.9 %all-to-all-start.1 = ((bf16[4,512,1280]{2,1,0:T(8,128)(2,1)}), bf16[4,512,1280]{2,1,0:T(8,128)(2,1)}, u32[]{:S(2)}, u32[]{:S(2)}) async-start(bf16[4,512,1280]{2,1,0:T(8,128)(2,1)} %copy-done.5), calls=%async_computation.1 | async-start | bytes 10485760 | tf_op jit(solution)/shard_map/all_to_all | solution.py:649
  112.5 83.3 %all-gather.9.cloned.1.call-start = ((), (), s32[]{:S(2)}) async-start(), calls=%async_computation.10 | async-start | bytes 5242880 | tf_op jit(solution)/shard_map/all_gather | solution.py:630
  113.2 200.0 %reduce-scatter.2.cloned.1.call-start = ((), (), s32[]{:S(2)}) async-start(), calls=%async_computation.9 | async-start | bytes 5242880 | tf_op jit(solution)/shard_map/reduce_scatter | solution.py:705
  164.0 17.1 %copy-start.13 = (bf16[1024,256]{1,0:T(8,128)(2,1)}, bf16[1024,256]{1,0:T(8,128)(2,1)S(1)}, u32[]{:S(2)}) copy-start(bf16[1024,256]{1,0:T(8,128)(2,1)S(1)} %get-tuple-element.229.b_ref.refs_7_) | copy-start | bytes 1572868
  171.8 10.8 %copy-start.9 = (f32[1024,768]{1,0:T(8,128)S(1)}, f32[1024,768]{1,0:T(8,128)}, u32[]{:S(2)}) copy-start(f32[1024,768]{1,0:T(8,128)} %line_product.2.qkv_ref) | copy-start | bytes 9437188
  181.1 14.6 %collective-permute-start.14 = (bf16[1024,2048]{1,0:T(8,128)(2,1)}, bf16[1024,2048]{1,0:T(8,128)(2,1)}, u32[]{:S(2)}, u32[]{:S(2)}) collective-permute-start(bf16[1024,2048]{1,0:T(8,128)(2,1)} %pair_product.4), channel_id=1, source_target_pairs={{0,1},{1,0},{2,3},{3,2},{4,5},{5,4},{6,7},{7,6},{8,9},{9,8},{10,11... | collective-permute-start | bytes 12582920 | tf_op jit(solution)/shard_map/ppermute | solution.py:35
  193.2 14.2 %copy-start.14 = (bf16[1024,256]{1,0:T(8,128)(2,1)}, bf16[1024,256]{1,0:T(8,128)(2,1)S(1)}, u32[]{:S(2)}) copy-start(bf16[1024,256]{1,0:T(8,128)(2,1)S(1)} %get-tuple-element.242.b_ref.refs_6_) | copy-start | bytes 1572868
  195.8 11.7 %collective-permute-start.15 = (bf16[1024,2048]{1,0:T(8,128)(2,1)}, bf16[1024,2048]{1,0:T(8,128)(2,1)S(1)}, u32[]{:S(2)}, u32[]{:S(2)}) collective-permute-start(bf16[1024,2048]{1,0:T(8,128)(2,1)} %all-gather.9.cloned.1.call-done), channel_id=1, source_target_pairs={{0,1},{1,0},{2,3},{3,2},{4,5},{5,4},{6,7},{7,6},{8,9},{9,8},{10,11... | collective-permute-start | bytes 12582920 | tf_op jit(solution)/shard_map/ppermute | solution.py:35
  222.9 52.3 %all-to-all-start.2 = ((bf16[4,512,1024]{2,1,0:T(8,128)(2,1)}), bf16[4,512,1024]{2,1,0:T(8,128)(2,1)}, u32[]{:S(2)}, u32[]{:S(2)}) async-start(bf16[4,512,1024]{2,1,0:T(8,128)(2,1)} %rows_product.3), calls=%async_computation.2 | async-start | bytes 8388608 | tf_op jit(solution)/shard_map/all_to_all | solution.py:637
  228.0 140.0 %all-gather.11.cloned.1.call-start = ((), (), s32[]{:S(2)}) async-start(), calls=%async_computation.11 | async-start | bytes 5242880 | tf_op jit(solution)/shard_map/all_gather | solution.py:643
  248.8 13.6 %copy-start.18 = (bf16[1024,768]{1,0:T(8,128)(2,1)S(1)}, bf16[1024,768]{1,0:T(8,128)(2,1)}, u32[]{:S(2)}) copy-start(bf16[1024,768]{1,0:T(8,128)(2,1)} %copy-done.17) | copy-start | bytes 4718596
  248.8 13.6 %copy-start.20 = (bf16[1024,256]{1,0:T(8,128)(2,1)S(1)}, bf16[1024,256]{1,0:T(8,128)(2,1)}, u32[]{:S(2)}) copy-start(bf16[1024,256]{1,0:T(8,128)(2,1)} %get-tuple-element.278.do_ref) | copy-start | bytes 1572868
  292.2 20.9 %collective-permute-start.16 = (bf16[1024,2048]{1,0:T(8,128)(2,1)}, bf16[1024,2048]{1,0:T(8,128)(2,1)}, u32[]{:S(2)}, u32[]{:S(2)}) collective-permute-start(bf16[1024,2048]{1,0:T(8,128)(2,1)} %pair_product.6), channel_id=1, source_target_pairs={{0,1},{1,0},{2,3},{3,2},{4,5},{5,4},{6,7},{7,6},{8,9},{9,8},{10,11... | collective-permute-start | bytes 12582920 | tf_op jit(solution)/shard_map/ppermute | solution.py:35
  292.9 52.7 %all-to-all-start.3 = ((bf16[4,512,1024]{2,1,0:T(8,128)(2,1)}), bf16[4,512,1024]{2,1,0:T(8,128)(2,1)}, u32[]{:S(2)}, u32[]{:S(2)}) async-start(bf16[4,512,1024]{2,1,0:T(8,128)(2,1)} %rows_product.4), calls=%async_computation.4 | async-start | bytes 8388608 | tf_op jit(solution)/shard_map/all_to_all | solution.py:637
  298.2 221.2 %all-gather.13.cloned.1.call-start = ((), (), s32[]{:S(2)}) async-start(), calls=%async_computation.12 | async-start | bytes 5242880 | tf_op jit(solution)/shard_map/all_gather | solution.py:643
  313.1 13.5 %copy-start.3 = (bf16[1024,768]{1,0:T(8,128)(2,1)}, bf16[1024,768]{1,0:T(8,128)(2,1)S(1)}, u32[]{:S(2)}) copy-start(bf16[1024,768]{1,0:T(8,128)(2,1)S(1)} %attend_back.3.b_ref.refs_2_) | copy-start | bytes 4718596
  368.0 55.3 %all-to-all-start.4 = ((bf16[4,512,1024]{2,1,0:T(8,128)(2,1)}), bf16[4,512,1024]{2,1,0:T(8,128)(2,1)}, u32[]{:S(2)}, u32[]{:S(2)}) async-start(bf16[4,512,1024]{2,1,0:T(8,128)(2,1)} %rows_product.5), calls=%async_computation.5 | async-start | bytes 8388608 | tf_op jit(solution)/shard_map/all_to_all | solution.py:637
  373.0 212.0 %all-gather.15.cloned.1.call-start = ((), (), s32[]{:S(2)}) async-start(), calls=%async_computation.13 | async-start | bytes 5242880 | tf_op jit(solution)/shard_map/all_gather | solution.py:643
  374.7 8.5 %copy-start.27 = (bf16[256,2048]{1,0:T(8,128)(2,1)}, bf16[256,2048]{1,0:T(8,128)(2,1)S(1)}, u32[]{:S(2)}) copy-start(bf16[256,2048]{1,0:T(8,128)(2,1)S(1)} %get-tuple-element.340) | copy-start | bytes 3145732
  374.7 8.5 %collective-permute-start.18 = (bf16[256,2048]{1,0:T(8,128)(2,1)S(1)}, bf16[256,2048]{1,0:T(8,128)(2,1)S(1)}, u32[]{:S(2)}, u32[]{:S(2)}) collective-permute-start(bf16[256,2048]{1,0:T(8,128)(2,1)S(1)} %get-tuple-element.340), channel_id=1, source_target_pairs={{0,2},{1,3},{8,10},{9,11},{16,18},{17,19},{24,26},{25,27}} | collective-permute-start | bytes 3145736 | tf_op jit(solution)/shard_map/ppermute | solution.py:55
  375.5 47.7 %collective-permute-start.19 = (bf16[256,2048]{1,0:T(8,128)(2,1)S(1)}, bf16[256,2048]{1,0:T(8,128)(2,1)}, u32[]{:S(2)}, u32[]{:S(2)}) collective-permute-start(bf16[256,2048]{1,0:T(8,128)(2,1)S(1)} %get-tuple-element.339), channel_id=1, source_target_pairs={{6,4},{7,5},{14,12},{15,13},{22,20},{23,21},{30,28},{31,29}} | collective-permute-start | bytes 3145736 | tf_op jit(solution)/shard_map/ppermute | solution.py:58
  383.2 49.0 %copy-start.46 = (bf16[2048]{0:T(1024)(128)(2,1)S(1)}, bf16[2048]{0:T(1024)(128)(2,1)}, u32[]{:S(2)}) copy-start(bf16[2048]{0:T(1024)(128)(2,1)} %param.31) | copy-start | bytes 12292
  383.2 49.0 %copy-start.47 = (bf16[2048]{0:T(1024)(128)(2,1)S(1)}, bf16[2048]{0:T(1024)(128)(2,1)}, u32[]{:S(2)}) copy-start(bf16[2048]{0:T(1024)(128)(2,1)} %param.35) | copy-start | bytes 12292
  426.7 49.9 %collective-permute-start.20 = (bf16[256,2048]{1,0:T(8,128)(2,1)}, bf16[256,2048]{1,0:T(8,128)(2,1)}, u32[]{:S(2)}, u32[]{:S(2)}) collective-permute-start(bf16[256,2048]{1,0:T(8,128)(2,1)} %get-tuple-element.338), channel_id=1, source_target_pairs={{0,2},{2,4},{1,3},{3,5},{8,10},{10,12},{9,11},{11,13},{16,18},{18,... | collective-permute-start | bytes 3145736 | tf_op jit(solution)/shard_map/ppermute | solution.py:55
  428.2 48.9 %collective-permute-start.21 = (bf16[256,2048]{1,0:T(8,128)(2,1)}, bf16[256,2048]{1,0:T(8,128)(2,1)}, u32[]{:S(2)}, u32[]{:S(2)}) collective-permute-start(bf16[256,2048]{1,0:T(8,128)(2,1)} %get-tuple-element.337), channel_id=1, source_target_pairs={{4,2},{6,4},{5,3},{7,5},{12,10},{14,12},{13,11},{15,13},{20,18},{2... | collective-permute-start | bytes 3145736 | tf_op jit(solution)/shard_map/ppermute | solution.py:58
  435.0 42.0 %copy-start.4 = (bf16[1024,768]{1,0:T(8,128)(2,1)S(1)}, bf16[1024,768]{1,0:T(8,128)(2,1)}, u32[]{:S(2)}) copy-start(bf16[1024,768]{1,0:T(8,128)(2,1)} %copy-done.3) | copy-start | bytes 4718596
  480.9 13.3 %copy-start.23 = (bf16[2,256,2048]{2,1,0:T(8,128)(2,1)S(1)}, bf16[2,256,2048]{2,1,0:T(8,128)(2,1)}, u32[]{:S(2)}) copy-start(bf16[2,256,2048]{2,1,0:T(8,128)(2,1)} %param.18) | copy-start | bytes 6291460
  480.9 35.1 %collective-permute-start.23 = (bf16[256,2048]{1,0:T(8,128)(2,1)}, bf16[256,2048]{1,0:T(8,128)(2,1)}, u32[]{:S(2)}, u32[]{:S(2)}) collective-permute-start(bf16[256,2048]{1,0:T(8,128)(2,1)} %add_convert_fusion), channel_id=1, source_target_pairs={{2,0},{4,2},{6,4},{3,1},{5,3},{7,5},{10,8},{12,10},{14,12},{11,9},... | collective-permute-start | bytes 3145736 | tf_op jit(solution)/shard_map/ppermute | solution.py:58
  486.3 29.6 %collective-permute-start.22 = (bf16[256,2048]{1,0:T(8,128)(2,1)}, bf16[256,2048]{1,0:T(8,128)(2,1)S(1)}, u32[]{:S(2)}, u32[]{:S(2)}) collective-permute-start(bf16[256,2048]{1,0:T(8,128)(2,1)} %add_convert_fusion.1), channel_id=1, source_target_pairs={{0,2},{2,4},{4,6},{1,3},{3,5},{5,7},{8,10},{10,12},{12,14},{9,11},... | collective-permute-start | bytes 3145736 | tf_op jit(solution)/shard_map/ppermute | solution.py:55
  490.5 13.7 %all-to-all-start.5 = ((f32[4,1,1792]{2,1,0:T(1,128)}), f32[4,1,1792]{2,1,0:T(1,128)S(1)}, u32[]{:S(2)}, u32[]{:S(2)}) async-start(f32[4,1,1792]{2,1,0:T(1,128)} %broadcast_in_dim.91), calls=%async_computation.6 | async-start | bytes 57344 | tf_op jit(solution)/shard_map/all_to_all | solution.py:39
  494.1 8.7 %copy-start.29 = (bf16[1,256,2048]{2,1,0:T(8,128)(2,1)S(1)}, bf16[1,256,2048]{2,1,0:T(8,128)(2,1)}, u32[]{:S(2)}) copy-start(bf16[1,256,2048]{2,1,0:T(8,128)(2,1)} %reduce-scatter.2.cloned.1.call-done) | copy-start | bytes 3145732
  496.8 51.9 %collective-permute-start.17 = (bf16[1,1,256,2048]{3,2,1,0:T(8,128)(2,1)}, bf16[1,1,256,2048]{3,2,1,0:T(8,128)(2,1)}, u32[]{:S(2)}, u32[]{:S(2)}) collective-permute-start(bf16[1,1,256,2048]{3,2,1,0:T(8,128)(2,1)} %fusion.20), channel_id=1, source_target_pairs={{0,1},{1,0},{2,3},{3,2},{4,5},{5,4},{6,7},{7,6},{8,9},{9,8},{10,11... | collective-permute-start | bytes 3145736 | tf_op jit(solution)/shard_map/ppermute | solution.py:35
  527.2 23.8 %all-to-all-start.6 = ((f32[4,1,7936]{2,1,0:T(1,128)}), f32[4,1,7936]{2,1,0:T(1,128)S(1)}, u32[]{:S(2)}, u32[]{:S(2)}) async-start(f32[4,1,7936]{2,1,0:T(1,128)} %broadcast_in_dim.92), calls=%async_computation.7 | async-start | bytes 253952 | tf_op jit(solution)/shard_map/all_to_all | solution.py:39
  535.6 28.0 %copy-start.31 = (bf16[2,256,2048]{2,1,0:T(8,128)(2,1)S(1)}, bf16[2,256,2048]{2,1,0:T(8,128)(2,1)}, u32[]{:S(2)}) copy-start(bf16[2,256,2048]{2,1,0:T(8,128)(2,1)} %copy-done.30) | copy-start | bytes 6291460
  535.6 28.0 %collective-permute-start.24 = (bf16[1,1,256,2048]{3,2,1,0:T(8,128)(2,1)}, bf16[1,1,256,2048]{3,2,1,0:T(8,128)(2,1)S(1)}, u32[]{:S(2)}, u32[]{:S(2)}) collective-permute-start(bf16[1,1,256,2048]{3,2,1,0:T(8,128)(2,1)} %bitcast.24), channel_id=1, source_target_pairs={{0,1},{1,0},{2,3},{3,2},{4,5},{5,4},{6,7},{7,6},{8,9},{9,8},{10,11... | collective-permute-start | bytes 3145736 | tf_op jit(solution)/shard_map/ppermute | solution.py:35
  551.8 6.6 %all-to-all-start.7 = ((f32[4,1,6144]{2,1,0:T(1,128)}), f32[4,1,6144]{2,1,0:T(1,128)S(1)}, u32[]{:S(2)}, u32[]{:S(2)}) async-start(f32[4,1,6144]{2,1,0:T(1,128)} %broadcast_in_dim.93), calls=%async_computation.8 | async-start | bytes 196608 | tf_op jit(solution)/shard_map/all_to_all | solution.py:39
  558.6 4.5 collective-permute-start.25
  563.8 27.2 %copy-start.32 = (bf16[2,256,2048]{2,1,0:T(8,128)(2,1)}, bf16[2,256,2048]{2,1,0:T(8,128)(2,1)S(1)}, u32[]{:S(2)}) copy-start(bf16[2,256,2048]{2,1,0:T(8,128)(2,1)S(1)} %bitcast_dynamic-update-slice_fusion) | copy-start | bytes 6291460
  (25 other events, 63.3 us)
Sparse Core Ops, SparseCore 0:
  114.9 80.8 all-gather.8
  209.6 76.8 reduce-scatter.1
  288.7 79.2 all-gather.10
  369.4 128.5 all-gather.12
  500.1 84.9 all-gather.14
